TPU v7x, 32 devices: a whole 2x2x4 slice. The times are simulated.
32 devices in a mesh: expert: 4 (over y, x), shard: 8 (over z, core).
Axes of the slice: x: 2, y: 2, z: 4, core: 2. Of those that a mesh axis runs over, the one named last changes fastest.
Arguments:
- tokens_in: bfloat16 [4096, 1536], P(('expert', 'shard')), may hold values from -6 to 6
- output_cotangent: bfloat16 [4096, 1536], P(('expert', 'shard')), may hold values from -6 to 6
- routes: int32 [4096, 8], P(('expert', 'shard')), may hold values from 0 to 39, all different within a row
- doc_ids: int32 [4, 1024], P('expert'), may hold values from 0 to 2, never falling along the last dimension, each value on 1 to 512 neighbouring positions
- picture_starts: int32 [4, 2], P('expert'), may hold values from 0 to 768, as said below
- qkv_weight: bfloat16 [1536, 2560], P('shard'), may hold values from -0.15625 to 0.15625
- out_weight: bfloat16 [1536, 1536], P('shard'), may hold values from -1.5 to 1.5
- router_weight: bfloat16 [1536, 40], P('shard'), may hold values from -0.078125 to 0.078125
- attn_gain: bfloat16 [1536], P('shard'), may hold values from 0.099609375 to 1.8984375
- moe_gain: bfloat16 [1536], P('shard'), may hold values from 0.099609375 to 1.8984375
- gate_up_weight: bfloat16 [1536, 40960], P('shard', 'expert'), may hold values from -0.15625 to 0.15625
- down_weight: bfloat16 [1536, 20480], P('shard', 'expert'), may hold values from -1 to 1
Outputs:
- output: bfloat16 [4096, 1536], P(('expert', 'shard'))
- input_grad: bfloat16 [4096, 1536], P(('expert', 'shard'))
- qkv_weight_grad: float32 [1536, 2560], P('shard')
- out_weight_grad: float32 [1536, 1536], P('shard')
- router_grad: float32 [1536, 40], P('shard')
- attn_gain_grad: float32 [1536], P('shard')
- moe_gain_grad: float32 [1536], P('shard')
- gate_up_grad: float32 [1536, 40960], P('shard', 'expert')
- down_grad: float32 [1536, 20480], P('shard', 'expert')
Inputs may be any that keep to these rules, and one draw needn't show every extreme that they name: `routes`: each token names 8 different experts. `doc_ids`: ids never fall along a sequence; each of the 3 documents holds one position or more. `picture_starts`: piece k of a sequence starts between k * 512 and k * 512 + 256.
All inputs are finite; a program needn't handle non-finite values.
Results may differ from a plain program's by a relative error of at most 0.023.
Values may be sent and summed in bfloat16 or wider, within the bound.
No kernel may reach another device: no remote copies, remote signals or barrier semaphores. Data moves between devices by JAX's collectives and lax.ppermute only.
A program may use at most 384 MiB of HBM per device.

v0:
```python
import jax
import jax.numpy as jnp
from jax import lax
from jax.sharding import PartitionSpec as P

D = 1536
HEADS = 24
KV_HEADS = 8
HEAD_DIM = 64
H = 512
EXPERTS = 40
TOP = 8
PIECE = 256
SLOT = 512
CAP = 32


norm_eps = 1e-06
rope_base = 10000.0
masked_score = -1e30


def rope_tables(positions, head_dim):
    half_dim = head_dim // 2
    frequency = rope_base ** (-2.0 * jnp.arange(half_dim, dtype=jnp.float32) / head_dim)
    angles = positions.astype(jnp.float32)[:, None] * frequency[None, :]
    return (jnp.cos(angles)[:, None, :], jnp.sin(angles)[:, None, :])


def rotate(values, cosine, sine_table):
    half_dim = values.shape[-1] // 2
    first_half = values[..., :half_dim]
    second = values[..., half_dim:]
    return jnp.concatenate(
        [first_half * cosine - second * sine_table, second * cosine + first_half * sine_table], -1
    )


def rotate_back(grad_rows, cosine, sine_table):
    half_dim = grad_rows.shape[-1] // 2
    first_half = grad_rows[..., :half_dim]
    second = grad_rows[..., half_dim:]
    return jnp.concatenate(
        [first_half * cosine + second * sine_table, second * cosine - first_half * sine_table], -1
    )


def rms_norm(values, gain):
    inverse = lax.rsqrt(jnp.mean(values * values, -1, keepdims=True) + norm_eps)
    normal = values * inverse
    return (normal * gain, normal, inverse)


def rms_back(grad_rows, gain, normal, inverse):
    scaled = grad_rows * gain
    grad_in = inverse * (scaled - normal * jnp.mean(scaled * normal, -1, keepdims=True))
    return (grad_in, jnp.sum(grad_rows * normal, 0))


def picture_ids(positions, starts, slot_len, piece_len):
    slot_index = positions // slot_len
    picked_slot = slot_index[:, None] == jnp.arange(starts.shape[0], dtype=jnp.int32)[None, :]
    piece_begin = jnp.sum(jnp.where(picked_slot, starts[None, :], 0), axis=1)
    inside = (positions >= piece_begin) & (positions < piece_begin + piece_len)
    return jnp.where(inside, slot_index, -1)


def allowed(query_pos, key_pos, query_doc, key_doc, query_pic, key_pic):
    same_doc = query_doc[:, None] == key_doc[None, :]
    earlier = key_pos[None, :] <= query_pos[:, None]
    same_pic = (query_pic[:, None] == key_pic[None, :]) & (query_pic[:, None] >= 0)
    return same_doc & (earlier | same_pic)


def local(
    tokens_in,
    output_cotangent,
    routes,
    doc_ids,
    picture_starts,
    qkv_weight,
    out_weight,
    router_weight,
    attn_gain,
    moe_gain,
    gate_up_weight,
    down_weight,
):
    qkv_full, out_full, router_full, gain_first, gain_second = (
        lax.all_gather(qkv_weight, "shard", axis=0, tiled=True),
        lax.all_gather(out_weight, "shard", axis=0, tiled=True),
        lax.all_gather(router_weight, "shard", axis=0, tiled=True),
        lax.all_gather(attn_gain, "shard", axis=0, tiled=True),
        lax.all_gather(moe_gain, "shard", axis=0, tiled=True),
    )
    gain_one = gain_first.astype(jnp.float32)
    gain_two = gain_second.astype(jnp.float32)
    tok_rows = tokens_in.shape[0]
    seq_len = doc_ids.shape[1]
    groups = HEADS // KV_HEADS
    q_width = HEADS * HEAD_DIM
    kv_width = KV_HEADS * HEAD_DIM
    score_scale = HEAD_DIM ** (-0.5)
    shard_at = lax.axis_index("shard")
    query_pos = shard_at * tok_rows + jnp.arange(tok_rows, dtype=jnp.int32)
    key_pos = jnp.arange(seq_len, dtype=jnp.int32)
    key_doc = doc_ids[0]
    key_pic = picture_ids(key_pos, picture_starts[0], SLOT, PIECE)
    query_doc = lax.dynamic_slice_in_dim(key_doc, shard_at * tok_rows, tok_rows)
    query_pic = lax.dynamic_slice_in_dim(key_pic, shard_at * tok_rows, tok_rows)
    tokens_f = tokens_in.astype(jnp.float32)
    normed_one, normal_one, inverse_one = rms_norm(tokens_f, gain_one)
    normed_in = normed_one.astype(jnp.bfloat16)
    qkv_rows = jnp.dot(normed_in, qkv_full, preferred_element_type=jnp.float32)
    cosine, sine_table = rope_tables(query_pos, HEAD_DIM)
    queries = (
        rotate(qkv_rows[:, :q_width].reshape(tok_rows, HEADS, HEAD_DIM), cosine, sine_table)
        .astype(jnp.bfloat16)
        .reshape(tok_rows, KV_HEADS, groups, HEAD_DIM)
    )
    key_local = (
        rotate(
            qkv_rows[:, q_width : q_width + kv_width].reshape(tok_rows, KV_HEADS, HEAD_DIM),
            cosine,
            sine_table,
        )
        .astype(jnp.bfloat16)
        .reshape(tok_rows, kv_width)
    )
    value_local = qkv_rows[:, q_width + kv_width :].astype(jnp.bfloat16)
    all_keys, all_values = (
        lax.all_gather(key_local, "shard", axis=0, tiled=True),
        lax.all_gather(value_local, "shard", axis=0, tiled=True),
    )
    span_len = min(512, seq_len)
    span_count = seq_len // span_len

    def block_scores(first_row, key_rows):
        key_block = lax.dynamic_slice_in_dim(key_rows, first_row, span_len, 0).reshape(
            span_len, KV_HEADS, HEAD_DIM
        )
        raw_scores = (
            jnp.einsum("tgrd,kgd->tgrk", queries, key_block, preferred_element_type=jnp.float32)
            * score_scale
        )
        block_pos = lax.dynamic_slice_in_dim(key_pos, first_row, span_len)
        block_doc = lax.dynamic_slice_in_dim(key_doc, first_row, span_len)
        block_pic = lax.dynamic_slice_in_dim(key_pic, first_row, span_len)
        visible = allowed(query_pos, block_pos, query_doc, block_doc, query_pic, block_pic)[
            :, None, None, :
        ]
        return (raw_scores, visible, key_block)

    def value_block_at(first_row, value_rows):
        return lax.dynamic_slice_in_dim(value_rows, first_row, span_len, 0).reshape(
            span_len, KV_HEADS, HEAD_DIM
        )

    def max_step(step_index, carry):
        run_max, run_sum = carry
        raw_scores, visible, key_block = block_scores(step_index * span_len, all_keys)
        masked = jnp.where(visible, raw_scores, masked_score)
        new_max = jnp.maximum(run_max, jnp.max(masked, -1))
        shifted = jnp.where(visible, jnp.exp(masked - new_max[..., None]), 0.0)
        return (new_max, run_sum * jnp.exp(run_max - new_max) + jnp.sum(shifted, -1))

    stat_shape = (tok_rows, KV_HEADS, groups)
    run_max, run_sum = lax.fori_loop(
        0,
        span_count,
        max_step,
        (jnp.full(stat_shape, masked_score, jnp.float32), jnp.zeros(stat_shape, jnp.float32)),
    )
    log_total = run_max + jnp.log(run_sum)

    def probs_of(raw_scores, visible):
        return jnp.exp(jnp.where(visible, raw_scores - log_total[..., None], masked_score))

    def value_step(step_index, summed):
        first_row = step_index * span_len
        raw_scores, visible, key_block = block_scores(first_row, all_keys)
        probs = probs_of(raw_scores, visible).astype(jnp.bfloat16)
        return summed + jnp.einsum(
            "tgrk,kgd->tgrd",
            probs,
            value_block_at(first_row, all_values),
            preferred_element_type=jnp.float32,
        )

    summed = lax.fori_loop(
        0, span_count, value_step, jnp.zeros((tok_rows, KV_HEADS, groups, HEAD_DIM), jnp.float32)
    )
    attended = summed.reshape(tok_rows, q_width).astype(jnp.bfloat16)
    branch = lax.dot_general(
        attended, out_full, (((1,), (1,)), ((), ())), preferred_element_type=jnp.float32
    )
    middle = tokens_f + branch
    normed_two, normal_two, inverse_two = rms_norm(middle, gain_two)
    normed_mid = normed_two.astype(jnp.bfloat16)
    logits = jnp.dot(normed_mid, router_full, preferred_element_type=jnp.float32)
    gates = jax.nn.softmax(jnp.take_along_axis(logits, routes, 1), axis=-1)
    route_hits = routes[:, :, None] == jnp.arange(EXPERTS, dtype=jnp.int32)[None, None, :]
    hit_count = jnp.sum(route_hits.astype(jnp.int32), 1)
    before = jnp.cumsum(hit_count, 0) - hit_count
    slot_index = jnp.take_along_axis(before, routes, 1)
    kept_pair = slot_index < CAP
    flat_slot = routes * CAP + slot_index
    capacity_rows = EXPERTS * CAP
    target = jnp.where(kept_pair, flat_slot, capacity_rows)
    token_ids = jnp.broadcast_to(jnp.arange(tok_rows, dtype=jnp.int32)[:, None], (tok_rows, TOP))
    owner_row = (
        jnp.full((capacity_rows + 1,), -1, jnp.int32)
        .at[target.reshape(-1)]
        .set(token_ids.reshape(-1))[:capacity_rows]
    )
    filled = owner_row >= 0
    source_row = jnp.maximum(owner_row, 0)
    expert_groups = lax.axis_size("expert")
    local_experts = EXPERTS // expert_groups
    send_rows = jnp.where(
        filled[:, None], normed_mid[source_row], jnp.zeros((), jnp.bfloat16)
    ).reshape(expert_groups, local_experts, CAP, D)
    received = lax.all_to_all(send_rows, "expert", split_axis=0, concat_axis=0, tiled=True)
    gate_up_full, down_full = (
        lax.all_gather(gate_up_weight, "shard", axis=0, tiled=True),
        lax.all_gather(down_weight, "shard", axis=0, tiled=True),
    )
    gate_up3 = gate_up_full.reshape(D, local_experts, 2 * H)
    down3 = down_full.reshape(D, local_experts, H)
    projected = jnp.einsum("secd,dej->secj", received, gate_up3, preferred_element_type=jnp.float32)
    gate_part = projected[..., :H]
    up_part = projected[..., H:]
    sigma = jax.nn.sigmoid(gate_part)
    silu_value = gate_part * sigma
    hidden = (silu_value * up_part).astype(jnp.bfloat16)
    expert_out = jnp.einsum(
        "secj,dej->secd", hidden, down3, preferred_element_type=jnp.float32
    ).astype(jnp.bfloat16)
    returned = lax.all_to_all(
        expert_out, "expert", split_axis=0, concat_axis=0, tiled=True
    ).reshape(capacity_rows, D)
    safe_flat = jnp.where(kept_pair, flat_slot, 0)
    picked = returned[safe_flat].astype(jnp.float32)
    pair_weight = jnp.where(kept_pair, gates, 0.0)
    moe_sum = jnp.einsum("tk,tkd->td", pair_weight, picked)
    output = (middle + moe_sum).astype(jnp.bfloat16)
    grad_out = output_cotangent.astype(jnp.float32)
    gate_grad = jnp.where(kept_pair, jnp.einsum("td,tkd->tk", grad_out, picked), 0.0)
    slot_gate = (
        jnp.zeros((capacity_rows + 1,), jnp.float32)
        .at[target.reshape(-1)]
        .set(gates.reshape(-1))[:capacity_rows]
    )
    grad_send = (
        jnp.where(filled[:, None], slot_gate[:, None] * grad_out[source_row], 0.0)
        .astype(jnp.bfloat16)
        .reshape(expert_groups, local_experts, CAP, D)
    )
    grad_received = lax.all_to_all(grad_send, "expert", split_axis=0, concat_axis=0, tiled=True)
    keys_back, values_back = (
        lax.all_gather(key_local, "shard", axis=0, tiled=True),
        lax.all_gather(value_local, "shard", axis=0, tiled=True),
    )
    again_up, again_down = (
        lax.all_gather(gate_up_weight, "shard", axis=0, tiled=True),
        lax.all_gather(down_weight, "shard", axis=0, tiled=True),
    )
    gate_up_back = again_up.reshape(D, local_experts, 2 * H)
    down_back = again_down.reshape(D, local_experts, H)
    hidden_grad = jnp.einsum(
        "secd,dej->secj", grad_received, down_back, preferred_element_type=jnp.float32
    )
    silu_slope = sigma * (1.0 + gate_part * (1.0 - sigma))
    proj_grad = jnp.concatenate(
        [hidden_grad * up_part * silu_slope, hidden_grad * silu_value], -1
    ).astype(jnp.bfloat16)
    row_grad = jnp.einsum(
        "secj,dej->secd", proj_grad, gate_up_back, preferred_element_type=jnp.float32
    ).astype(jnp.bfloat16)
    grad_back = lax.all_to_all(row_grad, "expert", split_axis=0, concat_axis=0, tiled=True).reshape(
        capacity_rows, D
    )
    row_count = gate_up_weight.shape[0] * lax.axis_size("shard")
    up_terms = jnp.einsum(
        "secd,secj->dej", received, proj_grad, preferred_element_type=jnp.float32
    ).reshape(row_count, local_experts * 2 * H)
    down_terms = jnp.einsum(
        "secd,secj->dej", grad_received, hidden, preferred_element_type=jnp.float32
    ).reshape(row_count, local_experts * H)
    expert_sums = lax.psum_scatter(
        jnp.concatenate([up_terms, down_terms], 1).astype(jnp.bfloat16),
        "shard",
        scatter_dimension=0,
        tiled=True,
    ).astype(jnp.float32)
    gate_up_grad = expert_sums[:, : local_experts * 2 * H]
    down_grad = expert_sums[:, local_experts * 2 * H :]
    mid_norm_grad = jnp.einsum(
        "tk,tkd->td", kept_pair.astype(jnp.float32), grad_back[safe_flat].astype(jnp.float32)
    )
    chosen_grad = gates * (gate_grad - jnp.sum(gates * gate_grad, -1, keepdims=True))
    logit_grad = jnp.sum(jnp.where(route_hits, chosen_grad[:, :, None], 0.0), 1).astype(
        jnp.bfloat16
    )
    mid_norm_grad = mid_norm_grad + lax.dot_general(
        logit_grad, router_full, (((1,), (1,)), ((), ())), preferred_element_type=jnp.float32
    )
    router_grad = lax.dot_general(
        normed_mid, logit_grad, (((0,), (0,)), ((), ())), preferred_element_type=jnp.float32
    )
    mid_part, moe_gain_grad = rms_back(mid_norm_grad, gain_two, normal_two, inverse_two)
    mid_grad = grad_out + mid_part
    branch_grad = mid_grad.astype(jnp.bfloat16)
    out_weight_grad = lax.dot_general(
        branch_grad, attended, (((0,), (0,)), ((), ())), preferred_element_type=jnp.float32
    )
    attended_grad = (
        jnp.dot(branch_grad, out_full, preferred_element_type=jnp.float32)
        .astype(jnp.bfloat16)
        .reshape(tok_rows, KV_HEADS, groups, HEAD_DIM)
    )

    def dot_step(step_index, row_dot):
        first_row = step_index * span_len
        raw_scores, visible, key_block = block_scores(first_row, keys_back)
        prob_full = probs_of(raw_scores, visible)
        prob_grad = jnp.einsum(
            "tgrd,kgd->tgrk",
            attended_grad,
            value_block_at(first_row, values_back),
            preferred_element_type=jnp.float32,
        )
        return row_dot + jnp.sum(prob_full * prob_grad, -1)

    row_dot = lax.fori_loop(0, span_count, dot_step, jnp.zeros(stat_shape, jnp.float32))

    def grad_step(step_index, carry):
        query_grad, key_terms, value_terms = carry
        first_row = step_index * span_len
        raw_scores, visible, key_block = block_scores(first_row, keys_back)
        prob_full = probs_of(raw_scores, visible)
        prob_grad = jnp.einsum(
            "tgrd,kgd->tgrk",
            attended_grad,
            value_block_at(first_row, values_back),
            preferred_element_type=jnp.float32,
        )
        score_grad = (prob_full * (prob_grad - row_dot[..., None])).astype(jnp.bfloat16)
        query_grad = query_grad + jnp.einsum(
            "tgrk,kgd->tgrd", score_grad, key_block, preferred_element_type=jnp.float32
        )
        key_part = (
            jnp.einsum(
                "tgrk,tgrd->kgd", score_grad, queries, preferred_element_type=jnp.float32
            ).reshape(span_len, kv_width)
            * score_scale
        )
        value_part = jnp.einsum(
            "tgrk,tgrd->kgd",
            prob_full.astype(jnp.bfloat16),
            attended_grad,
            preferred_element_type=jnp.float32,
        ).reshape(span_len, kv_width)
        key_terms = lax.dynamic_update_slice_in_dim(key_terms, key_part, first_row, 0)
        value_terms = lax.dynamic_update_slice_in_dim(value_terms, value_part, first_row, 0)
        return (query_grad, key_terms, value_terms)

    query_grad, key_terms, value_terms = lax.fori_loop(
        0,
        span_count,
        grad_step,
        (
            jnp.zeros((tok_rows, KV_HEADS, groups, HEAD_DIM), jnp.float32),
            jnp.zeros((seq_len, kv_width), jnp.float32),
            jnp.zeros((seq_len, kv_width), jnp.float32),
        ),
    )
    key_grad, value_grad = (
        lax.psum_scatter(
            key_terms.astype(jnp.bfloat16), "shard", scatter_dimension=0, tiled=True
        ).astype(jnp.float32),
        lax.psum_scatter(
            value_terms.astype(jnp.bfloat16), "shard", scatter_dimension=0, tiled=True
        ).astype(jnp.float32),
    )
    query_back = rotate_back(
        (query_grad * score_scale).reshape(tok_rows, HEADS, HEAD_DIM), cosine, sine_table
    ).reshape(tok_rows, q_width)
    key_back = rotate_back(
        key_grad.reshape(tok_rows, KV_HEADS, HEAD_DIM), cosine, sine_table
    ).reshape(tok_rows, kv_width)
    qkv_grad_rows = jnp.concatenate([query_back, key_back, value_grad], 1).astype(jnp.bfloat16)
    qkv_weight_grad = lax.dot_general(
        normed_in, qkv_grad_rows, (((0,), (0,)), ((), ())), preferred_element_type=jnp.float32
    )
    in_norm_grad = lax.dot_general(
        qkv_grad_rows, qkv_full, (((1,), (1,)), ((), ())), preferred_element_type=jnp.float32
    )
    in_part, attn_gain_grad = rms_back(in_norm_grad, gain_one, normal_one, inverse_one)
    input_grad = (mid_grad + in_part).astype(jnp.bfloat16)
    dense_sums = (
        lax.psum_scatter(
            qkv_weight_grad.astype(jnp.bfloat16), "shard", scatter_dimension=0, tiled=True
        ).astype(jnp.float32),
        lax.psum_scatter(
            out_weight_grad.astype(jnp.bfloat16), "shard", scatter_dimension=0, tiled=True
        ).astype(jnp.float32),
        lax.psum_scatter(
            router_grad.astype(jnp.bfloat16), "shard", scatter_dimension=0, tiled=True
        ).astype(jnp.float32),
        lax.psum_scatter(
            attn_gain_grad.astype(jnp.bfloat16), "shard", scatter_dimension=0, tiled=True
        ).astype(jnp.float32),
        lax.psum_scatter(
            moe_gain_grad.astype(jnp.bfloat16), "shard", scatter_dimension=0, tiled=True
        ).astype(jnp.float32),
    )
    dense_totals = (
        lax.psum(dense_sums[0].astype(jnp.bfloat16), "expert").astype(jnp.float32),
        lax.psum(dense_sums[1].astype(jnp.bfloat16), "expert").astype(jnp.float32),
        lax.psum(dense_sums[2].astype(jnp.bfloat16), "expert").astype(jnp.float32),
        lax.psum(dense_sums[3].astype(jnp.bfloat16), "expert").astype(jnp.float32),
        lax.psum(dense_sums[4].astype(jnp.bfloat16), "expert").astype(jnp.float32),
    )
    return (
        output,
        input_grad,
        dense_totals[0],
        dense_totals[1],
        dense_totals[2],
        dense_totals[3],
        dense_totals[4],
        gate_up_grad,
        down_grad,
    )


def solution(mesh):
    return jax.shard_map(
        local,
        mesh=mesh,
        in_specs=(
            P(("expert", "shard"), None),
            P(("expert", "shard"), None),
            P(("expert", "shard"), None),
            P("expert", None),
            P("expert", None),
            P("shard", None),
            P("shard", None),
            P("shard", None),
            P("shard"),
            P("shard"),
            P("shard", "expert"),
            P("shard", "expert"),
        ),
        out_specs=(
            P(("expert", "shard"), None),
            P(("expert", "shard"), None),
            P("shard", None),
            P("shard", None),
            P("shard", None),
            P("shard"),
            P("shard"),
            P("shard", "expert"),
            P("shard", "expert"),
        ),
        check_vma=False,
    )
```

profile of v0, /device:TPU:0, one launch (start us, length us, event | category | flops | bytes accessed | tf_op | source)
XLA Modules:
  0.0 1703.3 jit_solution(16371379552660737625)
XLA Ops:
  11.7 18.8 %all-reduce.5 = (bf16[1536]{0:T(1024)(128)(2,1)S(1)}, bf16[1536]{0:T(1024)(128)(2,1)S(1)}) all-reduce(bf16[1536]{0:T(1024)(128)(2,1)S(1)} %dynamic-update-slice, bf16[1536]{0:T(1024)(128)(2,1)S(1)} %dynamic-update-slice.1), channel_id=1, replica_groups=mesh['expert'=4,'shard'=8] {'shard'}, use_global_device_ids=true, to_apply=%add | all-reduce | flops 3072 | bytes 12288
  31.7 58.6 %all-gather.8.cloned.1.call-done = bf16[1536,2560]{1,0:T(8,128)(2,1)} async-done(((bf16[192,2560]{1,0:T(8,128)(2,1)}), bf16[1536,2560]{1,0:T(8,128)(2,1)}) %all-gather.8.cloned.1.call-update) | async-done | bytes 7864336 | tf_op jit(solution)/shard_map/all_gather | solution.py:90
  118.0 24.2 %all-gather.12.cloned.1.call-done = bf16[1024,512]{0,1:T(8,128)(2,1)} async-done(((bf16[128,512]{0,1:T(8,128)(2,1)}), bf16[1024,512]{0,1:T(8,128)(2,1)}) %all-gather.12.cloned.1.call-update) | async-done | bytes 1048592 | tf_op jit(solution)/shard_map/all_gather | solution.py:132
  162.9 31.2 %all-gather.14.cloned.1.call-done = bf16[1536,1536]{1,0:T(8,128)(2,1)} async-done(((bf16[192,1536]{1,0:T(8,128)(2,1)}), bf16[1536,1536]{1,0:T(8,128)(2,1)}) %all-gather.14.cloned.1.call-update) | async-done | bytes 4718608 | tf_op jit(solution)/shard_map/all_gather | solution.py:91
  215.2 121.8 %all-gather.18.cloned.1.call-done = bf16[1536,5120]{1,0:T(8,128)(2,1)} async-done(((bf16[192,5120]{1,0:T(8,128)(2,1)}), bf16[1536,5120]{1,0:T(8,128)(2,1)}) %all-gather.18.cloned.1.call-update) | async-done | bytes 15728656 | tf_op jit(solution)/shard_map/all_gather | solution.py:226
  336.9 21.1 %copy.163 = bf16[1536,5120]{0,1:T(8,128)(2,1)} copy(bf16[1536,5120]{1,0:T(8,128)(2,1)} %all-gather.18.cloned.1.call-done) | data formatting | bytes 31457280 | tf_op jit(solution)/shard_map/all_gather | solution.py:226
  358.0 250.1 %all-gather.16.cloned.1.call-done = bf16[1536,10240]{1,0:T(8,128)(2,1)} async-done(((bf16[192,10240]{1,0:T(8,128)(2,1)}), bf16[1536,10240]{1,0:T(8,128)(2,1)}) %all-gather.16.cloned.1.call-update) | async-done | bytes 31457296 | tf_op jit(solution)/shard_map/all_gather | solution.py:225
  608.1 40.6 %copy.160 = bf16[1536,10240]{0,1:T(8,128)(2,1)} copy(bf16[1536,10240]{1,0:T(8,128)(2,1)} %all-gather.16.cloned.1.call-done) | data formatting | bytes 62914560 | tf_op jit(solution)/shard_map/all_gather | solution.py:225
  648.7 18.2 %fusion.59 = f32[4,10,32,1024]{3,2,0,1:T(8,128)} fusion(bf16[1536,10,1024,1]{0,2,3,1:T(8,128)(2,1)} %bitcast.318, bf16[4,10,32,1536]{3,2,1,0:T(8,128)(2,1)} %all-to-all-done), kind=kOutput, calls=%fused_computation.105 | convolution fusion | flops 4026531840 | bytes 40632320 | tf_op jit(solution)/shard_map/secd,dej->secj/dot_general | solution.py:230
  713.6 17.4 %all-to-all-done.1 = bf16[4,10,32,1536]{3,2,1,0:T(8,128)(2,1)} async-done(((bf16[4,10,32,1536]{3,2,1,0:T(8,128)(2,1)}), bf16[4,10,32,1536]{3,2,1,0:T(8,128)(2,1)}, u32[]{:S(2)}, u32[]{:S(2)}) %all-to-all-start.1) | async-done | bytes 3932192 | tf_op jit(solution)/shard_map/all_to_all | solution.py:239
  752.2 48.3 %all_to_all.20 = bf16[4,10,32,1536]{3,2,1,0:T(8,128)(2,1)} all-to-all(bf16[4,10,32,1536]{3,2,1,0:T(8,128)(2,1)S(1)} %select_convert_fusion), channel_id=1, replica_groups=mesh['expert'=4,'shard'=8] {'expert'}, dimensions={0} | all-to-all | bytes 7864320 | tf_op jit(solution)/shard_map/all_to_all | solution.py:259
  811.4 17.1 %fusion.42 = bf16[4,10,32,1536]{3,2,0,1:T(8,128)(2,1)} fusion(bf16[1536,10,1024,1]{0,2,3,1:T(8,128)(2,1)} %bitcast.319, bf16[4,10,32,512]{3,2,0,1:T(8,128)(2,1)S(1)} %get-tuple-element.1391, bf16[4,10,32,512]{3,2,0,1:T(8,128)(2,1)S(1)} %get-tuple-element.1390), kind=kOutput, calls=%fused_computation.81 | convolution fusion | flops 4033740800 | bytes 38010880 | tf_op jit(solution)/shard_map/secj,dej->secd/dot_general | solution.py:277
  841.7 39.5 %all-to-all-done.3 = bf16[4,10,32,1536]{3,2,1,0:T(8,128)(2,1)} async-done(((bf16[4,10,32,1536]{3,2,1,0:T(8,128)(2,1)}), bf16[4,10,32,1536]{3,2,1,0:T(8,128)(2,1)}, u32[]{:S(2)}, u32[]{:S(2)}) %all-to-all-start.3) | async-done | bytes 3932192 | tf_op jit(solution)/shard_map/all_to_all | solution.py:280
  912.6 17.8 %while.65 = (s32[]{:T(128)}, f32[128,8,3,64]{0,3,2,1:T(8,128)S(1)}, bf16[1024,512]{0,1:T(8,128)(2,1)}, bf16[1024,512]{0,1:T(8,128)(2,1)}, bf16[1024,512]{0,1:T(8...) while((s32[]{:T(128)}, f32[128,8,3,64]{0,3,2,1:T(8,128)S(1)}, ...), condition=%wide.region_22.23_spmd.clone, body=%wide.region_21.22_spmd.clone.sunk | while | flops 1023672576 | bytes 56878236 | solution.py:368
  939.7 22.8 %reduce-scatter.19.cloned.1.call-done = bf16[128,512]{1,0:T(8,128)(2,1)} async-done(((bf16[1024,512]{1,0:T(8,128)(2,1)}), bf16[128,512]{1,0:T(8,128)(2,1)}) %reduce-scatter.19.cloned.1.call-update) | async-done | bytes 131088
  963.5 32.6 %reduce-scatter.21.cloned.1.call-done = bf16[128,512]{1,0:T(8,128)(2,1)} async-done(((bf16[1024,512]{1,0:T(8,128)(2,1)}), bf16[128,512]{1,0:T(8,128)(2,1)}) %reduce-scatter.21.cloned.1.call-update) | async-done | bytes 131088
  1005.0 16.4 bitcast_convert_fusion
  1031.3 20.8 %copy.178 = bf16[1536,5120]{1,0:T(8,128)(2,1)} copy(bf16[1536,5120]{0,1:T(8,128)(2,1)} %bitcast.330) | data formatting | bytes 31457280 | tf_op jit(solution)/shard_map/reshape | solution.py:289
  1052.1 37.3 %copy.177 = bf16[1536,10240]{1,0:T(8,128)(2,1)} copy(bf16[1536,10240]{0,1:T(8,128)(2,1)} %bitcast.328) | data formatting | bytes 62914560 | tf_op jit(solution)/shard_map/reshape | solution.py:286
  1089.4 48.0 %reduce-scatter.13.cloned.1.call-done = bf16[192,2560]{1,0:T(8,128)(2,1)} async-done(((bf16[1536,2560]{1,0:T(8,128)(2,1)}), bf16[192,2560]{1,0:T(8,128)(2,1)}) %reduce-scatter.13.cloned.1.call-update) | async-done | bytes 983056 | tf_op jit(solution)/shard_map/reduce_scatter | solution.py:402
  1137.5 31.8 %pad_maximum_fusion = bf16[1536,15360]{1,0:T(8,128)(2,1)} fusion(bf16[1536,5120]{1,0:T(8,128)(2,1)} %copy.178, bf16[1536,10240]{1,0:T(8,128)(2,1)} %copy.177), kind=kLoop, calls=%fused_computation.72 | loop fusion | flops 94371840 | bytes 94371840 | tf_op jit(solution)/shard_map/concatenate | solution.py:291
  1191.0 16.8 all-reduce.6
  1210.7 21.7 %all-reduce.10.cloned.1.call-done = (bf16[192,2560]{1,0:T(8,128)(2,1)}, bf16[192,1536]{1,0:T(8,128)(2,1)}) async-done(((bf16[192,2560]{1,0:T(8,128)(2,1)}, bf16[192,1536]{1,0:T(8,128)(2,1)}), (bf16[192,2560]{1,0:T(8,128)(2,1)}, bf16[192,1536]{1,0:T(8,128)(2,1)})) %all-reduce.10.cloned.1.call-update) | async-done | bytes 1572880 | tf_op jit(solution)/shard_map/psum | solution.py:419
  1237.3 451.1 %reduce-scatter.17.cloned.1.call-done = bf16[192,15360]{1,0:T(8,128)(2,1)} async-done(((bf16[1536,15360]{1,0:T(8,128)(2,1)}), bf16[192,15360]{1,0:T(8,128)(2,1)}) %reduce-scatter.17.cloned.1.call-update) | async-done | bytes 5898256 | tf_op jit(solution)/shard_map/reduce_scatter | solution.py:290
  (398 shorter events, 305.9 us)
Async XLA Ops:
  7.2 83.1 %all-gather.8.cloned.1.call-start = ((), (), s32[]{:S(2)}) async-start(), calls=%async_computation.10 | async-start | bytes 8847360 | tf_op jit(solution)/shard_map/all_gather | solution.py:90
  7.9 108.6 %all-gather.10.cloned.1.call-start = ((), (), s32[]{:S(2)}) async-start(), calls=%async_computation.11 | async-start | bytes 1179648 | tf_op jit(solution)/shard_map/all_gather | solution.py:133
  30.5 64.4 %copy-start.36 = (f32[1536]{0:T(1024)}, f32[1536]{0:T(1024)S(1)}, u32[]{:S(2)}) copy-start(f32[1536]{0:T(1024)S(1)} %convert_element_type.155) | copy-start | bytes 18436
  31.7 63.3 %copy-start.56 = (f32[128]{0:T(128)}, f32[128]{0:T(128)S(1)}, u32[]{:S(2)}) copy-start(f32[128]{0:T(128)S(1)} %add_rsqrt_fusion.1) | copy-start | bytes 1540
  95.7 46.6 %all-gather.12.cloned.1.call-start = ((), (), s32[]{:S(2)}) async-start(), calls=%async_computation.12 | async-start | bytes 1179648 | tf_op jit(solution)/shard_map/all_gather | solution.py:132
  96.8 97.3 %all-gather.14.cloned.1.call-start = ((), (), s32[]{:S(2)}) async-start(), calls=%async_computation.13 | async-start | bytes 5308416 | tf_op jit(solution)/shard_map/all_gather | solution.py:91
  97.4 239.6 %all-gather.18.cloned.1.call-start = ((), (), s32[]{:S(2)}) async-start(), calls=%async_computation.15 | async-start | bytes 17694720 | tf_op jit(solution)/shard_map/all_gather | solution.py:226
  98.0 510.2 %all-gather.16.cloned.1.call-start = ((), (), s32[]{:S(2)}) async-start(), calls=%async_computation.14 | async-start | bytes 35389440 | tf_op jit(solution)/shard_map/all_gather | solution.py:225
  98.6 99.6 %copy-start.44 = (f32[1536]{0:T(1024)}, f32[1536]{0:T(1024)S(1)}, u32[]{:S(2)}) copy-start(f32[1536]{0:T(1024)S(1)} %convert_element_type.162) | copy-start | bytes 18436
  199.3 506.9 %copy-start = (bf16[128,1536]{1,0:T(8,128)(2,1)}, bf16[128,1536]{1,0:T(8,128)(2,1)S(1)}, u32[]{:S(2)}) copy-start(bf16[128,1536]{1,0:T(8,128)(2,1)S(1)} %multiply_convert_fusion.1) | copy-start | bytes 1179652
  210.2 438.5 %all-to-all-start = ((bf16[4,10,32,1536]{3,2,1,0:T(8,128)(2,1)}), bf16[4,10,32,1536]{3,2,1,0:T(8,128)(2,1)}, u32[]{:S(2)}, u32[]{:S(2)}) async-start(bf16[4,10,32,1536]{3,2,1,0:T(8,128)(2,1)} %broadcast_select_fusion), calls=%async_computation | async-start | bytes 7864320 | tf_op jit(solution)/shard_map/all_to_all | solution.py:223
  680.7 50.3 %all-to-all-start.1 = ((bf16[4,10,32,1536]{3,2,1,0:T(8,128)(2,1)}), bf16[4,10,32,1536]{3,2,1,0:T(8,128)(2,1)}, u32[]{:S(2)}, u32[]{:S(2)}) async-start(bf16[4,10,32,1536]{3,2,1,0:T(8,128)(2,1)} %copy.165), calls=%async_computation.1 | async-start | bytes 7864320 | tf_op jit(solution)/shard_map/all_to_all | solution.py:239
  833.0 48.1 %all-to-all-start.3 = ((bf16[4,10,32,1536]{3,2,1,0:T(8,128)(2,1)}), bf16[4,10,32,1536]{3,2,1,0:T(8,128)(2,1)}, u32[]{:S(2)}, u32[]{:S(2)}) async-start(bf16[4,10,32,1536]{3,2,1,0:T(8,128)(2,1)} %copy.171), calls=%async_computation.3 | async-start | bytes 7864320 | tf_op jit(solution)/shard_map/all_to_all | solution.py:280
  838.0 124.4 %reduce-scatter.19.cloned.1.call-start = ((), (), s32[]{:S(2)}) async-start(), calls=%async_computation.19 | async-start | bytes 1179648
  838.8 55.2 %copy-start.48 = (bf16[128,40]{0,1:T(8,128)(2,1)}, bf16[128,40]{0,1:T(8,128)(2,1)S(1)}, u32[]{:S(2)}) copy-start(bf16[128,40]{0,1:T(8,128)(2,1)S(1)} %select_reduce_fusion.1) | copy-start | bytes 30724
  932.8 63.3 %reduce-scatter.21.cloned.1.call-start = ((), (), s32[]{:S(2)}) async-start(), calls=%async_computation.20 | async-start | bytes 1179648
  935.1 154.3 %reduce-scatter.15.cloned.1.call-start = ((), (), s32[]{:S(2)}) async-start(), calls=%async_computation.17 | async-start | bytes 5308416 | tf_op jit(solution)/shard_map/reduce_scatter | solution.py:405
  938.8 58.4 %copy-start.11 = (bf16[128,1536]{1,0:T(8,128)(2,1)S(1)}, bf16[128,1536]{1,0:T(8,128)(2,1)}, u32[]{:S(2)}) copy-start(bf16[128,1536]{1,0:T(8,128)(2,1)} %param.20) | copy-start | bytes 1179652
  938.8 58.4 %copy-start.37 = (f32[1536]{0:T(1024)S(1)}, f32[1536]{0:T(1024)}, u32[]{:S(2)}) copy-start(f32[1536]{0:T(1024)} %copy-done.36) | copy-start | bytes 18436
  938.8 58.4 %copy-start.57 = (f32[128]{0:T(128)S(1)}, f32[128]{0:T(128)}, u32[]{:S(2)}) copy-start(f32[128]{0:T(128)} %copy-done.56) | copy-start | bytes 1540
  938.8 198.6 %reduce-scatter.13.cloned.1.call-start = ((), (), s32[]{:S(2)}) async-start(), calls=%async_computation.16 | async-start | bytes 8847360 | tf_op jit(solution)/shard_map/reduce_scatter | solution.py:402
  1002.8 167.1 %reduce-scatter.23.cloned.1.call-start = ((), (), s32[]{:S(2)}) async-start(), calls=%async_computation.21 | async-start | bytes 442368
  1004.9 227.5 %all-reduce.10.cloned.1.call-start = ((), (), s32[]{:S(2)}) async-start(), calls=%async_computation.22 | async-start | bytes 3145728 | tf_op jit(solution)/shard_map/psum | solution.py:419
  1137.5 550.9 %reduce-scatter.17.cloned.1.call-start = ((), (), s32[]{:S(2)}) async-start(), calls=%async_computation.18 | async-start | bytes 53084160 | tf_op jit(solution)/shard_map/reduce_scatter | solution.py:290
  (60 other events, 643.0 us)
Sparse Core Ops, SparseCore 0:
  9.7 80.5 all-gather.7
  95.8 20.7 all-gather.9
  118.7 23.4 all-gather.11
  143.7 50.3 all-gather.13
  195.6 141.3 all-gather.17
  338.4 269.6 all-gather.15
  932.9 29.4 reduce-scatter.18
  965.3 30.7 reduce-scatter.20
  998.4 53.2 reduce-scatter.14
  1054.4 82.9 reduce-scatter.12
  1140.3 28.9 reduce-scatter.22
  1172.6 59.7 all-reduce.9
  1234.8 453.5 reduce-scatter.16
where the time goes:
time: 1710 us; the launch traced here: 1700 us
  waiting for transfers between devices  1130 us (66%)
  local copies, waits for them, and re-layouts  222 us (13%)
  matrix products  147 us (9%)
  blocking collectives  112 us (7%)
  other arithmetic  63.3 us (4%)
    reduce_scatter x1, waiting for transfers between devices, local(): lax.psum_scatter(jnp.concatenate([up_terms, down_terms], 1).astype(jnp.bf...  451 us
    all_gather x1, waiting for transfers between devices, local(): lax.all_gather(gate_up_weight, 'shard', axis=0, tiled=True)  250 us
    all_gather x1, waiting for transfers between devices, local(): lax.all_gather(down_weight, 'shard', axis=0, tiled=True)  122 us
    all_gather x1, waiting for transfers between devices, local(): lax.all_gather(qkv_weight, 'shard', axis=0, tiled=True)  58.6 us
    unnamed x16, waiting for transfers between devices  57.8 us
    all_to_all x1, blocking collectives, local(): lax.all_to_all(grad_send, 'expert', split_axis=0, concat_axis=0, tiled=True)  48.3 us
    reduce_scatter x1, waiting for transfers between devices, local(): lax.psum_scatter(qkv_weight_grad.astype(jnp.bfloat16), 'shard', scatter_d...  48 us
    all_gather x1, local copies, waits for them, and re-layouts, local(): lax.all_gather(gate_up_weight, 'shard', axis=0, tiled=True)  40.6 us
  transfers between devices with their start and end apart: 16, of which 13 were waited for; matrix products, arithmetic and copies ran while one was open for 16% of the time, Pallas kernels for 0%

commit v1 on v0

--- a/solution.py
+++ b/solution.py
@@ -435,9 +435,394 @@
     )
 
 
+def hop(values, pairs):
+    return lax.ppermute(values, ("expert", "shard"), pairs)
+
+
+def hop_pairs(step):
+    return [
+        (e * SHARDS + s, step(e, s)[0] * SHARDS + step(e, s)[1])
+        for e in range(GROUPS)
+        for s in range(SHARDS)
+    ]
+
+
+GROUPS = 4
+SHARDS = 8
+to_core = hop_pairs(lambda e, s: (e, s ^ 1))
+to_line = [hop_pairs(lambda e, s, k=k: (e, s ^ (2 * k))) for k in range(4)]
+to_first = hop_pairs(lambda e, s: (e ^ (1 + s % 2), s))
+to_second = hop_pairs(lambda e, s: (e ^ (2 - s % 2), s))
+
+
+def add_low(one, two):
+    return (one.astype(jnp.float32) + two.astype(jnp.float32)).astype(jnp.bfloat16)
+
+
+def spread(own):
+    line = [own] + [hop(own, to_line[k]) for k in (1, 2, 3)]
+    parts = []
+    for piece in line:
+        first = hop(piece, to_first)
+        second = hop(jnp.stack([piece, first]), to_second)
+        half = jnp.concatenate([piece[None], first[None], second])
+        parts += [half, hop(half, to_core)]
+    return jnp.concatenate(parts)
+
+
+def collect(blocks):
+    rows = blocks.shape[1:]
+    blocks = blocks.reshape((4, 2, 4) + rows)
+    line = []
+    for k in (3, 2, 1, 0):
+        half = add_low(blocks[k, 0], hop(blocks[k, 1], to_core))
+        pair = add_low(half[:2], hop(half[2:], to_second))
+        one = add_low(pair[0], hop(pair[1], to_first))
+        line.append(hop(one, to_line[k]) if k else one)
+    return sum(piece.astype(jnp.float32) for piece in line)
+
+
+def gather_line(own):
+    line = jnp.stack([own] + [hop(own, to_line[k]) for k in (1, 2, 3)])
+    return jnp.stack([line, hop(line, to_core)], 1)
+
+
+def sum_line(blocks):
+    half = add_low(blocks[:, 0], hop(blocks[:, 1], to_core))
+    return half[0].astype(jnp.float32) + sum(
+        hop(half[k], to_line[k]).astype(jnp.float32) for k in (1, 2, 3)
+    )
+
+
+def dot(one, two, dims):
+    return lax.dot_general(one, two, (dims, ((), ())), preferred_element_type=jnp.float32)
+
+
+def local_hops(
+    tokens_in,
+    output_cotangent,
+    routes,
+    doc_ids,
+    picture_starts,
+    qkv_weight,
+    out_weight,
+    router_weight,
+    attn_gain,
+    moe_gain,
+    gate_up_weight,
+    down_weight,
+):
+    low = jnp.bfloat16
+    full = jnp.float32
+    rows = tokens_in.shape[0]
+    seq_len = doc_ids.shape[1]
+    groups = HEADS // KV_HEADS
+    q_width = HEADS * HEAD_DIM
+    kv_width = KV_HEADS * HEAD_DIM
+    qkv_width = q_width + 2 * kv_width
+    score_scale = HEAD_DIM ** (-0.5)
+    group_at = lax.axis_index("expert")
+    shard_at = lax.axis_index("shard")
+    own_experts = EXPERTS // GROUPS
+    whole = own_experts // SHARDS * SHARDS
+    split = own_experts - whole
+    share = SHARDS // split
+    part = H // share
+    depth = gate_up_weight.shape[0]
+    pad = 128 - EXPERTS
+    gain_one = attn_gain.astype(full)[:, None]
+    gain_two = moe_gain.astype(full)[:, None]
+
+    expert_ids = jnp.arange(EXPERTS, dtype=jnp.int32)
+    hits = jnp.any(routes[:, :, None] == expert_ids[None, None, :], 1)
+    earlier = jnp.arange(rows)[:, None] > jnp.arange(rows)[None, :]
+    before = dot(earlier.astype(low), hits.astype(low), ((1,), (0,)))
+    slots = jnp.where(hits & (before < CAP), before, -1.0)
+    kept = slots >= 0
+    grad_pay = jnp.concatenate(
+        [output_cotangent, jnp.pad(slots.astype(low), ((0, 0), (0, pad)))], 1
+    )
+
+    dense_own = jnp.concatenate(
+        [
+            (qkv_weight.astype(full) * gain_one).astype(low),
+            jnp.pad((router_weight.astype(full) * gain_two).astype(low), ((0, 0), (0, pad))),
+        ],
+        1,
+    )
+    dense_full = lax.all_gather(dense_own, "shard", axis=0, tiled=True)
+    qkv_full = dense_full[:, :qkv_width]
+    router_full = dense_full[:, qkv_width:]
+    out_full = lax.all_gather(out_weight, "shard", axis=0, tiled=True)
+
+    up3 = (gate_up_weight.astype(full) * gain_two).astype(low).reshape(depth, own_experts, 2 * H)
+    down3 = down_weight.reshape(depth, own_experts, H)
+    halves = up3[:, whole:].reshape(depth, split, 2, share, part)
+    pack = jnp.concatenate(
+        [
+            up3[:, :whole].transpose(1, 0, 2),
+            down3[:, :whole].transpose(1, 0, 2),
+            halves.transpose(1, 3, 0, 2, 4).reshape(SHARDS, depth, 2 * part),
+            down3[:, whole:]
+            .reshape(depth, split, share, part)
+            .transpose(1, 2, 0, 3)
+            .reshape(SHARDS, depth, part),
+        ],
+        2,
+    )
+    owned = lax.all_to_all(pack, "shard", split_axis=0, concat_axis=0, tiled=True)
+    owned = owned.reshape(SHARDS * depth, 3 * H + 3 * part)
+    up_one = owned[:, : 2 * H]
+    down_one = owned[:, 2 * H : 3 * H]
+    up_two = owned[:, 3 * H : 3 * H + 2 * part]
+    down_two = owned[:, 3 * H + 2 * part :]
+
+    tokens_f = tokens_in.astype(full)
+    inverse_one = lax.rsqrt(jnp.mean(tokens_f * tokens_f, -1, keepdims=True) + norm_eps)
+    normal_one = tokens_f * inverse_one
+    normed_in = normal_one.astype(low)
+    qkv_rows = dot(normed_in, qkv_full, ((1,), (0,)))
+    query_pos = shard_at * rows + jnp.arange(rows, dtype=jnp.int32)
+    cosine, sine_table = rope_tables(query_pos, HEAD_DIM)
+    queries = (
+        rotate(qkv_rows[:, :q_width].reshape(rows, HEADS, HEAD_DIM), cosine, sine_table)
+        .astype(low)
+        .reshape(rows, KV_HEADS, groups, HEAD_DIM)
+    )
+    key_local = rotate(
+        qkv_rows[:, q_width : q_width + kv_width].reshape(rows, KV_HEADS, HEAD_DIM),
+        cosine,
+        sine_table,
+    ).reshape(rows, kv_width)
+    key_value = jnp.concatenate([key_local, qkv_rows[:, q_width + kv_width :]], 1).astype(low)
+    all_kv = gather_line(key_value).reshape(seq_len, 2 * KV_HEADS, HEAD_DIM)
+    keys = all_kv[:, :KV_HEADS]
+    values = all_kv[:, KV_HEADS:]
+    block_order = shard_at ^ jnp.arange(SHARDS, dtype=jnp.int32)
+    key_pos = (
+        block_order[:, None] * rows + jnp.arange(rows, dtype=jnp.int32)[None, :]
+    ).reshape(seq_len)
+    doc_blocks = doc_ids[0].reshape(SHARDS, rows)
+    key_doc = jnp.concatenate(
+        [
+            lax.dynamic_index_in_dim(doc_blocks, shard_at ^ k, 0, keepdims=False)
+            for k in range(SHARDS)
+        ]
+    )
+    query_doc = key_doc[:rows]
+    key_pic = picture_ids(key_pos, picture_starts[0], SLOT, PIECE)
+    query_pic = key_pic[:rows]
+    visible = allowed(query_pos, key_pos, query_doc, key_doc, query_pic, key_pic)
+    visible = visible[None, None]
+    raw_scores = (
+        jnp.einsum("tgrd,kgd->grtk", queries, keys, preferred_element_type=full) * score_scale
+    )
+    masked = jnp.where(visible, raw_scores, masked_score)
+    top = jnp.max(masked, -1, keepdims=True)
+    raised = jnp.exp(masked - top)
+    total = jnp.sum(raised, -1, keepdims=True)
+    prob_full = raised / total
+    probs = prob_full.astype(low)
+    attended = (
+        jnp.einsum("grtk,kgd->tgrd", probs, values, preferred_element_type=full)
+        .astype(low)
+        .reshape(rows, q_width)
+    )
+    branch = dot(attended, out_full, ((1,), (1,)))
+    middle = tokens_f + branch
+    inverse_two = lax.rsqrt(jnp.mean(middle * middle, -1, keepdims=True) + norm_eps)
+    normal_two = middle * inverse_two
+    normed_mid = normal_two.astype(low)
+    logits = dot(normed_mid, router_full, ((1,), (0,)))[:, :EXPERTS]
+    logits = jnp.where(hits, logits, masked_score)
+    gates = jnp.exp(logits - jnp.max(logits, -1, keepdims=True))
+    gates = jnp.where(hits, gates, 0.0)
+    gates = gates / jnp.sum(gates, -1, keepdims=True)
+    gate_low = gates.astype(low)
+    gate_rest = (gates - gate_low.astype(full)).astype(low)
+    row_pay = jnp.concatenate(
+        [normed_mid, gate_low, gate_rest, jnp.zeros((rows, 128 - 2 * EXPERTS), low)], 1
+    )
+
+    grad_all = spread(grad_pay)
+    row_all = spread(row_pay)
+
+    def column(extra, index):
+        return lax.dynamic_slice_in_dim(extra, index, 1, 2)
+
+    slot_cols = grad_all[:, :, D:].astype(full)
+    gate_cols = row_all[:, :, D:].astype(full)
+    expert_one = group_at * own_experts + shard_at
+    expert_two = group_at * own_experts + whole + shard_at // share
+    slot_ids = jnp.arange(CAP, dtype=full)[None, None, :]
+
+    def pick_of(index):
+        pick = column(slot_cols, index) == slot_ids
+        gate = column(gate_cols, index) + column(gate_cols, index + EXPERTS)
+        slot_gate = jnp.sum(jnp.where(pick, gate, 0.0), 1).reshape(-1, 1)
+        return pick.astype(low), slot_gate
+
+    def dispatch(pick, blocks):
+        return jnp.einsum(
+            "btc,btd->bcd", pick, blocks[:, :, :D], preferred_element_type=full
+        ).astype(low).reshape(-1, D)
+
+    def expert(index, up_weight, down_cols):
+        width = down_cols.shape[1]
+        pick, slot_gate = pick_of(index)
+        rows_in = dispatch(pick, row_all)
+        grads_in = dispatch(pick, grad_all)
+        projected = dot(rows_in, up_weight, ((1,), (0,)))
+        plain = dot(grads_in, down_cols, ((1,), (0,)))
+        gate_part = projected[:, :width]
+        up_part = projected[:, width:]
+        sigma = jax.nn.sigmoid(gate_part)
+        silu_value = gate_part * sigma
+        hidden = silu_value * up_part
+        gate_grad = jnp.sum(hidden * plain, -1, keepdims=True)
+        hidden_gated = (hidden * slot_gate).astype(low)
+        hidden_grad = plain * slot_gate
+        silu_slope = sigma * (1.0 + gate_part * (1.0 - sigma))
+        proj_grad = jnp.concatenate(
+            [hidden_grad * up_part * silu_slope, hidden_grad * silu_value], -1
+        ).astype(low)
+        out_rows = dot(hidden_gated, down_cols, ((1,), (1,))).astype(low)
+        row_grad = dot(proj_grad, up_weight, ((1,), (1,))).astype(low)
+        up_terms = dot(rows_in, proj_grad, ((0,), (0,))).astype(low)
+        down_terms = dot(grads_in, hidden_gated, ((0,), (0,))).astype(low)
+        token_gate = jnp.einsum(
+            "btc,bc->bt", pick.astype(full), gate_grad.reshape(-1, CAP)
+        )[:, :, None]
+        return (
+            pick,
+            out_rows.reshape(-1, CAP, D),
+            row_grad.reshape(-1, CAP, D),
+            token_gate,
+            up_terms,
+            down_terms,
+        )
+
+    one = expert(expert_one, up_one, down_one)
+    two = expert(expert_two, up_two, down_two)
+    picks = jnp.concatenate([one[0], two[0]], 2)
+
+    def combine(slot_one, slot_two):
+        return jnp.einsum(
+            "btc,bcd->btd",
+            picks,
+            jnp.concatenate([slot_one, slot_two], 1),
+            preferred_element_type=full,
+        ).astype(low)
+
+    lane = jnp.arange(128, dtype=jnp.int32)[None, None, :]
+    gate_lanes = (
+        jnp.where(lane == expert_one, one[3], 0.0) + jnp.where(lane == expert_two, two[3], 0.0)
+    ).astype(low)
+    grad_back = jnp.concatenate([combine(one[2], two[2]), gate_lanes], 2)
+    grad_sum = collect(grad_back)
+    moe_sum = collect(combine(one[1], two[1]))
+    output = (middle + moe_sum).astype(low)
+
+    terms = jnp.concatenate([one[4], one[5], two[4], two[5]], 1)
+    terms = lax.all_to_all(
+        terms.reshape(SHARDS, depth, -1), "shard", split_axis=0, concat_axis=0, tiled=True
+    ).astype(full)
+    up_whole = terms[:, :, : 2 * H].transpose(1, 0, 2).reshape(depth, whole * 2 * H)
+    up_parts = (
+        terms[:, :, 3 * H : 3 * H + 2 * part]
+        .reshape(split, share, depth, 2, part)
+        .transpose(2, 0, 3, 1, 4)
+        .reshape(depth, split * 2 * H)
+    )
+    gate_up_grad = jnp.concatenate([up_whole, up_parts], 1) * gain_two
+    down_whole = terms[:, :, 2 * H : 3 * H].transpose(1, 0, 2).reshape(depth, whole * H)
+    down_parts = (
+        terms[:, :, 3 * H + 2 * part :]
+        .reshape(split, share, depth, part)
+        .transpose(2, 0, 1, 3)
+        .reshape(depth, split * H)
+    )
+    down_grad = jnp.concatenate([down_whole, down_parts], 1)
+
+    gate_grad = jnp.where(kept, grad_sum[:, D : D + EXPERTS], 0.0)
+    logit_grad = gates * (gate_grad - jnp.sum(gates * gate_grad, -1, keepdims=True))
+    logit_grad = jnp.pad(logit_grad.astype(low), ((0, 0), (0, pad)))
+    scaled_two = grad_sum[:, :D] + dot(logit_grad, router_full, ((1,), (1,)))
+    grad_out = output_cotangent.astype(full)
+    mean_two = jnp.mean(scaled_two * normal_two, -1, keepdims=True)
+    mid_grad = grad_out + inverse_two * (scaled_two - normal_two * mean_two)
+    moe_gain_part = jnp.sum(scaled_two * normal_two, 0)
+    router_part = dot(normed_mid, logit_grad, ((0,), (0,)))
+    branch_grad = mid_grad.astype(low)
+    out_part = dot(branch_grad, attended, ((0,), (0,)))
+    attended_grad = (
+        dot(branch_grad, out_full, ((1,), (0,)))
+        .astype(low)
+        .reshape(rows, KV_HEADS, groups, HEAD_DIM)
+    )
+
+    prob_grad = jnp.einsum("tgrd,kgd->grtk", attended_grad, values, preferred_element_type=full)
+    row_dot = jnp.sum(prob_full * prob_grad, -1, keepdims=True)
+    score_grad = (prob_full * (prob_grad - row_dot)).astype(low)
+    query_grad = jnp.einsum("grtk,kgd->tgrd", score_grad, keys, preferred_element_type=full)
+    key_part = (
+        jnp.einsum("grtk,tgrd->kgd", score_grad, queries, preferred_element_type=full)
+        * score_scale
+    ).reshape(seq_len, kv_width)
+    value_part = jnp.einsum(
+        "grtk,tgrd->kgd", probs, attended_grad, preferred_element_type=full
+    ).reshape(seq_len, kv_width)
+    kv_part = jnp.concatenate([key_part, value_part], 1).astype(low)
+    kv_grad = sum_line(kv_part.reshape(4, 2, rows, 2 * kv_width))
+    query_back = rotate_back(
+        (query_grad * score_scale).reshape(rows, HEADS, HEAD_DIM), cosine, sine_table
+    ).reshape(rows, q_width)
+    key_back = rotate_back(
+        kv_grad[:, :kv_width].reshape(rows, KV_HEADS, HEAD_DIM), cosine, sine_table
+    ).reshape(rows, kv_width)
+    qkv_grad_rows = jnp.concatenate([query_back, key_back, kv_grad[:, kv_width:]], 1).astype(low)
+    qkv_part = dot(normed_in, qkv_grad_rows, ((0,), (0,)))
+    scaled_one = dot(qkv_grad_rows, qkv_full, ((1,), (1,)))
+    mean_one = jnp.mean(scaled_one * normal_one, -1, keepdims=True)
+    input_grad = mid_grad + inverse_one * (scaled_one - normal_one * mean_one)
+    attn_gain_part = jnp.sum(scaled_one * normal_one, 0)
+
+    def dense_sum(parts):
+        joined = lax.psum_scatter(
+            parts.astype(low), "shard", scatter_dimension=0, tiled=True
+        )
+        return lax.psum(joined, "expert").astype(full)
+
+    out_sum = dense_sum(out_part)
+    small = jnp.concatenate(
+        [
+            router_part[:, :EXPERTS],
+            moe_gain_part[:, None],
+            attn_gain_part[:, None],
+            jnp.zeros((router_part.shape[0], pad - 2), full),
+        ],
+        1,
+    )
+    late_sum = dense_sum(jnp.concatenate([qkv_part, small], 1))
+    return (
+        output,
+        input_grad.astype(low),
+        late_sum[:, :qkv_width] * gain_one,
+        out_sum,
+        late_sum[:, qkv_width : qkv_width + EXPERTS] * gain_two,
+        late_sum[:, qkv_width + EXPERTS + 1] / gain_one[:, 0],
+        late_sum[:, qkv_width + EXPERTS] / gain_two[:, 0],
+        gate_up_grad,
+        down_grad,
+    )
+
+
 def solution(mesh):
+    body = local
+    if mesh.shape["expert"] == GROUPS and mesh.shape["shard"] == SHARDS:
+        body = local_hops
     return jax.shard_map(
-        local,
+        body,
         mesh=mesh,
         in_specs=(
             P(("expert", "shard"), None),

time: 1710 us -> 1190 us (0.70)
  waiting for transfers between devices: 1130 us -> 632 us
  blocking collectives: 112 us -> 0 us
  starting transfers between devices: 15.8 us -> 118 us
  local copies, waits for them, and re-layouts: 222 us -> 155 us
  other arithmetic: 63.3 us -> 105 us
    reduce_scatter x3 -> x1, waiting for transfers between devices: 499 us -> 20 us  [dense_sum(): lax.psum_scatter(parts.astype(low), 'shard', scatter_dimension=0, tiled=T...]
    all_gather x6 -> x2, waiting for transfers between devices: 490 us -> 37.5 us  [the longest x1 37.5 us: local_hops(): dense_full = lax.all_gather(dense_own, 'shard', axis=0, tiled=True)]
    ppermute x0 -> x68, waiting for transfers between devices: none -> 333 us  [hop(): return lax.ppermute(values, ('expert', 'shard'), pairs)]
    all_to_all x3 -> x2, waiting for transfers between devices: 56.9 us -> 178 us  [the longest x1 178 us: local_hops(): lax.all_to_all(terms.reshape(SHARDS, depth, -1), 'shard', split_axis=0, c...]
    ppermute x0 -> x68, starting transfers between devices: none -> 107 us  [hop(): return lax.ppermute(values, ('expert', 'shard'), pairs)]
    all_gather x3 -> x0, local copies, waits for them, and re-layouts: 61.7 us -> none  [the longest x1 40.6 us: local(): lax.all_gather(gate_up_weight, 'shard', axis=0, tiled=True)]
    unnamed x16 -> x6, waiting for transfers between devices: 57.8 us -> 0.76 us
    all_to_all x1 -> x0, blocking collectives: 48.3 us -> none  [local(): lax.all_to_all(grad_send, 'expert', split_axis=0, concat_axis=0, tiled=True)]
  transfers between devices with their start and end apart: 16 -> 75, of which waited for: 13 -> 34; matrix products, arithmetic and copies ran while one was open for 16% -> 23% of each run, Pallas kernels for 0% -> 0%
where the time goes in v1:
time: 1190 us; the launch traced here: 1180 us
  waiting for transfers between devices  632 us (53%)
  local copies, waits for them, and re-layouts  155 us (13%)
  matrix products  155 us (13%)
  starting transfers between devices  118 us (10%)
  other arithmetic  105 us (9%)
  between operations  16.2 us (1%)
    ppermute x68, waiting for transfers between devices, hop(): return lax.ppermute(values, ('expert', 'shard'), pairs)  333 us
    all_to_all x1, waiting for transfers between devices, local_hops(): lax.all_to_all(terms.reshape(SHARDS, depth, -1), 'shard', split_axis=0, c...  178 us
    ppermute x68, starting transfers between devices, hop(): return lax.ppermute(values, ('expert', 'shard'), pairs)  107 us
    dot_general x22, matrix products, dot(): lax.dot_general(one, two, (dims, ((), ())), preferred_element_type=jnp.fl...  73.3 us
    psum x1, waiting for transfers between devices, dense_sum(): return lax.psum(joined, 'expert').astype(full)  63.6 us
    unnamed x207, local copies, waits for them, and re-layouts  55.9 us
    all_gather x1, waiting for transfers between devices, local_hops(): dense_full = lax.all_gather(dense_own, 'shard', axis=0, tiled=True)  37.5 us
    dot_general x4, matrix products, dispatch(): jnp.einsum('btc,btd->bcd', pick, blocks[:, :, :D], preferred_element_type...  25.7 us
  transfers between devices with their start and end apart: 75, of which 34 were waited for; matrix products, arithmetic and copies ran while one was open for 23% of the time, Pallas kernels for 0%

profile of v1, /device:TPU:0, one launch (start us, length us, event | category | flops | bytes accessed | tf_op | source)
XLA Modules:
  0.0 1181.3 jit_solution(9462670470667075507)
XLA Ops:
  47.0 9.9 copy.234
  139.6 37.5 %all-gather.3.cloned.1.call-done = bf16[1536,2688]{1,0:T(8,128)(2,1)} async-done(((bf16[192,2688]{1,0:T(8,128)(2,1)}), bf16[1536,2688]{1,0:T(8,128)(2,1)}) %all-gather.3.cloned.1.call-update) | async-done | bytes 8257552 | tf_op jit(solution)/shard_map/all_gather | solution.py:553
  183.7 16.6 %collective-permute-start.2 = (bf16[128,1024]{1,0:T(8,128)(2,1)}, bf16[128,1024]{1,0:T(8,128)(2,1)S(1)}, u32[]{:S(2)}, u32[]{:S(2)}) collective-permute-start(bf16[128,1024]{1,0:T(8,128)(2,1)} %pad_maximum_fusion.33), channel_id=1, source_target_pairs={{0,6},{1,7},{2,4},{3,5},{4,2},{5,3},{6,0},{7,1},{8,14},{9,15},{10,... | collective-permute-start | bytes 786440 | tf_op jit(solution)/shard_map/ppermute | solution.py:439
  204.9 24.4 %collective-permute-done.2 = bf16[128,1024]{1,0:T(8,128)(2,1)S(1)} collective-permute-done((bf16[128,1024]{1,0:T(8,128)(2,1)}, bf16[128,1024]{1,0:T(8,128)(2,1)S(1)}, u32[]{:S(2)}, u32[]{:S(2)}) %collective-permute-start.2) | collective-permute-done | bytes 262176 | tf_op jit(solution)/shard_map/ppermute | solution.py:439
  229.4 82.9 %collective-permute-done.1 = bf16[128,1024]{1,0:T(8,128)(2,1)S(1)} collective-permute-done((bf16[128,1024]{1,0:T(8,128)(2,1)}, bf16[128,1024]{1,0:T(8,128)(2,1)S(1)}, u32[]{:S(2)}, u32[]{:S(2)}) %collective-permute-start.1) | collective-permute-done | bytes 262176 | tf_op jit(solution)/shard_map/ppermute | solution.py:439
  348.4 13.6 %fusion.161 = (f32[8,3,128]{2,1,0:T(4,128)S(1)}, f32[8,3,128,1024]{2,3,1,0:T(8,128)S(1)}) fusion(f32[8,1024,128,3]{2,1,3,0:T(8,128)} %fusion.79, pred[128,1024]{0,1:T(8,128)(4,1)S(1)} %copy-done.51), kind=kOutput, calls=%fused_computation.397 | output fusion | flops 18875392 | bytes 25309184 | tf_op jit(solution)/shard_map/sub | solution.py:622
  394.7 13.8 %collective-permute-done.22 = bf16[128,1664]{1,0:T(8,128)(2,1)S(1)} collective-permute-done((bf16[128,1664]{1,0:T(8,128)(2,1)S(1)}, bf16[128,1664]{1,0:T(8,128)(2,1)S(1)}, u32[]{:S(2)}, u32[]{:S(2)}) %collective-permute-start.22) | collective-permute-done | bytes 426016 | tf_op jit(solution)/shard_map/ppermute | solution.py:439
  410.5 10.9 collective-permute-done.26
  424.2 10.0 collective-permute-done.27
  510.7 9.9 convolution_convert_fusion.1
  536.7 9.8 convolution_convert_fusion
  604.6 10.1 collective-permute-done.58
  616.7 11.3 collective-permute-done.54
  630.0 11.4 collective-permute-done.50
  643.4 11.3 collective-permute-done.62
  689.3 17.5 %collective-permute-done.56 = bf16[128,1664]{1,0:T(8,128)(2,1)S(1)} collective-permute-done((bf16[128,1664]{1,0:T(8,128)(2,1)S(1)}, bf16[128,1664]{1,0:T(8,128)(2,1)S(1)}, u32[]{:S(2)}, u32[]{:S(2)}) %collective-permute-start.56) | collective-permute-done | bytes 426016 | tf_op jit(solution)/shard_map/ppermute | solution.py:439
  710.4 30.8 %collective-permute-done.41 = bf16[128,1536]{1,0:T(8,128)(2,1)S(1)} collective-permute-done((bf16[128,1536]{1,0:T(8,128)(2,1)S(1)}, bf16[128,1536]{1,0:T(8,128)(2,1)S(1)}, u32[]{:S(2)}, u32[]{:S(2)}) %collective-permute-start.41) | collective-permute-done | bytes 393248 | tf_op jit(solution)/shard_map/ppermute | solution.py:439
  744.3 10.4 fusion.1
  800.7 16.7 %collective-permute-done.66 = bf16[128,1024]{0,1:T(8,128)(2,1)S(1)} collective-permute-done((bf16[128,1024]{0,1:T(8,128)(2,1)S(1)}, bf16[128,1024]{0,1:T(8,128)(2,1)S(1)}, u32[]{:S(2)}, u32[]{:S(2)}) %collective-permute-start.66) | collective-permute-done | bytes 262176 | tf_op jit(solution)/shard_map/ppermute | solution.py:439
  826.5 13.1 %concatenate.170 = bf16[1536,2688]{1,0:T(8,128)(2,1)} concatenate(bf16[1536,2560]{1,0:T(8,128)(2,1)} %convolution_convert_fusion.2, bf16[1536,40]{1,0:T(8,128)(2,1)S(1)} %bitcast.448, bf16[1536,1]{1,0:T(8,128)(2,1)S(1)} %broadcast_in_dim.227, bf16[1536,1]{1,0:T(8,128)(2,1)S(1)} %broadcast_in_dim.228, bf16[1536,86]{1,0:T(8,128)(2,1)S(1)} %broadcast_in_dim.226), dimensions={1} | concatenate | bytes 16515072 | tf_op jit(solution)/shard_map/concatenate | solution.py:806
  856.0 8.7 copy.249
  874.6 177.8 %all-to-all-done.1 = bf16[8,192,1920]{2,1,0:T(8,128)(2,1)} async-done(((bf16[8,192,1920]{2,1,0:T(8,128)(2,1)}), bf16[8,192,1920]{2,1,0:T(8,128)(2,1)}, u32[]{:S(2)}, u32[]{:S(2)}) %all-to-all-start.1) | async-done | bytes 5898272 | tf_op jit(solution)/shard_map/all_to_all | solution.py:727
  1076.5 20.0 %reduce-scatter.5.cloned.1.call-done = bf16[192,1536]{1,0:T(8,128)(2,1)} async-done(((bf16[1536,1536]{1,0:T(8,128)(2,1)}), bf16[192,1536]{1,0:T(8,128)(2,1)}) %reduce-scatter.5.cloned.1.call-update) | async-done | bytes 589840 | tf_op jit(solution)/shard_map/reduce_scatter | solution.py:791
  1103.4 63.6 %all-reduce.6.cloned.1.call-done = (bf16[192,2688]{0,1:T(8,128)(2,1)}, bf16[192,1536]{1,0:T(8,128)(2,1)}) async-done(((bf16[192,2688]{0,1:T(8,128)(2,1)}, bf16[192,1536]{1,0:T(8,128)(2,1)}), (bf16[192,2688]{0,1:T(8,128)(2,1)}, bf16[192,1536]{1,0:T(8,128)(2,1)})) %all-reduce.6.cloned.1.call-update) | async-done | bytes 1622032 | tf_op jit(solution)/shard_map/psum | solution.py:794
  (548 shorter events, 523.1 us)
Async XLA Ops:
  7.2 169.9 %all-gather.3.cloned.1.call-start = ((), (), s32[]{:S(2)}) async-start(), calls=%async_computation.4 | async-start | bytes 9289728 | tf_op jit(solution)/shard_map/all_gather | solution.py:553
  15.0 52.3 %collective-permute-start.4 = (bf16[128,1664]{1,0:T(8,128)(2,1)}, bf16[128,1664]{1,0:T(8,128)(2,1)}, u32[]{:S(2)}, u32[]{:S(2)}) collective-permute-start(bf16[128,1664]{1,0:T(8,128)(2,1)} %get-tuple-element.123), channel_id=1, source_target_pairs={{0,8},{1,17},{2,10},{3,19},{4,12},{5,21},{6,14},{7,23},{8,0},{9,25... | collective-permute-start | bytes 1277960 | tf_op jit(solution)/shard_map/ppermute | solution.py:439
  17.9 48.5 %collective-permute-start.7 = (bf16[128,1664]{1,0:T(8,128)(2,1)}, bf16[128,1664]{1,0:T(8,128)(2,1)}, u32[]{:S(2)}, u32[]{:S(2)}) collective-permute-start(bf16[128,1664]{1,0:T(8,128)(2,1)} %get-tuple-element.123), channel_id=1, source_target_pairs={{0,2},{1,3},{2,0},{3,1},{4,6},{5,7},{6,4},{7,5},{8,10},{9,11},{10,... | collective-permute-start | bytes 1277960 | tf_op jit(solution)/shard_map/ppermute | solution.py:439
  19.5 50.7 %collective-permute-start.11 = (bf16[128,1664]{1,0:T(8,128)(2,1)}, bf16[128,1664]{1,0:T(8,128)(2,1)}, u32[]{:S(2)}, u32[]{:S(2)}) collective-permute-start(bf16[128,1664]{1,0:T(8,128)(2,1)} %get-tuple-element.123), channel_id=1, source_target_pairs={{0,4},{1,5},{2,6},{3,7},{4,0},{5,1},{6,2},{7,3},{8,12},{9,13},{10,... | collective-permute-start | bytes 1277960 | tf_op jit(solution)/shard_map/ppermute | solution.py:439
  22.1 51.3 %collective-permute-start.15 = (bf16[128,1664]{1,0:T(8,128)(2,1)}, bf16[128,1664]{1,0:T(8,128)(2,1)}, u32[]{:S(2)}, u32[]{:S(2)}) collective-permute-start(bf16[128,1664]{1,0:T(8,128)(2,1)} %get-tuple-element.123), channel_id=1, source_target_pairs={{0,6},{1,7},{2,4},{3,5},{4,2},{5,3},{6,0},{7,1},{8,14},{9,15},{10,... | collective-permute-start | bytes 1277960 | tf_op jit(solution)/shard_map/ppermute | solution.py:439
  56.9 424.4 %all-to-all-start = ((bf16[8,192,1920]{2,1,0:T(8,128)(2,1)}), bf16[8,192,1920]{2,1,0:T(8,128)(2,1)}, u32[]{:S(2)}, u32[]{:S(2)}) async-start(bf16[8,192,1920]{2,1,0:T(8,128)(2,1)} %copy.234), calls=%async_computation | async-start | bytes 11796480 | tf_op jit(solution)/shard_map/all_to_all | solution.py:573
  61.9 308.0 %all-gather.5.cloned.1.call-start = ((), (), s32[]{:S(2)}) async-start(), calls=%async_computation.5 | async-start | bytes 5308416 | tf_op jit(solution)/shard_map/all_gather | solution.py:556
  62.6 1011.4 %reduce-scatter.7.cloned.1.call-start = ((), (), s32[]{:S(2)}) async-start(), calls=%async_computation.7 | async-start | bytes 9289728
  183.7 45.6 %collective-permute-start.2 = (bf16[128,1024]{1,0:T(8,128)(2,1)}, bf16[128,1024]{1,0:T(8,128)(2,1)S(1)}, u32[]{:S(2)}, u32[]{:S(2)}) collective-permute-start(bf16[128,1024]{1,0:T(8,128)(2,1)} %pad_maximum_fusion.33), channel_id=1, source_target_pairs={{0,6},{1,7},{2,4},{3,5},{4,2},{5,3},{6,0},{7,1},{8,14},{9,15},{10,... | collective-permute-start | bytes 786440 | tf_op jit(solution)/shard_map/ppermute | solution.py:439
  200.3 111.9 %collective-permute-start.1 = (bf16[128,1024]{1,0:T(8,128)(2,1)}, bf16[128,1024]{1,0:T(8,128)(2,1)S(1)}, u32[]{:S(2)}, u32[]{:S(2)}) collective-permute-start(bf16[128,1024]{1,0:T(8,128)(2,1)} %pad_maximum_fusion.33), channel_id=1, source_target_pairs={{0,4},{1,5},{2,6},{3,7},{4,0},{5,1},{6,2},{7,3},{8,12},{9,13},{10,... | collective-permute-start | bytes 786440 | tf_op jit(solution)/shard_map/ppermute | solution.py:439
  200.3 111.9 %collective-permute-start = (bf16[128,1024]{1,0:T(8,128)(2,1)}, bf16[128,1024]{1,0:T(8,128)(2,1)S(1)}, u32[]{:S(2)}, u32[]{:S(2)}) collective-permute-start(bf16[128,1024]{1,0:T(8,128)(2,1)} %pad_maximum_fusion.33), channel_id=1, source_target_pairs={{0,2},{1,3},{2,0},{3,1},{4,6},{5,7},{6,4},{7,5},{8,10},{9,11},{10,... | collective-permute-start | bytes 786440 | tf_op jit(solution)/shard_map/ppermute | solution.py:439
  394.2 40.6 %collective-permute-start.20 = (bf16[2,128,1664]{2,1,0:T(8,128)(2,1)S(1)}, bf16[2,128,1664]{2,1,0:T(8,128)(2,1)S(1)}, u32[]{:S(2)}, u32[]{:S(2)}) collective-permute-start(bf16[2,128,1664]{2,1,0:T(8,128)(2,1)S(1)} %pad_maximum_fusion.21), channel_id=1, source_target_pairs={{0,16},{1,9},{2,18},{3,11},{4,20},{5,13},{6,22},{7,15},{8,24},{9,1... | collective-permute-start | bytes 2555912 | tf_op jit(solution)/shard_map/ppermute | solution.py:439
  571.9 42.8 %collective-permute-start.58 = (bf16[2,128,1664]{2,1,0:T(8,128)(2,1)S(1)}, bf16[2,128,1664]{2,1,0:T(8,128)(2,1)S(1)}, u32[]{:S(2)}, u32[]{:S(2)}) collective-permute-start(bf16[2,128,1664]{2,1,0:T(8,128)(2,1)S(1)} %slice.472), channel_id=1, source_target_pairs={{0,16},{1,9},{2,18},{3,11},{4,20},{5,13},{6,22},{7,15},{8,24},{9,1... | collective-permute-start | bytes 2555912 | tf_op jit(solution)/shard_map/ppermute | solution.py:439
  576.2 51.9 %collective-permute-start.54 = (bf16[2,128,1664]{2,1,0:T(8,128)(2,1)S(1)}, bf16[2,128,1664]{2,1,0:T(8,128)(2,1)S(1)}, u32[]{:S(2)}, u32[]{:S(2)}) collective-permute-start(bf16[2,128,1664]{2,1,0:T(8,128)(2,1)S(1)} %slice.466), channel_id=1, source_target_pairs={{0,16},{1,9},{2,18},{3,11},{4,20},{5,13},{6,22},{7,15},{8,24},{9,1... | collective-permute-start | bytes 2555912 | tf_op jit(solution)/shard_map/ppermute | solution.py:439
  584.6 56.8 %collective-permute-start.50 = (bf16[2,128,1664]{2,1,0:T(8,128)(2,1)S(1)}, bf16[2,128,1664]{2,1,0:T(8,128)(2,1)S(1)}, u32[]{:S(2)}, u32[]{:S(2)}) collective-permute-start(bf16[2,128,1664]{2,1,0:T(8,128)(2,1)S(1)} %slice.460), channel_id=1, source_target_pairs={{0,16},{1,9},{2,18},{3,11},{4,20},{5,13},{6,22},{7,15},{8,24},{9,1... | collective-permute-start | bytes 2555912 | tf_op jit(solution)/shard_map/ppermute | solution.py:439
  593.0 61.7 %collective-permute-start.62 = (bf16[2,128,1664]{2,1,0:T(8,128)(2,1)S(1)}, bf16[2,128,1664]{2,1,0:T(8,128)(2,1)S(1)}, u32[]{:S(2)}, u32[]{:S(2)}) collective-permute-start(bf16[2,128,1664]{2,1,0:T(8,128)(2,1)S(1)} %slice.478), channel_id=1, source_target_pairs={{0,16},{1,9},{2,18},{3,11},{4,20},{5,13},{6,22},{7,15},{8,24},{9,1... | collective-permute-start | bytes 2555912 | tf_op jit(solution)/shard_map/ppermute | solution.py:439
  601.5 109.0 %collective-permute-start.48 = (bf16[128,1536]{1,0:T(8,128)(2,1)S(1)}, bf16[128,1536]{1,0:T(8,128)(2,1)S(1)}, u32[]{:S(2)}, u32[]{:S(2)}) collective-permute-start(bf16[128,1536]{1,0:T(8,128)(2,1)S(1)} %slice_bitcast_fusion.36), channel_id=1, source_target_pairs={{0,8},{1,17},{2,10},{3,19},{4,12},{5,21},{6,14},{7,23},{8,0},{9,25... | collective-permute-start | bytes 1179656 | tf_op jit(solution)/shard_map/ppermute | solution.py:439
  614.7 42.0 %collective-permute-start.44 = (bf16[128,1536]{1,0:T(8,128)(2,1)S(1)}, bf16[128,1536]{1,0:T(8,128)(2,1)S(1)}, u32[]{:S(2)}, u32[]{:S(2)}) collective-permute-start(bf16[128,1536]{1,0:T(8,128)(2,1)S(1)} %slice_bitcast_fusion.38), channel_id=1, source_target_pairs={{0,8},{1,17},{2,10},{3,19},{4,12},{5,21},{6,14},{7,23},{8,0},{9,25... | collective-permute-start | bytes 1179656 | tf_op jit(solution)/shard_map/ppermute | solution.py:439
  641.4 36.6 %collective-permute-start.36 = (bf16[128,1536]{1,0:T(8,128)(2,1)S(1)}, bf16[128,1536]{1,0:T(8,128)(2,1)S(1)}, u32[]{:S(2)}, u32[]{:S(2)}) collective-permute-start(bf16[128,1536]{1,0:T(8,128)(2,1)S(1)} %slice_bitcast_fusion.42), channel_id=1, source_target_pairs={{0,8},{1,17},{2,10},{3,19},{4,12},{5,21},{6,14},{7,23},{8,0},{9,25... | collective-permute-start | bytes 1179656 | tf_op jit(solution)/shard_map/ppermute | solution.py:439
  688.8 52.4 %collective-permute-start.41 = (bf16[128,1536]{1,0:T(8,128)(2,1)S(1)}, bf16[128,1536]{1,0:T(8,128)(2,1)S(1)}, u32[]{:S(2)}, u32[]{:S(2)}) collective-permute-start(bf16[128,1536]{1,0:T(8,128)(2,1)S(1)} %fusion.87), channel_id=1, source_target_pairs={{0,4},{1,5},{2,6},{3,7},{4,0},{5,1},{6,2},{7,3},{8,12},{9,13},{10,... | collective-permute-start | bytes 1179656 | tf_op jit(solution)/shard_map/ppermute | solution.py:439
  706.8 34.4 %collective-permute-start.37 = (bf16[128,1536]{1,0:T(8,128)(2,1)S(1)}, bf16[128,1536]{1,0:T(8,128)(2,1)S(1)}, u32[]{:S(2)}, u32[]{:S(2)}) collective-permute-start(bf16[128,1536]{1,0:T(8,128)(2,1)S(1)} %fusion.88), channel_id=1, source_target_pairs={{0,6},{1,7},{2,4},{3,5},{4,2},{5,3},{6,0},{7,1},{8,14},{9,15},{10,... | collective-permute-start | bytes 1179656 | tf_op jit(solution)/shard_map/ppermute | solution.py:439
  864.6 187.7 %all-to-all-start.1 = ((bf16[8,192,1920]{2,1,0:T(8,128)(2,1)}), bf16[8,192,1920]{2,1,0:T(8,128)(2,1)}, u32[]{:S(2)}, u32[]{:S(2)}) async-start(bf16[8,192,1920]{2,1,0:T(8,128)(2,1)} %bitcast.389), calls=%async_computation.2 | async-start | bytes 11796480 | tf_op jit(solution)/shard_map/all_to_all | solution.py:727
  869.5 227.0 %reduce-scatter.5.cloned.1.call-start = ((), (), s32[]{:S(2)}) async-start(), calls=%async_computation.6 | async-start | bytes 5308416 | tf_op jit(solution)/shard_map/reduce_scatter | solution.py:791
  873.4 293.6 %all-reduce.6.cloned.1.call-start = ((), (), s32[]{:S(2)}) async-start(), calls=%async_computation.8 | async-start | bytes 3932160 | tf_op jit(solution)/shard_map/psum | solution.py:794
  (133 other events, 2633.5 us)
Sparse Core Ops, SparseCore 0:
  13.3 163.7 all-gather.2
  178.7 102.0 all-gather.4
  839.8 151.0 reduce-scatter.6
  993.7 102.6 reduce-scatter.4
  1100.4 66.5 all-reduce.5

commit v2 on v0

--- a/solution.py
+++ b/solution.py
@@ -1,6 +1,8 @@
 import jax
 import jax.numpy as jnp
 from jax import lax
+from jax.experimental import pallas as pl
+from jax.experimental.pallas import tpu as pltpu
 from jax.sharding import PartitionSpec as P
 
 D = 1536
@@ -435,9 +437,939 @@
     )
 
 
+GROUPS = 4
+SHARDS = 8
+rows_by_cols = ((1,), (0,))
+rows_by_rows = ((1,), (1,))
+cols_by_cols = ((0,), (0,))
+
+
+def dot(one, two, dims):
+    return lax.dot_general(one, two, (dims, ((), ())), preferred_element_type=jnp.float32)
+
+
+def whole_spec(shape):
+    return pl.BlockSpec(shape, lambda i, ids: (0,) * len(shape), pipeline_mode=pl.Buffered(1))
+
+
+def block_spec(shape, index):
+    return pl.BlockSpec(shape, lambda i, ids: index, pipeline_mode=pl.Buffered(1))
+
+
+def out_spec(shape, index):
+    return pl.BlockSpec(shape, lambda i, ids: index)
+
+
+in_place = pl.BlockSpec(memory_space=pl.ANY)
+
+
+def shaped(shape, dtype=jnp.bfloat16):
+    return jax.ShapeDtypeStruct(shape, dtype)
+
+
+def call(kernel, name, out_shape, in_specs, out_specs, args, scratch=(), aliases=None, flops=0, steps=1):
+    moved = sum(a.size * a.dtype.itemsize for a in args[1:])
+    return pl.pallas_call(
+        kernel,
+        name=name,
+        out_shape=out_shape,
+        grid_spec=pltpu.PrefetchScalarGridSpec(
+            num_scalar_prefetch=1,
+            grid=(steps,),
+            in_specs=in_specs,
+            out_specs=out_specs,
+            scratch_shapes=list(scratch),
+        ),
+        input_output_aliases=aliases or {},
+        compiler_params=pltpu.CompilerParams(
+            vmem_limit_bytes=58 * 1024 * 1024, dimension_semantics=("arbitrary",)
+        ),
+        cost_estimate=pl.CostEstimate(flops=flops, transcendentals=0, bytes_accessed=moved),
+    )(*args)
+
+
+def place_rows(offsets, parts, height):
+    count, fine, width = parts[0].shape
+
+    def kernel(at, *refs):
+        sources, target, done = refs[: len(parts)], refs[len(parts)], refs[-1]
+        copies = []
+        for n, source in enumerate(sources):
+            for i in range(count):
+                row = pl.multiple_of(at[n * count + i], 16)
+                copies.append(
+                    pltpu.make_async_copy(
+                        source.at[i], target.at[pl.ds(row, fine)], done.at[n * count + i]
+                    )
+                )
+        for copy in copies:
+            copy.start()
+        for copy in copies:
+            copy.wait()
+
+    return call(
+        kernel,
+        "place_rows",
+        shaped((height, width), parts[0].dtype),
+        [in_place] * len(parts),
+        out_spec((height, width), (0, 0)),
+        (offsets,) + tuple(parts),
+        scratch=[pltpu.SemaphoreType.DMA((len(parts) * count,))],
+    )
+
+
+def take_rows(offsets, array, parts, count, fine):
+    width = array.shape[1]
+
+    def kernel(at, source, *refs):
+        targets, done = refs[:parts], refs[-1]
+        copies = []
+        for n, target in enumerate(targets):
+            for i in range(count):
+                row = pl.multiple_of(at[n * count + i], 16)
+                copies.append(
+                    pltpu.make_async_copy(
+                        source.at[pl.ds(row, fine)], target.at[i], done.at[n * count + i]
+                    )
+                )
+        for copy in copies:
+            copy.start()
+        for copy in copies:
+            copy.wait()
+
+    return call(
+        kernel,
+        "take_rows",
+        [shaped((count, fine, width), array.dtype)] * parts,
+        [in_place],
+        [out_spec((count, fine, width), (0, 0, 0))] * parts,
+        (offsets, array),
+        scratch=[pltpu.SemaphoreType.DMA((parts * count,))],
+    )
+
+
+def pack_kernel(ids, up, gate_part, up_part, down, down_part, gain, ups, downs):
+    width = up.shape[1]
+    part = gate_part.shape[1]
+    scale = gain[...]
+
+    def scaled(ref):
+        return (ref[...].astype(jnp.float32) * scale).astype(jnp.bfloat16)
+
+    ups[0, :, :width] = scaled(up)
+    ups[0, :, width : width + part] = scaled(gate_part)
+    ups[0, :, width + part :] = scaled(up_part)
+    downs[0, :, : down.shape[1]] = down[...]
+    downs[0, :, down.shape[1] :] = down_part[...]
+
+
+def unpack_kernel(ids, up, up_parts, down, down_parts, gain, up_grad, down_grad):
+    part = down_parts.shape[2]
+    scale = gain[...]
+    expert = pl.program_id(0)
+    whole = pl.num_programs(0) - 2
+
+    @pl.when(expert < whole)
+    def _():
+        up_grad[...] = up[0].astype(jnp.float32) * scale
+        down_grad[...] = down[0].astype(jnp.float32)
+
+    @pl.when(expert >= whole)
+    def _():
+        for i in range(up_parts.shape[0]):
+            at = i * part
+            up_grad[:, at : at + part] = up_parts[i, :, :part].astype(jnp.float32) * scale
+            up_grad[:, H + at : H + at + part] = up_parts[i, :, part:].astype(jnp.float32) * scale
+            down_grad[:, at : at + part] = down_parts[i].astype(jnp.float32)
+
+
+def turn(rows, cosine, sine):
+    width = rows.shape[1]
+    lanes = lax.broadcasted_iota(jnp.int32, (rows.shape[0], 128), 1)
+    first = lanes % HEAD_DIM < HEAD_DIM // 2
+    turned = []
+    for at in range(0, width, 128):
+        piece = rows[:, at : at + 128]
+        swapped = jnp.where(
+            first,
+            pltpu.roll(piece, 128 - HEAD_DIM // 2, 1),
+            pltpu.roll(piece, HEAD_DIM // 2, 1),
+        )
+        turned.append(piece * cosine + swapped * sine)
+    return jnp.concatenate(turned, 1)
+
+
+def qkv_kernel(ids, normed, weight, cosine, sine, queries, key_value):
+    step = pl.program_id(0)
+    found = dot(normed[...], weight[...], rows_by_cols)
+
+    @pl.when(step < 3)
+    def _():
+        queries[...] = turn(found, cosine[...], sine[...]).astype(jnp.bfloat16)
+
+    @pl.when(step == 3)
+    def _():
+        key_value[...] = turn(found, cosine[...], sine[...]).astype(jnp.bfloat16)
+
+    @pl.when(step == 4)
+    def _():
+        key_value[...] = found.astype(jnp.bfloat16)
+
+
+def attend_kernel(ids, queries, key_line, key_other, value_line, value_other, bias, attended, logs):
+    scale = HEAD_DIM ** (-0.5)
+    groups = HEADS // KV_HEADS
+    hidden = bias[...]
+    keys = jnp.concatenate([key_line[...], key_other[...]], 0)
+    values = jnp.concatenate([value_line[...], value_other[...]], 0)
+    lanes = lax.broadcasted_iota(jnp.int32, (queries.shape[0], 128), 1)
+    totals = jnp.zeros((queries.shape[0], 128), jnp.float32)
+    found = []
+    for n in range(2 * groups):
+        at = n // groups * HEAD_DIM
+        scores = dot(
+            queries[:, n * HEAD_DIM : (n + 1) * HEAD_DIM], keys[:, at : at + HEAD_DIM], rows_by_rows
+        )
+        scores = scores * scale + hidden
+        top = jnp.max(scores, 1, keepdims=True)
+        raised = jnp.exp(scores - top)
+        total = jnp.sum(raised, 1, keepdims=True)
+        probs = (raised / total).astype(jnp.bfloat16)
+        found.append(dot(probs, values[:, at : at + HEAD_DIM], rows_by_cols))
+        totals = jnp.where(lanes == n, top + jnp.log(total), totals)
+    attended[...] = jnp.concatenate(found, 1).astype(jnp.bfloat16)
+    logs[0] = totals
+
+
+def attend_back_kernel(
+    ids, queries, grads, key_line, key_other, value_line, value_other, bias, logs, cosine, sine,
+    query_grad, key_mine, key_theirs, value_mine, value_theirs,
+):
+    scale = HEAD_DIM ** (-0.5)
+    groups = HEADS // KV_HEADS
+    hidden = bias[...]
+    keys = jnp.concatenate([key_line[...], key_other[...]], 0)
+    values = jnp.concatenate([value_line[...], value_other[...]], 0)
+    half = key_line.shape[0]
+    found = []
+    key_found, value_found = [], []
+    for n in range(2 * groups):
+        own = n // groups
+        at = own * HEAD_DIM
+        head = slice(n * HEAD_DIM, (n + 1) * HEAD_DIM)
+        query = queries[:, head]
+        grad = grads[:, head]
+        scores = dot(query, keys[:, at : at + HEAD_DIM], rows_by_rows) * scale + hidden
+        probs = jnp.exp(scores - lane_value(logs[0], n))
+        prob_grad = dot(grad, values[:, at : at + HEAD_DIM], rows_by_rows)
+        row_dot = jnp.sum(probs * prob_grad, 1, keepdims=True)
+        score_grad = (probs * (prob_grad - row_dot)).astype(jnp.bfloat16)
+        found.append(dot(score_grad, keys[:, at : at + HEAD_DIM], rows_by_cols))
+        key_part = dot(score_grad, query, cols_by_cols)
+        value_part = dot(probs.astype(jnp.bfloat16), grad, cols_by_cols)
+        if n % groups:
+            key_found[own] = key_found[own] + key_part
+            value_found[own] = value_found[own] + value_part
+        else:
+            key_found.append(key_part)
+            value_found.append(value_part)
+    found = jnp.concatenate(found, 1) * scale
+    query_grad[...] = turn(found, cosine[...], -sine[...]).astype(jnp.bfloat16)
+    key_found = (jnp.concatenate(key_found, 1) * scale).astype(jnp.bfloat16)
+    value_found = jnp.concatenate(value_found, 1).astype(jnp.bfloat16)
+    key_mine[...] = key_found[:half]
+    key_theirs[...] = key_found[half:]
+    value_mine[...] = value_found[:half]
+    value_theirs[...] = value_found[half:]
+
+
+def lane_value(rows, index):
+    lanes = lax.broadcasted_iota(jnp.int32, rows.shape, 1)
+    return jnp.sum(jnp.where(lanes == index, rows, 0.0), 1, keepdims=True)
+
+
+def picks_of(extra, one, two):
+    extra = extra.astype(jnp.float32)
+    lanes = lax.broadcasted_iota(jnp.int32, (extra.shape[0], 2 * CAP), 1)
+    wanted = jnp.where(lanes < CAP, lane_value(extra, one), lane_value(extra, two))
+    place = jnp.where(lanes < CAP, lanes, lanes - CAP).astype(jnp.float32)
+    return jnp.where(wanted == place, 1.0, 0.0).astype(jnp.bfloat16)
+
+
+def grad_side_kernel(ids, half, other, down_one, down_two, kept_gs, gs, plain):
+    count = half.shape[0]
+    for i in range(2 * count):
+        source = half if i < count else other
+        pick = picks_of(source[i % count, :, D:], ids[0], ids[1])
+        found = dot(pick, source[i % count, :, :D], cols_by_cols).astype(jnp.bfloat16)
+        gs[0, i * CAP : (i + 1) * CAP] = found[:CAP]
+        gs[1, i * CAP : (i + 1) * CAP] = found[CAP:]
+    width = down_one.shape[1]
+    plain[:, :width] = dot(gs[0], down_one[...], rows_by_cols)
+    plain[:, width:] = dot(gs[1], down_two[...], rows_by_cols)
+
+
+def combine_rows(ids, rows, slots_half, slots_other, back_half, back_other):
+    count = slots_half.shape[0]
+    for i in range(2 * count):
+        target = back_half if i < count else back_other
+        slots = slots_half if i < count else slots_other
+        pick = picks_of(slots[i % count], ids[0], ids[1])
+        at = slice(i * CAP, (i + 1) * CAP)
+        both = jnp.concatenate([rows[0, at], rows[1, at]], 0)
+        target[i % count] = dot(pick, both, rows_by_cols).astype(jnp.bfloat16)
+
+
+def row_side_kernel(
+    ids, half, other, slots_half, slots_other, plain, up_one, up_two, kept_xs, kept_hid, kept_pg,
+    back_half, back_other, xs, hid, pg, gates, tokens, back_rows,
+):
+    total = xs.shape[1]
+    count = half.shape[0]
+    for i in range(2 * count):
+        source = half if i < count else other
+        slots = slots_half if i < count else slots_other
+        pick = picks_of(slots[i % count], ids[0], ids[1])
+        found = dot(pick, source[i % count], cols_by_cols)
+        extra = found[:, D:]
+        found = found.astype(jnp.bfloat16)
+        at = slice(i * CAP, (i + 1) * CAP)
+        for n in range(2):
+            xs[n, at] = found[n * CAP : (n + 1) * CAP, :D]
+            own = extra[n * CAP : (n + 1) * CAP]
+            gates[n, at] = lane_value(own, ids[n]) + lane_value(own, ids[n] + EXPERTS)
+    first = 0
+    for n, up in ((0, up_one), (1, up_two)):
+        width = up.shape[1] // 2
+        projected = dot(xs[n], up[...], rows_by_cols)
+        gate_part = projected[:, :width]
+        up_part = projected[:, width:]
+        own_plain = plain[:, first : first + width]
+        sigma = 1.0 / (1.0 + jnp.exp(-gate_part))
+        silu_value = gate_part * sigma
+        hidden = silu_value * up_part
+        tokens[n] = jnp.sum(hidden * own_plain, 1, keepdims=True)
+        hid[:, first : first + width] = (hidden * gates[n]).astype(jnp.bfloat16)
+        hidden_grad = own_plain * gates[n]
+        slope = sigma * (1.0 + gate_part * (1.0 - sigma))
+        pg[:, 2 * first : 2 * first + width] = (hidden_grad * up_part * slope).astype(jnp.bfloat16)
+        pg[:, 2 * first + width : 2 * first + 2 * width] = (hidden_grad * silu_value).astype(
+            jnp.bfloat16
+        )
+        own_pg = pg[:, 2 * first : 2 * first + 2 * width]
+        back_rows[n, :, :D] = dot(own_pg, up[...], rows_by_rows).astype(jnp.bfloat16)
+        lanes = lax.broadcasted_iota(jnp.int32, (total, 128), 1)
+        back_rows[n, :, D:] = jnp.where(lanes == ids[n], tokens[n], 0.0).astype(jnp.bfloat16)
+        first += width
+    combine_rows(ids, back_rows, slots_half, slots_other, back_half, back_other)
+
+
+def out_side_kernel(
+    ids, hid, slots_half, slots_other, down_one, down_two, back_half, back_other, out_rows
+):
+    width = down_one.shape[1]
+    out_rows[0] = dot(hid[:, :width], down_one[...], rows_by_rows).astype(jnp.bfloat16)
+    out_rows[1] = dot(hid[:, width:], down_two[...], rows_by_rows).astype(jnp.bfloat16)
+    combine_rows(ids, out_rows, slots_half, slots_other, back_half, back_other)
+
+
+def terms_kernel(ids, xs, gs, pg, hid, terms_up, terms_down):
+    depth = terms_up.shape[1]
+    width = terms_down.shape[2]
+    pieces = (
+        (terms_up, xs, pg, 0, 0, 2 * H),
+        (terms_up, xs, pg, 1, 2 * H, 2 * width),
+        (terms_down, gs, hid, 0, 0, H),
+        (terms_down, gs, hid, 1, H, width),
+    )
+    for target, one, two, n, left, right in pieces:
+        found = dot(one[n], two[:, left:right], cols_by_cols).astype(jnp.bfloat16)
+        for i in range(2):
+            target[i, :, left:right] = found[i * depth : (i + 1) * depth]
+
+
+def hop(values, pairs):
+    return lax.ppermute(values, ("expert", "shard"), pairs)
+
+
+def hop_pairs(step):
+    return [
+        (e * SHARDS + s, step(e, s)[0] * SHARDS + step(e, s)[1])
+        for e in range(GROUPS)
+        for s in range(SHARDS)
+    ]
+
+
+to_core = hop_pairs(lambda e, s: (e, s ^ 1))
+to_line = [hop_pairs(lambda e, s, k=k: (e, s ^ (2 * k))) for k in range(4)]
+to_first = hop_pairs(lambda e, s: (e ^ (1 + s % 2), s))
+to_second = hop_pairs(lambda e, s: (e ^ (2 - s % 2), s))
+
+
+def add_low(one, two):
+    return (one.astype(jnp.float32) + two.astype(jnp.float32)).astype(jnp.bfloat16)
+
+
+def total_of(line):
+    return sum(piece.astype(jnp.float32) for piece in line)
+
+
+class Flow:
+    def __init__(self, steps):
+        self.steps = steps
+        self.result = None
+        self.feed(None)
+
+    def feed(self, values):
+        try:
+            self.want = self.steps.send(values)
+        except StopIteration as stop:
+            self.want = None
+            self.result = stop.value
+
+
+class Order:
+    def __init__(self, mark):
+        self.mark = mark
+
+    def tie(self, values):
+        values, self.mark = lax.optimization_barrier((values, self.mark))
+        return values
+
+    def round(self, flows, work=None):
+        values, self.mark = lax.optimization_barrier(([f.want[0] for f in flows], self.mark))
+        found = [hop(v, f.want[1]) for v, f in zip(values, flows)]
+        found, work, self.mark = lax.optimization_barrier((found, work, self.mark))
+        for flow, values in zip(flows, found):
+            flow.feed(values)
+        return work
+
+
+def one_hop(values, pairs):
+    found = yield values, pairs
+    return found
+
+
+def line_flows(own):
+    return [Flow(one_hop(own, to_line[k])) for k in (1, 2, 3)]
+
+
+def spread_pair(pieces):
+    two = jnp.stack(pieces)
+    first = yield two, to_first
+    four = jnp.concatenate([two, first])
+    second = yield four, to_second
+    eight = jnp.concatenate([four, second])
+    other = yield eight, to_core
+    return eight, other
+
+
+def collect_pair(mine, theirs):
+    found = yield theirs, to_core
+    keep, give = add_low(mine[:4], found[:4]), add_low(mine[4:], found[4:])
+    found = yield give, to_second
+    keep, give = add_low(keep[:2], found[:2]), add_low(keep[2:], found[2:])
+    found = yield give, to_first
+    return [add_low(keep[i], found[i]) for i in range(2)]
+
+
+def collect_all(mine, theirs):
+    found = yield theirs, to_core
+    keep, give = add_low(mine[:8], found[:8]), add_low(mine[8:], found[8:])
+    found = yield give, to_second
+    keep, give = add_low(keep[:4], found[:4]), add_low(keep[4:], found[4:])
+    found = yield give, to_first
+    return [add_low(keep[i], found[i]) for i in range(4)]
+
+
+def share_flow(own, places):
+    first = yield own, to_first
+    pair = jnp.stack([own, first])
+    second = yield pair, to_second
+    quarters = jnp.concatenate([pair, second])
+    return jnp.concatenate(
+        [lax.dynamic_index_in_dim(quarters, place, 0, keepdims=False) for place in places]
+    )
+
+
+def local_hops(
+    tokens_in,
+    output_cotangent,
+    routes,
+    doc_ids,
+    picture_starts,
+    qkv_weight,
+    out_weight,
+    router_weight,
+    attn_gain,
+    moe_gain,
+    gate_up_weight,
+    down_weight,
+):
+    low = jnp.bfloat16
+    full = jnp.float32
+    rows = tokens_in.shape[0]
+    seq_len = doc_ids.shape[1]
+    q_width = HEADS * HEAD_DIM
+    kv_width = KV_HEADS * HEAD_DIM
+    qkv_width = q_width + 2 * kv_width
+    group_at = lax.axis_index("expert")
+    shard_at = lax.axis_index("shard")
+    own_experts = EXPERTS // GROUPS
+    whole = own_experts // SHARDS * SHARDS
+    split = own_experts - whole
+    share = SHARDS // split
+    part = H // share
+    hid_width = H + part
+    depth = gate_up_weight.shape[0]
+    height = SHARDS * depth
+    fine = depth // GROUPS
+    pad = 128 - EXPERTS
+    gain_one = attn_gain.astype(full)[:, None]
+    gain_two = moe_gain.astype(full)[:, None]
+    expert_one = group_at * own_experts + shard_at
+    expert_two = group_at * own_experts + whole + shard_at // share
+    ids = jnp.stack([expert_one, expert_two])
+    order = Order(jnp.zeros((8, 128), full))
+
+    spot = jnp.arange(GROUPS * SHARDS, dtype=jnp.int32)
+    spot_core = spot // 8 % 2
+    spot_mate = 1 + (shard_at % 2 ^ spot_core)
+    spot_q = spot % 8 // 2
+    spot_group = jnp.where(spot_q == 1, spot_mate, jnp.where(spot_q == 2, 3 - spot_mate, spot_q))
+    spot_line = spot // 16 * 2 + spot % 2
+    fine_at = (shard_at ^ (2 * spot_line + spot_core)) * depth + (group_at ^ spot_group) * fine
+
+    expert_ids = jnp.arange(EXPERTS, dtype=jnp.int32)
+    hits = jnp.any(routes[:, :, None] == expert_ids[None, None, :], 1)
+    earlier = jnp.arange(rows)[:, None] > jnp.arange(rows)[None, :]
+    before = dot(earlier.astype(low), hits.astype(low), rows_by_cols)
+    slots = jnp.where(hits & (before < CAP), before, -1.0)
+    kept = slots >= 0
+    grad_pay = jnp.concatenate(
+        [output_cotangent, jnp.pad(slots.astype(low), ((0, 0), (0, pad)))], 1
+    )
+
+    def fine_rows(array):
+        return lax.dynamic_slice_in_dim(array, group_at * fine, fine, 0)
+
+    qkv_own = fine_rows(qkv_weight).astype(full) * fine_rows(gain_one)
+    router_own = fine_rows(router_weight).astype(full) * fine_rows(gain_two)
+    dense_own = jnp.concatenate([qkv_own, jnp.pad(router_own, ((0, 0), (0, pad)))], 1).astype(low)
+    out_own = fine_rows(out_weight)
+
+    def column_spec(width, index):
+        return pl.BlockSpec((depth, width), lambda d, ids: (0, index(d)))
+
+    to_parts = H // part
+    pack_up, pack_down = call(
+        pack_kernel,
+        "pack",
+        (shaped((SHARDS, depth, 2 * hid_width)), shaped((SHARDS, depth, hid_width))),
+        [
+            column_spec(2 * H, lambda d: d),
+            column_spec(part, lambda d: (whole + d // share) * 2 * to_parts + d % share),
+            column_spec(part, lambda d: (whole + d // share) * 2 * to_parts + to_parts + d % share),
+            column_spec(H, lambda d: d),
+            column_spec(part, lambda d: (whole + d // share) * to_parts + d % share),
+            pl.BlockSpec((depth, 1), lambda d, ids: (0, 0)),
+        ],
+        [
+            pl.BlockSpec((1, depth, 2 * hid_width), lambda d, ids: (d, 0, 0)),
+            pl.BlockSpec((1, depth, hid_width), lambda d, ids: (d, 0, 0)),
+        ],
+        (ids, gate_up_weight, gate_up_weight, gate_up_weight, down_weight, down_weight, gain_two),
+        steps=SHARDS,
+    )
+
+    def exchange(packed):
+        return lax.all_to_all(packed, "shard", split_axis=0, concat_axis=0, tiled=True)
+
+    w = line_flows(dense_own)
+    order.round(w[:2])
+    w_near = Flow(spread_pair([dense_own, w[0].result]))
+    order.round([w[2], w_near])
+    w_far = Flow(spread_pair([w[1].result, w[2].result]))
+    owned_down = exchange(order.tie(pack_down)).reshape(height, hid_width)
+    order.round([w_near, w_far])
+    order.round([w_near, w_far])
+    o = line_flows(out_own)
+    order.round([w_far] + o)
+    dense_full = place_rows(fine_at, w_near.result + w_far.result, height)
+    router_full = dense_full[:, qkv_width:]
+    owned_up = exchange(order.tie(pack_up)).reshape(height, 2 * hid_width)
+
+    tokens_f = tokens_in.astype(full)
+    inverse_one = lax.rsqrt(jnp.mean(tokens_f * tokens_f, -1, keepdims=True) + norm_eps)
+    normal_one = tokens_f * inverse_one
+    normed_in = normal_one.astype(low)
+    query_pos = shard_at * rows + jnp.arange(rows, dtype=jnp.int32)
+    cosine, sine = rope_tables(query_pos, HEAD_DIM)
+    cosine = jnp.tile(cosine[:, 0], (1, 4))
+    sine = jnp.tile(jnp.concatenate([-sine[:, 0], sine[:, 0]], 1), (1, 2))
+    tile = 512
+    queries, key_value = call(
+        qkv_kernel,
+        "qkv",
+        (shaped((rows, q_width)), shaped((rows, 2 * kv_width))),
+        [
+            whole_spec((rows, D)),
+            pl.BlockSpec((D, tile), lambda j, ids: (0, j)),
+            whole_spec((rows, 128)),
+            whole_spec((rows, 128)),
+        ],
+        [
+            pl.BlockSpec((rows, tile), lambda j, ids: (0, jnp.minimum(j, 2))),
+            pl.BlockSpec((rows, tile), lambda j, ids: (0, jnp.maximum(j - 3, 0))),
+        ],
+        (ids, normed_in, dense_full, cosine, sine),
+        flops=2 * rows * D * qkv_width,
+        steps=qkv_width // tile,
+    )
+    o_pairs = [
+        Flow(spread_pair([out_own, o[0].result])),
+        Flow(spread_pair([o[1].result, o[2].result])),
+    ]
+    queries, key_value = order.round(o_pairs, (queries, key_value))
+    kv = line_flows(key_value)
+    order.round(kv + o_pairs)
+    kv_line = jnp.concatenate([key_value] + [flow.result for flow in kv])
+    kv_core = Flow(one_hop(kv_line, to_core))
+    owned_down = order.round([kv_core] + o_pairs, owned_down)
+    kv_other = kv_core.result
+    out_full = place_rows(fine_at, o_pairs[0].result + o_pairs[1].result, height)
+    block_order = jnp.arange(SHARDS, dtype=jnp.int32)
+    block_order = shard_at ^ (block_order % 4 * 2 + block_order // 4)
+    key_pos = (
+        block_order[:, None] * rows + jnp.arange(rows, dtype=jnp.int32)[None, :]
+    ).reshape(seq_len)
+    doc_blocks = doc_ids[0].reshape(SHARDS, rows)
+    block_hits = block_order[:, None] == jnp.arange(SHARDS)[None, :]
+    key_doc = jnp.sum(
+        jnp.where(block_hits[:, :, None], doc_blocks[None], 0), 1
+    ).reshape(seq_len)
+    query_doc = key_doc[:rows]
+    key_pic = picture_ids(key_pos, picture_starts[0], SLOT, PIECE)
+    query_pic = key_pic[:rows]
+    visible = allowed(query_pos, key_pos, query_doc, key_doc, query_pic, key_pic)
+    bias = jnp.where(visible, 0.0, masked_score)
+    pairs = KV_HEADS // 2
+    q_tile = q_width // pairs
+    kv_tile = kv_width // pairs
+    half_len = seq_len // 2
+
+    def kv_specs(first):
+        return [pl.BlockSpec((half_len, kv_tile), lambda j, ids: (0, first + j))] * 2
+
+    q_spec = pl.BlockSpec((rows, q_tile), lambda j, ids: (0, j))
+    log_spec = pl.BlockSpec((1, rows, 128), lambda j, ids: (j, 0, 0))
+    attended, logs = call(
+        attend_kernel,
+        "attend",
+        (shaped((rows, q_width)), shaped((pairs, rows, 128), full)),
+        [q_spec] + kv_specs(0) + kv_specs(pairs) + [whole_spec((rows, seq_len))],
+        [q_spec, log_spec],
+        (ids, queries, kv_line, kv_other, kv_line, kv_other, bias),
+        flops=4 * rows * seq_len * q_width,
+        steps=pairs,
+    )
+    branch = dot(attended, out_full, rows_by_rows)
+    middle = tokens_f + branch
+    inverse_two = lax.rsqrt(jnp.mean(middle * middle, -1, keepdims=True) + norm_eps)
+    normal_two = middle * inverse_two
+    normed_mid = normal_two.astype(low)
+    logits = dot(normed_mid, router_full, rows_by_cols)[:, :EXPERTS]
+    logits = jnp.where(hits, logits, masked_score)
+    gates = jnp.exp(logits - jnp.max(logits, -1, keepdims=True))
+    gates = jnp.where(hits, gates, 0.0)
+    gates = gates / jnp.sum(gates, -1, keepdims=True)
+    gate_low = gates.astype(low)
+    gate_rest = (gates - gate_low.astype(full)).astype(low)
+    row_pay = jnp.concatenate(
+        [normed_mid, gate_low, gate_rest, jnp.zeros((rows, 128 - 2 * EXPERTS), low)], 1
+    )
+
+    g = line_flows(grad_pay)
+    row_pay = order.round(g[:2], row_pay)
+    g_near = Flow(spread_pair([grad_pay, g[0].result]))
+    x = line_flows(row_pay)
+    order.round([x[0], g[2], g_near])
+    g_far = Flow(spread_pair([g[1].result, g[2].result]))
+    x_near = Flow(spread_pair([row_pay, x[0].result]))
+    order.round([x[1], x_near, g_near])
+    order.round([x[2], x_near, g_near, g_far])
+    x_far = Flow(spread_pair([x[1].result, x[2].result]))
+    owned_up = order.round([x_near, x_far, g_far], owned_up)
+    order.round([x_far, g_far])
+    grad_parts = [g_near.result, g_far.result]
+    row_parts = [x_near, x_far]
+
+    slot_rows = GROUPS * SHARDS * CAP
+    step_rows = slot_rows // 2
+    blocks = 2 * GROUPS
+    pay_spec = whole_spec((blocks, rows, D + 128))
+    pay_out = out_spec((blocks, rows, D + 128), (0, 0, 0))
+    slot_spec = block_spec((blocks, rows, 128), (0, 0, D // 128))
+    up_specs = [
+        block_spec((height, 2 * H), (0, 0)),
+        block_spec((height, 2 * part), (0, H // part)),
+    ]
+    down_specs = [
+        block_spec((height, H), (0, 0)),
+        block_spec((height, part), (0, H // part)),
+    ]
+    back_shape = shaped((blocks, rows, D + 128))
+    gs = jnp.zeros((2, slot_rows, D), low)
+    xs = jnp.zeros((2, slot_rows, D), low)
+    hid = jnp.zeros((slot_rows, hid_width), low)
+    pg = jnp.zeros((slot_rows, 2 * hid_width), low)
+
+    def like(array):
+        return shaped(array.shape, array.dtype)
+
+    plain = []
+    for k in range(2):
+        gs, found = call(
+            grad_side_kernel,
+            "grad_side",
+            (like(gs), shaped((step_rows, hid_width), full)),
+            [pay_spec, pay_spec] + down_specs + [in_place],
+            [
+                out_spec((2, step_rows, D), (0, k, 0)),
+                out_spec((step_rows, hid_width), (0, 0)),
+            ],
+            (ids,) + grad_parts[k] + (owned_down, owned_down, gs),
+            aliases={5: 0},
+            flops=2 * step_rows * D * (hid_width + 2 * rows),
+        )
+        plain.append(found)
+
+    def row_side(k):
+        nonlocal xs, hid, pg
+        half_back, other_back, xs, hid, pg = call(
+            row_side_kernel,
+            "row_side",
+            (back_shape, back_shape, like(xs), like(hid), like(pg)),
+            [pay_spec, pay_spec, slot_spec, slot_spec, whole_spec((step_rows, hid_width))]
+            + up_specs
+            + [in_place] * 3,
+            [
+                pay_out,
+                pay_out,
+                out_spec((2, step_rows, D), (0, k, 0)),
+                out_spec((step_rows, hid_width), (k, 0)),
+                out_spec((step_rows, 2 * hid_width), (k, 0)),
+            ],
+            (ids,) + row_parts[k].result + grad_parts[k] + (plain[k], owned_up, owned_up, xs, hid, pg),
+            scratch=[
+                pltpu.VMEM((2, step_rows, 1), full),
+                pltpu.VMEM((2, step_rows, 1), full),
+                pltpu.VMEM((2, step_rows, D + 128), low),
+            ],
+            aliases={8: 2, 9: 3, 10: 4},
+            flops=8 * step_rows * D * (hid_width + rows),
+        )
+        return half_back, other_back
+
+    back_near = order.round([x_far], row_side(0))
+    b_near = Flow(collect_pair(*back_near))
+    back_far = order.round([b_near], row_side(1))
+    b_far = Flow(collect_pair(*back_far))
+
+    def lane_block(i, ids):
+        return (0, 0, i)
+
+    terms = call(
+        terms_kernel,
+        "terms",
+        (shaped((SHARDS, depth, 2 * hid_width)), shaped((SHARDS, depth, hid_width))),
+        [
+            pl.BlockSpec((2, slot_rows, 2 * depth), lane_block),
+            pl.BlockSpec((2, slot_rows, 2 * depth), lane_block),
+            whole_spec((slot_rows, 2 * hid_width)),
+            whole_spec((slot_rows, hid_width)),
+        ],
+        [
+            pl.BlockSpec((2, depth, 2 * hid_width), lambda i, ids: (i, 0, 0)),
+            pl.BlockSpec((2, depth, hid_width), lambda i, ids: (i, 0, 0)),
+        ],
+        (ids, xs, gs, pg, hid),
+        flops=2 * slot_rows * D * 3 * hid_width,
+        steps=4,
+    )
+    terms = order.round([b_near, b_far], terms)
+    order.round([b_near, b_far])
+    b_line = [Flow(one_hop(b_near.result[1], to_line[1]))]
+    terms_down = exchange(order.tie(terms[1]))
+    order.round([b_far] + b_line)
+
+    def out_side(k):
+        return call(
+            out_side_kernel,
+            "out_side",
+            (shaped((blocks, rows, D)),) * 2,
+            [block_spec((step_rows, hid_width), (k, 0)), slot_spec, slot_spec] + down_specs,
+            [out_spec((blocks, rows, D), (0, 0, 0))] * 2,
+            (ids, hid) + grad_parts[k] + (owned_down, owned_down),
+            scratch=[pltpu.VMEM((2, step_rows, D), low)],
+            flops=2 * step_rows * D * (hid_width + 2 * rows),
+        )
+
+    b_line += [Flow(one_hop(b_far.result[i], to_line[2 + i])) for i in range(2)]
+    out_near, out_far = order.round(b_line[1:], (out_side(0), out_side(1)))
+    m_near, m_far = Flow(collect_pair(*out_near)), Flow(collect_pair(*out_far))
+    grad_sum = total_of([b_near.result[0]] + [flow.result for flow in b_line])
+    terms_up = exchange(order.tie(terms[0]))
+
+    gate_grad = jnp.where(kept, grad_sum[:, D : D + EXPERTS], 0.0)
+    logit_grad = gates * (gate_grad - jnp.sum(gates * gate_grad, -1, keepdims=True))
+    logit_grad = jnp.pad(logit_grad.astype(low), ((0, 0), (0, pad)))
+    scaled_two = grad_sum[:, :D] + dot(logit_grad, router_full, rows_by_rows)
+    grad_out = output_cotangent.astype(full)
+    mean_two = jnp.mean(scaled_two * normal_two, -1, keepdims=True)
+    mid_grad = grad_out + inverse_two * (scaled_two - normal_two * mean_two)
+    moe_gain_part = jnp.sum(scaled_two * normal_two, 0)
+    router_part = dot(normed_mid, logit_grad, cols_by_cols)
+    branch_grad = mid_grad.astype(low)
+    attended_grad = dot(branch_grad, out_full, rows_by_cols).astype(low)
+
+    kv_out = pl.BlockSpec((half_len, kv_tile), lambda j, ids: (0, j))
+    query_back, key_mine, key_theirs, value_mine, value_theirs = call(
+        attend_back_kernel,
+        "attend_back",
+        (shaped((rows, q_width)),) + (shaped((half_len, kv_width)),) * 4,
+        [q_spec, q_spec]
+        + kv_specs(0)
+        + kv_specs(pairs)
+        + [whole_spec((rows, seq_len)), log_spec, whole_spec((rows, 128)), whole_spec((rows, 128))],
+        [q_spec] + [kv_out] * 4,
+        (ids, queries, attended_grad, kv_line, kv_other, kv_line, kv_other, bias, logs, cosine, sine),
+        flops=10 * rows * seq_len * q_width,
+        steps=pairs,
+    )
+    kv_theirs = jnp.concatenate([key_theirs, value_theirs], 1)
+    kv_mine = jnp.concatenate([key_mine, value_mine], 1)
+    kv_theirs, kv_mine = order.round([m_near, m_far], (kv_theirs, kv_mine))
+    kv_core = Flow(one_hop(kv_theirs, to_core))
+    order.round([kv_core, m_near])
+    kv_half = add_low(kv_mine, kv_core.result).reshape(4, rows, 2 * kv_width)
+    kv = [Flow(one_hop(kv_half[k], to_line[k])) for k in (1, 2, 3)]
+    early_part = jnp.concatenate(
+        [
+            dot(branch_grad, attended, cols_by_cols).astype(low),
+            dot(normed_in, query_back, cols_by_cols).astype(low),
+        ],
+        1,
+    )
+    early_part, terms_down = order.round(kv + [m_far, m_near], (early_part, terms_down))
+    kv_grad = total_of([kv_half[0]] + [flow.result for flow in kv])
+
+    def dense_flow(parts):
+        found = take_rows(fine_at, parts, 4, 8, fine)
+        mine, theirs = ([found[core], found[2 + core]] for core in range(2))
+        return [Flow(collect_pair(mine[i], theirs[i])) for i in range(2)]
+
+    def line_of(near, far):
+        return [Flow(one_hop(near[1], to_line[1]))] + [
+            Flow(one_hop(far[i], to_line[2 + i])) for i in range(2)
+        ]
+
+    early = dense_flow(early_part)
+
+    def swapped(values):
+        lanes = jnp.arange(values.shape[1]) % HEAD_DIM < HEAD_DIM // 2
+        return jnp.where(
+            lanes[None], jnp.roll(values, -HEAD_DIM // 2, 1), jnp.roll(values, HEAD_DIM // 2, 1)
+        )
+
+    key_grad = kv_grad[:, :kv_width]
+    key_back = key_grad * jnp.tile(cosine, (1, pairs)) - swapped(key_grad) * jnp.tile(sine, (1, pairs))
+    kv_rows = jnp.concatenate([key_back, kv_grad[:, kv_width:]], 1).astype(low)
+    scaled_one = dot(query_back, dense_full[:, :q_width], rows_by_rows) + dot(
+        kv_rows, dense_full[:, q_width:qkv_width], rows_by_rows
+    )
+    mean_one = jnp.mean(scaled_one * normal_one, -1, keepdims=True)
+    input_grad = mid_grad + inverse_one * (scaled_one - normal_one * mean_one)
+    attn_gain_part = jnp.sum(scaled_one * normal_one, 0)
+    small = jnp.concatenate(
+        [
+            router_part[:, :EXPERTS],
+            moe_gain_part[:, None],
+            attn_gain_part[:, None],
+            jnp.zeros((height, pad - 2), full),
+        ],
+        1,
+    )
+    late_part = jnp.concatenate(
+        [dot(normed_in, kv_rows, cols_by_cols).astype(low), small.astype(low)], 1
+    )
+    late_part, input_grad = order.round(early + [m_far], (late_part, input_grad.astype(low)))
+    late = dense_flow(late_part)
+    order.round(late + early)
+    order.round(late + early)
+    early_line = line_of(early[0].result, early[1].result)
+    order.round(late + early_line)
+    late_line = line_of(late[0].result, late[1].result)
+    spots = jnp.arange(GROUPS, dtype=jnp.int32) ^ group_at
+    mate = 1 + shard_at % 2
+    spots = jnp.where(spots == mate, 1, jnp.where(spots == 3 - mate, 2, spots))
+    places = [spots[i] for i in range(GROUPS)]
+
+    def shared(first, line):
+        own = total_of([first] + [flow.result for flow in line]).astype(low)
+        return Flow(share_flow(own, places))
+
+    early_share = shared(early[0].result[0], early_line)
+    terms_up = order.round(late_line + [early_share], terms_up)
+    late_share = shared(late[0].result[0], late_line)
+    order.round([late_share, early_share])
+    m_line = line_of(m_near.result, m_far.result)
+    order.round([late_share] + m_line)
+    output = (middle + total_of([m_near.result[0]] + [flow.result for flow in m_line])).astype(low)
+    early_sum = early_share.result.astype(full)
+    late_sum = late_share.result.astype(full)
+
+    gate_up_grad, down_grad = call(
+        unpack_kernel,
+        "unpack",
+        (shaped(gate_up_weight.shape, full), shaped(down_weight.shape, full)),
+        [
+            pl.BlockSpec((1, depth, 2 * H), lambda j, ids: (jnp.minimum(j, whole - 1), 0, 0)),
+            pl.BlockSpec(
+                (share, depth, 2 * part), lambda j, ids: (jnp.maximum(j - whole, 0), 0, to_parts)
+            ),
+            pl.BlockSpec((1, depth, H), lambda j, ids: (jnp.minimum(j, whole - 1), 0, 0)),
+            pl.BlockSpec(
+                (share, depth, part), lambda j, ids: (jnp.maximum(j - whole, 0), 0, to_parts)
+            ),
+            whole_spec((depth, 1)),
+        ],
+        [
+            pl.BlockSpec((depth, 2 * H), lambda j, ids: (0, j)),
+            pl.BlockSpec((depth, H), lambda j, ids: (0, j)),
+        ],
+        (ids, terms_up, terms_up, terms_down, terms_down, gain_two),
+        steps=own_experts,
+    )
+    return (
+        output,
+        input_grad,
+        jnp.concatenate([early_sum[:, q_width:], late_sum[:, : 2 * kv_width]], 1) * gain_one,
+        early_sum[:, :q_width],
+        late_sum[:, 2 * kv_width : 2 * kv_width + EXPERTS] * gain_two,
+        late_sum[:, 2 * kv_width + EXPERTS + 1] / gain_one[:, 0],
+        late_sum[:, 2 * kv_width + EXPERTS] / gain_two[:, 0],
+        gate_up_grad,
+        down_grad,
+    )
+
+
 def solution(mesh):
+    body = local
+    if mesh.shape["expert"] == GROUPS and mesh.shape["shard"] == SHARDS:
+        body = local_hops
     return jax.shard_map(
-        local,
+        body,
         mesh=mesh,
         in_specs=(
             P(("expert", "shard"), None),

time: 1710 us -> 986 us (0.58)
  waiting for transfers between devices: 1130 us -> 468 us
  local copies, waits for them, and re-layouts: 222 us -> 33.4 us
  Pallas kernels: 0 us -> 170 us
  starting transfers between devices: 15.8 us -> 170 us
  matrix products: 147 us -> 20.3 us
  blocking collectives: 112 us -> 0 us
  other arithmetic: 63.3 us -> 100 us
    reduce_scatter x3 -> x0, waiting for transfers between devices: 499 us -> none  [the longest x1 451 us: local(): lax.psum_scatter(jnp.concatenate([up_terms, down_terms], 1).astype(jnp.bf...]
    all_gather x6 -> x0, waiting for transfers between devices: 490 us -> none  [the longest x1 250 us: local(): lax.all_gather(gate_up_weight, 'shard', axis=0, tiled=True)]
    ppermute x0 -> x84, waiting for transfers between devices: none -> 435 us  [hop(): return lax.ppermute(values, ('expert', 'shard'), pairs)]
    pallas_call x0 -> x16, Pallas kernels: none -> 170 us  [call(): pl.pallas_call(kernel, name=name, out_shape=out_shape, grid_spec=pltpu.Pr...]
    ppermute x0 -> x84, starting transfers between devices: none -> 143 us  [hop(): return lax.ppermute(values, ('expert', 'shard'), pairs)]
    dot_general x36 -> x11, matrix products: 147 us -> 20.3 us  [dot(): lax.dot_general(one, two, (dims, ((), ())), preferred_element_type=jnp.fl...]
    all_gather x3 -> x0, local copies, waits for them, and re-layouts: 61.7 us -> none  [the longest x1 40.6 us: local(): lax.all_gather(gate_up_weight, 'shard', axis=0, tiled=True)]
    reshape x4 -> x0, local copies, waits for them, and re-layouts: 58.3 us -> none  [the longest x1 37.3 us: local(): up_terms = jnp.einsum('secd,secj->dej', received, proj_grad, preferred_el...]
  transfers between devices with their start and end apart: 16 -> 88, of which waited for: 13 -> 43; matrix products, arithmetic and copies ran while one was open for 16% -> 10% of each run, Pallas kernels for 0% -> 14%
where the time goes in v2:
time: 986 us; the launch traced here: 971 us
  waiting for transfers between devices  468 us (47%)
  starting transfers between devices  170 us (17%)
  Pallas kernels  170 us (17%)
  other arithmetic  100 us (10%)
  local copies, waits for them, and re-layouts  33.4 us (3%)
  matrix products  20.3 us (2%)
    ppermute x84, waiting for transfers between devices, hop(): return lax.ppermute(values, ('expert', 'shard'), pairs)  435 us
    pallas_call x16, Pallas kernels, call(): pl.pallas_call(kernel, name=name, out_shape=out_shape, grid_spec=pltpu.Pr...  170 us
    ppermute x84, starting transfers between devices, hop(): return lax.ppermute(values, ('expert', 'shard'), pairs)  143 us
    convert_element_type x25, other arithmetic, add_low(): (one.astype(jnp.float32) + two.astype(jnp.float32)).astype(jnp.bfloat16)  43.9 us
    all_to_all x4, waiting for transfers between devices, exchange(): lax.all_to_all(packed, 'shard', split_axis=0, concat_axis=0, tiled=True)  32.9 us
    all_to_all x4, starting transfers between devices, exchange(): lax.all_to_all(packed, 'shard', split_axis=0, concat_axis=0, tiled=True)  26.3 us
    dot_general x11, matrix products, dot(): lax.dot_general(one, two, (dims, ((), ())), preferred_element_type=jnp.fl...  20.3 us
  transfers between devices with their start and end apart: 88, of which 43 were waited for; matrix products, arithmetic and copies ran while one was open for 10% of the time, Pallas kernels for 14%

profile of v2, /device:TPU:0, one launch (start us, length us, event | category | flops | bytes accessed | tf_op | source)
XLA Modules:
  0.0 971.1 jit_solution(9624765618801862867)
XLA Ops:
  37.8 13.2 %collective-permute-done.5 = bf16[2,48,2688]{2,1,0:T(8,128)(2,1)S(1)} collective-permute-done((bf16[2,48,2688]{2,1,0:T(8,128)(2,1)S(1)}, bf16[2,48,2688]{2,1,0:T(8,128)(2,1)S(1)}, u32[]{:S(2)}, u32[]{:S(2)}) %collective-permute-start.5) | collective-permute-done | bytes 516128 | tf_op jit(solution)/shard_map/ppermute | solution.py:792
  55.2 14.3 %collective-permute-done.7 = bf16[4,48,2688]{2,1,0:T(8,128)(2,1)} collective-permute-done((bf16[4,48,2688]{2,1,0:T(8,128)(2,1)}, bf16[4,48,2688]{2,1,0:T(8,128)(2,1)}, u32[]{:S(2)}, u32[]{:S(2)}) %collective-permute-start.7) | collective-permute-done | bytes 1032224 | tf_op jit(solution)/shard_map/ppermute | solution.py:792
  121.1 14.9 %collective-permute-done.14 = bf16[128,1024]{1,0:T(8,128)(2,1)S(1)} collective-permute-done((bf16[128,1024]{1,0:T(8,128)(2,1)S(1)}, bf16[128,1024]{1,0:T(8,128)(2,1)S(1)}, u32[]{:S(2)}, u32[]{:S(2)}) %collective-permute-start.14) | collective-permute-done | bytes 262176 | tf_op jit(solution)/shard_map/ppermute | solution.py:792
  136.0 25.0 %collective-permute-done.15 = bf16[128,1024]{1,0:T(8,128)(2,1)S(1)} collective-permute-done((bf16[128,1024]{1,0:T(8,128)(2,1)S(1)}, bf16[128,1024]{1,0:T(8,128)(2,1)S(1)}, u32[]{:S(2)}, u32[]{:S(2)}) %collective-permute-start.15) | collective-permute-done | bytes 262176 | tf_op jit(solution)/shard_map/ppermute | solution.py:792
  178.4 14.8 %attend.1 = (bf16[128,1536]{1,0:T(8,128)(2,1)}, f32[4,128,128]{2,1,0:T(8,128)}) custom-call(s32[2]{0:T(128)} %pad_add_fusion.ids, bf16[128,1536]{1,0:T(8,128)(2,1)} %get-tuple-element.336.queries, bf16[512,1024]{1,0:T(8,128)(2,1)} %constant_dynamic-update-slice_fusion.key_line.value_line, bf16[512,1024]{1,0:T(8,128)(2,1)} %collective-permute-done.19.key_other.value_other, ...), custom_call_target="tpu_custom_call" | custom-call | flops 805306368 | bytes 5111808 | tf_op jit(solution)/shard_map/attend/pallas_call | solution.py:472
  205.2 16.1 %collective-permute-done.22 = bf16[128,1664]{1,0:T(8,128)(2,1)S(1)} collective-permute-done((bf16[128,1664]{1,0:T(8,128)(2,1)}, bf16[128,1664]{1,0:T(8,128)(2,1)S(1)}, u32[]{:S(2)}, u32[]{:S(2)}) %collective-permute-start.22) | collective-permute-done | bytes 426016 | tf_op jit(solution)/shard_map/ppermute | solution.py:792
  227.8 10.8 %collective-permute-done.24 = bf16[128,1664]{1,0:T(8,128)(2,1)S(1)} collective-permute-done((bf16[128,1664]{1,0:T(8,128)(2,1)S(1)}, bf16[128,1664]{1,0:T(8,128)(2,1)S(1)}, u32[]{:S(2)}, u32[]{:S(2)}) %collective-permute-start.24) | collective-permute-done | bytes 426016 | tf_op jit(solution)/shard_map/ppermute | solution.py:792
  250.7 16.6 %collective-permute-done.27 = bf16[128,1664]{1,0:T(8,128)(2,1)S(1)} collective-permute-done((bf16[128,1664]{1,0:T(8,128)(2,1)S(1)}, bf16[128,1664]{1,0:T(8,128)(2,1)S(1)}, u32[]{:S(2)}, u32[]{:S(2)}) %collective-permute-start.27) | collective-permute-done | bytes 426016 | tf_op jit(solution)/shard_map/ppermute | solution.py:792
  289.1 70.3 %collective-permute-done.30 = bf16[128,1664]{1,0:T(8,128)(2,1)S(1)} collective-permute-done((bf16[128,1664]{1,0:T(8,128)(2,1)}, bf16[128,1664]{1,0:T(8,128)(2,1)S(1)}, u32[]{:S(2)}, u32[]{:S(2)}) %collective-permute-start.30) | collective-permute-done | bytes 426016 | tf_op jit(solution)/shard_map/ppermute | solution.py:792
  368.9 11.1 %all-to-all-done.1 = bf16[8,192,1280]{2,1,0:T(8,128)(2,1)} async-done(((bf16[8,192,1280]{2,1,0:T(8,128)(2,1)}), bf16[8,192,1280]{2,1,0:T(8,128)(2,1)}, u32[]{:S(2)}, u32[]{:S(2)}) %all-to-all-start.1) | async-done | bytes 3932192 | tf_op jit(solution)/shard_map/all_to_all | solution.py:986
  402.9 20.1 %collective-permute-done.37 = bf16[4,128,1664]{2,1,0:T(8,128)(2,1)S(1)} collective-permute-done((bf16[4,128,1664]{2,1,0:T(8,128)(2,1)S(1)}, bf16[4,128,1664]{2,1,0:T(8,128)(2,1)S(1)}, u32[]{:S(2)}, u32[]{:S(2)}) %collective-permute-start.37) | collective-permute-done | bytes 1703968 | tf_op jit(solution)/shard_map/ppermute | solution.py:792
  445.0 18.0 %row_side.2 = (bf16[8,128,1664]{2,1,0:T(8,128)(2,1)}, bf16[8,128,1664]{2,1,0:T(8,128)(2,1)}, bf16[2,1024,1536]{2,1,0:T(8,128)(2,1)}, bf16[1024,640]{1,0:T(8,128)(2,1)}, bf16[1024,1280]{1,0:T(8,128)(2,1)}) custom-call(s32[2]{0:T(128)} %pad_add_fusion.ids, ...), custom_call_target="tpu_custom_call", output_to_operand_aliasing={{2}: (8, {}), {3}: (9, {}), {4}: (10, {})} | custom-call | flops 4831838208 | bytes 33030144 | tf_op jit(solution)/shard_map/row_side/pallas_call | solution.py:472
  473.2 18.4 %row_side.3 = (bf16[8,128,1664]{2,1,0:T(8,128)(2,1)}, bf16[8,128,1664]{2,1,0:T(8,128)(2,1)}, bf16[2,1024,1536]{2,1,0:T(8,128)(2,1)}, bf16[1024,640]{1,0:T(8,128)(2,1)}, bf16[1024,1280]{1,0:T(8,128)(2,1)}) custom-call(s32[2]{0:T(128)} %pad_add_fusion.ids, ...), custom_call_target="tpu_custom_call", output_to_operand_aliasing={{2}: (8, {}), {3}: (9, {}), {4}: (10, {})} | custom-call | flops 4831838208 | bytes 33030144 | tf_op jit(solution)/shard_map/row_side/pallas_call | solution.py:472
  497.3 12.4 %terms.1 = (bf16[8,192,1280]{2,1,0:T(8,128)(2,1)}, bf16[8,192,640]{2,1,0:T(8,128)(2,1)}) custom-call(s32[2]{0:T(128)} %pad_add_fusion.ids, bf16[2,1024,1536]{2,1,0:T(8,128)(2,1)} %get-tuple-element.437.xs, bf16[2,1024,1536]{2,1,0:T(8,128)(2,1)} %get-tuple-element.438.gs, bf16[1024,1280]{1,0:T(8,128)(2,1)} %get-tuple-element.439.pg, ...), custom_call_target="tpu_custom_call" | custom-call | flops 6039797760 | bytes 16515072 | tf_op jit(solution)/shard_map/terms/pallas_call | solution.py:472
  524.1 20.7 %collective-permute-done.43 = bf16[2,128,1664]{2,1,0:T(8,128)(2,1)S(1)} collective-permute-done((bf16[2,128,1664]{2,1,0:T(8,128)(2,1)S(1)}, bf16[2,128,1664]{2,1,0:T(8,128)(2,1)S(1)}, u32[]{:S(2)}, u32[]{:S(2)}) %collective-permute-start.43) | collective-permute-done | bytes 852000 | tf_op jit(solution)/shard_map/ppermute | solution.py:792
  553.1 29.7 %collective-permute-start.46 = (bf16[128,1664]{1,0:T(8,128)(2,1)S(1)}, bf16[128,1664]{1,0:T(8,128)(2,1)S(1)}, u32[]{:S(2)}, u32[]{:S(2)}) collective-permute-start(bf16[128,1664]{1,0:T(8,128)(2,1)S(1)} %fusion.28), channel_id=1, source_target_pairs={{0,2},{1,3},{2,0},{3,1},{4,6},{5,7},{6,4},{7,5},{8,10},{9,11},{10,... | collective-permute-start | bytes 1277960 | tf_op jit(solution)/shard_map/ppermute | solution.py:792
  613.6 11.5 %collective-permute-done.47 = bf16[128,1664]{1,0:T(8,128)(2,1)} collective-permute-done((bf16[128,1664]{1,0:T(8,128)(2,1)}, bf16[128,1664]{1,0:T(8,128)(2,1)}, u32[]{:S(2)}, u32[]{:S(2)}) %collective-permute-start.47) | collective-permute-done | bytes 426016 | tf_op jit(solution)/shard_map/ppermute | solution.py:792
  630.9 18.5 %attend_back.1 = (bf16[128,1536]{1,0:T(8,128)(2,1)}, bf16[512,512]{1,0:T(8,128)(2,1)}, bf16[512,512]{1,0:T(8,128)(2,1)}, bf16[512,512]{1,0:T(8,128)(2,1)}, bf16[512,512]{1,0:T(8,128)(2,1)}) custom-call(s32[2]{0:T(128)} %pad_add_fusion.ids, bf16[128,1536]{1,0:T(8,128)(2,1)} %get-tuple-element.336.queries, bf16[128,1536]{1,0:T(8,128)(2,1)} %convolution_convert_fusion.3.grads, ...), custom_call_target="tpu_custom_call" | custom-call | flops 2013265920 | bytes 5898240 | tf_op jit(solution)/shard_map/attend_back/pallas_call | solution.py:472
  704.9 21.7 %all-to-all-done.2.down.down_parts = bf16[8,192,640]{2,1,0:T(8,128)(2,1)S(1)} async-done(((bf16[8,192,640]{2,1,0:T(8,128)(2,1)}), bf16[8,192,640]{2,1,0:T(8,128)(2,1)S(1)}, u32[]{:S(2)}, u32[]{:S(2)}) %all-to-all-start.2) | async-done | bytes 1966112 | tf_op jit(solution)/shard_map/all_to_all | solution.py:986
  794.0 12.6 %collective-permute-done.64 = bf16[4,48,3072]{2,1,0:T(8,128)(2,1)} collective-permute-done((bf16[4,48,3072]{2,1,0:T(8,128)(2,1)}, bf16[4,48,3072]{2,1,0:T(8,128)(2,1)}, u32[]{:S(2)}, u32[]{:S(2)}) %collective-permute-start.64) | collective-permute-done | bytes 1179680 | tf_op jit(solution)/shard_map/ppermute | solution.py:792
  817.2 11.1 %collective-permute-done.65 = bf16[4,48,1152]{2,1,0:T(8,128)(2,1)S(1)} collective-permute-done((bf16[4,48,1152]{2,1,0:T(8,128)(2,1)S(1)}, bf16[4,48,1152]{2,1,0:T(8,128)(2,1)S(1)}, u32[]{:S(2)}, u32[]{:S(2)}) %collective-permute-start.65) | collective-permute-done | bytes 442400 | tf_op jit(solution)/shard_map/ppermute | solution.py:792
  857.9 37.0 %collective-permute-done.72 = bf16[48,3072]{1,0:T(8,128)(2,1)S(1)} collective-permute-done((bf16[48,3072]{1,0:T(8,128)(2,1)S(1)}, bf16[48,3072]{1,0:T(8,128)(2,1)S(1)}, u32[]{:S(2)}, u32[]{:S(2)}) %collective-permute-start.72) | collective-permute-done | bytes 294944 | tf_op jit(solution)/shard_map/ppermute | solution.py:792
  920.8 10.6 %unpack.1 = (f32[192,10240]{1,0:T(8,128)}, f32[192,5120]{1,0:T(8,128)}) custom-call(s32[2]{0:T(128)} %pad_add_fusion.ids, bf16[8,192,1280]{2,1,0:T(8,128)(2,1)} %all-to-all-done.3.up.up_parts, bf16[8,192,1280]{2,1,0:T(8,128)(2,1)} %all-to-all-done.3.up.up_parts, bf16[8,192,640]{2,1,0:T(8,128)(2,1)} %copy-done.7, bf16[8,192,640]{2,1,0:T(8,128)(2,1)} %copy-done.7, ...), custom_call_target="tpu_custom_call" | custom-call | bytes 11797248 | tf_op jit(solution)/shard_map/unpack/pallas_call | solution.py:472
  948.1 14.9 %collective-permute-done.82 = bf16[128,1536]{1,0:T(8,128)(2,1)S(1)} collective-permute-done((bf16[128,1536]{1,0:T(8,128)(2,1)S(1)}, bf16[128,1536]{1,0:T(8,128)(2,1)S(1)}, u32[]{:S(2)}, u32[]{:S(2)}) %collective-permute-start.82) | collective-permute-done | bytes 393248 | tf_op jit(solution)/shard_map/ppermute | solution.py:792
  (503 shorter events, 497.1 us)
Async XLA Ops:
  92.5 76.9 %all-to-all-start = ((bf16[8,192,640]{2,1,0:T(8,128)(2,1)}), bf16[8,192,640]{2,1,0:T(8,128)(2,1)S(1)}, u32[]{:S(2)}, u32[]{:S(2)}) async-start(bf16[8,192,640]{2,1,0:T(8,128)(2,1)} %get-tuple-element.356), calls=%async_computation | async-start | bytes 3932160 | tf_op jit(solution)/shard_map/all_to_all | solution.py:986
  113.6 47.4 %collective-permute-start.17 = (bf16[4,48,1536]{2,1,0:T(8,128)(2,1)S(1)}, bf16[4,48,1536]{2,1,0:T(8,128)(2,1)S(1)}, u32[]{:S(2)}, u32[]{:S(2)}) collective-permute-start(bf16[4,48,1536]{2,1,0:T(8,128)(2,1)S(1)} %pad_maximum_fusion.22), channel_id=1, source_target_pairs={{0,16},{1,9},{2,18},{3,11},{4,20},{5,13},{6,22},{7,15},{8,24},{9,1... | collective-permute-start | bytes 1769480 | tf_op jit(solution)/shard_map/ppermute | solution.py:792
  114.3 46.7 %collective-permute-start.18 = (bf16[4,48,1536]{2,1,0:T(8,128)(2,1)S(1)}, bf16[4,48,1536]{2,1,0:T(8,128)(2,1)S(1)}, u32[]{:S(2)}, u32[]{:S(2)}) collective-permute-start(bf16[4,48,1536]{2,1,0:T(8,128)(2,1)S(1)} %pad_maximum_fusion.23), channel_id=1, source_target_pairs={{0,16},{1,9},{2,18},{3,11},{4,20},{5,13},{6,22},{7,15},{8,24},{9,1... | collective-permute-start | bytes 1769480 | tf_op jit(solution)/shard_map/ppermute | solution.py:792
  117.9 43.1 %collective-permute-start.15 = (bf16[128,1024]{1,0:T(8,128)(2,1)S(1)}, bf16[128,1024]{1,0:T(8,128)(2,1)S(1)}, u32[]{:S(2)}, u32[]{:S(2)}) collective-permute-start(bf16[128,1024]{1,0:T(8,128)(2,1)S(1)} %copy-done.71), channel_id=1, source_target_pairs={{0,4},{1,5},{2,6},{3,7},{4,0},{5,1},{6,2},{7,3},{8,12},{9,13},{10,... | collective-permute-start | bytes 786440 | tf_op jit(solution)/shard_map/ppermute | solution.py:792
  120.2 40.8 %collective-permute-start.16 = (bf16[128,1024]{1,0:T(8,128)(2,1)S(1)}, bf16[128,1024]{1,0:T(8,128)(2,1)S(1)}, u32[]{:S(2)}, u32[]{:S(2)}) collective-permute-start(bf16[128,1024]{1,0:T(8,128)(2,1)S(1)} %copy-done.71), channel_id=1, source_target_pairs={{0,6},{1,7},{2,4},{3,5},{4,2},{5,3},{6,0},{7,1},{8,14},{9,15},{10,... | collective-permute-start | bytes 786440 | tf_op jit(solution)/shard_map/ppermute | solution.py:792
  276.7 82.7 %collective-permute-start.32 = (bf16[8,128,1664]{2,1,0:T(8,128)(2,1)S(1)}, bf16[8,128,1664]{2,1,0:T(8,128)(2,1)}, u32[]{:S(2)}, u32[]{:S(2)}) collective-permute-start(bf16[8,128,1664]{2,1,0:T(8,128)(2,1)S(1)} %pad_maximum_fusion.1.half.slots_half), channel_id=1, source_target_pairs={{0,1},{1,0},{2,3},{3,2},{4,5},{5,4},{6,7},{7,6},{8,9},{9,8},{10,11... | collective-permute-start | bytes 10223624 | tf_op jit(solution)/shard_map/ppermute | solution.py:792
  277.4 102.6 %all-to-all-start.1 = ((bf16[8,192,1280]{2,1,0:T(8,128)(2,1)}), bf16[8,192,1280]{2,1,0:T(8,128)(2,1)}, u32[]{:S(2)}, u32[]{:S(2)}) async-start(bf16[8,192,1280]{2,1,0:T(8,128)(2,1)} %get-tuple-element.398), calls=%async_computation.1 | async-start | bytes 7864320 | tf_op jit(solution)/shard_map/all_to_all | solution.py:986
  282.0 77.4 %collective-permute-start.31 = (bf16[4,128,1664]{2,1,0:T(8,128)(2,1)}, bf16[4,128,1664]{2,1,0:T(8,128)(2,1)S(1)}, u32[]{:S(2)}, u32[]{:S(2)}) collective-permute-start(bf16[4,128,1664]{2,1,0:T(8,128)(2,1)} %pad_maximum_fusion.8), channel_id=1, source_target_pairs={{0,16},{1,9},{2,18},{3,11},{4,20},{5,13},{6,22},{7,15},{8,24},{9,1... | collective-permute-start | bytes 5111816 | tf_op jit(solution)/shard_map/ppermute | solution.py:792
  283.8 75.6 %collective-permute-start.33 = (bf16[2,128,1664]{2,1,0:T(8,128)(2,1)}, bf16[2,128,1664]{2,1,0:T(8,128)(2,1)S(1)}, u32[]{:S(2)}, u32[]{:S(2)}) collective-permute-start(bf16[2,128,1664]{2,1,0:T(8,128)(2,1)} %pad_maximum_fusion.20), channel_id=1, source_target_pairs={{0,8},{1,17},{2,10},{3,19},{4,12},{5,21},{6,14},{7,23},{8,0},{9,25... | collective-permute-start | bytes 2555912 | tf_op jit(solution)/shard_map/ppermute | solution.py:792
  285.5 73.9 %collective-permute-start.30 = (bf16[128,1664]{1,0:T(8,128)(2,1)}, bf16[128,1664]{1,0:T(8,128)(2,1)S(1)}, u32[]{:S(2)}, u32[]{:S(2)}) collective-permute-start(bf16[128,1664]{1,0:T(8,128)(2,1)} %copy-done.15), channel_id=1, source_target_pairs={{0,6},{1,7},{2,4},{3,5},{4,2},{5,3},{6,0},{7,1},{8,14},{9,15},{10,... | collective-permute-start | bytes 1277960 | tf_op jit(solution)/shard_map/ppermute | solution.py:792
  365.3 31.4 %collective-permute-start.34 = (bf16[8,128,1664]{2,1,0:T(8,128)(2,1)S(1)}, bf16[8,128,1664]{2,1,0:T(8,128)(2,1)}, u32[]{:S(2)}, u32[]{:S(2)}) collective-permute-start(bf16[8,128,1664]{2,1,0:T(8,128)(2,1)S(1)} %pad_maximum_fusion.2.half), channel_id=1, source_target_pairs={{0,1},{1,0},{2,3},{3,2},{4,5},{5,4},{6,7},{7,6},{8,9},{9,8},{10,11... | collective-permute-start | bytes 10223624 | tf_op jit(solution)/shard_map/ppermute | solution.py:792
  426.4 36.6 %collective-permute-start.39 = (bf16[8,128,1664]{2,1,0:T(8,128)(2,1)}, bf16[8,128,1664]{2,1,0:T(8,128)(2,1)}, u32[]{:S(2)}, u32[]{:S(2)}) collective-permute-start(bf16[8,128,1664]{2,1,0:T(8,128)(2,1)} %pad_maximum_fusion.4.half), channel_id=1, source_target_pairs={{0,1},{1,0},{2,3},{3,2},{4,5},{5,4},{6,7},{7,6},{8,9},{9,8},{10,11... | collective-permute-start | bytes 10223624 | tf_op jit(solution)/shard_map/ppermute | solution.py:792
  552.2 40.4 %collective-permute-start.45 = (bf16[2,128,1664]{2,1,0:T(8,128)(2,1)S(1)}, bf16[2,128,1664]{2,1,0:T(8,128)(2,1)S(1)}, u32[]{:S(2)}, u32[]{:S(2)}) collective-permute-start(bf16[2,128,1664]{2,1,0:T(8,128)(2,1)S(1)} %get-tuple-element.455), channel_id=1, source_target_pairs={{0,8},{1,17},{2,10},{3,19},{4,12},{5,21},{6,14},{7,23},{8,0},{9,25... | collective-permute-start | bytes 2555912 | tf_op jit(solution)/shard_map/ppermute | solution.py:792
  553.1 39.5 %collective-permute-start.46 = (bf16[128,1664]{1,0:T(8,128)(2,1)S(1)}, bf16[128,1664]{1,0:T(8,128)(2,1)S(1)}, u32[]{:S(2)}, u32[]{:S(2)}) collective-permute-start(bf16[128,1664]{1,0:T(8,128)(2,1)S(1)} %fusion.28), channel_id=1, source_target_pairs={{0,2},{1,3},{2,0},{3,1},{4,6},{5,7},{6,4},{7,5},{8,10},{9,11},{10,... | collective-permute-start | bytes 1277960 | tf_op jit(solution)/shard_map/ppermute | solution.py:792
  593.6 31.5 %collective-permute-start.47 = (bf16[128,1664]{1,0:T(8,128)(2,1)}, bf16[128,1664]{1,0:T(8,128)(2,1)}, u32[]{:S(2)}, u32[]{:S(2)}) collective-permute-start(bf16[128,1664]{1,0:T(8,128)(2,1)} %get-tuple-element.460), channel_id=1, source_target_pairs={{0,4},{1,5},{2,6},{3,7},{4,0},{5,1},{6,2},{7,3},{8,12},{9,13},{10,... | collective-permute-start | bytes 1277960 | tf_op jit(solution)/shard_map/ppermute | solution.py:792
  658.9 67.8 %all-to-all-start.2 = ((bf16[8,192,640]{2,1,0:T(8,128)(2,1)}), bf16[8,192,640]{2,1,0:T(8,128)(2,1)S(1)}, u32[]{:S(2)}, u32[]{:S(2)}) async-start(bf16[8,192,640]{2,1,0:T(8,128)(2,1)} %get-tuple-element.502), calls=%async_computation.2 | async-start | bytes 3932160 | tf_op jit(solution)/shard_map/all_to_all | solution.py:986
  684.1 48.3 %collective-permute-start.56 = (bf16[4,128,1536]{2,1,0:T(8,128)(2,1)}, bf16[4,128,1536]{2,1,0:T(8,128)(2,1)}, u32[]{:S(2)}, u32[]{:S(2)}) collective-permute-start(bf16[4,128,1536]{2,1,0:T(8,128)(2,1)} %get-tuple-element.499), channel_id=1, source_target_pairs={{0,16},{1,9},{2,18},{3,11},{4,20},{5,13},{6,22},{7,15},{8,24},{9,1... | collective-permute-start | bytes 4718600 | tf_op jit(solution)/shard_map/ppermute | solution.py:792
  686.9 45.5 %collective-permute-start.57 = (bf16[2,128,1536]{2,1,0:T(8,128)(2,1)}, bf16[2,128,1536]{2,1,0:T(8,128)(2,1)}, u32[]{:S(2)}, u32[]{:S(2)}) collective-permute-start(bf16[2,128,1536]{2,1,0:T(8,128)(2,1)} %get-tuple-element.500), channel_id=1, source_target_pairs={{0,8},{1,17},{2,10},{3,19},{4,12},{5,21},{6,14},{7,23},{8,0},{9,25... | collective-permute-start | bytes 2359304 | tf_op jit(solution)/shard_map/ppermute | solution.py:792
  687.9 38.7 %collective-permute-start.53 = (bf16[128,1024]{1,0:T(8,128)(2,1)}, bf16[128,1024]{1,0:T(8,128)(2,1)S(1)}, u32[]{:S(2)}, u32[]{:S(2)}) collective-permute-start(bf16[128,1024]{1,0:T(8,128)(2,1)} %get-tuple-element.496), channel_id=1, source_target_pairs={{0,2},{1,3},{2,0},{3,1},{4,6},{5,7},{6,4},{7,5},{8,10},{9,11},{10,... | collective-permute-start | bytes 786440 | tf_op jit(solution)/shard_map/ppermute | solution.py:792
  695.5 36.9 %collective-permute-start.54 = (bf16[128,1024]{1,0:T(8,128)(2,1)}, bf16[128,1024]{1,0:T(8,128)(2,1)}, u32[]{:S(2)}, u32[]{:S(2)}) collective-permute-start(bf16[128,1024]{1,0:T(8,128)(2,1)} %get-tuple-element.497), channel_id=1, source_target_pairs={{0,4},{1,5},{2,6},{3,7},{4,0},{5,1},{6,2},{7,3},{8,12},{9,13},{10,... | collective-permute-start | bytes 786440 | tf_op jit(solution)/shard_map/ppermute | solution.py:792
  696.6 35.8 %collective-permute-start.55 = (bf16[128,1024]{1,0:T(8,128)(2,1)}, bf16[128,1024]{1,0:T(8,128)(2,1)}, u32[]{:S(2)}, u32[]{:S(2)}) collective-permute-start(bf16[128,1024]{1,0:T(8,128)(2,1)} %get-tuple-element.498), channel_id=1, source_target_pairs={{0,6},{1,7},{2,4},{3,5},{4,2},{5,3},{6,0},{7,1},{8,14},{9,15},{10,... | collective-permute-start | bytes 786440 | tf_op jit(solution)/shard_map/ppermute | solution.py:792
  780.1 133.6 %all-to-all-start.3 = ((bf16[8,192,1280]{2,1,0:T(8,128)(2,1)}), bf16[8,192,1280]{2,1,0:T(8,128)(2,1)}, u32[]{:S(2)}, u32[]{:S(2)}) async-start(bf16[8,192,1280]{2,1,0:T(8,128)(2,1)} %get-tuple-element.554), calls=%async_computation.3 | async-start | bytes 7864320 | tf_op jit(solution)/shard_map/all_to_all | solution.py:986
  844.2 50.7 %collective-permute-start.72 = (bf16[48,3072]{1,0:T(8,128)(2,1)S(1)}, bf16[48,3072]{1,0:T(8,128)(2,1)S(1)}, u32[]{:S(2)}, u32[]{:S(2)}) collective-permute-start(bf16[48,3072]{1,0:T(8,128)(2,1)S(1)} %get-tuple-element.543), channel_id=1, source_target_pairs={{0,4},{1,5},{2,6},{3,7},{4,0},{5,1},{6,2},{7,3},{8,12},{9,13},{10,... | collective-permute-start | bytes 884744 | tf_op jit(solution)/shard_map/ppermute | solution.py:792
  844.2 50.7 %collective-permute-start.73 = (bf16[48,3072]{1,0:T(8,128)(2,1)S(1)}, bf16[48,3072]{1,0:T(8,128)(2,1)S(1)}, u32[]{:S(2)}, u32[]{:S(2)}) collective-permute-start(bf16[48,3072]{1,0:T(8,128)(2,1)S(1)} %get-tuple-element.544), channel_id=1, source_target_pairs={{0,6},{1,7},{2,4},{3,5},{4,2},{5,3},{6,0},{7,1},{8,14},{9,15},{10,... | collective-permute-start | bytes 884744 | tf_op jit(solution)/shard_map/ppermute | solution.py:792
  (151 other events, 2317.1 us)

commit v3 on v2

--- a/solution.py
+++ b/solution.py
@@ -518,33 +518,34 @@
     )
 
 
-def take_rows(offsets, array, parts, count, fine):
-    width = array.shape[1]
-
-    def kernel(at, source, *refs):
-        targets, done = refs[:parts], refs[-1]
-        copies = []
+def dense_terms(offsets, products, parts, count, fine):
+    height = products[0][0].shape[1]
+    width = max(first + two.shape[1] for _, two, first in products)
+    firsts = [first for _, _, first in products]
+
+    def kernel(at, *refs):
+        sources, targets, held = refs[: 2 * len(firsts)], refs[2 * len(firsts) : -1], refs[-1]
+        total = {}
+        for n, first in enumerate(firsts):
+            found = dot(sources[2 * n][...], sources[2 * n + 1][...], cols_by_cols)
+            total[first] = total[first] + found if first in total else found
+        for first, found in total.items():
+            held[:, first : first + found.shape[1]] = found.astype(jnp.bfloat16)
         for n, target in enumerate(targets):
             for i in range(count):
                 row = pl.multiple_of(at[n * count + i], 16)
-                copies.append(
-                    pltpu.make_async_copy(
-                        source.at[pl.ds(row, fine)], target.at[i], done.at[n * count + i]
-                    )
-                )
-        for copy in copies:
-            copy.start()
-        for copy in copies:
-            copy.wait()
-
+                target[i] = held[pl.ds(row, fine)]
+
+    operands = [array for one, two, _ in products for array in (one, two)]
     return call(
         kernel,
-        "take_rows",
-        [shaped((count, fine, width), array.dtype)] * parts,
-        [in_place],
+        "dense_terms",
+        [shaped((count, fine, width))] * parts,
+        [whole_spec(array.shape) for array in operands],
         [out_spec((count, fine, width), (0, 0, 0))] * parts,
-        (offsets, array),
-        scratch=[pltpu.SemaphoreType.DMA((parts * count,))],
+        (offsets,) + tuple(operands),
+        scratch=[pltpu.VMEM((height, width), jnp.bfloat16)],
+        flops=2 * height * width * products[0][0].shape[0],
     )
 
 
@@ -802,6 +803,13 @@
 
 to_core = hop_pairs(lambda e, s: (e, s ^ 1))
 to_line = [hop_pairs(lambda e, s, k=k: (e, s ^ (2 * k))) for k in range(4)]
+over_middle = [
+    (e * SHARDS + s, e * SHARDS + (s ^ 6)) for e in range(GROUPS) for s in range(2, 6)
+]
+from_middle = [
+    (e * SHARDS + s, e * SHARDS + (s ^ 2)) for e in range(GROUPS) for s in range(2, 6)
+]
+to_middle = [(there, here) for here, there in from_middle]
 to_first = hop_pairs(lambda e, s: (e ^ (1 + s % 2), s))
 to_second = hop_pairs(lambda e, s: (e ^ (2 - s % 2), s))
 
@@ -854,8 +862,35 @@
     return [Flow(one_hop(own, to_line[k])) for k in (1, 2, 3)]
 
 
+def line_spread(own, marks):
+    near = yield own, to_line[1]
+    marks.append(near)
+    two = jnp.stack([own, near])
+    crossed = yield two, over_middle
+    passed = yield crossed, from_middle
+    at = lax.axis_index("shard") // 2
+    return jnp.where((at == 1) | (at == 2), crossed, passed)
+
+
+def line_collect(near, far):
+    passed = yield jnp.stack(far), to_middle
+    far = add_low(jnp.stack(far), passed)
+    crossed = yield far, over_middle
+    at = lax.axis_index("shard") // 2
+    middle = (at == 1) | (at == 2)
+    both = jnp.stack(near).astype(jnp.float32) + jnp.where(middle, crossed, 0).astype(jnp.float32)
+    back = yield both[1].astype(jnp.bfloat16), to_line[1]
+    return both[0] + back.astype(jnp.float32)
+
+
+def by_distance(far):
+    at = lax.axis_index("shard") // 2
+    middle = (at == 1) | (at == 2)
+    return [jnp.where(middle, far[1 - i], far[i]) for i in range(2)]
+
+
 def spread_pair(pieces):
-    two = jnp.stack(pieces)
+    two = jnp.stack(pieces) if isinstance(pieces, list) else pieces
     first = yield two, to_first
     four = jnp.concatenate([two, first])
     second = yield four, to_second
@@ -986,13 +1021,16 @@
         return lax.all_to_all(packed, "shard", split_axis=0, concat_axis=0, tiled=True)
 
     w = line_flows(dense_own)
+    g_marks, x_marks = [], []
+    g_line = Flow(line_spread(grad_pay, g_marks))
     order.round(w[:2])
     w_near = Flow(spread_pair([dense_own, w[0].result]))
-    order.round([w[2], w_near])
+    order.round([w[2], w_near, g_line])
     w_far = Flow(spread_pair([w[1].result, w[2].result]))
+    g_near = Flow(spread_pair([grad_pay, g_marks[0]]))
     owned_down = exchange(order.tie(pack_down)).reshape(height, hid_width)
     order.round([w_near, w_far])
-    order.round([w_near, w_far])
+    order.round([w_near, w_far, g_line])
     o = line_flows(out_own)
     order.round([w_far] + o)
     dense_full = place_rows(fine_at, w_near.result + w_far.result, height)
@@ -1030,12 +1068,13 @@
         Flow(spread_pair([out_own, o[0].result])),
         Flow(spread_pair([o[1].result, o[2].result])),
     ]
-    queries, key_value = order.round(o_pairs, (queries, key_value))
+    queries, key_value = order.round(o_pairs + [g_line, g_near], (queries, key_value))
+    g_far = Flow(spread_pair(g_line.result))
     kv = line_flows(key_value)
-    order.round(kv + o_pairs)
+    order.round(kv + o_pairs + [g_near])
     kv_line = jnp.concatenate([key_value] + [flow.result for flow in kv])
     kv_core = Flow(one_hop(kv_line, to_core))
-    owned_down = order.round([kv_core] + o_pairs, owned_down)
+    owned_down = order.round([kv_core] + o_pairs + [g_near, g_far], owned_down)
     kv_other = kv_core.result
     out_full = place_rows(fine_at, o_pairs[0].result + o_pairs[1].result, height)
     block_order = jnp.arange(SHARDS, dtype=jnp.int32)
@@ -1089,20 +1128,12 @@
         [normed_mid, gate_low, gate_rest, jnp.zeros((rows, 128 - 2 * EXPERTS), low)], 1
     )
 
-    g = line_flows(grad_pay)
-    row_pay = order.round(g[:2], row_pay)
-    g_near = Flow(spread_pair([grad_pay, g[0].result]))
-    x = line_flows(row_pay)
-    order.round([x[0], g[2], g_near])
-    g_far = Flow(spread_pair([g[1].result, g[2].result]))
-    x_near = Flow(spread_pair([row_pay, x[0].result]))
-    order.round([x[1], x_near, g_near])
-    order.round([x[2], x_near, g_near, g_far])
-    x_far = Flow(spread_pair([x[1].result, x[2].result]))
-    owned_up = order.round([x_near, x_far, g_far], owned_up)
-    order.round([x_far, g_far])
+    row_pay = order.round([g_far], row_pay)
+    x_line = Flow(line_spread(row_pay, x_marks))
+    order.round([x_line, g_far])
+    x_near = Flow(spread_pair([row_pay, x_marks[0]]))
     grad_parts = [g_near.result, g_far.result]
-    row_parts = [x_near, x_far]
+    row_parts = [x_near, None]
 
     slot_rows = GROUPS * SHARDS * CAP
     step_rows = slot_rows // 2
@@ -1143,6 +1174,11 @@
             flops=2 * step_rows * D * (hid_width + 2 * rows),
         )
         plain.append(found)
+    order.round([x_line, x_near])
+    plain = order.round([x_line, x_near], plain)
+    x_far = Flow(spread_pair(x_line.result))
+    row_parts[1] = x_far
+    owned_up = order.round([x_near, x_far], owned_up)
 
     def row_side(k):
         nonlocal xs, hid, pg
@@ -1173,6 +1209,7 @@
 
     back_near = order.round([x_far], row_side(0))
     b_near = Flow(collect_pair(*back_near))
+    order.round([x_far, b_near])
     back_far = order.round([b_near], row_side(1))
     b_far = Flow(collect_pair(*back_far))
 
@@ -1198,9 +1235,8 @@
         steps=4,
     )
     terms = order.round([b_near, b_far], terms)
-    order.round([b_near, b_far])
+    terms_down = exchange(order.tie(terms[1]))
     b_line = [Flow(one_hop(b_near.result[1], to_line[1]))]
-    terms_down = exchange(order.tie(terms[1]))
     order.round([b_far] + b_line)
 
     def out_side(k):
@@ -1215,9 +1251,11 @@
             flops=2 * step_rows * D * (hid_width + 2 * rows),
         )
 
-    b_line += [Flow(one_hop(b_far.result[i], to_line[2 + i])) for i in range(2)]
-    out_near, out_far = order.round(b_line[1:], (out_side(0), out_side(1)))
-    m_near, m_far = Flow(collect_pair(*out_near)), Flow(collect_pair(*out_far))
+    out_near = order.round([b_far], out_side(0))
+    m_near = Flow(collect_pair(*out_near))
+    b_line += [Flow(one_hop(piece, to_line[2 + i])) for i, piece in enumerate(by_distance(b_far.result))]
+    out_far, terms_down = order.round(b_line[1:] + [m_near], (out_side(1), terms_down))
+    m_far = Flow(collect_pair(*out_far))
     grad_sum = total_of([b_near.result[0]] + [flow.result for flow in b_line])
     terms_up = exchange(order.tie(terms[0]))
 
@@ -1228,8 +1266,6 @@
     grad_out = output_cotangent.astype(full)
     mean_two = jnp.mean(scaled_two * normal_two, -1, keepdims=True)
     mid_grad = grad_out + inverse_two * (scaled_two - normal_two * mean_two)
-    moe_gain_part = jnp.sum(scaled_two * normal_two, 0)
-    router_part = dot(normed_mid, logit_grad, cols_by_cols)
     branch_grad = mid_grad.astype(low)
     attended_grad = dot(branch_grad, out_full, rows_by_cols).astype(low)
 
@@ -1249,32 +1285,27 @@
     )
     kv_theirs = jnp.concatenate([key_theirs, value_theirs], 1)
     kv_mine = jnp.concatenate([key_mine, value_mine], 1)
-    kv_theirs, kv_mine = order.round([m_near, m_far], (kv_theirs, kv_mine))
+    def dense_flow(products):
+        found = dense_terms(fine_at, products, 4, 8, fine)
+        return found, [[found[core], found[2 + core]] for core in range(2)]
+
+    out_found, out_blocks = dense_flow([(branch_grad, attended, 0)])
+    kv_theirs, kv_mine, out_blocks = order.round([m_near, m_far], (kv_theirs, kv_mine, out_blocks))
+    early = [Flow(collect_pair(out_blocks[0][i], out_blocks[1][i])) for i in range(2)]
     kv_core = Flow(one_hop(kv_theirs, to_core))
-    order.round([kv_core, m_near])
+    order.round([kv_core] + early)
     kv_half = add_low(kv_mine, kv_core.result).reshape(4, rows, 2 * kv_width)
     kv = [Flow(one_hop(kv_half[k], to_line[k])) for k in (1, 2, 3)]
-    early_part = jnp.concatenate(
-        [
-            dot(branch_grad, attended, cols_by_cols).astype(low),
-            dot(normed_in, query_back, cols_by_cols).astype(low),
-        ],
-        1,
-    )
-    early_part, terms_down = order.round(kv + [m_far, m_near], (early_part, terms_down))
+    query_blocks = dense_flow([(normed_in, query_back, 0)])[1]
+    query_blocks = order.round(kv + [m_far] + early, query_blocks)
+    middle_flows = [Flow(collect_pair(query_blocks[0][i], query_blocks[1][i])) for i in range(2)]
     kv_grad = total_of([kv_half[0]] + [flow.result for flow in kv])
-
-    def dense_flow(parts):
-        found = take_rows(fine_at, parts, 4, 8, fine)
-        mine, theirs = ([found[core], found[2 + core]] for core in range(2))
-        return [Flow(collect_pair(mine[i], theirs[i])) for i in range(2)]
 
     def line_of(near, far):
         return [Flow(one_hop(near[1], to_line[1]))] + [
             Flow(one_hop(far[i], to_line[2 + i])) for i in range(2)
         ]
 
-    early = dense_flow(early_part)
 
     def swapped(values):
         lanes = jnp.arange(values.shape[1]) % HEAD_DIM < HEAD_DIM // 2
@@ -1290,24 +1321,27 @@
     )
     mean_one = jnp.mean(scaled_one * normal_one, -1, keepdims=True)
     input_grad = mid_grad + inverse_one * (scaled_one - normal_one * mean_one)
-    attn_gain_part = jnp.sum(scaled_one * normal_one, 0)
-    small = jnp.concatenate(
+    pad_lanes = jnp.arange(128)[None, :]
+
+    def marker(lane):
+        return jnp.broadcast_to(jnp.where(pad_lanes == lane, 1.0, 0.0), (rows, 128)).astype(low)
+
+    late_blocks = dense_flow(
         [
-            router_part[:, :EXPERTS],
-            moe_gain_part[:, None],
-            attn_gain_part[:, None],
-            jnp.zeros((height, pad - 2), full),
-        ],
-        1,
-    )
-    late_part = jnp.concatenate(
-        [dot(normed_in, kv_rows, cols_by_cols).astype(low), small.astype(low)], 1
-    )
-    late_part, input_grad = order.round(early + [m_far], (late_part, input_grad.astype(low)))
-    late = dense_flow(late_part)
-    order.round(late + early)
-    order.round(late + early)
+            (normed_in, kv_rows, 0),
+            (normed_mid, logit_grad, 2 * kv_width),
+            ((scaled_two * normal_two).astype(low), marker(EXPERTS), 2 * kv_width),
+            ((scaled_one * normal_one).astype(low), marker(EXPERTS + 1), 2 * kv_width),
+        ]
+    )[1]
+    late_blocks, input_grad = order.round(
+        early + middle_flows, (late_blocks, input_grad.astype(low))
+    )
+    late = [Flow(collect_pair(late_blocks[0][i], late_blocks[1][i])) for i in range(2)]
     early_line = line_of(early[0].result, early[1].result)
+    order.round(late + middle_flows)
+    order.round(late + middle_flows + [m_near])
+    middle_line = line_of(middle_flows[0].result, middle_flows[1].result)
     order.round(late + early_line)
     late_line = line_of(late[0].result, late[1].result)
     spots = jnp.arange(GROUPS, dtype=jnp.int32) ^ group_at
@@ -1320,13 +1354,16 @@
         return Flow(share_flow(own, places))
 
     early_share = shared(early[0].result[0], early_line)
-    terms_up = order.round(late_line + [early_share], terms_up)
+    order.round(late_line + [early_share, m_far])
     late_share = shared(late[0].result[0], late_line)
-    order.round([late_share, early_share])
-    m_line = line_of(m_near.result, m_far.result)
-    order.round([late_share] + m_line)
+    terms_up = order.round([late_share, early_share] + middle_line, terms_up)
+    middle_share = shared(middle_flows[0].result[0], middle_line)
+    order.round([late_share, middle_share])
+    m_line = line_of(m_near.result, by_distance(m_far.result))
+    order.round([middle_share] + m_line)
     output = (middle + total_of([m_near.result[0]] + [flow.result for flow in m_line])).astype(low)
-    early_sum = early_share.result.astype(full)
+    out_sum = early_share.result.astype(full)
+    query_sum = middle_share.result.astype(full)
     late_sum = late_share.result.astype(full)
 
     gate_up_grad, down_grad = call(
@@ -1354,8 +1391,8 @@
     return (
         output,
         input_grad,
-        jnp.concatenate([early_sum[:, q_width:], late_sum[:, : 2 * kv_width]], 1) * gain_one,
-        early_sum[:, :q_width],
+        jnp.concatenate([query_sum, late_sum[:, : 2 * kv_width]], 1) * gain_one,
+        out_sum,
         late_sum[:, 2 * kv_width : 2 * kv_width + EXPERTS] * gain_two,
         late_sum[:, 2 * kv_width + EXPERTS + 1] / gain_one[:, 0],
         late_sum[:, 2 * kv_width + EXPERTS] / gain_two[:, 0],

time: 986 us -> 881 us (0.89); the launches traced: 971 us -> 876 us
  waiting for transfers between devices: 468 us -> 381 us
  starting transfers between devices: 170 us -> 155 us
    ppermute x84 -> x95, waiting for transfers between devices: 435 us -> 355 us  [hop(): return lax.ppermute(values, ('expert', 'shard'), pairs)]
    concatenate x8, other arithmetic: 14 us -> 26 us  [spread_pair(): eight = jnp.concatenate([four, second])]
    unnamed x177 -> x209, local copies, waits for them, and re-layouts: 5.53 us -> 16.5 us
    convert_element_type x25 -> x29, other arithmetic: 43.9 us -> 33.4 us  [add_low(): (one.astype(jnp.float32) + two.astype(jnp.float32)).astype(jnp.bfloat16)]
    ppermute x84 -> x95, starting transfers between devices: 143 us -> 137 us  [hop(): return lax.ppermute(values, ('expert', 'shard'), pairs)]
    dot_general x11 -> x7, matrix products: 20.3 us -> 17.4 us  [dot(): lax.dot_general(one, two, (dims, ((), ())), preferred_element_type=jnp.fl...]
    pallas_call x16 -> x17, Pallas kernels: 170 us -> 172 us  [call(): pl.pallas_call(kernel, name=name, out_shape=out_shape, grid_spec=pltpu.Pr...]
  transfers between devices with their start and end apart: 88 -> 99, of which waited for: 43 -> 34; matrix products, arithmetic and copies ran while one was open for 10% -> 10% of each run, Pallas kernels for 14% -> 20%
where the time goes in v3:
time: 881 us; the launch traced here: 876 us
  waiting for transfers between devices  381 us (43%)
  Pallas kernels  172 us (20%)
  starting transfers between devices  155 us (18%)
  other arithmetic  105 us (12%)
  local copies, waits for them, and re-layouts  36.3 us (4%)
  matrix products  17.4 us (2%)
  between operations  10.1 us (1%)
    ppermute x95, waiting for transfers between devices, hop(): return lax.ppermute(values, ('expert', 'shard'), pairs)  355 us
    pallas_call x17, Pallas kernels, call(): pl.pallas_call(kernel, name=name, out_shape=out_shape, grid_spec=pltpu.Pr...  172 us
    ppermute x95, starting transfers between devices, hop(): return lax.ppermute(values, ('expert', 'shard'), pairs)  137 us
    convert_element_type x29, other arithmetic, add_low(): (one.astype(jnp.float32) + two.astype(jnp.float32)).astype(jnp.bfloat16)  33.4 us
    concatenate x8, other arithmetic, spread_pair(): eight = jnp.concatenate([four, second])  26 us
    all_to_all x4, waiting for transfers between devices, exchange(): lax.all_to_all(packed, 'shard', split_axis=0, concat_axis=0, tiled=True)  25.9 us
  transfers between devices with their start and end apart: 99, of which 34 were waited for; matrix products, arithmetic and copies ran while one was open for 10% of the time, Pallas kernels for 20%

profile of v3, /device:TPU:0, one launch (start us, length us, event | category | flops | bytes accessed | tf_op | source)
XLA Modules:
  0.0 876.0 jit_solution(18084394718337386711)
XLA Ops:
  42.9 13.1 %collective-permute-done.6 = bf16[2,48,2688]{2,1,0:T(8,128)(2,1)S(1)} collective-permute-done((bf16[2,48,2688]{2,1,0:T(8,128)(2,1)S(1)}, bf16[2,48,2688]{2,1,0:T(8,128)(2,1)S(1)}, u32[]{:S(2)}, u32[]{:S(2)}) %collective-permute-start.6) | collective-permute-done | bytes 516128 | tf_op jit(solution)/shard_map/ppermute | solution.py:793
  62.3 12.9 %collective-permute-done.8 = bf16[4,48,2688]{2,1,0:T(8,128)(2,1)S(1)} collective-permute-done((bf16[4,48,2688]{2,1,0:T(8,128)(2,1)S(1)}, bf16[4,48,2688]{2,1,0:T(8,128)(2,1)S(1)}, u32[]{:S(2)}, u32[]{:S(2)}) %collective-permute-start.8) | collective-permute-done | bytes 1032224 | tf_op jit(solution)/shard_map/ppermute | solution.py:793
  142.2 53.0 %collective-permute-done.19 = bf16[128,1024]{1,0:T(8,128)(2,1)S(1)} collective-permute-done((bf16[128,1024]{1,0:T(8,128)(2,1)}, bf16[128,1024]{1,0:T(8,128)(2,1)S(1)}, u32[]{:S(2)}, u32[]{:S(2)}) %collective-permute-start.19) | collective-permute-done | bytes 262176 | tf_op jit(solution)/shard_map/ppermute | solution.py:793
  206.8 11.0 %collective-permute-done.28 = bf16[2,128,1664]{2,1,0:T(8,128)(2,1)} collective-permute-done((bf16[2,128,1664]{2,1,0:T(8,128)(2,1)S(1)}, bf16[2,128,1664]{2,1,0:T(8,128)(2,1)}, u32[]{:S(2)}, u32[]{:S(2)}) %collective-permute-start.28) | collective-permute-done | bytes 852000 | tf_op jit(solution)/shard_map/ppermute | solution.py:793
  221.6 14.8 %attend.1 = (bf16[128,1536]{1,0:T(8,128)(2,1)}, f32[4,128,128]{2,1,0:T(8,128)}) custom-call(s32[2]{0:T(128)} %pad_add_fusion.ids, bf16[128,1536]{1,0:T(8,128)(2,1)} %get-tuple-element.382.queries, bf16[512,1024]{1,0:T(8,128)(2,1)} %constant_dynamic-update-slice_fusion.key_line.value_line, bf16[512,1024]{1,0:T(8,128)(2,1)} %collective-permute-done.24.key_other.value_other, ...), custom_call_target="tpu_custom_call" | custom-call | flops 805306368 | bytes 5111808 | tf_op jit(solution)/shard_map/attend/pallas_call | solution.py:472
  257.9 10.4 %collective-permute-done.30 = bf16[128,1664]{1,0:T(8,128)(2,1)S(1)} collective-permute-done((bf16[128,1664]{1,0:T(8,128)(2,1)S(1)}, bf16[128,1664]{1,0:T(8,128)(2,1)S(1)}, u32[]{:S(2)}, u32[]{:S(2)}) %collective-permute-start.30) | collective-permute-done | bytes 426016 | tf_op jit(solution)/shard_map/ppermute | solution.py:793
  292.7 9.6 %grad_side.2 = (bf16[2,1024,1536]{2,1,0:T(8,128)(2,1)}, f32[512,640]{1,0:T(8,128)}) custom-call(s32[2]{0:T(128)} %pad_add_fusion.ids, bf16[8,128,1664]{2,1,0:T(8,128)(2,1)} %pad_maximum_fusion.half.slots_half, bf16[8,128,1664]{2,1,0:T(8,128)(2,1)} %collective-permute-done.27.other.slots_other, ...), custom_call_target="tpu_custom_call", output_to_operand_aliasing={{0}: (5, {})} | custom-call | flops 1409286144 | bytes 17039360 | tf_op jit(solution)/shard_map/grad_side/pallas_call | solution.py:472
  302.3 9.6 %grad_side.3 = (bf16[2,1024,1536]{2,1,0:T(8,128)(2,1)}, f32[512,640]{1,0:T(8,128)}) custom-call(s32[2]{0:T(128)} %pad_add_fusion.ids, bf16[8,128,1664]{2,1,0:T(8,128)(2,1)} %copy-done.3, bf16[8,128,1664]{2,1,0:T(8,128)(2,1)} %copy-done.4, bf16[1536,640]{1,0:T(8,128)(2,1)} %bitcast.173, bf16[1536,640]{1,0:T(8,128)(2,1)} %bitcast.174, ...), custom_call_target="tpu_custom_call", output_to_operand_aliasing={{0}: (5, {})} | custom-call | flops 1409286144 | bytes 17039360 | tf_op jit(solution)/shard_map/grad_side/pallas_call | solution.py:472
  311.9 35.4 %collective-permute-done.34 = bf16[2,128,1664]{2,1,0:T(8,128)(2,1)S(1)} collective-permute-done((bf16[2,128,1664]{2,1,0:T(8,128)(2,1)}, bf16[2,128,1664]{2,1,0:T(8,128)(2,1)S(1)}, u32[]{:S(2)}, u32[]{:S(2)}) %collective-permute-start.34) | collective-permute-done | bytes 852000 | tf_op jit(solution)/shard_map/ppermute | solution.py:793
  353.4 25.9 %all-to-all-done.1 = bf16[8,192,1280]{2,1,0:T(8,128)(2,1)} async-done(((bf16[8,192,1280]{2,1,0:T(8,128)(2,1)}), bf16[8,192,1280]{2,1,0:T(8,128)(2,1)}, u32[]{:S(2)}, u32[]{:S(2)}) %all-to-all-start.1) | async-done | bytes 3932192 | tf_op jit(solution)/shard_map/all_to_all | solution.py:1021
  387.5 18.0 %row_side.2 = (bf16[8,128,1664]{2,1,0:T(8,128)(2,1)}, bf16[8,128,1664]{2,1,0:T(8,128)(2,1)}, bf16[2,1024,1536]{2,1,0:T(8,128)(2,1)}, bf16[1024,640]{1,0:T(8,128)(2,1)}, bf16[1024,1280]{1,0:T(8,128)(2,1)}) custom-call(s32[2]{0:T(128)} %pad_add_fusion.ids, ...), custom_call_target="tpu_custom_call", output_to_operand_aliasing={{2}: (8, {}), {3}: (9, {}), {4}: (10, {})} | custom-call | flops 4831838208 | bytes 33030144 | tf_op jit(solution)/shard_map/row_side/pallas_call | solution.py:472
  405.5 13.3 %pad_maximum_fusion.3.half = bf16[8,128,1664]{2,1,0:T(8,128)(2,1)S(1)} fusion(bf16[4,128,1664]{2,1,0:T(8,128)(2,1)} %collective-permute-done.38, bf16[2,128,1664]{2,1,0:T(8,128)(2,1)} %collective-permute-done.37, bf16[2,128,1664]{2,1,0:T(8,128)(2,1)} %broadcast_select_fusion), kind=kLoop, calls=%fused_computation.5 | loop fusion | flops 3407872 | bytes 6815744 | tf_op jit(solution)/shard_map/concatenate | solution.py:897
  433.2 18.1 %row_side.3 = (bf16[8,128,1664]{2,1,0:T(8,128)(2,1)}, bf16[8,128,1664]{2,1,0:T(8,128)(2,1)}, bf16[2,1024,1536]{2,1,0:T(8,128)(2,1)}, bf16[1024,640]{1,0:T(8,128)(2,1)}, bf16[1024,1280]{1,0:T(8,128)(2,1)}) custom-call(s32[2]{0:T(128)} %pad_add_fusion.ids, ...), custom_call_target="tpu_custom_call", output_to_operand_aliasing={{2}: (8, {}), {3}: (9, {}), {4}: (10, {})} | custom-call | flops 4831838208 | bytes 33030144 | tf_op jit(solution)/shard_map/row_side/pallas_call | solution.py:472
  455.1 12.6 %terms.1 = (bf16[8,192,1280]{2,1,0:T(8,128)(2,1)}, bf16[8,192,640]{2,1,0:T(8,128)(2,1)}) custom-call(s32[2]{0:T(128)} %pad_add_fusion.ids, bf16[2,1024,1536]{2,1,0:T(8,128)(2,1)} %get-tuple-element.481.xs, bf16[2,1024,1536]{2,1,0:T(8,128)(2,1)} %get-tuple-element.482.gs, bf16[1024,1280]{1,0:T(8,128)(2,1)} %get-tuple-element.483.pg, ...), custom_call_target="tpu_custom_call" | custom-call | flops 6039797760 | bytes 16515072 | tf_op jit(solution)/shard_map/terms/pallas_call | solution.py:472
  472.5 11.6 %collective-permute-done.45 = bf16[128,1664]{1,0:T(8,128)(2,1)S(1)} collective-permute-done((bf16[128,1664]{1,0:T(8,128)(2,1)S(1)}, bf16[128,1664]{1,0:T(8,128)(2,1)S(1)}, u32[]{:S(2)}, u32[]{:S(2)}) %collective-permute-start.45) | collective-permute-done | bytes 426016 | tf_op jit(solution)/shard_map/ppermute | solution.py:793
  520.4 60.6 %collective-permute-done.47 = bf16[128,1664]{1,0:T(8,128)(2,1)S(1)} collective-permute-done((bf16[128,1664]{1,0:T(8,128)(2,1)S(1)}, bf16[128,1664]{1,0:T(8,128)(2,1)S(1)}, u32[]{:S(2)}, u32[]{:S(2)}) %collective-permute-start.47) | collective-permute-done | bytes 426016 | tf_op jit(solution)/shard_map/ppermute | solution.py:793
  602.3 18.2 %attend_back.1 = (bf16[128,1536]{1,0:T(8,128)(2,1)}, bf16[512,512]{1,0:T(8,128)(2,1)}, bf16[512,512]{1,0:T(8,128)(2,1)}, bf16[512,512]{1,0:T(8,128)(2,1)}, bf16[512,512]{1,0:T(8,128)(2,1)}) custom-call(s32[2]{0:T(128)} %pad_add_fusion.ids, bf16[128,1536]{1,0:T(8,128)(2,1)} %get-tuple-element.382.queries, bf16[128,1536]{1,0:T(8,128)(2,1)} %convolution_convert_fusion.grads, ...), custom_call_target="tpu_custom_call" | custom-call | flops 2013265920 | bytes 5898240 | tf_op jit(solution)/shard_map/attend_back/pallas_call | solution.py:472
  633.2 9.2 %collective-permute-start.55 = (bf16[128,1024]{1,0:T(8,128)(2,1)}, bf16[128,1024]{1,0:T(8,128)(2,1)}, u32[]{:S(2)}, u32[]{:S(2)}) collective-permute-start(bf16[128,1024]{1,0:T(8,128)(2,1)} %get-tuple-element.551), channel_id=1, source_target_pairs={{0,2},{1,3},{2,0},{3,1},{4,6},{5,7},{6,4},{7,5},{8,10},{9,11},{10,... | collective-permute-start | bytes 786440 | tf_op jit(solution)/shard_map/ppermute | solution.py:793
  665.9 11.5 %collective-permute-done.56 = bf16[128,1024]{1,0:T(8,128)(2,1)} collective-permute-done((bf16[128,1024]{1,0:T(8,128)(2,1)S(1)}, bf16[128,1024]{1,0:T(8,128)(2,1)}, u32[]{:S(2)}, u32[]{:S(2)}) %collective-permute-start.56) | collective-permute-done | bytes 262176 | tf_op jit(solution)/shard_map/ppermute | solution.py:793
  730.4 17.3 %collective-permute-done.71 = bf16[2,48,1536]{2,1,0:T(8,128)(2,1)S(1)} collective-permute-done((bf16[2,48,1536]{2,1,0:T(8,128)(2,1)S(1)}, bf16[2,48,1536]{2,1,0:T(8,128)(2,1)S(1)}, u32[]{:S(2)}, u32[]{:S(2)}) %collective-permute-start.71) | collective-permute-done | bytes 294944 | tf_op jit(solution)/shard_map/ppermute | solution.py:793
  753.2 22.0 %collective-permute-start.76 = (bf16[48,1536]{1,0:T(8,128)(2,1)S(1)}, bf16[48,1536]{1,0:T(8,128)(2,1)S(1)}, u32[]{:S(2)}, u32[]{:S(2)}) collective-permute-start(bf16[48,1536]{1,0:T(8,128)(2,1)S(1)} %fusion.44), channel_id=1, source_target_pairs={{0,2},{1,3},{2,0},{3,1},{4,6},{5,7},{6,4},{7,5},{8,10},{9,11},{10,... | collective-permute-start | bytes 442376 | tf_op jit(solution)/shard_map/ppermute | solution.py:793
  824.7 10.6 %unpack.1 = (f32[192,10240]{1,0:T(8,128)}, f32[192,5120]{1,0:T(8,128)}) custom-call(s32[2]{0:T(128)} %pad_add_fusion.ids, bf16[8,192,1280]{2,1,0:T(8,128)(2,1)} %all-to-all-done.3.up.up_parts, bf16[8,192,1280]{2,1,0:T(8,128)(2,1)} %all-to-all-done.3.up.up_parts, bf16[8,192,640]{2,1,0:T(8,128)(2,1)} %copy-done.7, bf16[8,192,640]{2,1,0:T(8,128)(2,1)} %copy-done.7, ...), custom_call_target="tpu_custom_call" | custom-call | bytes 11797248 | tf_op jit(solution)/shard_map/unpack/pallas_call | solution.py:472
  844.9 9.8 %collective-permute-done.92 = bf16[128,1536]{1,0:T(8,128)(2,1)S(1)} collective-permute-done((bf16[128,1536]{1,0:T(8,128)(2,1)}, bf16[128,1536]{1,0:T(8,128)(2,1)S(1)}, u32[]{:S(2)}, u32[]{:S(2)}) %collective-permute-start.92) | collective-permute-done | bytes 393248 | tf_op jit(solution)/shard_map/ppermute | solution.py:793
  854.6 15.9 %collective-permute-done.93 = bf16[128,1536]{1,0:T(8,128)(2,1)} collective-permute-done((bf16[128,1536]{1,0:T(8,128)(2,1)}, bf16[128,1536]{1,0:T(8,128)(2,1)}, u32[]{:S(2)}, u32[]{:S(2)}) %collective-permute-start.93) | collective-permute-done | bytes 393248 | tf_op jit(solution)/shard_map/ppermute | solution.py:793
  (564 shorter events, 421.8 us)
Async XLA Ops:
  123.5 71.8 %collective-permute-start.23 = (bf16[4,128,1664]{2,1,0:T(8,128)(2,1)}, bf16[4,128,1664]{2,1,0:T(8,128)(2,1)}, u32[]{:S(2)}, u32[]{:S(2)}) collective-permute-start(bf16[4,128,1664]{2,1,0:T(8,128)(2,1)} %pad_maximum_fusion.6), channel_id=1, source_target_pairs={{0,16},{1,9},{2,18},{3,11},{4,20},{5,13},{6,22},{7,15},{8,24},{9,1... | collective-permute-start | bytes 5111816 | tf_op jit(solution)/shard_map/ppermute | solution.py:793
  128.0 78.8 %all-to-all-start = ((bf16[8,192,640]{2,1,0:T(8,128)(2,1)}), bf16[8,192,640]{2,1,0:T(8,128)(2,1)S(1)}, u32[]{:S(2)}, u32[]{:S(2)}) async-start(bf16[8,192,640]{2,1,0:T(8,128)(2,1)} %get-tuple-element.408), calls=%async_computation | async-start | bytes 3932160 | tf_op jit(solution)/shard_map/all_to_all | solution.py:1021
  131.8 63.5 %collective-permute-start.19 = (bf16[128,1024]{1,0:T(8,128)(2,1)}, bf16[128,1024]{1,0:T(8,128)(2,1)S(1)}, u32[]{:S(2)}, u32[]{:S(2)}) collective-permute-start(bf16[128,1024]{1,0:T(8,128)(2,1)} %get-tuple-element.390), channel_id=1, source_target_pairs={{0,4},{1,5},{2,6},{3,7},{4,0},{5,1},{6,2},{7,3},{8,12},{9,13},{10,... | collective-permute-start | bytes 786440 | tf_op jit(solution)/shard_map/ppermute | solution.py:793
  134.7 60.5 %collective-permute-start.20 = (bf16[128,1024]{1,0:T(8,128)(2,1)}, bf16[128,1024]{1,0:T(8,128)(2,1)S(1)}, u32[]{:S(2)}, u32[]{:S(2)}) collective-permute-start(bf16[128,1024]{1,0:T(8,128)(2,1)} %get-tuple-element.390), channel_id=1, source_target_pairs={{0,6},{1,7},{2,4},{3,5},{4,2},{5,3},{6,0},{7,1},{8,14},{9,15},{10,... | collective-permute-start | bytes 786440 | tf_op jit(solution)/shard_map/ppermute | solution.py:793
  136.2 59.1 %collective-permute-start.21 = (bf16[4,48,1536]{2,1,0:T(8,128)(2,1)}, bf16[4,48,1536]{2,1,0:T(8,128)(2,1)S(1)}, u32[]{:S(2)}, u32[]{:S(2)}) collective-permute-start(bf16[4,48,1536]{2,1,0:T(8,128)(2,1)} %pad_maximum_fusion.18), channel_id=1, source_target_pairs={{0,16},{1,9},{2,18},{3,11},{4,20},{5,13},{6,22},{7,15},{8,24},{9,1... | collective-permute-start | bytes 1769480 | tf_op jit(solution)/shard_map/ppermute | solution.py:793
  138.1 57.2 %collective-permute-start.22 = (bf16[4,48,1536]{2,1,0:T(8,128)(2,1)}, bf16[4,48,1536]{2,1,0:T(8,128)(2,1)S(1)}, u32[]{:S(2)}, u32[]{:S(2)}) collective-permute-start(bf16[4,48,1536]{2,1,0:T(8,128)(2,1)} %pad_maximum_fusion.19), channel_id=1, source_target_pairs={{0,16},{1,9},{2,18},{3,11},{4,20},{5,13},{6,22},{7,15},{8,24},{9,1... | collective-permute-start | bytes 1769480 | tf_op jit(solution)/shard_map/ppermute | solution.py:793
  220.4 29.5 %collective-permute-start.29 = (bf16[4,128,1664]{2,1,0:T(8,128)(2,1)}, bf16[4,128,1664]{2,1,0:T(8,128)(2,1)}, u32[]{:S(2)}, u32[]{:S(2)}) collective-permute-start(bf16[4,128,1664]{2,1,0:T(8,128)(2,1)} %pad_maximum_fusion.7), channel_id=1, source_target_pairs={{0,16},{1,9},{2,18},{3,11},{4,20},{5,13},{6,22},{7,15},{8,24},{9,1... | collective-permute-start | bytes 5111816 | tf_op jit(solution)/shard_map/ppermute | solution.py:793
  273.5 105.8 %all-to-all-start.1 = ((bf16[8,192,1280]{2,1,0:T(8,128)(2,1)}), bf16[8,192,1280]{2,1,0:T(8,128)(2,1)}, u32[]{:S(2)}, u32[]{:S(2)}) async-start(bf16[8,192,1280]{2,1,0:T(8,128)(2,1)} %get-tuple-element.446), calls=%async_computation.1 | async-start | bytes 7864320 | tf_op jit(solution)/shard_map/all_to_all | solution.py:1021
  287.2 60.0 %collective-permute-start.35 = (bf16[4,128,1664]{2,1,0:T(8,128)(2,1)S(1)}, bf16[4,128,1664]{2,1,0:T(8,128)(2,1)S(1)}, u32[]{:S(2)}, u32[]{:S(2)}) collective-permute-start(bf16[4,128,1664]{2,1,0:T(8,128)(2,1)S(1)} %pad_maximum_fusion.8), channel_id=1, source_target_pairs={{0,16},{1,9},{2,18},{3,11},{4,20},{5,13},{6,22},{7,15},{8,24},{9,1... | collective-permute-start | bytes 5111816 | tf_op jit(solution)/shard_map/ppermute | solution.py:793
  288.1 59.2 %collective-permute-start.34 = (bf16[2,128,1664]{2,1,0:T(8,128)(2,1)}, bf16[2,128,1664]{2,1,0:T(8,128)(2,1)S(1)}, u32[]{:S(2)}, u32[]{:S(2)}) collective-permute-start(bf16[2,128,1664]{2,1,0:T(8,128)(2,1)} %collective-permute-done.32), channel_id=1, source_target_pairs={{2,0},{3,1},{4,6},{5,7},{10,8},{11,9},{12,14},{13,15},{18,16},{19,... | collective-permute-start | bytes 2555912 | tf_op jit(solution)/shard_map/ppermute | solution.py:793
  502.9 78.0 %all-to-all-start.2 = ((bf16[8,192,640]{2,1,0:T(8,128)(2,1)}), bf16[8,192,640]{2,1,0:T(8,128)(2,1)S(1)}, u32[]{:S(2)}, u32[]{:S(2)}) async-start(bf16[8,192,640]{2,1,0:T(8,128)(2,1)} %get-tuple-element.511), calls=%async_computation.2 | async-start | bytes 3932160 | tf_op jit(solution)/shard_map/all_to_all | solution.py:1021
  508.5 72.5 %collective-permute-start.49 = (bf16[8,128,1536]{2,1,0:T(8,128)(2,1)}, bf16[8,128,1536]{2,1,0:T(8,128)(2,1)}, u32[]{:S(2)}, u32[]{:S(2)}) collective-permute-start(bf16[8,128,1536]{2,1,0:T(8,128)(2,1)} %get-tuple-element.508), channel_id=1, source_target_pairs={{0,1},{1,0},{2,3},{3,2},{4,5},{5,4},{6,7},{7,6},{8,9},{9,8},{10,11... | collective-permute-start | bytes 9437192 | tf_op jit(solution)/shard_map/ppermute | solution.py:793
  508.9 72.1 %collective-permute-start.47 = (bf16[128,1664]{1,0:T(8,128)(2,1)S(1)}, bf16[128,1664]{1,0:T(8,128)(2,1)S(1)}, u32[]{:S(2)}, u32[]{:S(2)}) collective-permute-start(bf16[128,1664]{1,0:T(8,128)(2,1)S(1)} %get-tuple-element.506), channel_id=1, source_target_pairs={{0,4},{1,5},{2,6},{3,7},{4,0},{5,1},{6,2},{7,3},{8,12},{9,13},{10,... | collective-permute-start | bytes 1277960 | tf_op jit(solution)/shard_map/ppermute | solution.py:793
  511.5 69.5 %collective-permute-start.48 = (bf16[128,1664]{1,0:T(8,128)(2,1)S(1)}, bf16[128,1664]{1,0:T(8,128)(2,1)S(1)}, u32[]{:S(2)}, u32[]{:S(2)}) collective-permute-start(bf16[128,1664]{1,0:T(8,128)(2,1)S(1)} %get-tuple-element.507), channel_id=1, source_target_pairs={{0,6},{1,7},{2,4},{3,5},{4,2},{5,3},{6,0},{7,1},{8,14},{9,15},{10,... | collective-permute-start | bytes 1277960 | tf_op jit(solution)/shard_map/ppermute | solution.py:793
  588.0 34.2 %collective-permute-start.51 = (bf16[8,128,1536]{2,1,0:T(8,128)(2,1)}, bf16[8,128,1536]{2,1,0:T(8,128)(2,1)}, u32[]{:S(2)}, u32[]{:S(2)}) collective-permute-start(bf16[8,128,1536]{2,1,0:T(8,128)(2,1)} %get-tuple-element.519), channel_id=1, source_target_pairs={{0,1},{1,0},{2,3},{3,2},{4,5},{5,4},{6,7},{7,6},{8,9},{9,8},{10,11... | collective-permute-start | bytes 9437192 | tf_op jit(solution)/shard_map/ppermute | solution.py:793
  588.1 34.2 %collective-permute-start.50 = (bf16[4,128,1536]{2,1,0:T(8,128)(2,1)}, bf16[4,128,1536]{2,1,0:T(8,128)(2,1)}, u32[]{:S(2)}, u32[]{:S(2)}) collective-permute-start(bf16[4,128,1536]{2,1,0:T(8,128)(2,1)} %get-tuple-element.518), channel_id=1, source_target_pairs={{0,16},{1,9},{2,18},{3,11},{4,20},{5,13},{6,22},{7,15},{8,24},{9,1... | collective-permute-start | bytes 4718600 | tf_op jit(solution)/shard_map/ppermute | solution.py:793
  632.4 45.1 %collective-permute-start.58 = (bf16[4,128,1536]{2,1,0:T(8,128)(2,1)}, bf16[4,128,1536]{2,1,0:T(8,128)(2,1)}, u32[]{:S(2)}, u32[]{:S(2)}) collective-permute-start(bf16[4,128,1536]{2,1,0:T(8,128)(2,1)} %get-tuple-element.554), channel_id=1, source_target_pairs={{0,16},{1,9},{2,18},{3,11},{4,20},{5,13},{6,22},{7,15},{8,24},{9,1... | collective-permute-start | bytes 4718600 | tf_op jit(solution)/shard_map/ppermute | solution.py:793
  642.3 35.1 %collective-permute-start.59 = (bf16[4,48,1536]{2,1,0:T(8,128)(2,1)}, bf16[4,48,1536]{2,1,0:T(8,128)(2,1)}, u32[]{:S(2)}, u32[]{:S(2)}) collective-permute-start(bf16[4,48,1536]{2,1,0:T(8,128)(2,1)} %get-tuple-element.555), channel_id=1, source_target_pairs={{0,16},{1,9},{2,18},{3,11},{4,20},{5,13},{6,22},{7,15},{8,24},{9,1... | collective-permute-start | bytes 1769480 | tf_op jit(solution)/shard_map/ppermute | solution.py:793
  643.6 33.8 %collective-permute-start.60 = (bf16[4,48,1536]{2,1,0:T(8,128)(2,1)}, bf16[4,48,1536]{2,1,0:T(8,128)(2,1)}, u32[]{:S(2)}, u32[]{:S(2)}) collective-permute-start(bf16[4,48,1536]{2,1,0:T(8,128)(2,1)} %get-tuple-element.556), channel_id=1, source_target_pairs={{0,16},{1,9},{2,18},{3,11},{4,20},{5,13},{6,22},{7,15},{8,24},{9,1... | collective-permute-start | bytes 1769480 | tf_op jit(solution)/shard_map/ppermute | solution.py:793
  655.1 156.8 %all-to-all-start.3 = ((bf16[8,192,1280]{2,1,0:T(8,128)(2,1)}), bf16[8,192,1280]{2,1,0:T(8,128)(2,1)}, u32[]{:S(2)}, u32[]{:S(2)}) async-start(bf16[8,192,1280]{2,1,0:T(8,128)(2,1)} %get-tuple-element.633), calls=%async_computation.3 | async-start | bytes 7864320 | tf_op jit(solution)/shard_map/all_to_all | solution.py:1021
  751.1 37.5 %collective-permute-start.74 = (bf16[2,48,1152]{2,1,0:T(8,128)(2,1)S(1)}, bf16[2,48,1152]{2,1,0:T(8,128)(2,1)S(1)}, u32[]{:S(2)}, u32[]{:S(2)}) collective-permute-start(bf16[2,48,1152]{2,1,0:T(8,128)(2,1)S(1)} %get-tuple-element.607), channel_id=1, source_target_pairs={{0,8},{1,17},{2,10},{3,19},{4,12},{5,21},{6,14},{7,23},{8,0},{9,25... | collective-permute-start | bytes 663560 | tf_op jit(solution)/shard_map/ppermute | solution.py:793
  752.3 36.2 %collective-permute-start.75 = (bf16[2,48,1152]{2,1,0:T(8,128)(2,1)S(1)}, bf16[2,48,1152]{2,1,0:T(8,128)(2,1)S(1)}, u32[]{:S(2)}, u32[]{:S(2)}) collective-permute-start(bf16[2,48,1152]{2,1,0:T(8,128)(2,1)S(1)} %get-tuple-element.608), channel_id=1, source_target_pairs={{0,8},{1,17},{2,10},{3,19},{4,12},{5,21},{6,14},{7,23},{8,0},{9,25... | collective-permute-start | bytes 663560 | tf_op jit(solution)/shard_map/ppermute | solution.py:793
  840.4 30.1 %collective-permute-start.93 = (bf16[128,1536]{1,0:T(8,128)(2,1)}, bf16[128,1536]{1,0:T(8,128)(2,1)}, u32[]{:S(2)}, u32[]{:S(2)}) collective-permute-start(bf16[128,1536]{1,0:T(8,128)(2,1)} %get-tuple-element.644), channel_id=1, source_target_pairs={{0,4},{1,5},{2,6},{3,7},{4,0},{5,1},{6,2},{7,3},{8,12},{9,13},{10,... | collective-permute-start | bytes 1179656 | tf_op jit(solution)/shard_map/ppermute | solution.py:793
  841.6 29.0 %collective-permute-start.94 = (bf16[128,1536]{1,0:T(8,128)(2,1)S(1)}, bf16[128,1536]{1,0:T(8,128)(2,1)}, u32[]{:S(2)}, u32[]{:S(2)}) collective-permute-start(bf16[128,1536]{1,0:T(8,128)(2,1)S(1)} %get-tuple-element.645), channel_id=1, source_target_pairs={{0,6},{1,7},{2,4},{3,5},{4,2},{5,3},{6,0},{7,1},{8,14},{9,15},{10,... | collective-permute-start | bytes 1179656 | tf_op jit(solution)/shard_map/ppermute | solution.py:793
  (178 other events, 2522.8 us)

commit v4 on v3

--- a/solution.py
+++ b/solution.py
@@ -549,39 +549,52 @@
     )
 
 
-def pack_kernel(ids, up, gate_part, up_part, down, down_part, gain, ups, downs):
-    width = up.shape[1]
-    part = gate_part.shape[1]
+def pack_kernel(ids, up, gate_part, up_part, down, down_part, gain, *packs):
+    width = down.shape[1]
     scale = gain[...]
-
-    def scaled(ref):
-        return (ref[...].astype(jnp.float32) * scale).astype(jnp.bfloat16)
-
-    ups[0, :, :width] = scaled(up)
-    ups[0, :, width : width + part] = scaled(gate_part)
-    ups[0, :, width + part :] = scaled(up_part)
-    downs[0, :, : down.shape[1]] = down[...]
-    downs[0, :, down.shape[1] :] = down_part[...]
-
-
-def unpack_kernel(ids, up, up_parts, down, down_parts, gain, up_grad, down_grad):
-    part = down_parts.shape[2]
+    step = pl.program_id(0)
+
+    def scaled(rows):
+        return (rows.astype(jnp.float32) * scale).astype(jnp.bfloat16)
+
+    for k in range(SHARDS):
+
+        @pl.when(step == k)
+        def _(k=k):
+            downs, ups = packs[2 * k : 2 * k + 2]
+            downs[0, :, :width] = down[...]
+            downs[0, :, width:] = down_part[...]
+            ups[0, :, : 2 * width] = scaled(up[...])
+            part = down_part.shape[1]
+            ups[0, :, 2 * width : 2 * width + part] = scaled(gate_part[...])
+            ups[0, :, 2 * width + part :] = scaled(up_part[...])
+
+
+def unpack_kernel(ids, *refs):
+    pieces, gain, up_grad, down_grad = refs[: 2 * SHARDS], refs[-3], refs[-2], refs[-1]
     scale = gain[...]
-    expert = pl.program_id(0)
-    whole = pl.num_programs(0) - 2
-
-    @pl.when(expert < whole)
-    def _():
-        up_grad[...] = up[0].astype(jnp.float32) * scale
-        down_grad[...] = down[0].astype(jnp.float32)
-
-    @pl.when(expert >= whole)
-    def _():
-        for i in range(up_parts.shape[0]):
-            at = i * part
-            up_grad[:, at : at + part] = up_parts[i, :, :part].astype(jnp.float32) * scale
-            up_grad[:, H + at : H + at + part] = up_parts[i, :, part:].astype(jnp.float32) * scale
-            down_grad[:, at : at + part] = down_parts[i].astype(jnp.float32)
+    step = pl.program_id(0)
+    share = SHARDS // (pl.num_programs(0) - SHARDS)
+    part = (pieces[1].shape[2] - H) // 3
+    for k in range(SHARDS):
+        one, two = pieces[2 * k : 2 * k + 2]
+        source = ids[2] ^ k
+
+        @pl.when(step == k)
+        def _(one=one, two=two):
+            down_grad[...] = one[0, :, :H].astype(jnp.float32)
+            up_grad[:, :H] = one[0, :, H:].astype(jnp.float32) * scale
+            up_grad[:, H:] = two[0, :, :H].astype(jnp.float32) * scale
+
+        @pl.when(step == SHARDS + source // share)
+        def _(two=two, source=source):
+            at = pl.multiple_of(source % share * part, part)
+            at_up = pl.multiple_of(H + source % share * part, part)
+            down_grad[:, pl.ds(at, part)] = two[0, :, H : H + part].astype(jnp.float32)
+            gate = two[0, :, H + part : H + 2 * part].astype(jnp.float32)
+            up_grad[:, pl.ds(at, part)] = gate * scale
+            up = two[0, :, H + 2 * part :].astype(jnp.float32)
+            up_grad[:, pl.ds(at_up, part)] = up * scale
 
 
 def turn(rows, cosine, sine):
@@ -697,7 +710,8 @@
     return jnp.where(wanted == place, 1.0, 0.0).astype(jnp.bfloat16)
 
 
-def grad_side_kernel(ids, half, other, down_one, down_two, kept_gs, gs, plain):
+def grad_side_kernel(ids, half, other, down_one, down_two, *refs):
+    gs, plain = refs[-2:]
     count = half.shape[0]
     for i in range(2 * count):
         source = half if i < count else other
@@ -722,9 +736,9 @@
 
 
 def row_side_kernel(
-    ids, half, other, slots_half, slots_other, plain, up_one, up_two, kept_xs, kept_hid, kept_pg,
-    back_half, back_other, xs, hid, pg, gates, tokens, back_rows,
+    ids, half, other, slots_half, slots_other, plain, gate_one, gate_two, up_one, up_two, *refs
 ):
+    back_half, back_other, xs, hid, pg, gates, tokens, back_rows = refs[-8:]
     total = xs.shape[1]
     count = half.shape[0]
     for i in range(2 * count):
@@ -740,25 +754,26 @@
             own = extra[n * CAP : (n + 1) * CAP]
             gates[n, at] = lane_value(own, ids[n]) + lane_value(own, ids[n] + EXPERTS)
     first = 0
-    for n, up in ((0, up_one), (1, up_two)):
-        width = up.shape[1] // 2
-        projected = dot(xs[n], up[...], rows_by_cols)
-        gate_part = projected[:, :width]
-        up_part = projected[:, width:]
-        own_plain = plain[:, first : first + width]
+    second = hid.shape[1]
+    for n, gate_weight, up_weight in ((0, gate_one, up_one), (1, gate_two, up_two)):
+        width = up_weight.shape[1]
+        gate_part = dot(xs[n], gate_weight[...], rows_by_cols)
+        up_part = dot(xs[n], up_weight[...], rows_by_cols)
+        at = slice(first, first + width)
+        at_up = slice(second + first, second + first + width)
+        own_plain = plain[:, at]
         sigma = 1.0 / (1.0 + jnp.exp(-gate_part))
         silu_value = gate_part * sigma
         hidden = silu_value * up_part
         tokens[n] = jnp.sum(hidden * own_plain, 1, keepdims=True)
-        hid[:, first : first + width] = (hidden * gates[n]).astype(jnp.bfloat16)
+        hid[:, at] = (hidden * gates[n]).astype(jnp.bfloat16)
         hidden_grad = own_plain * gates[n]
         slope = sigma * (1.0 + gate_part * (1.0 - sigma))
-        pg[:, 2 * first : 2 * first + width] = (hidden_grad * up_part * slope).astype(jnp.bfloat16)
-        pg[:, 2 * first + width : 2 * first + 2 * width] = (hidden_grad * silu_value).astype(
-            jnp.bfloat16
-        )
-        own_pg = pg[:, 2 * first : 2 * first + 2 * width]
-        back_rows[n, :, :D] = dot(own_pg, up[...], rows_by_rows).astype(jnp.bfloat16)
+        pg[:, at] = (hidden_grad * up_part * slope).astype(jnp.bfloat16)
+        pg[:, at_up] = (hidden_grad * silu_value).astype(jnp.bfloat16)
+        row_grad = dot(pg[:, at], gate_weight[...], rows_by_rows)
+        row_grad = row_grad + dot(pg[:, at_up], up_weight[...], rows_by_rows)
+        back_rows[n, :, :D] = row_grad.astype(jnp.bfloat16)
         lanes = lax.broadcasted_iota(jnp.int32, (total, 128), 1)
         back_rows[n, :, D:] = jnp.where(lanes == ids[n], tokens[n], 0.0).astype(jnp.bfloat16)
         first += width
@@ -774,19 +789,21 @@
     combine_rows(ids, out_rows, slots_half, slots_other, back_half, back_other)
 
 
-def terms_kernel(ids, xs, gs, pg, hid, terms_up, terms_down):
-    depth = terms_up.shape[1]
-    width = terms_down.shape[2]
-    pieces = (
-        (terms_up, xs, pg, 0, 0, 2 * H),
-        (terms_up, xs, pg, 1, 2 * H, 2 * width),
-        (terms_down, gs, hid, 0, 0, H),
-        (terms_down, gs, hid, 1, H, width),
-    )
-    for target, one, two, n, left, right in pieces:
-        found = dot(one[n], two[:, left:right], cols_by_cols).astype(jnp.bfloat16)
+def terms_kernel(ids, xs, gs, pg, hid, terms):
+    depth = terms.shape[1]
+    width = hid.shape[1]
+    for one, two, n, shift, first, count in (
+        (gs, hid, 0, 0, 0, H),
+        (xs, pg, 0, 0, H, H),
+        (xs, pg, 0, width, 2 * H, H),
+        (gs, hid, 1, H, 3 * H, width - H),
+        (xs, pg, 1, H, 2 * H + width, width - H),
+        (xs, pg, 1, width + H, H + 2 * width, width - H),
+    ):
+        found = dot(one[n], two[:, shift : shift + count], cols_by_cols).astype(jnp.bfloat16)
         for i in range(2):
-            target[i, :, left:right] = found[i * depth : (i + 1) * depth]
+            at = i ^ ids[2] % 2
+            terms[pl.ds(at, 1), :, first : first + count] = found[i * depth : (i + 1) * depth][None]
 
 
 def hop(values, pairs):
@@ -897,6 +914,16 @@
     eight = jnp.concatenate([four, second])
     other = yield eight, to_core
     return eight, other
+
+
+def spread_all(line):
+    four = jnp.stack(line)
+    first = yield four, to_first
+    eight = jnp.concatenate([four, first])
+    second = yield eight, to_second
+    half = jnp.concatenate([eight, second])
+    other = yield half, to_core
+    return half, other
 
 
 def collect_pair(mine, theirs):
@@ -964,7 +991,7 @@
     gain_two = moe_gain.astype(full)[:, None]
     expert_one = group_at * own_experts + shard_at
     expert_two = group_at * own_experts + whole + shard_at // share
-    ids = jnp.stack([expert_one, expert_two])
+    ids = jnp.stack([expert_one, expert_two, shard_at])
     order = Order(jnp.zeros((8, 128), full))
 
     spot = jnp.arange(GROUPS * SHARDS, dtype=jnp.int32)
@@ -974,6 +1001,11 @@
     spot_group = jnp.where(spot_q == 1, spot_mate, jnp.where(spot_q == 2, 3 - spot_mate, spot_q))
     spot_line = spot // 16 * 2 + spot % 2
     fine_at = (shard_at ^ (2 * spot_line + spot_core)) * depth + (group_at ^ spot_group) * fine
+    half_core = spot // 16
+    half_mate = 1 + (shard_at % 2 ^ half_core)
+    half_q = spot % 16 // 4
+    half_group = jnp.where(half_q == 1, half_mate, jnp.where(half_q == 2, 3 - half_mate, half_q))
+    half_at = (shard_at ^ (2 * (spot % 4) + half_core)) * depth + (group_at ^ half_group) * fine
 
     expert_ids = jnp.arange(EXPERTS, dtype=jnp.int32)
     hits = jnp.any(routes[:, :, None] == expert_ids[None, None, :], 1)
@@ -994,13 +1026,13 @@
     out_own = fine_rows(out_weight)
 
     def column_spec(width, index):
-        return pl.BlockSpec((depth, width), lambda d, ids: (0, index(d)))
+        return pl.BlockSpec((depth, width), lambda k, ids: (0, index(ids[2] ^ k)))
 
     to_parts = H // part
-    pack_up, pack_down = call(
+    packs = call(
         pack_kernel,
         "pack",
-        (shaped((SHARDS, depth, 2 * hid_width)), shaped((SHARDS, depth, hid_width))),
+        [shaped((1, depth, hid_width)), shaped((1, depth, 2 * hid_width))] * SHARDS,
         [
             column_spec(2 * H, lambda d: d),
             column_spec(part, lambda d: (whole + d // share) * 2 * to_parts + d % share),
@@ -1010,17 +1042,37 @@
             pl.BlockSpec((depth, 1), lambda d, ids: (0, 0)),
         ],
         [
-            pl.BlockSpec((1, depth, 2 * hid_width), lambda d, ids: (d, 0, 0)),
-            pl.BlockSpec((1, depth, hid_width), lambda d, ids: (d, 0, 0)),
-        ],
+            out_spec((1, depth, hid_width), (0, 0, 0)),
+            out_spec((1, depth, 2 * hid_width), (0, 0, 0)),
+        ]
+        * SHARDS,
         (ids, gate_up_weight, gate_up_weight, gate_up_weight, down_weight, down_weight, gain_two),
         steps=SHARDS,
     )
 
-    def exchange(packed):
-        return lax.all_to_all(packed, "shard", split_axis=0, concat_axis=0, tiled=True)
+    to_shard = [hop_pairs(lambda e, s, k=k: (e, s ^ k)) for k in range(SHARDS)]
+    shard_rows = (shard_at ^ jnp.arange(SHARDS, dtype=jnp.int32)) * depth
+
+    def exchange(pieces):
+        flows = [[Flow(one_hop(piece, to_shard[k])) for piece in pieces[k]] for k in range(1, SHARDS)]
+        near = [flows[k - 1][n] for n in range(len(pieces[0])) for k in (2, 3)]
+        far = [flows[k - 1][n] for n in range(len(pieces[0])) for k in (4, 5, 6, 7)]
+        return flows, flows[0], near, far
+
+    def exchanged(pieces, flows, n):
+        parts = [pieces[0][n]] + [flow[n].result for flow in flows]
+        return place_rows(shard_rows, parts, height)
+
+    s_pieces = [packs[2 * k : 2 * k + 2] for k in range(SHARDS)]
+    s_flows, core, near, far = exchange(s_pieces)
+
+    def some(flows, count):
+        taken = flows[:count]
+        del flows[:count]
+        return taken
 
     w = line_flows(dense_own)
+    o = line_flows(out_own)
     g_marks, x_marks = [], []
     g_line = Flow(line_spread(grad_pay, g_marks))
     order.round(w[:2])
@@ -1028,14 +1080,12 @@
     order.round([w[2], w_near, g_line])
     w_far = Flow(spread_pair([w[1].result, w[2].result]))
     g_near = Flow(spread_pair([grad_pay, g_marks[0]]))
-    owned_down = exchange(order.tie(pack_down)).reshape(height, hid_width)
-    order.round([w_near, w_far])
-    order.round([w_near, w_far, g_line])
-    o = line_flows(out_own)
-    order.round([w_far] + o)
+    order.round([w_near, w_far] + some(far, 1) + some(near, 1) + core)
+    order.round([w_near, w_far] + o)
+    o_all = Flow(spread_all([out_own] + [flow.result for flow in o]))
+    order.round([w_far, o_all])
     dense_full = place_rows(fine_at, w_near.result + w_far.result, height)
     router_full = dense_full[:, qkv_width:]
-    owned_up = exchange(order.tie(pack_up)).reshape(height, 2 * hid_width)
 
     tokens_f = tokens_in.astype(full)
     inverse_one = lax.rsqrt(jnp.mean(tokens_f * tokens_f, -1, keepdims=True) + norm_eps)
@@ -1064,19 +1114,16 @@
         flops=2 * rows * D * qkv_width,
         steps=qkv_width // tile,
     )
-    o_pairs = [
-        Flow(spread_pair([out_own, o[0].result])),
-        Flow(spread_pair([o[1].result, o[2].result])),
-    ]
-    queries, key_value = order.round(o_pairs + [g_line, g_near], (queries, key_value))
-    g_far = Flow(spread_pair(g_line.result))
+    queries, key_value = order.round(
+        [o_all, g_near, g_line] + some(near, 1), (queries, key_value)
+    )
     kv = line_flows(key_value)
-    order.round(kv + o_pairs + [g_near])
+    order.round(kv + [o_all, g_near])
     kv_line = jnp.concatenate([key_value] + [flow.result for flow in kv])
     kv_core = Flow(one_hop(kv_line, to_core))
-    owned_down = order.round([kv_core] + o_pairs + [g_near, g_far], owned_down)
+    out_full = place_rows(half_at, o_all.result, height)
+    out_full = order.round([kv_core], out_full)
     kv_other = kv_core.result
-    out_full = place_rows(fine_at, o_pairs[0].result + o_pairs[1].result, height)
     block_order = jnp.arange(SHARDS, dtype=jnp.int32)
     block_order = shard_at ^ (block_order % 4 * 2 + block_order // 4)
     key_pos = (
@@ -1128,13 +1175,6 @@
         [normed_mid, gate_low, gate_rest, jnp.zeros((rows, 128 - 2 * EXPERTS), low)], 1
     )
 
-    row_pay = order.round([g_far], row_pay)
-    x_line = Flow(line_spread(row_pay, x_marks))
-    order.round([x_line, g_far])
-    x_near = Flow(spread_pair([row_pay, x_marks[0]]))
-    grad_parts = [g_near.result, g_far.result]
-    row_parts = [x_near, None]
-
     slot_rows = GROUPS * SHARDS * CAP
     step_rows = slot_rows // 2
     blocks = 2 * GROUPS
@@ -1142,53 +1182,49 @@
     pay_out = out_spec((blocks, rows, D + 128), (0, 0, 0))
     slot_spec = block_spec((blocks, rows, 128), (0, 0, D // 128))
     up_specs = [
-        block_spec((height, 2 * H), (0, 0)),
-        block_spec((height, 2 * part), (0, H // part)),
+        block_spec((height, H), (0, 0)),
+        block_spec((height, part), (0, 2 * to_parts)),
+        block_spec((height, H), (0, 1)),
+        block_spec((height, part), (0, 2 * to_parts + 1)),
     ]
     down_specs = [
         block_spec((height, H), (0, 0)),
         block_spec((height, part), (0, H // part)),
     ]
     back_shape = shaped((blocks, rows, D + 128))
-    gs = jnp.zeros((2, slot_rows, D), low)
-    xs = jnp.zeros((2, slot_rows, D), low)
-    hid = jnp.zeros((slot_rows, hid_width), low)
-    pg = jnp.zeros((slot_rows, 2 * hid_width), low)
-
-    def like(array):
-        return shaped(array.shape, array.dtype)
-
-    plain = []
-    for k in range(2):
-        gs, found = call(
+    gs_shape = shaped((2, slot_rows, D))
+    kept_shapes = (gs_shape, shaped((slot_rows, hid_width)), shaped((slot_rows, 2 * hid_width)))
+    kept_rows = ()
+
+    gs, plain = (), []
+
+    def grad_side(k):
+        nonlocal gs
+        gs_next, found = call(
             grad_side_kernel,
             "grad_side",
-            (like(gs), shaped((step_rows, hid_width), full)),
-            [pay_spec, pay_spec] + down_specs + [in_place],
+            (gs_shape, shaped((step_rows, hid_width), full)),
+            [pay_spec, pay_spec] + down_specs + [in_place] * len(gs),
             [
                 out_spec((2, step_rows, D), (0, k, 0)),
                 out_spec((step_rows, hid_width), (0, 0)),
             ],
-            (ids,) + grad_parts[k] + (owned_down, owned_down, gs),
-            aliases={5: 0},
+            (ids,) + (g_near, g_far)[k].result + (owned_down, owned_down) + gs,
+            aliases={5: 0} if gs else None,
             flops=2 * step_rows * D * (hid_width + 2 * rows),
         )
-        plain.append(found)
-    order.round([x_line, x_near])
-    plain = order.round([x_line, x_near], plain)
-    x_far = Flow(spread_pair(x_line.result))
-    row_parts[1] = x_far
-    owned_up = order.round([x_near, x_far], owned_up)
+        gs = (gs_next,)
+        return found
 
     def row_side(k):
-        nonlocal xs, hid, pg
-        half_back, other_back, xs, hid, pg = call(
+        nonlocal kept_rows
+        half_back, other_back, *kept_next = call(
             row_side_kernel,
             "row_side",
-            (back_shape, back_shape, like(xs), like(hid), like(pg)),
+            (back_shape, back_shape) + kept_shapes,
             [pay_spec, pay_spec, slot_spec, slot_spec, whole_spec((step_rows, hid_width))]
             + up_specs
-            + [in_place] * 3,
+            + [in_place] * len(kept_rows),
             [
                 pay_out,
                 pay_out,
@@ -1196,48 +1232,64 @@
                 out_spec((step_rows, hid_width), (k, 0)),
                 out_spec((step_rows, 2 * hid_width), (k, 0)),
             ],
-            (ids,) + row_parts[k].result + grad_parts[k] + (plain[k], owned_up, owned_up, xs, hid, pg),
+            (ids,)
+            + (x_near, x_far)[k].result
+            + (g_near, g_far)[k].result
+            + (plain[k],)
+            + (owned_up,) * 4
+            + kept_rows,
             scratch=[
                 pltpu.VMEM((2, step_rows, 1), full),
                 pltpu.VMEM((2, step_rows, 1), full),
                 pltpu.VMEM((2, step_rows, D + 128), low),
             ],
-            aliases={8: 2, 9: 3, 10: 4},
+            aliases={10: 2, 11: 3, 12: 4} if kept_rows else None,
             flops=8 * step_rows * D * (hid_width + rows),
         )
+        kept_rows = tuple(kept_next)
         return half_back, other_back
 
+    row_pay = order.round([g_near, g_line] + some(far, 3), row_pay)
+    x_line = Flow(line_spread(row_pay, x_marks))
+    g_far = Flow(spread_pair(g_line.result))
+    order.round([x_line] + some(far, 1))
+    x_near = Flow(spread_pair([row_pay, x_marks[0]]))
+    owned_down = exchanged(s_pieces, s_flows, 0)
+    owned_down = order.round([x_line, x_near, g_far] + some(near, 1), owned_down)
+    plain = [order.round([x_line, x_near, g_far] + some(far, 1), grad_side(0))]
+    x_far = Flow(spread_pair(x_line.result))
+    order.round([x_near, x_far, g_far] + some(far, 1) + near)
+    plain.append(order.round([x_far] + far, grad_side(1)))
+    owned_up = exchanged(s_pieces, s_flows, 1)
     back_near = order.round([x_far], row_side(0))
     b_near = Flow(collect_pair(*back_near))
-    order.round([x_far, b_near])
     back_far = order.round([b_near], row_side(1))
     b_far = Flow(collect_pair(*back_far))
 
+    xs, hid, pg = kept_rows
+
     def lane_block(i, ids):
-        return (0, 0, i)
+        return (0, 0, i ^ ids[2] // 2)
 
     terms = call(
         terms_kernel,
         "terms",
-        (shaped((SHARDS, depth, 2 * hid_width)), shaped((SHARDS, depth, hid_width))),
+        shaped((SHARDS, depth, 3 * hid_width)),
         [
             pl.BlockSpec((2, slot_rows, 2 * depth), lane_block),
             pl.BlockSpec((2, slot_rows, 2 * depth), lane_block),
             whole_spec((slot_rows, 2 * hid_width)),
             whole_spec((slot_rows, hid_width)),
         ],
-        [
-            pl.BlockSpec((2, depth, 2 * hid_width), lambda i, ids: (i, 0, 0)),
-            pl.BlockSpec((2, depth, hid_width), lambda i, ids: (i, 0, 0)),
-        ],
-        (ids, xs, gs, pg, hid),
+        pl.BlockSpec((2, depth, 3 * hid_width), lambda i, ids: (i, 0, 0)),
+        (ids, xs, gs[0], pg, hid),
         flops=2 * slot_rows * D * 3 * hid_width,
         steps=4,
     )
     terms = order.round([b_near, b_far], terms)
-    terms_down = exchange(order.tie(terms[1]))
-    b_line = [Flow(one_hop(b_near.result[1], to_line[1]))]
-    order.round([b_far] + b_line)
+    t_edge = 2 * H
+    t_pieces = [[terms[k, :, :t_edge][None], terms[k, :, t_edge:][None]] for k in range(SHARDS)]
+    t_flows, core, near, far = exchange(t_pieces)
 
     def out_side(k):
         return call(
@@ -1246,18 +1298,20 @@
             (shaped((blocks, rows, D)),) * 2,
             [block_spec((step_rows, hid_width), (k, 0)), slot_spec, slot_spec] + down_specs,
             [out_spec((blocks, rows, D), (0, 0, 0))] * 2,
-            (ids, hid) + grad_parts[k] + (owned_down, owned_down),
+            (ids, hid) + (g_near, g_far)[k].result + (owned_down, owned_down),
             scratch=[pltpu.VMEM((2, step_rows, D), low)],
             flops=2 * step_rows * D * (hid_width + 2 * rows),
         )
 
-    out_near = order.round([b_far], out_side(0))
-    m_near = Flow(collect_pair(*out_near))
-    b_line += [Flow(one_hop(piece, to_line[2 + i])) for i, piece in enumerate(by_distance(b_far.result))]
-    out_far, terms_down = order.round(b_line[1:] + [m_near], (out_side(1), terms_down))
-    m_far = Flow(collect_pair(*out_far))
+    out_near = order.round([b_near, b_far] + some(near, 1) + some(far, 1), out_side(0))
+    b_line = [Flow(one_hop(b_near.result[1], to_line[1]))]
+    out_far = order.round([b_far] + b_line + core, out_side(1))
+    b_line += [
+        Flow(one_hop(piece, to_line[2 + i])) for i, piece in enumerate(by_distance(b_far.result))
+    ]
+    m_near, m_far = Flow(collect_pair(*out_near)), Flow(collect_pair(*out_far))
+    order.round(b_line[1:] + [m_near, m_far])
     grad_sum = total_of([b_near.result[0]] + [flow.result for flow in b_line])
-    terms_up = exchange(order.tie(terms[0]))
 
     gate_grad = jnp.where(kept, grad_sum[:, D : D + EXPERTS], 0.0)
     logit_grad = gates * (gate_grad - jnp.sum(gates * gate_grad, -1, keepdims=True))
@@ -1286,26 +1340,23 @@
     kv_theirs = jnp.concatenate([key_theirs, value_theirs], 1)
     kv_mine = jnp.concatenate([key_mine, value_mine], 1)
     def dense_flow(products):
-        found = dense_terms(fine_at, products, 4, 8, fine)
-        return found, [[found[core], found[2 + core]] for core in range(2)]
-
-    out_found, out_blocks = dense_flow([(branch_grad, attended, 0)])
-    kv_theirs, kv_mine, out_blocks = order.round([m_near, m_far], (kv_theirs, kv_mine, out_blocks))
-    early = [Flow(collect_pair(out_blocks[0][i], out_blocks[1][i])) for i in range(2)]
+        return dense_terms(half_at, products, 2, 4 * GROUPS, fine)
+
+    kv_theirs, kv_mine = order.round(
+        [m_near, m_far] + some(far, 3) + some(near, 2), (kv_theirs, kv_mine)
+    )
     kv_core = Flow(one_hop(kv_theirs, to_core))
-    order.round([kv_core] + early)
+    order.round([kv_core, m_near, m_far])
+    m_line = Flow(line_collect(m_near.result, m_far.result))
     kv_half = add_low(kv_mine, kv_core.result).reshape(4, rows, 2 * kv_width)
     kv = [Flow(one_hop(kv_half[k], to_line[k])) for k in (1, 2, 3)]
-    query_blocks = dense_flow([(normed_in, query_back, 0)])[1]
-    query_blocks = order.round(kv + [m_far] + early, query_blocks)
-    middle_flows = [Flow(collect_pair(query_blocks[0][i], query_blocks[1][i])) for i in range(2)]
+    early_blocks = dense_flow([(branch_grad, attended, 0), (normed_in, query_back, q_width)])
+    early_blocks = order.round(kv, early_blocks)
+    early = Flow(collect_all(*early_blocks))
     kv_grad = total_of([kv_half[0]] + [flow.result for flow in kv])
 
-    def line_of(near, far):
-        return [Flow(one_hop(near[1], to_line[1]))] + [
-            Flow(one_hop(far[i], to_line[2 + i])) for i in range(2)
-        ]
-
+    def line_of(blocks):
+        return [Flow(one_hop(blocks[k], to_line[k])) for k in (1, 2, 3)]
 
     def swapped(values):
         lanes = jnp.arange(values.shape[1]) % HEAD_DIM < HEAD_DIM // 2
@@ -1331,19 +1382,17 @@
             (normed_in, kv_rows, 0),
             (normed_mid, logit_grad, 2 * kv_width),
             ((scaled_two * normal_two).astype(low), marker(EXPERTS), 2 * kv_width),
-            ((scaled_one * normal_one).astype(low), marker(EXPERTS + 1), 2 * kv_width),
         ]
-    )[1]
-    late_blocks, input_grad = order.round(
-        early + middle_flows, (late_blocks, input_grad.astype(low))
-    )
-    late = [Flow(collect_pair(late_blocks[0][i], late_blocks[1][i])) for i in range(2)]
-    early_line = line_of(early[0].result, early[1].result)
-    order.round(late + middle_flows)
-    order.round(late + middle_flows + [m_near])
-    middle_line = line_of(middle_flows[0].result, middle_flows[1].result)
-    order.round(late + early_line)
-    late_line = line_of(late[0].result, late[1].result)
+    )
+    late_blocks = order.round([early] + some(far, 1) + some(near, 1), late_blocks)
+    late = Flow(collect_all(*late_blocks))
+    input_grad = order.round(
+        [late, early, m_line] + some(far, 1), input_grad.astype(low)
+    )
+    order.round([late, early] + some(far, 1))
+    early_line = line_of(early.result)
+    order.round([late, m_line] + early_line[:1] + some(far, 1))
+    late_line = line_of(late.result)
     spots = jnp.arange(GROUPS, dtype=jnp.int32) ^ group_at
     mate = 1 + shard_at % 2
     spots = jnp.where(spots == mate, 1, jnp.where(spots == 3 - mate, 2, spots))
@@ -1353,48 +1402,39 @@
         own = total_of([first] + [flow.result for flow in line]).astype(low)
         return Flow(share_flow(own, places))
 
-    early_share = shared(early[0].result[0], early_line)
-    order.round(late_line + [early_share, m_far])
-    late_share = shared(late[0].result[0], late_line)
-    terms_up = order.round([late_share, early_share] + middle_line, terms_up)
-    middle_share = shared(middle_flows[0].result[0], middle_line)
-    order.round([late_share, middle_share])
-    m_line = line_of(m_near.result, by_distance(m_far.result))
-    order.round([middle_share] + m_line)
-    output = (middle + total_of([m_near.result[0]] + [flow.result for flow in m_line])).astype(low)
-    out_sum = early_share.result.astype(full)
-    query_sum = middle_share.result.astype(full)
+    order.round(late_line + early_line[1:] + [m_line])
+    late_share = shared(late.result[0], late_line)
+    early_share = shared(early.result[0], early_line)
+    order.round([late_share, early_share] + far)
+    order.round([late_share, early_share])
+    output = (middle + m_line.result).astype(low)
+    early_sum = early_share.result.astype(full)
+    out_sum, query_sum = early_sum[:, :q_width], early_sum[:, q_width:]
     late_sum = late_share.result.astype(full)
+
+    t_parts = t_pieces[0] + [flow.result for flows in t_flows for flow in flows]
+
+    def to_expert(k, ids):
+        return (0, jnp.where(k < SHARDS, ids[2] ^ k, k))
 
     gate_up_grad, down_grad = call(
         unpack_kernel,
         "unpack",
         (shaped(gate_up_weight.shape, full), shaped(down_weight.shape, full)),
-        [
-            pl.BlockSpec((1, depth, 2 * H), lambda j, ids: (jnp.minimum(j, whole - 1), 0, 0)),
-            pl.BlockSpec(
-                (share, depth, 2 * part), lambda j, ids: (jnp.maximum(j - whole, 0), 0, to_parts)
-            ),
-            pl.BlockSpec((1, depth, H), lambda j, ids: (jnp.minimum(j, whole - 1), 0, 0)),
-            pl.BlockSpec(
-                (share, depth, part), lambda j, ids: (jnp.maximum(j - whole, 0), 0, to_parts)
-            ),
-            whole_spec((depth, 1)),
-        ],
-        [
-            pl.BlockSpec((depth, 2 * H), lambda j, ids: (0, j)),
-            pl.BlockSpec((depth, H), lambda j, ids: (0, j)),
-        ],
-        (ids, terms_up, terms_up, terms_down, terms_down, gain_two),
+        [whole_spec((1, depth, t_edge)), whole_spec((1, depth, 3 * hid_width - t_edge))] * SHARDS
+        + [whole_spec((depth, 1))],
+        [pl.BlockSpec((depth, 2 * H), to_expert), pl.BlockSpec((depth, H), to_expert)],
+        (ids,) + tuple(t_parts) + (gain_two,),
         steps=own_experts,
     )
+    qkv_sum = jnp.concatenate([query_sum, late_sum[:, : 2 * kv_width]], 1)
     return (
         output,
         input_grad,
-        jnp.concatenate([query_sum, late_sum[:, : 2 * kv_width]], 1) * gain_one,
+        qkv_sum * gain_one,
         out_sum,
         late_sum[:, 2 * kv_width : 2 * kv_width + EXPERTS] * gain_two,
-        late_sum[:, 2 * kv_width + EXPERTS + 1] / gain_one[:, 0],
+        jnp.sum(qkv_sum * qkv_weight.astype(full), 1),
         late_sum[:, 2 * kv_width + EXPERTS] / gain_two[:, 0],
         gate_up_grad,
         down_grad,

time: 881 us -> 837 us (0.950)
  other arithmetic: 105 us -> 73.4 us
  waiting for transfers between devices: 381 us -> 360 us
    all_to_all x4 -> x0, waiting for transfers between devices: 25.9 us -> none  [exchange(): lax.all_to_all(packed, 'shard', split_axis=0, concat_axis=0, tiled=True)]
    all_to_all x4 -> x0, starting transfers between devices: 17.4 us -> none  [exchange(): lax.all_to_all(packed, 'shard', split_axis=0, concat_axis=0, tiled=True)]
    concatenate x8 -> x6, other arithmetic: 26 us -> 9.93 us  [spread_pair(): eight = jnp.concatenate([four, second])]
    ppermute x95 -> x103, starting transfers between devices: 137 us -> 151 us  [hop(): return lax.ppermute(values, ('expert', 'shard'), pairs)]
    unnamed x209 -> x215, local copies, waits for them, and re-layouts: 16.5 us -> 25.9 us
    pallas_call x17 -> x18, Pallas kernels: 172 us -> 180 us  [call(): pl.pallas_call(kernel, name=name, out_shape=out_shape, grid_spec=pltpu.Pr...]
    ppermute x95 -> x103, waiting for transfers between devices: 355 us -> 360 us  [hop(): return lax.ppermute(values, ('expert', 'shard'), pairs)]
    convert_element_type x29 -> x19, other arithmetic: 33.4 us -> 29.6 us  [add_low(): (one.astype(jnp.float32) + two.astype(jnp.float32)).astype(jnp.bfloat16)]
  transfers between devices with their start and end apart: 99 -> 103, of which waited for: 34 -> 44; matrix products, arithmetic and copies ran while one was open for 10% -> 6% of each run, Pallas kernels for 20% -> 22%
where the time goes in v4:
time: 837 us; the launch traced here: 829 us
  waiting for transfers between devices  360 us (43%)
  Pallas kernels  180 us (22%)
  starting transfers between devices  151 us (18%)
  other arithmetic  73.4 us (9%)
  local copies, waits for them, and re-layouts  43.9 us (5%)
  matrix products  11.6 us (1%)
  between operations  10.2 us (1%)
    ppermute x103, waiting for transfers between devices, hop(): return lax.ppermute(values, ('expert', 'shard'), pairs)  360 us
    pallas_call x18, Pallas kernels, call(): pl.pallas_call(kernel, name=name, out_shape=out_shape, grid_spec=pltpu.Pr...  180 us
    ppermute x103, starting transfers between devices, hop(): return lax.ppermute(values, ('expert', 'shard'), pairs)  151 us
    convert_element_type x19, other arithmetic, add_low(): (one.astype(jnp.float32) + two.astype(jnp.float32)).astype(jnp.bfloat16)  29.6 us
    unnamed x215, local copies, waits for them, and re-layouts  25.9 us
  transfers between devices with their start and end apart: 103, of which 44 were waited for; matrix products, arithmetic and copies ran while one was open for 6% of the time, Pallas kernels for 22%

profile of v4, /device:TPU:0, one launch (start us, length us, event | category | flops | bytes accessed | tf_op | source)
XLA Modules:
  0.0 829.3 jit_solution(7349406729889057323)
XLA Ops:
  27.0 9.2 %pack.1 = (bf16[1,192,640]{2,1,0:T(8,128)(2,1)}, bf16[1,192,1280]{2,1,0:T(8,128)(2,1)}, bf16[1,192,640]{2,1,0:T(8,128)(2,1)}, bf16[1,192,1280]{2,1,0:T(8,128)(2,...) custom-call(s32[3]{0:T(128)} %pad_add_fusion.ids, ...), custom_call_target="tpu_custom_call" | custom-call | bytes 15729408 | tf_op jit(solution)/shard_map/pack/pallas_call | solution.py:472
  135.5 9.5 %collective-permute-done.23 = bf16[128,1024]{1,0:T(8,128)(2,1)S(1)} collective-permute-done((bf16[128,1024]{1,0:T(8,128)(2,1)S(1)}, bf16[128,1024]{1,0:T(8,128)(2,1)S(1)}, u32[]{:S(2)}, u32[]{:S(2)}) %collective-permute-start.23) | collective-permute-done | bytes 262176 | tf_op jit(solution)/shard_map/ppermute | solution.py:810
  169.2 14.8 %attend.1 = (bf16[128,1536]{1,0:T(8,128)(2,1)}, f32[4,128,128]{2,1,0:T(8,128)}) custom-call(s32[3]{0:T(128)} %pad_add_fusion.ids, bf16[128,1536]{1,0:T(8,128)(2,1)} %get-tuple-element.386.queries, bf16[512,1024]{1,0:T(8,128)(2,1)} %constant_dynamic-update-slice_fusion.11.key_line.value_line, bf16[512,1024]{1,0:T(8,128)(2,1)} %collective-permute-done.27.key_other.value_other, ...), custom_call_target="tpu_custom_call" | custom-call | flops 805306368 | bytes 5111808 | tf_op jit(solution)/shard_map/attend/pallas_call | solution.py:472
  203.6 16.7 %collective-permute-done.33 = bf16[128,1664]{1,0:T(8,128)(2,1)S(1)} collective-permute-done((bf16[128,1664]{1,0:T(8,128)(2,1)}, bf16[128,1664]{1,0:T(8,128)(2,1)S(1)}, u32[]{:S(2)}, u32[]{:S(2)}) %collective-permute-start.33) | collective-permute-done | bytes 426016 | tf_op jit(solution)/shard_map/ppermute | solution.py:810
  254.1 9.5 %grad_side.2 = (bf16[2,1024,1536]{2,1,0:T(8,128)(2,1)}, f32[512,640]{1,0:T(8,128)}) custom-call(s32[3]{0:T(128)} %pad_add_fusion.ids, bf16[8,128,1664]{2,1,0:T(8,128)(2,1)} %copy-done.3, bf16[8,128,1664]{2,1,0:T(8,128)(2,1)} %collective-permute-done.28.other.slots_other, bf16[1536,640]{1,0:T(8,128)(2,1)} %place_rows.6.down_one.down_two, ...), custom_call_target="tpu_custom_call" | custom-call | flops 1409286144 | bytes 10747904 | tf_op jit(solution)/shard_map/grad_side/pallas_call | solution.py:472
  263.7 12.3 %collective-permute-done.42.refs_5_ = bf16[1,192,1280]{2,1,0:T(8,128)(2,1)} collective-permute-done((bf16[1,192,1280]{2,1,0:T(8,128)(2,1)}, bf16[1,192,1280]{2,1,0:T(8,128)(2,1)}, u32[]{:S(2)}, u32[]{:S(2)}) %collective-permute-start.42) | collective-permute-done | bytes 491552 | tf_op jit(solution)/shard_map/ppermute | solution.py:810
  298.8 13.7 %collective-permute-done.46.refs_6_ = bf16[1,192,1280]{2,1,0:T(8,128)(2,1)S(1)} collective-permute-done((bf16[1,192,1280]{2,1,0:T(8,128)(2,1)S(1)}, bf16[1,192,1280]{2,1,0:T(8,128)(2,1)S(1)}, u32[]{:S(2)}, u32[]{:S(2)}) %collective-permute-start.46) | collective-permute-done | bytes 491552 | tf_op jit(solution)/shard_map/ppermute | solution.py:810
  312.6 9.5 %collective-permute-done.47.refs_3_ = bf16[1,192,1280]{2,1,0:T(8,128)(2,1)S(1)} collective-permute-done((bf16[1,192,1280]{2,1,0:T(8,128)(2,1)S(1)}, bf16[1,192,1280]{2,1,0:T(8,128)(2,1)S(1)}, u32[]{:S(2)}, u32[]{:S(2)}) %collective-permute-start.47) | collective-permute-done | bytes 491552 | tf_op jit(solution)/shard_map/ppermute | solution.py:810
  328.1 9.5 %grad_side.3 = (bf16[2,1024,1536]{2,1,0:T(8,128)(2,1)}, f32[512,640]{1,0:T(8,128)}) custom-call(s32[3]{0:T(128)} %pad_add_fusion.ids, bf16[8,128,1664]{2,1,0:T(8,128)(2,1)} %copy-done.2, bf16[8,128,1664]{2,1,0:T(8,128)(2,1)} %copy-done.4, bf16[1536,640]{1,0:T(8,128)(2,1)} %place_rows.6.down_one.down_two, ...), custom_call_target="tpu_custom_call", output_to_operand_aliasing={{0}: (5, {})} | custom-call | flops 1409286144 | bytes 17039360 | tf_op jit(solution)/shard_map/grad_side/pallas_call | solution.py:472
  355.5 17.9 %row_side.2 = (bf16[8,128,1664]{2,1,0:T(8,128)(2,1)}, bf16[8,128,1664]{2,1,0:T(8,128)(2,1)}, bf16[2,1024,1536]{2,1,0:T(8,128)(2,1)}, bf16[1024,640]{1,0:T(8,128)(2,1)}, bf16[1024,1280]{1,0:T(8,128)(2,1)}) custom-call(s32[3]{0:T(128)} %pad_add_fusion.ids, bf16[8,128,1664]{2,1,0:T(8,128)(2,1)} %copy-done.7, bf16[8,128,1664]{2,1,0:T(8,128)(2,1)} %copy-done.30, ...), custom_call_target="tpu_custom_call" | custom-call | flops 4831838208 | bytes 30670848 | tf_op jit(solution)/shard_map/row_side/pallas_call | solution.py:472
  373.4 18.4 %row_side.3 = (bf16[8,128,1664]{2,1,0:T(8,128)(2,1)}, bf16[8,128,1664]{2,1,0:T(8,128)(2,1)}, bf16[2,1024,1536]{2,1,0:T(8,128)(2,1)}, bf16[1024,640]{1,0:T(8,128)(2,1)}, bf16[1024,1280]{1,0:T(8,128)(2,1)}) custom-call(s32[3]{0:T(128)} %pad_add_fusion.ids, ...), custom_call_target="tpu_custom_call", output_to_operand_aliasing={{2}: (10, {}), {3}: (11, {}), {4}: (12, {})} | custom-call | flops 4831838208 | bytes 40894464 | tf_op jit(solution)/shard_map/row_side/pallas_call | solution.py:472
  396.9 13.6 %terms.1 = bf16[8,192,1920]{2,1,0:T(8,128)(2,1)} custom-call(s32[3]{0:T(128)} %pad_add_fusion.ids, bf16[2,1024,1536]{2,1,0:T(8,128)(2,1)} %get-tuple-element.509.xs, bf16[2,1024,1536]{2,1,0:T(8,128)(2,1)} %get-tuple-element.510.gs, bf16[1024,1280]{1,0:T(8,128)(2,1)} %get-tuple-element.511.pg, bf16[1024,640]{1,0:T(8,128)(2,1)} %get-tuple-element.512.hid), custom_call_target="tpu_custom_call" | custom-call | flops 6039797760 | bytes 16515072 | tf_op jit(solution)/shard_map/terms/pallas_call | solution.py:472
  477.2 27.4 %collective-permute-done.62 = bf16[128,1664]{1,0:T(8,128)(2,1)S(1)} collective-permute-done((bf16[128,1664]{1,0:T(8,128)(2,1)S(1)}, bf16[128,1664]{1,0:T(8,128)(2,1)S(1)}, u32[]{:S(2)}, u32[]{:S(2)}) %collective-permute-start.62) | collective-permute-done | bytes 426016 | tf_op jit(solution)/shard_map/ppermute | solution.py:810
  525.5 21.4 %collective-permute-done.72.refs_5_ = bf16[1,192,896]{2,1,0:T(8,128)(2,1)S(1)} collective-permute-done((bf16[1,192,896]{2,1,0:T(8,128)(2,1)S(1)}, bf16[1,192,896]{2,1,0:T(8,128)(2,1)S(1)}, u32[]{:S(2)}, u32[]{:S(2)}) %collective-permute-start.72) | collective-permute-done | bytes 344096 | tf_op jit(solution)/shard_map/ppermute | solution.py:810
  550.6 18.1 %attend_back.1 = (bf16[128,1536]{1,0:T(8,128)(2,1)}, bf16[512,512]{1,0:T(8,128)(2,1)}, bf16[512,512]{1,0:T(8,128)(2,1)}, bf16[512,512]{1,0:T(8,128)(2,1)}, bf16[512,512]{1,0:T(8,128)(2,1)}) custom-call(s32[3]{0:T(128)} %pad_add_fusion.ids, bf16[128,1536]{1,0:T(8,128)(2,1)} %get-tuple-element.386.queries, bf16[128,1536]{1,0:T(8,128)(2,1)} %convolution_convert_fusion.grads, ...), custom_call_target="tpu_custom_call" | custom-call | flops 2013265920 | bytes 5898240 | tf_op jit(solution)/shard_map/attend_back/pallas_call | solution.py:472
  578.1 10.0 %collective-permute-done.74 = bf16[2,128,1536]{2,1,0:T(8,128)(2,1)S(1)} collective-permute-done((bf16[2,128,1536]{2,1,0:T(8,128)(2,1)S(1)}, bf16[2,128,1536]{2,1,0:T(8,128)(2,1)S(1)}, u32[]{:S(2)}, u32[]{:S(2)}) %collective-permute-start.74) | collective-permute-done | bytes 786464 | tf_op jit(solution)/shard_map/ppermute | solution.py:810
  613.8 10.7 %collective-permute-done.77 = bf16[128,1024]{1,0:T(8,128)(2,1)} collective-permute-done((bf16[128,1024]{1,0:T(8,128)(2,1)}, bf16[128,1024]{1,0:T(8,128)(2,1)}, u32[]{:S(2)}, u32[]{:S(2)}) %collective-permute-start.77) | collective-permute-done | bytes 262176 | tf_op jit(solution)/shard_map/ppermute | solution.py:810
  659.8 24.5 %collective-permute-done.85.refs_11_ = bf16[1,192,896]{2,1,0:T(8,128)(2,1)S(1)} collective-permute-done((bf16[1,192,896]{2,1,0:T(8,128)(2,1)S(1)}, bf16[1,192,896]{2,1,0:T(8,128)(2,1)S(1)}, u32[]{:S(2)}, u32[]{:S(2)}) %collective-permute-start.85) | collective-permute-done | bytes 344096 | tf_op jit(solution)/shard_map/ppermute | solution.py:810
  699.9 11.2 %collective-permute-done.86 = bf16[8,48,1152]{2,1,0:T(8,128)(2,1)S(1)} collective-permute-done((bf16[8,48,1152]{2,1,0:T(8,128)(2,1)S(1)}, bf16[8,48,1152]{2,1,0:T(8,128)(2,1)S(1)}, u32[]{:S(2)}, u32[]{:S(2)}) %collective-permute-start.86) | collective-permute-done | bytes 884768 | tf_op jit(solution)/shard_map/ppermute | solution.py:810
  719.9 12.6 %collective-permute-done.91 = bf16[48,3072]{1,0:T(8,128)(2,1)S(1)} collective-permute-done((bf16[48,3072]{1,0:T(8,128)(2,1)S(1)}, bf16[48,3072]{1,0:T(8,128)(2,1)S(1)}, u32[]{:S(2)}, u32[]{:S(2)}) %collective-permute-start.91) | collective-permute-done | bytes 294944 | tf_op jit(solution)/shard_map/ppermute | solution.py:810
  733.2 18.3 %collective-permute-start.98 = (bf16[128,1536]{1,0:T(8,128)(2,1)S(1)}, bf16[128,1536]{1,0:T(8,128)(2,1)S(1)}, u32[]{:S(2)}, u32[]{:S(2)}) collective-permute-start(bf16[128,1536]{1,0:T(8,128)(2,1)S(1)} %fusion.29), channel_id=1, source_target_pairs={{0,2},{1,3},{2,0},{3,1},{4,6},{5,7},{6,4},{7,5},{8,10},{9,11},{10,... | collective-permute-start | bytes 1179656 | tf_op jit(solution)/shard_map/ppermute | solution.py:810
  756.2 19.9 %collective-permute-done.93 = bf16[48,1152]{1,0:T(8,128)(2,1)S(1)} collective-permute-done((bf16[48,1152]{1,0:T(8,128)(2,1)S(1)}, bf16[48,1152]{1,0:T(8,128)(2,1)S(1)}, u32[]{:S(2)}, u32[]{:S(2)}) %collective-permute-start.93) | collective-permute-done | bytes 110624 | tf_op jit(solution)/shard_map/ppermute | solution.py:810
  777.9 10.5 %collective-permute-done.94 = bf16[48,1152]{1,0:T(8,128)(2,1)S(1)} collective-permute-done((bf16[48,1152]{1,0:T(8,128)(2,1)S(1)}, bf16[48,1152]{1,0:T(8,128)(2,1)S(1)}, u32[]{:S(2)}, u32[]{:S(2)}) %collective-permute-start.94) | collective-permute-done | bytes 110624 | tf_op jit(solution)/shard_map/ppermute | solution.py:810
  806.8 10.5 %unpack.1 = (f32[192,10240]{1,0:T(8,128)}, f32[192,5120]{1,0:T(8,128)}) custom-call(s32[3]{0:T(128)} %pad_add_fusion.ids, bf16[1,192,1024]{2,1,0:T(8,128)(2,1)} %get-tuple-element.705.refs_0_, bf16[1,192,896]{2,1,0:T(8,128)(2,1)} %get-tuple-element.697.refs_1_, bf16[1,192,1024]{2,1,0:T(8,128)(2,1)} %copy-done.66, bf16[1,192,896]{2,1,0:T(8,128)(2,1)} %copy-done.70, ...), custom_call_target="tpu_custom_call" | custom-call | bytes 5899008 | tf_op jit(solution)/shard_map/unpack/pallas_call | solution.py:472
  (559 shorter events, 469.4 us)
Async XLA Ops:
  156.6 43.5 %collective-permute-start.28 = (bf16[8,128,1664]{2,1,0:T(8,128)(2,1)S(1)}, bf16[8,128,1664]{2,1,0:T(8,128)(2,1)}, u32[]{:S(2)}, u32[]{:S(2)}) collective-permute-start(bf16[8,128,1664]{2,1,0:T(8,128)(2,1)S(1)} %pad_maximum_fusion.half.slots_half), channel_id=1, source_target_pairs={{0,1},{1,0},{2,3},{3,2},{4,5},{5,4},{6,7},{7,6},{8,9},{9,8},{10,11... | collective-permute-start | bytes 10223624 | tf_op jit(solution)/shard_map/ppermute | solution.py:810
  158.7 41.3 %collective-permute-start.29 = (bf16[2,128,1664]{2,1,0:T(8,128)(2,1)}, bf16[2,128,1664]{2,1,0:T(8,128)(2,1)}, u32[]{:S(2)}, u32[]{:S(2)}) collective-permute-start(bf16[2,128,1664]{2,1,0:T(8,128)(2,1)} %collective-permute-done.20), channel_id=1, source_target_pairs={{2,0},{3,1},{4,6},{5,7},{10,8},{11,9},{12,14},{13,15},{18,16},{19,... | collective-permute-start | bytes 2555912 | tf_op jit(solution)/shard_map/ppermute | solution.py:810
  160.3 33.8 %collective-permute-start.30 = (bf16[1,192,640]{2,1,0:T(8,128)(2,1)}, bf16[1,192,640]{2,1,0:T(8,128)(2,1)}, u32[]{:S(2)}, u32[]{:S(2)}) collective-permute-start(bf16[1,192,640]{2,1,0:T(8,128)(2,1)} %get-tuple-element.415), channel_id=1, source_target_pairs={{0,5},{1,4},{2,7},{3,6},{4,1},{5,0},{6,3},{7,2},{8,13},{9,12},{10,... | collective-permute-start | bytes 737288 | tf_op jit(solution)/shard_map/ppermute | solution.py:810
  165.8 28.2 %collective-permute-start.31 = (bf16[1,192,640]{2,1,0:T(8,128)(2,1)}, bf16[1,192,640]{2,1,0:T(8,128)(2,1)}, u32[]{:S(2)}, u32[]{:S(2)}) collective-permute-start(bf16[1,192,640]{2,1,0:T(8,128)(2,1)} %get-tuple-element.416), channel_id=1, source_target_pairs={{0,6},{1,7},{2,4},{3,5},{4,2},{5,3},{6,0},{7,1},{8,14},{9,15},{10,... | collective-permute-start | bytes 737288 | tf_op jit(solution)/shard_map/ppermute | solution.py:810
  248.7 34.0 %collective-permute-start.40 = (bf16[4,128,1664]{2,1,0:T(8,128)(2,1)}, bf16[4,128,1664]{2,1,0:T(8,128)(2,1)}, u32[]{:S(2)}, u32[]{:S(2)}) collective-permute-start(bf16[4,128,1664]{2,1,0:T(8,128)(2,1)} %pad_maximum_fusion.8), channel_id=1, source_target_pairs={{0,16},{1,9},{2,18},{3,11},{4,20},{5,13},{6,22},{7,15},{8,24},{9,1... | collective-permute-start | bytes 5111816 | tf_op jit(solution)/shard_map/ppermute | solution.py:810
  250.3 38.8 %collective-permute-start.41 = (bf16[4,128,1664]{2,1,0:T(8,128)(2,1)S(1)}, bf16[4,128,1664]{2,1,0:T(8,128)(2,1)}, u32[]{:S(2)}, u32[]{:S(2)}) collective-permute-start(bf16[4,128,1664]{2,1,0:T(8,128)(2,1)S(1)} %pad_maximum_fusion.9), channel_id=1, source_target_pairs={{0,16},{1,9},{2,18},{3,11},{4,20},{5,13},{6,22},{7,15},{8,24},{9,1... | collective-permute-start | bytes 5111816 | tf_op jit(solution)/shard_map/ppermute | solution.py:810
  250.7 32.0 %collective-permute-start.39 = (bf16[2,128,1664]{2,1,0:T(8,128)(2,1)S(1)}, bf16[2,128,1664]{2,1,0:T(8,128)(2,1)}, u32[]{:S(2)}, u32[]{:S(2)}) collective-permute-start(bf16[2,128,1664]{2,1,0:T(8,128)(2,1)S(1)} %collective-permute-done.35), channel_id=1, source_target_pairs={{2,0},{3,1},{4,6},{5,7},{10,8},{11,9},{12,14},{13,15},{18,16},{19,... | collective-permute-start | bytes 2555912 | tf_op jit(solution)/shard_map/ppermute | solution.py:810
  294.6 30.0 %collective-permute-start.45 = (bf16[8,128,1664]{2,1,0:T(8,128)(2,1)S(1)}, bf16[8,128,1664]{2,1,0:T(8,128)(2,1)S(1)}, u32[]{:S(2)}, u32[]{:S(2)}) collective-permute-start(bf16[8,128,1664]{2,1,0:T(8,128)(2,1)S(1)} %pad_maximum_fusion.2.half.slots_half), channel_id=1, source_target_pairs={{0,1},{1,0},{2,3},{3,2},{4,5},{5,4},{6,7},{7,6},{8,9},{9,8},{10,11... | collective-permute-start | bytes 10223624 | tf_op jit(solution)/shard_map/ppermute | solution.py:810
  427.4 30.1 %collective-permute-start.55 = (bf16[4,128,1664]{2,1,0:T(8,128)(2,1)}, bf16[4,128,1664]{2,1,0:T(8,128)(2,1)S(1)}, u32[]{:S(2)}, u32[]{:S(2)}) collective-permute-start(bf16[4,128,1664]{2,1,0:T(8,128)(2,1)} %get-tuple-element.520), channel_id=1, source_target_pairs={{0,16},{1,9},{2,18},{3,11},{4,20},{5,13},{6,22},{7,15},{8,24},{9,1... | collective-permute-start | bytes 5111816 | tf_op jit(solution)/shard_map/ppermute | solution.py:810
  472.0 32.6 %collective-permute-start.64 = (bf16[8,128,1536]{2,1,0:T(8,128)(2,1)}, bf16[8,128,1536]{2,1,0:T(8,128)(2,1)S(1)}, u32[]{:S(2)}, u32[]{:S(2)}) collective-permute-start(bf16[8,128,1536]{2,1,0:T(8,128)(2,1)} %get-tuple-element.543), channel_id=1, source_target_pairs={{0,1},{1,0},{2,3},{3,2},{4,5},{5,4},{6,7},{7,6},{8,9},{9,8},{10,11... | collective-permute-start | bytes 9437192 | tf_op jit(solution)/shard_map/ppermute | solution.py:810
  472.1 32.6 %collective-permute-start.65 = (bf16[8,128,1536]{2,1,0:T(8,128)(2,1)}, bf16[8,128,1536]{2,1,0:T(8,128)(2,1)S(1)}, u32[]{:S(2)}, u32[]{:S(2)}) collective-permute-start(bf16[8,128,1536]{2,1,0:T(8,128)(2,1)} %get-tuple-element.544), channel_id=1, source_target_pairs={{0,1},{1,0},{2,3},{3,2},{4,5},{5,4},{6,7},{7,6},{8,9},{9,8},{10,11... | collective-permute-start | bytes 9437192 | tf_op jit(solution)/shard_map/ppermute | solution.py:810
  472.6 32.1 %collective-permute-start.62 = (bf16[128,1664]{1,0:T(8,128)(2,1)S(1)}, bf16[128,1664]{1,0:T(8,128)(2,1)S(1)}, u32[]{:S(2)}, u32[]{:S(2)}) collective-permute-start(bf16[128,1664]{1,0:T(8,128)(2,1)S(1)} %get-tuple-element.541), channel_id=1, source_target_pairs={{0,4},{1,5},{2,6},{3,7},{4,0},{5,1},{6,2},{7,3},{8,12},{9,13},{10,... | collective-permute-start | bytes 1277960 | tf_op jit(solution)/shard_map/ppermute | solution.py:810
  475.7 28.9 %collective-permute-start.63 = (bf16[128,1664]{1,0:T(8,128)(2,1)S(1)}, bf16[128,1664]{1,0:T(8,128)(2,1)S(1)}, u32[]{:S(2)}, u32[]{:S(2)}) collective-permute-start(bf16[128,1664]{1,0:T(8,128)(2,1)S(1)} %get-tuple-element.542), channel_id=1, source_target_pairs={{0,6},{1,7},{2,4},{3,5},{4,2},{5,3},{6,0},{7,1},{8,14},{9,15},{10,... | collective-permute-start | bytes 1277960 | tf_op jit(solution)/shard_map/ppermute | solution.py:810
  511.0 59.4 %collective-permute-start.66 = (bf16[4,128,1536]{2,1,0:T(8,128)(2,1)}, bf16[4,128,1536]{2,1,0:T(8,128)(2,1)}, u32[]{:S(2)}, u32[]{:S(2)}) collective-permute-start(bf16[4,128,1536]{2,1,0:T(8,128)(2,1)} %get-tuple-element.550), channel_id=1, source_target_pairs={{0,16},{1,9},{2,18},{3,11},{4,20},{5,13},{6,22},{7,15},{8,24},{9,1... | collective-permute-start | bytes 4718600 | tf_op jit(solution)/shard_map/ppermute | solution.py:810
  512.1 58.2 %collective-permute-start.67 = (bf16[4,128,1536]{2,1,0:T(8,128)(2,1)}, bf16[4,128,1536]{2,1,0:T(8,128)(2,1)}, u32[]{:S(2)}, u32[]{:S(2)}) collective-permute-start(bf16[4,128,1536]{2,1,0:T(8,128)(2,1)} %get-tuple-element.551), channel_id=1, source_target_pairs={{0,16},{1,9},{2,18},{3,11},{4,20},{5,13},{6,22},{7,15},{8,24},{9,1... | collective-permute-start | bytes 4718600 | tf_op jit(solution)/shard_map/ppermute | solution.py:810
  513.4 36.4 %collective-permute-start.68 = (bf16[1,192,1024]{2,1,0:T(8,128)(2,1)S(1)}, bf16[1,192,1024]{2,1,0:T(8,128)(2,1)S(1)}, u32[]{:S(2)}, u32[]{:S(2)}) collective-permute-start(bf16[1,192,1024]{2,1,0:T(8,128)(2,1)S(1)} %copy-done.69), channel_id=1, source_target_pairs={{0,5},{1,4},{2,7},{3,6},{4,1},{5,0},{6,3},{7,2},{8,13},{9,12},{10,... | collective-permute-start | bytes 1179656 | tf_op jit(solution)/shard_map/ppermute | solution.py:810
  521.3 49.1 %collective-permute-start.69 = (bf16[1,192,1024]{2,1,0:T(8,128)(2,1)}, bf16[1,192,1024]{2,1,0:T(8,128)(2,1)}, u32[]{:S(2)}, u32[]{:S(2)}) collective-permute-start(bf16[1,192,1024]{2,1,0:T(8,128)(2,1)} %get-tuple-element.553), channel_id=1, source_target_pairs={{0,6},{1,7},{2,4},{3,5},{4,2},{5,3},{6,0},{7,1},{8,14},{9,15},{10,... | collective-permute-start | bytes 1179656 | tf_op jit(solution)/shard_map/ppermute | solution.py:810
  655.5 28.9 %collective-permute-start.83 = (bf16[8,48,3072]{2,1,0:T(8,128)(2,1)S(1)}, bf16[8,48,3072]{2,1,0:T(8,128)(2,1)S(1)}, u32[]{:S(2)}, u32[]{:S(2)}) collective-permute-start(bf16[8,48,3072]{2,1,0:T(8,128)(2,1)S(1)} %get-tuple-element.600), channel_id=1, source_target_pairs={{0,16},{1,9},{2,18},{3,11},{4,20},{5,13},{6,22},{7,15},{8,24},{9,1... | collective-permute-start | bytes 7077896 | tf_op jit(solution)/shard_map/ppermute | solution.py:810
  656.2 28.1 %collective-permute-start.82 = (bf16[16,48,1152]{2,1,0:T(8,128)(2,1)S(1)}, bf16[16,48,1152]{2,1,0:T(8,128)(2,1)S(1)}, u32[]{:S(2)}, u32[]{:S(2)}) collective-permute-start(bf16[16,48,1152]{2,1,0:T(8,128)(2,1)S(1)} %copy-done.89), channel_id=1, source_target_pairs={{0,1},{1,0},{2,3},{3,2},{4,5},{5,4},{6,7},{7,6},{8,9},{9,8},{10,11... | collective-permute-start | bytes 5308424 | tf_op jit(solution)/shard_map/ppermute | solution.py:810
  656.2 28.1 %collective-permute-start.84 = (bf16[2,128,1536]{2,1,0:T(8,128)(2,1)S(1)}, bf16[2,128,1536]{2,1,0:T(8,128)(2,1)S(1)}, u32[]{:S(2)}, u32[]{:S(2)}) collective-permute-start(bf16[2,128,1536]{2,1,0:T(8,128)(2,1)S(1)} %copy-done.50), channel_id=1, source_target_pairs={{0,2},{1,3},{6,4},{7,5},{8,10},{9,11},{14,12},{15,13},{16,18},{17,... | collective-permute-start | bytes 2359304 | tf_op jit(solution)/shard_map/ppermute | solution.py:810
  733.2 55.2 %collective-permute-start.98 = (bf16[128,1536]{1,0:T(8,128)(2,1)S(1)}, bf16[128,1536]{1,0:T(8,128)(2,1)S(1)}, u32[]{:S(2)}, u32[]{:S(2)}) collective-permute-start(bf16[128,1536]{1,0:T(8,128)(2,1)S(1)} %fusion.29), channel_id=1, source_target_pairs={{0,2},{1,3},{2,0},{3,1},{4,6},{5,7},{6,4},{7,5},{8,10},{9,11},{10,... | collective-permute-start | bytes 1179656 | tf_op jit(solution)/shard_map/ppermute | solution.py:810
  751.5 36.9 %collective-permute-start.96 = (bf16[48,3072]{1,0:T(8,128)(2,1)S(1)}, bf16[48,3072]{1,0:T(8,128)(2,1)S(1)}, u32[]{:S(2)}, u32[]{:S(2)}) collective-permute-start(bf16[48,3072]{1,0:T(8,128)(2,1)S(1)} %get-tuple-element.620), channel_id=1, source_target_pairs={{0,4},{1,5},{2,6},{3,7},{4,0},{5,1},{6,2},{7,3},{8,12},{9,13},{10,... | collective-permute-start | bytes 884744 | tf_op jit(solution)/shard_map/ppermute | solution.py:810
  751.8 36.6 %collective-permute-start.97 = (bf16[48,3072]{1,0:T(8,128)(2,1)S(1)}, bf16[48,3072]{1,0:T(8,128)(2,1)S(1)}, u32[]{:S(2)}, u32[]{:S(2)}) collective-permute-start(bf16[48,3072]{1,0:T(8,128)(2,1)S(1)} %get-tuple-element.621), channel_id=1, source_target_pairs={{0,6},{1,7},{2,4},{3,5},{4,2},{5,3},{6,0},{7,1},{8,14},{9,15},{10,... | collective-permute-start | bytes 884744 | tf_op jit(solution)/shard_map/ppermute | solution.py:810
  755.0 33.4 %collective-permute-start.94 = (bf16[48,1152]{1,0:T(8,128)(2,1)S(1)}, bf16[48,1152]{1,0:T(8,128)(2,1)S(1)}, u32[]{:S(2)}, u32[]{:S(2)}) collective-permute-start(bf16[48,1152]{1,0:T(8,128)(2,1)S(1)} %get-tuple-element.618), channel_id=1, source_target_pairs={{0,4},{1,5},{2,6},{3,7},{4,0},{5,1},{6,2},{7,3},{8,12},{9,13},{10,... | collective-permute-start | bytes 331784 | tf_op jit(solution)/shard_map/ppermute | solution.py:810
  (181 other events, 2514.9 us)

commit v5 on v4

--- a/solution.py
+++ b/solution.py
@@ -571,30 +571,38 @@
 
 
 def unpack_kernel(ids, *refs):
-    pieces, gain, up_grad, down_grad = refs[: 2 * SHARDS], refs[-3], refs[-2], refs[-1]
+    pieces, gain, up_grad, down_grad = refs[: SHARDS + 2], refs[-3], refs[-2], refs[-1]
     scale = gain[...]
     step = pl.program_id(0)
     share = SHARDS // (pl.num_programs(0) - SHARDS)
-    part = (pieces[1].shape[2] - H) // 3
+    part = pieces[0].shape[2] // 3 - H
+    edge = pieces[6].shape[2]
+
+    def columns(k, first, count):
+        if k < 6:
+            found = pieces[k][0, :, first : first + count]
+        elif first < edge:
+            found = pieces[2 * k - 6][0, :, first : first + count]
+        else:
+            found = pieces[2 * k - 5][0, :, first - edge : first - edge + count]
+        return found.astype(jnp.float32)
+
     for k in range(SHARDS):
-        one, two = pieces[2 * k : 2 * k + 2]
         source = ids[2] ^ k
 
         @pl.when(step == k)
-        def _(one=one, two=two):
-            down_grad[...] = one[0, :, :H].astype(jnp.float32)
-            up_grad[:, :H] = one[0, :, H:].astype(jnp.float32) * scale
-            up_grad[:, H:] = two[0, :, :H].astype(jnp.float32) * scale
+        def _(k=k):
+            down_grad[...] = columns(k, 0, H)
+            up_grad[:, :H] = columns(k, H, H) * scale
+            up_grad[:, H:] = columns(k, 2 * H, H) * scale
 
         @pl.when(step == SHARDS + source // share)
-        def _(two=two, source=source):
+        def _(k=k, source=source):
             at = pl.multiple_of(source % share * part, part)
             at_up = pl.multiple_of(H + source % share * part, part)
-            down_grad[:, pl.ds(at, part)] = two[0, :, H : H + part].astype(jnp.float32)
-            gate = two[0, :, H + part : H + 2 * part].astype(jnp.float32)
-            up_grad[:, pl.ds(at, part)] = gate * scale
-            up = two[0, :, H + 2 * part :].astype(jnp.float32)
-            up_grad[:, pl.ds(at_up, part)] = up * scale
+            down_grad[:, pl.ds(at, part)] = columns(k, 3 * H, part)
+            up_grad[:, pl.ds(at, part)] = columns(k, 3 * H + part, part) * scale
+            up_grad[:, pl.ds(at_up, part)] = columns(k, 3 * H + 2 * part, part) * scale
 
 
 def turn(rows, cosine, sine):
@@ -780,13 +788,20 @@
     combine_rows(ids, back_rows, slots_half, slots_other, back_half, back_other)
 
 
-def out_side_kernel(
-    ids, hid, slots_half, slots_other, down_one, down_two, back_half, back_other, out_rows
-):
+def out_side_kernel(ids, hid, *refs):
+    slots, (down_one, down_two), (mine, theirs, out_rows) = refs[:4], refs[4:6], refs[6:]
     width = down_one.shape[1]
+    count = slots[0].shape[0]
     out_rows[0] = dot(hid[:, :width], down_one[...], rows_by_rows).astype(jnp.bfloat16)
     out_rows[1] = dot(hid[:, width:], down_two[...], rows_by_rows).astype(jnp.bfloat16)
-    combine_rows(ids, out_rows, slots_half, slots_other, back_half, back_other)
+    for n, own in enumerate(slots):
+        target = theirs if n % 2 else mine
+        for i in range(count):
+            pick = picks_of(own[i], ids[0], ids[1])
+            at = slice((n * count + i) * CAP, (n * count + i + 1) * CAP)
+            both = jnp.concatenate([out_rows[0, at], out_rows[1, at]], 0)
+            place = i // 2 * 4 + n // 2 * 2 + i % 2
+            target[place] = dot(pick, both, rows_by_cols).astype(jnp.bfloat16)
 
 
 def terms_kernel(ids, xs, gs, pg, hid, terms):
@@ -1252,14 +1267,14 @@
     row_pay = order.round([g_near, g_line] + some(far, 3), row_pay)
     x_line = Flow(line_spread(row_pay, x_marks))
     g_far = Flow(spread_pair(g_line.result))
-    order.round([x_line] + some(far, 1))
+    order.round([x_line, g_far] + some(far, 1))
     x_near = Flow(spread_pair([row_pay, x_marks[0]]))
     owned_down = exchanged(s_pieces, s_flows, 0)
     owned_down = order.round([x_line, x_near, g_far] + some(near, 1), owned_down)
     plain = [order.round([x_line, x_near, g_far] + some(far, 1), grad_side(0))]
     x_far = Flow(spread_pair(x_line.result))
-    order.round([x_near, x_far, g_far] + some(far, 1) + near)
-    plain.append(order.round([x_far] + far, grad_side(1)))
+    plain.append(order.round([x_near, x_far] + some(far, 1) + near, grad_side(1)))
+    order.round([x_far] + far)
     owned_up = exchanged(s_pieces, s_flows, 1)
     back_near = order.round([x_far], row_side(0))
     b_near = Flow(collect_pair(*back_near))
@@ -1288,29 +1303,30 @@
     )
     terms = order.round([b_near, b_far], terms)
     t_edge = 2 * H
-    t_pieces = [[terms[k, :, :t_edge][None], terms[k, :, t_edge:][None]] for k in range(SHARDS)]
-    t_flows, core, near, far = exchange(t_pieces)
-
-    def out_side(k):
-        return call(
-            out_side_kernel,
-            "out_side",
-            (shaped((blocks, rows, D)),) * 2,
-            [block_spec((step_rows, hid_width), (k, 0)), slot_spec, slot_spec] + down_specs,
-            [out_spec((blocks, rows, D), (0, 0, 0))] * 2,
-            (ids, hid) + (g_near, g_far)[k].result + (owned_down, owned_down),
-            scratch=[pltpu.VMEM((2, step_rows, D), low)],
-            flops=2 * step_rows * D * (hid_width + 2 * rows),
-        )
-
-    out_near = order.round([b_near, b_far] + some(near, 1) + some(far, 1), out_side(0))
+    t_pieces = [[terms[k][None]] for k in range(6)]
+    t_pieces += [[terms[k, :, :t_edge][None], terms[k, :, t_edge:][None]] for k in (6, 7)]
+    t_flows = [[Flow(one_hop(piece, to_shard[k])) for piece in t_pieces[k]] for k in range(1, SHARDS)]
+    core, near = t_flows[0], t_flows[1] + t_flows[2]
+    far = t_flows[5][:1] + t_flows[3] + t_flows[4] + t_flows[5][1:] + t_flows[6]
+
+    order.round([b_near, b_far] + some(far, 1))
     b_line = [Flow(one_hop(b_near.result[1], to_line[1]))]
-    out_far = order.round([b_far] + b_line + core, out_side(1))
+    moe_blocks = call(
+        out_side_kernel,
+        "out_side",
+        (shaped((2 * blocks, rows, D)),) * 2,
+        [whole_spec((slot_rows, hid_width))] + [slot_spec] * 4 + down_specs,
+        [out_spec((2 * blocks, rows, D), (0, 0, 0))] * 2,
+        (ids, hid) + g_near.result + g_far.result + (owned_down, owned_down),
+        scratch=[pltpu.VMEM((2, slot_rows, D), low)],
+        flops=2 * slot_rows * D * (hid_width + 2 * rows),
+    )
+    moe_blocks = order.round([b_far] + b_line + core, moe_blocks)
     b_line += [
         Flow(one_hop(piece, to_line[2 + i])) for i, piece in enumerate(by_distance(b_far.result))
     ]
-    m_near, m_far = Flow(collect_pair(*out_near)), Flow(collect_pair(*out_far))
-    order.round(b_line[1:] + [m_near, m_far])
+    moe = Flow(collect_all(*moe_blocks))
+    order.round(b_line[1:] + [moe] + some(near, 1))
     grad_sum = total_of([b_near.result[0]] + [flow.result for flow in b_line])
 
     gate_grad = jnp.where(kept, grad_sum[:, D : D + EXPERTS], 0.0)
@@ -1343,15 +1359,15 @@
         return dense_terms(half_at, products, 2, 4 * GROUPS, fine)
 
     kv_theirs, kv_mine = order.round(
-        [m_near, m_far] + some(far, 3) + some(near, 2), (kv_theirs, kv_mine)
+        [moe] + some(far, 2) + near, (kv_theirs, kv_mine)
     )
     kv_core = Flow(one_hop(kv_theirs, to_core))
-    order.round([kv_core, m_near, m_far])
-    m_line = Flow(line_collect(m_near.result, m_far.result))
+    order.round([kv_core])
     kv_half = add_low(kv_mine, kv_core.result).reshape(4, rows, 2 * kv_width)
     kv = [Flow(one_hop(kv_half[k], to_line[k])) for k in (1, 2, 3)]
     early_blocks = dense_flow([(branch_grad, attended, 0), (normed_in, query_back, q_width)])
-    early_blocks = order.round(kv, early_blocks)
+    early_blocks = order.round(kv + [moe], early_blocks)
+    m_line = Flow(line_collect(moe.result[:2], moe.result[2:]))
     early = Flow(collect_all(*early_blocks))
     kv_grad = total_of([kv_half[0]] + [flow.result for flow in kv])
 
@@ -1384,34 +1400,21 @@
             ((scaled_two * normal_two).astype(low), marker(EXPERTS), 2 * kv_width),
         ]
     )
-    late_blocks = order.round([early] + some(far, 1) + some(near, 1), late_blocks)
+    late_blocks = order.round([early, m_line] + some(far, 1), late_blocks)
     late = Flow(collect_all(*late_blocks))
     input_grad = order.round(
-        [late, early, m_line] + some(far, 1), input_grad.astype(low)
-    )
-    order.round([late, early] + some(far, 1))
-    early_line = line_of(early.result)
-    order.round([late, m_line] + early_line[:1] + some(far, 1))
-    late_line = line_of(late.result)
+        [late, early, m_line], input_grad.astype(low)
+    )
+    order.round([late, early, m_line] + some(far, 1))
+    order.round([late] + far)
+    dense_line = line_of(
+        [jnp.concatenate(pair, 1) for pair in zip(early.result, late.result)]
+    )
     spots = jnp.arange(GROUPS, dtype=jnp.int32) ^ group_at
     mate = 1 + shard_at % 2
     spots = jnp.where(spots == mate, 1, jnp.where(spots == 3 - mate, 2, spots))
     places = [spots[i] for i in range(GROUPS)]
 
-    def shared(first, line):
-        own = total_of([first] + [flow.result for flow in line]).astype(low)
-        return Flow(share_flow(own, places))
-
-    order.round(late_line + early_line[1:] + [m_line])
-    late_share = shared(late.result[0], late_line)
-    early_share = shared(early.result[0], early_line)
-    order.round([late_share, early_share] + far)
-    order.round([late_share, early_share])
-    output = (middle + m_line.result).astype(low)
-    early_sum = early_share.result.astype(full)
-    out_sum, query_sum = early_sum[:, :q_width], early_sum[:, q_width:]
-    late_sum = late_share.result.astype(full)
-
     t_parts = t_pieces[0] + [flow.result for flows in t_flows for flow in flows]
 
     def to_expert(k, ids):
@@ -1421,12 +1424,22 @@
         unpack_kernel,
         "unpack",
         (shaped(gate_up_weight.shape, full), shaped(down_weight.shape, full)),
-        [whole_spec((1, depth, t_edge)), whole_spec((1, depth, 3 * hid_width - t_edge))] * SHARDS
-        + [whole_spec((depth, 1))],
+        [whole_spec(piece.shape) for piece in t_parts] + [whole_spec((depth, 1))],
         [pl.BlockSpec((depth, 2 * H), to_expert), pl.BlockSpec((depth, H), to_expert)],
         (ids,) + tuple(t_parts) + (gain_two,),
         steps=own_experts,
     )
+    gate_up_grad, down_grad = order.round(dense_line, (gate_up_grad, down_grad))
+    own_sum = jnp.concatenate([early.result[0], late.result[0]], 1)
+    own_sum = total_of([own_sum] + [flow.result for flow in dense_line]).astype(low)
+    share_all = Flow(share_flow(own_sum, places))
+    order.round([share_all])
+    order.round([share_all])
+    output = (middle + m_line.result).astype(low)
+    dense_sums = share_all.result.astype(full)
+    early_sum, late_sum = dense_sums[:, : 2 * q_width], dense_sums[:, 2 * q_width :]
+    out_sum, query_sum = early_sum[:, :q_width], early_sum[:, q_width:]
+
     qkv_sum = jnp.concatenate([query_sum, late_sum[:, : 2 * kv_width]], 1)
     return (
         output,

time: 837 us -> 811 us (0.969)
  starting transfers between devices: 151 us -> 120 us
    ppermute x103 -> x90, starting transfers between devices: 151 us -> 120 us  [hop(): return lax.ppermute(values, ('expert', 'shard'), pairs)]
    unnamed x215 -> x197, local copies, waits for them, and re-layouts: 25.9 us -> 21.7 us
    convert_element_type x19 -> x16, other arithmetic: 29.6 us -> 32 us  [add_low(): (one.astype(jnp.float32) + two.astype(jnp.float32)).astype(jnp.bfloat16)]
    ppermute x103 -> x90, waiting for transfers between devices: 360 us -> 361 us  [hop(): return lax.ppermute(values, ('expert', 'shard'), pairs)]
    pallas_call x18 -> x17, Pallas kernels: 180 us -> 179 us  [call(): pl.pallas_call(kernel, name=name, out_shape=out_shape, grid_spec=pltpu.Pr...]
  transfers between devices with their start and end apart: 103 -> 90, of which waited for: 44 -> 44; matrix products, arithmetic and copies ran while one was open for 6% -> 7% of each run, Pallas kernels for 22% -> 22%
where the time goes in v5:
time: 811 us; the launch traced here: 798 us
  waiting for transfers between devices  361 us (45%)
  Pallas kernels  179 us (22%)
  starting transfers between devices  120 us (15%)
  other arithmetic  76.2 us (9%)
  local copies, waits for them, and re-layouts  40.4 us (5%)
  matrix products  11.5 us (1%)
  between operations  10.1 us (1%)
    ppermute x90, waiting for transfers between devices, hop(): return lax.ppermute(values, ('expert', 'shard'), pairs)  361 us
    pallas_call x17, Pallas kernels, call(): pl.pallas_call(kernel, name=name, out_shape=out_shape, grid_spec=pltpu.Pr...  179 us
    ppermute x90, starting transfers between devices, hop(): return lax.ppermute(values, ('expert', 'shard'), pairs)  120 us
    convert_element_type x16, other arithmetic, add_low(): (one.astype(jnp.float32) + two.astype(jnp.float32)).astype(jnp.bfloat16)  32 us
    unnamed x197, local copies, waits for them, and re-layouts  21.7 us
  transfers between devices with their start and end apart: 90, of which 44 were waited for; matrix products, arithmetic and copies ran while one was open for 7% of the time, Pallas kernels for 22%

profile of v5, /device:TPU:0, one launch (start us, length us, event | category | flops | bytes accessed | tf_op | source)
XLA Modules:
  0.0 797.6 jit_solution(18316639566784169458)
XLA Ops:
  27.1 9.2 %pack.1 = (bf16[1,192,640]{2,1,0:T(8,128)(2,1)}, bf16[1,192,1280]{2,1,0:T(8,128)(2,1)}, bf16[1,192,640]{2,1,0:T(8,128)(2,1)}, bf16[1,192,1280]{2,1,0:T(8,128)(2,...) custom-call(s32[3]{0:T(128)} %pad_add_fusion.ids, ...), custom_call_target="tpu_custom_call" | custom-call | bytes 15729408 | tf_op jit(solution)/shard_map/pack/pallas_call | solution.py:472
  135.6 9.5 %collective-permute-done.23 = bf16[128,1024]{1,0:T(8,128)(2,1)S(1)} collective-permute-done((bf16[128,1024]{1,0:T(8,128)(2,1)S(1)}, bf16[128,1024]{1,0:T(8,128)(2,1)S(1)}, u32[]{:S(2)}, u32[]{:S(2)}) %collective-permute-start.23) | collective-permute-done | bytes 262176 | tf_op jit(solution)/shard_map/ppermute | solution.py:825
  169.3 14.7 %attend.1 = (bf16[128,1536]{1,0:T(8,128)(2,1)}, f32[4,128,128]{2,1,0:T(8,128)}) custom-call(s32[3]{0:T(128)} %pad_add_fusion.ids, bf16[128,1536]{1,0:T(8,128)(2,1)} %get-tuple-element.354.queries, bf16[512,1024]{1,0:T(8,128)(2,1)} %constant_dynamic-update-slice_fusion.11.key_line.value_line, bf16[512,1024]{1,0:T(8,128)(2,1)} %collective-permute-done.27.key_other.value_other, ...), custom_call_target="tpu_custom_call" | custom-call | flops 805306368 | bytes 5111808 | tf_op jit(solution)/shard_map/attend/pallas_call | solution.py:472
  205.2 17.6 %collective-permute-done.33 = bf16[128,1664]{1,0:T(8,128)(2,1)S(1)} collective-permute-done((bf16[128,1664]{1,0:T(8,128)(2,1)S(1)}, bf16[128,1664]{1,0:T(8,128)(2,1)S(1)}, u32[]{:S(2)}, u32[]{:S(2)}) %collective-permute-start.33) | collective-permute-done | bytes 426016 | tf_op jit(solution)/shard_map/ppermute | solution.py:825
  267.7 9.5 %grad_side.2 = (bf16[2,1024,1536]{2,1,0:T(8,128)(2,1)}, f32[512,640]{1,0:T(8,128)}) custom-call(s32[3]{0:T(128)} %pad_add_fusion.ids, bf16[8,128,1664]{2,1,0:T(8,128)(2,1)} %copy-done.3, bf16[8,128,1664]{2,1,0:T(8,128)(2,1)} %collective-permute-done.28.other.slots_other.refs_1_, bf16[1536,640]{1,0:T(8,128)(2,1)} %place_rows.6.down_one.down_two.refs_4_.refs_5_, ...), custom_call_target="tpu_custom_call" | custom-call | flops 1409286144 | bytes 10747904 | tf_op jit(solution)/shard_map/grad_side/pallas_call | solution.py:472
  277.2 13.1 %collective-permute-done.43.refs_5_ = bf16[1,192,1280]{2,1,0:T(8,128)(2,1)} collective-permute-done((bf16[1,192,1280]{2,1,0:T(8,128)(2,1)}, bf16[1,192,1280]{2,1,0:T(8,128)(2,1)}, u32[]{:S(2)}, u32[]{:S(2)}) %collective-permute-start.43) | collective-permute-done | bytes 491552 | tf_op jit(solution)/shard_map/ppermute | solution.py:825
  302.6 9.6 %grad_side.3 = (bf16[2,1024,1536]{2,1,0:T(8,128)(2,1)}, f32[512,640]{1,0:T(8,128)}) custom-call(s32[3]{0:T(128)} %pad_add_fusion.ids, bf16[8,128,1664]{2,1,0:T(8,128)(2,1)} %copy-done.2, bf16[8,128,1664]{2,1,0:T(8,128)(2,1)} %collective-permute-done.42.other.slots_other.refs_3_, ...), custom_call_target="tpu_custom_call", output_to_operand_aliasing={{0}: (5, {})} | custom-call | flops 1409286144 | bytes 17039360 | tf_op jit(solution)/shard_map/grad_side/pallas_call | solution.py:472
  316.6 9.8 %collective-permute-done.47.refs_3_ = bf16[1,192,1280]{2,1,0:T(8,128)(2,1)} collective-permute-done((bf16[1,192,1280]{2,1,0:T(8,128)(2,1)}, bf16[1,192,1280]{2,1,0:T(8,128)(2,1)}, u32[]{:S(2)}, u32[]{:S(2)}) %collective-permute-start.47) | collective-permute-done | bytes 491552 | tf_op jit(solution)/shard_map/ppermute | solution.py:825
  328.6 13.9 %collective-permute-done.49.refs_7_ = bf16[1,192,1280]{2,1,0:T(8,128)(2,1)S(1)} collective-permute-done((bf16[1,192,1280]{2,1,0:T(8,128)(2,1)S(1)}, bf16[1,192,1280]{2,1,0:T(8,128)(2,1)S(1)}, u32[]{:S(2)}, u32[]{:S(2)}) %collective-permute-start.49) | collective-permute-done | bytes 491552 | tf_op jit(solution)/shard_map/ppermute | solution.py:825
  354.5 17.9 %row_side.2 = (bf16[8,128,1664]{2,1,0:T(8,128)(2,1)}, bf16[8,128,1664]{2,1,0:T(8,128)(2,1)}, bf16[2,1024,1536]{2,1,0:T(8,128)(2,1)}, bf16[1024,640]{1,0:T(8,128)(2,1)}, bf16[1024,1280]{1,0:T(8,128)(2,1)}) custom-call(s32[3]{0:T(128)} %pad_add_fusion.ids, bf16[8,128,1664]{2,1,0:T(8,128)(2,1)} %copy-done.6, ...), custom_call_target="tpu_custom_call" | custom-call | flops 4831838208 | bytes 30670848 | tf_op jit(solution)/shard_map/row_side/pallas_call | solution.py:472
  372.5 18.5 %row_side.3 = (bf16[8,128,1664]{2,1,0:T(8,128)(2,1)}, bf16[8,128,1664]{2,1,0:T(8,128)(2,1)}, bf16[2,1024,1536]{2,1,0:T(8,128)(2,1)}, bf16[1024,640]{1,0:T(8,128)(2,1)}, bf16[1024,1280]{1,0:T(8,128)(2,1)}) custom-call(s32[3]{0:T(128)} %pad_add_fusion.ids, ...), custom_call_target="tpu_custom_call", output_to_operand_aliasing={{2}: (10, {}), {3}: (11, {}), {4}: (12, {})} | custom-call | flops 4831838208 | bytes 40894464 | tf_op jit(solution)/shard_map/row_side/pallas_call | solution.py:472
  396.5 13.7 %terms.1 = bf16[8,192,1920]{2,1,0:T(8,128)(2,1)} custom-call(s32[3]{0:T(128)} %pad_add_fusion.ids, bf16[2,1024,1536]{2,1,0:T(8,128)(2,1)} %get-tuple-element.478.xs, bf16[2,1024,1536]{2,1,0:T(8,128)(2,1)} %get-tuple-element.479.gs, bf16[1024,1280]{1,0:T(8,128)(2,1)} %get-tuple-element.480.pg, bf16[1024,640]{1,0:T(8,128)(2,1)} %get-tuple-element.481.hid), custom_call_target="tpu_custom_call" | custom-call | flops 6039797760 | bytes 16515072 | tf_op jit(solution)/shard_map/terms/pallas_call | solution.py:472
  461.6 12.8 %out_side.1 = (bf16[16,128,1536]{2,1,0:T(8,128)(2,1)}, bf16[16,128,1536]{2,1,0:T(8,128)(2,1)}) custom-call(s32[3]{0:T(128)} %pad_add_fusion.ids, bf16[1024,640]{1,0:T(8,128)(2,1)} %get-tuple-element.481.hid, bf16[8,128,1664]{2,1,0:T(8,128)(2,1)} %copy-done.3, bf16[8,128,1664]{2,1,0:T(8,128)(2,1)} %collective-permute-done.28.other.slots_other.refs_1_, ...), custom_call_target="tpu_custom_call" | custom-call | flops 2818572288 | bytes 18874368 | tf_op jit(solution)/shard_map/out_side/pallas_call | solution.py:472
  480.2 21.6 %collective-permute-done.60 = bf16[128,1664]{1,0:T(8,128)(2,1)S(1)} collective-permute-done((bf16[128,1664]{1,0:T(8,128)(2,1)S(1)}, bf16[128,1664]{1,0:T(8,128)(2,1)S(1)}, u32[]{:S(2)}, u32[]{:S(2)}) %collective-permute-start.60) | collective-permute-done | bytes 426016 | tf_op jit(solution)/shard_map/ppermute | solution.py:825
  501.8 11.2 %collective-permute-done.61 = bf16[128,1664]{1,0:T(8,128)(2,1)S(1)} collective-permute-done((bf16[128,1664]{1,0:T(8,128)(2,1)S(1)}, bf16[128,1664]{1,0:T(8,128)(2,1)S(1)}, u32[]{:S(2)}, u32[]{:S(2)}) %collective-permute-start.61) | collective-permute-done | bytes 426016 | tf_op jit(solution)/shard_map/ppermute | solution.py:825
  530.5 18.5 %attend_back.1 = (bf16[128,1536]{1,0:T(8,128)(2,1)}, bf16[512,512]{1,0:T(8,128)(2,1)}, bf16[512,512]{1,0:T(8,128)(2,1)}, bf16[512,512]{1,0:T(8,128)(2,1)}, bf16[512,512]{1,0:T(8,128)(2,1)}) custom-call(s32[3]{0:T(128)} %pad_add_fusion.ids, bf16[128,1536]{1,0:T(8,128)(2,1)} %get-tuple-element.354.queries, bf16[128,1536]{1,0:T(8,128)(2,1)} %convolution_convert_fusion.grads, ...), custom_call_target="tpu_custom_call" | custom-call | flops 2013265920 | bytes 5898240 | tf_op jit(solution)/shard_map/attend_back/pallas_call | solution.py:472
  550.7 22.5 %collective-permute-done.65.refs_4_ = bf16[1,192,1920]{2,1,0:T(8,128)(2,1)} collective-permute-done((bf16[1,192,1920]{2,1,0:T(8,128)(2,1)}, bf16[1,192,1920]{2,1,0:T(8,128)(2,1)}, u32[]{:S(2)}, u32[]{:S(2)}) %collective-permute-start.65) | collective-permute-done | bytes 737312 | tf_op jit(solution)/shard_map/ppermute | solution.py:825
  573.2 12.9 %collective-permute-done.66.refs_5_ = bf16[1,192,1920]{2,1,0:T(8,128)(2,1)} collective-permute-done((bf16[1,192,1920]{2,1,0:T(8,128)(2,1)}, bf16[1,192,1920]{2,1,0:T(8,128)(2,1)}, u32[]{:S(2)}, u32[]{:S(2)}) %collective-permute-start.66) | collective-permute-done | bytes 737312 | tf_op jit(solution)/shard_map/ppermute | solution.py:825
  642.3 13.2 %collective-permute-done.75.refs_7_ = bf16[1,192,896]{2,1,0:T(8,128)(2,1)S(1)} collective-permute-done((bf16[1,192,896]{2,1,0:T(8,128)(2,1)}, bf16[1,192,896]{2,1,0:T(8,128)(2,1)S(1)}, u32[]{:S(2)}, u32[]{:S(2)}) %collective-permute-start.75) | collective-permute-done | bytes 344096 | tf_op jit(solution)/shard_map/ppermute | solution.py:825
  667.3 23.4 %collective-permute-done.77 = bf16[8,48,3072]{2,1,0:T(8,128)(2,1)S(1)} collective-permute-done((bf16[8,48,3072]{2,1,0:T(8,128)(2,1)S(1)}, bf16[8,48,3072]{2,1,0:T(8,128)(2,1)S(1)}, u32[]{:S(2)}, u32[]{:S(2)}) %collective-permute-start.77) | collective-permute-done | bytes 2359328 | tf_op jit(solution)/shard_map/ppermute | solution.py:825
  698.2 11.5 %collective-permute-done.81 = bf16[128,1536]{1,0:T(8,128)(2,1)S(1)} collective-permute-done((bf16[128,1536]{1,0:T(8,128)(2,1)S(1)}, bf16[128,1536]{1,0:T(8,128)(2,1)S(1)}, u32[]{:S(2)}, u32[]{:S(2)}) %collective-permute-start.81) | collective-permute-done | bytes 393248 | tf_op jit(solution)/shard_map/ppermute | solution.py:825
  723.0 10.1 %collective-permute-done.84.refs_9_ = bf16[1,192,896]{2,1,0:T(8,128)(2,1)S(1)} collective-permute-done((bf16[1,192,896]{2,1,0:T(8,128)(2,1)S(1)}, bf16[1,192,896]{2,1,0:T(8,128)(2,1)S(1)}, u32[]{:S(2)}, u32[]{:S(2)}) %collective-permute-start.84) | collective-permute-done | bytes 344096 | tf_op jit(solution)/shard_map/ppermute | solution.py:825
  741.5 10.3 %unpack.1 = (f32[192,10240]{1,0:T(8,128)}, f32[192,5120]{1,0:T(8,128)}) custom-call(s32[3]{0:T(128)} %pad_add_fusion.ids, bf16[1,192,1920]{2,1,0:T(8,128)(2,1)} %get-tuple-element.642.refs_0_, bf16[1,192,1920]{2,1,0:T(8,128)(2,1)} %copy-done.50, bf16[1,192,1920]{2,1,0:T(8,128)(2,1)} %copy-done.51, bf16[1,192,1920]{2,1,0:T(8,128)(2,1)} %collective-permute-done.67.refs_3_, ...), custom_call_target="tpu_custom_call" | custom-call | bytes 5899008 | tf_op jit(solution)/shard_map/unpack/pallas_call | solution.py:472
  756.2 13.4 %collective-permute-done.86 = bf16[48,4224]{1,0:T(8,128)(2,1)S(1)} collective-permute-done((bf16[48,4224]{1,0:T(8,128)(2,1)S(1)}, bf16[48,4224]{1,0:T(8,128)(2,1)S(1)}, u32[]{:S(2)}, u32[]{:S(2)}) %collective-permute-start.86) | collective-permute-done | bytes 405536 | tf_op jit(solution)/shard_map/ppermute | solution.py:825
  (510 shorter events, 449.2 us)
Async XLA Ops:
  156.7 43.4 %collective-permute-start.28 = (bf16[8,128,1664]{2,1,0:T(8,128)(2,1)S(1)}, bf16[8,128,1664]{2,1,0:T(8,128)(2,1)}, u32[]{:S(2)}, u32[]{:S(2)}) collective-permute-start(bf16[8,128,1664]{2,1,0:T(8,128)(2,1)S(1)} %pad_maximum_fusion.half.slots_half.refs_0_), channel_id=1, source_target_pairs={{0,1},{1,0},{2,3},{3,2},{4,5},{5,4},{6,7},{7,6},{8,9},{9,8},{10,11... | collective-permute-start | bytes 10223624 | tf_op jit(solution)/shard_map/ppermute | solution.py:825
  158.8 41.3 %collective-permute-start.29 = (bf16[2,128,1664]{2,1,0:T(8,128)(2,1)}, bf16[2,128,1664]{2,1,0:T(8,128)(2,1)}, u32[]{:S(2)}, u32[]{:S(2)}) collective-permute-start(bf16[2,128,1664]{2,1,0:T(8,128)(2,1)} %collective-permute-done.20), channel_id=1, source_target_pairs={{2,0},{3,1},{4,6},{5,7},{10,8},{11,9},{12,14},{13,15},{18,16},{19,... | collective-permute-start | bytes 2555912 | tf_op jit(solution)/shard_map/ppermute | solution.py:825
  160.4 33.8 %collective-permute-start.30 = (bf16[1,192,640]{2,1,0:T(8,128)(2,1)}, bf16[1,192,640]{2,1,0:T(8,128)(2,1)}, u32[]{:S(2)}, u32[]{:S(2)}) collective-permute-start(bf16[1,192,640]{2,1,0:T(8,128)(2,1)} %get-tuple-element.383), channel_id=1, source_target_pairs={{0,5},{1,4},{2,7},{3,6},{4,1},{5,0},{6,3},{7,2},{8,13},{9,12},{10,... | collective-permute-start | bytes 737288 | tf_op jit(solution)/shard_map/ppermute | solution.py:825
  165.9 28.3 %collective-permute-start.31 = (bf16[1,192,640]{2,1,0:T(8,128)(2,1)}, bf16[1,192,640]{2,1,0:T(8,128)(2,1)}, u32[]{:S(2)}, u32[]{:S(2)}) collective-permute-start(bf16[1,192,640]{2,1,0:T(8,128)(2,1)} %get-tuple-element.384), channel_id=1, source_target_pairs={{0,6},{1,7},{2,4},{3,5},{4,2},{5,3},{6,0},{7,1},{8,14},{9,15},{10,... | collective-permute-start | bytes 737288 | tf_op jit(solution)/shard_map/ppermute | solution.py:825
  227.3 31.1 %collective-permute-start.38 = (bf16[4,128,1664]{2,1,0:T(8,128)(2,1)S(1)}, bf16[4,128,1664]{2,1,0:T(8,128)(2,1)}, u32[]{:S(2)}, u32[]{:S(2)}) collective-permute-start(bf16[4,128,1664]{2,1,0:T(8,128)(2,1)S(1)} %pad_maximum_fusion.7), channel_id=1, source_target_pairs={{0,16},{1,9},{2,18},{3,11},{4,20},{5,13},{6,22},{7,15},{8,24},{9,1... | collective-permute-start | bytes 5111816 | tf_op jit(solution)/shard_map/ppermute | solution.py:825
  261.7 34.7 %collective-permute-start.42 = (bf16[8,128,1664]{2,1,0:T(8,128)(2,1)S(1)}, bf16[8,128,1664]{2,1,0:T(8,128)(2,1)}, u32[]{:S(2)}, u32[]{:S(2)}) collective-permute-start(bf16[8,128,1664]{2,1,0:T(8,128)(2,1)S(1)} %pad_maximum_fusion.1.half.slots_half.refs_2_), channel_id=1, source_target_pairs={{0,1},{1,0},{2,3},{3,2},{4,5},{5,4},{6,7},{7,6},{8,9},{9,8},{10,11... | collective-permute-start | bytes 10223624 | tf_op jit(solution)/shard_map/ppermute | solution.py:825
  261.7 34.6 %collective-permute-start.41 = (bf16[4,128,1664]{2,1,0:T(8,128)(2,1)}, bf16[4,128,1664]{2,1,0:T(8,128)(2,1)}, u32[]{:S(2)}, u32[]{:S(2)}) collective-permute-start(bf16[4,128,1664]{2,1,0:T(8,128)(2,1)} %pad_maximum_fusion.8), channel_id=1, source_target_pairs={{0,16},{1,9},{2,18},{3,11},{4,20},{5,13},{6,22},{7,15},{8,24},{9,1... | collective-permute-start | bytes 5111816 | tf_op jit(solution)/shard_map/ppermute | solution.py:825
  262.1 34.2 %collective-permute-start.40 = (bf16[2,128,1664]{2,1,0:T(8,128)(2,1)S(1)}, bf16[2,128,1664]{2,1,0:T(8,128)(2,1)}, u32[]{:S(2)}, u32[]{:S(2)}) collective-permute-start(bf16[2,128,1664]{2,1,0:T(8,128)(2,1)S(1)} %copy-done.49), channel_id=1, source_target_pairs={{2,0},{3,1},{4,6},{5,7},{10,8},{11,9},{12,14},{13,15},{18,16},{19,... | collective-permute-start | bytes 2555912 | tf_op jit(solution)/shard_map/ppermute | solution.py:825
  263.4 26.9 %collective-permute-start.43 = (bf16[1,192,1280]{2,1,0:T(8,128)(2,1)}, bf16[1,192,1280]{2,1,0:T(8,128)(2,1)}, u32[]{:S(2)}, u32[]{:S(2)}) collective-permute-start(bf16[1,192,1280]{2,1,0:T(8,128)(2,1)} %get-tuple-element.420), channel_id=1, source_target_pairs={{0,5},{1,4},{2,7},{3,6},{4,1},{5,0},{6,3},{7,2},{8,13},{9,12},{10,... | collective-permute-start | bytes 1474568 | tf_op jit(solution)/shard_map/ppermute | solution.py:825
  299.3 27.1 %collective-permute-start.44 = (bf16[8,128,1664]{2,1,0:T(8,128)(2,1)S(1)}, bf16[8,128,1664]{2,1,0:T(8,128)(2,1)}, u32[]{:S(2)}, u32[]{:S(2)}) collective-permute-start(bf16[8,128,1664]{2,1,0:T(8,128)(2,1)S(1)} %pad_maximum_fusion.2.half), channel_id=1, source_target_pairs={{0,1},{1,0},{2,3},{3,2},{4,5},{5,4},{6,7},{7,6},{8,9},{9,8},{10,11... | collective-permute-start | bytes 10223624 | tf_op jit(solution)/shard_map/ppermute | solution.py:825
  299.3 27.0 %collective-permute-start.45 = (bf16[2,128,1664]{2,1,0:T(8,128)(2,1)S(1)}, bf16[2,128,1664]{2,1,0:T(8,128)(2,1)S(1)}, u32[]{:S(2)}, u32[]{:S(2)}) collective-permute-start(bf16[2,128,1664]{2,1,0:T(8,128)(2,1)S(1)} %broadcast_select_fusion), channel_id=1, source_target_pairs={{0,8},{1,17},{2,10},{3,19},{4,12},{5,21},{6,14},{7,23},{8,0},{9,25... | collective-permute-start | bytes 2555912 | tf_op jit(solution)/shard_map/ppermute | solution.py:825
  425.6 29.5 %collective-permute-start.55 = (bf16[4,128,1664]{2,1,0:T(8,128)(2,1)S(1)}, bf16[4,128,1664]{2,1,0:T(8,128)(2,1)S(1)}, u32[]{:S(2)}, u32[]{:S(2)}) collective-permute-start(bf16[4,128,1664]{2,1,0:T(8,128)(2,1)S(1)} %get-tuple-element.488), channel_id=1, source_target_pairs={{0,16},{1,9},{2,18},{3,11},{4,20},{5,13},{6,22},{7,15},{8,24},{9,1... | collective-permute-start | bytes 5111816 | tf_op jit(solution)/shard_map/ppermute | solution.py:825
  474.7 38.3 %collective-permute-start.62 = (bf16[16,128,1536]{2,1,0:T(8,128)(2,1)}, bf16[16,128,1536]{2,1,0:T(8,128)(2,1)S(1)}, u32[]{:S(2)}, u32[]{:S(2)}) collective-permute-start(bf16[16,128,1536]{2,1,0:T(8,128)(2,1)} %get-tuple-element.506), channel_id=1, source_target_pairs={{0,1},{1,0},{2,3},{3,2},{4,5},{5,4},{6,7},{7,6},{8,9},{9,8},{10,11... | collective-permute-start | bytes 18874376 | tf_op jit(solution)/shard_map/ppermute | solution.py:825
  475.8 37.2 %collective-permute-start.63 = (bf16[1,192,1920]{2,1,0:T(8,128)(2,1)S(1)}, bf16[1,192,1920]{2,1,0:T(8,128)(2,1)S(1)}, u32[]{:S(2)}, u32[]{:S(2)}) collective-permute-start(bf16[1,192,1920]{2,1,0:T(8,128)(2,1)S(1)} %copy-done.52), channel_id=1, source_target_pairs={{0,2},{1,3},{2,0},{3,1},{4,6},{5,7},{6,4},{7,5},{8,10},{9,11},{10,... | collective-permute-start | bytes 2211848 | tf_op jit(solution)/shard_map/ppermute | solution.py:825
  478.4 34.7 %collective-permute-start.61 = (bf16[128,1664]{1,0:T(8,128)(2,1)S(1)}, bf16[128,1664]{1,0:T(8,128)(2,1)S(1)}, u32[]{:S(2)}, u32[]{:S(2)}) collective-permute-start(bf16[128,1664]{1,0:T(8,128)(2,1)S(1)} %get-tuple-element.505), channel_id=1, source_target_pairs={{0,6},{1,7},{2,4},{3,5},{4,2},{5,3},{6,0},{7,1},{8,14},{9,15},{10,... | collective-permute-start | bytes 1277960 | tf_op jit(solution)/shard_map/ppermute | solution.py:825
  518.7 67.4 %collective-permute-start.64 = (bf16[8,128,1536]{2,1,0:T(8,128)(2,1)}, bf16[8,128,1536]{2,1,0:T(8,128)(2,1)}, u32[]{:S(2)}, u32[]{:S(2)}) collective-permute-start(bf16[8,128,1536]{2,1,0:T(8,128)(2,1)} %get-tuple-element.511), channel_id=1, source_target_pairs={{0,16},{1,9},{2,18},{3,11},{4,20},{5,13},{6,22},{7,15},{8,24},{9,1... | collective-permute-start | bytes 9437192 | tf_op jit(solution)/shard_map/ppermute | solution.py:825
  519.9 53.3 %collective-permute-start.65 = (bf16[1,192,1920]{2,1,0:T(8,128)(2,1)}, bf16[1,192,1920]{2,1,0:T(8,128)(2,1)}, u32[]{:S(2)}, u32[]{:S(2)}) collective-permute-start(bf16[1,192,1920]{2,1,0:T(8,128)(2,1)} %get-tuple-element.512), channel_id=1, source_target_pairs={{0,4},{1,5},{2,6},{3,7},{4,0},{5,1},{6,2},{7,3},{8,12},{9,13},{10,... | collective-permute-start | bytes 2211848 | tf_op jit(solution)/shard_map/ppermute | solution.py:825
  524.0 62.0 %collective-permute-start.66 = (bf16[1,192,1920]{2,1,0:T(8,128)(2,1)}, bf16[1,192,1920]{2,1,0:T(8,128)(2,1)}, u32[]{:S(2)}, u32[]{:S(2)}) collective-permute-start(bf16[1,192,1920]{2,1,0:T(8,128)(2,1)} %get-tuple-element.513), channel_id=1, source_target_pairs={{0,5},{1,4},{2,7},{3,6},{4,1},{5,0},{6,3},{7,2},{8,13},{9,12},{10,... | collective-permute-start | bytes 2211848 | tf_op jit(solution)/shard_map/ppermute | solution.py:825
  524.0 62.0 %collective-permute-start.67 = (bf16[1,192,1920]{2,1,0:T(8,128)(2,1)}, bf16[1,192,1920]{2,1,0:T(8,128)(2,1)}, u32[]{:S(2)}, u32[]{:S(2)}) collective-permute-start(bf16[1,192,1920]{2,1,0:T(8,128)(2,1)} %get-tuple-element.514), channel_id=1, source_target_pairs={{0,3},{1,2},{2,1},{3,0},{4,7},{5,6},{6,5},{7,4},{8,11},{9,10},{10,... | collective-permute-start | bytes 2211848 | tf_op jit(solution)/shard_map/ppermute | solution.py:825
  620.2 35.3 %collective-permute-start.73 = (bf16[16,48,3072]{2,1,0:T(8,128)(2,1)}, bf16[16,48,3072]{2,1,0:T(8,128)(2,1)}, u32[]{:S(2)}, u32[]{:S(2)}) collective-permute-start(bf16[16,48,3072]{2,1,0:T(8,128)(2,1)} %get-tuple-element.542), channel_id=1, source_target_pairs={{0,1},{1,0},{2,3},{3,2},{4,5},{5,4},{6,7},{7,6},{8,9},{9,8},{10,11... | collective-permute-start | bytes 14155784 | tf_op jit(solution)/shard_map/ppermute | solution.py:825
  622.1 33.4 %collective-permute-start.74 = (bf16[2,128,1536]{2,1,0:T(8,128)(2,1)}, bf16[2,128,1536]{2,1,0:T(8,128)(2,1)}, u32[]{:S(2)}, u32[]{:S(2)}) collective-permute-start(bf16[2,128,1536]{2,1,0:T(8,128)(2,1)} %pad_maximum_fusion.18), channel_id=1, source_target_pairs={{0,2},{1,3},{6,4},{7,5},{8,10},{9,11},{14,12},{15,13},{16,18},{17,... | collective-permute-start | bytes 2359304 | tf_op jit(solution)/shard_map/ppermute | solution.py:825
  661.8 28.9 %collective-permute-start.77 = (bf16[8,48,3072]{2,1,0:T(8,128)(2,1)S(1)}, bf16[8,48,3072]{2,1,0:T(8,128)(2,1)S(1)}, u32[]{:S(2)}, u32[]{:S(2)}) collective-permute-start(bf16[8,48,3072]{2,1,0:T(8,128)(2,1)S(1)} %get-tuple-element.555), channel_id=1, source_target_pairs={{0,16},{1,9},{2,18},{3,11},{4,20},{5,13},{6,22},{7,15},{8,24},{9,1... | collective-permute-start | bytes 7077896 | tf_op jit(solution)/shard_map/ppermute | solution.py:825
  739.1 30.6 %collective-permute-start.86 = (bf16[48,4224]{1,0:T(8,128)(2,1)S(1)}, bf16[48,4224]{1,0:T(8,128)(2,1)S(1)}, u32[]{:S(2)}, u32[]{:S(2)}) collective-permute-start(bf16[48,4224]{1,0:T(8,128)(2,1)S(1)} %pad_maximum_fusion.23), channel_id=1, source_target_pairs={{0,4},{1,5},{2,6},{3,7},{4,0},{5,1},{6,2},{7,3},{8,12},{9,13},{10,... | collective-permute-start | bytes 1216520 | tf_op jit(solution)/shard_map/ppermute | solution.py:825
  739.3 30.4 %collective-permute-start.87 = (bf16[48,4224]{1,0:T(8,128)(2,1)S(1)}, bf16[48,4224]{1,0:T(8,128)(2,1)S(1)}, u32[]{:S(2)}, u32[]{:S(2)}) collective-permute-start(bf16[48,4224]{1,0:T(8,128)(2,1)S(1)} %pad_maximum_fusion.24), channel_id=1, source_target_pairs={{0,6},{1,7},{2,4},{3,5},{4,2},{5,3},{6,0},{7,1},{8,14},{9,15},{10,... | collective-permute-start | bytes 1216520 | tf_op jit(solution)/shard_map/ppermute | solution.py:825
  (159 other events, 2325.7 us)

commit v6 on v5

--- a/solution.py
+++ b/solution.py
@@ -1309,8 +1309,6 @@
     core, near = t_flows[0], t_flows[1] + t_flows[2]
     far = t_flows[5][:1] + t_flows[3] + t_flows[4] + t_flows[5][1:] + t_flows[6]
 
-    order.round([b_near, b_far] + some(far, 1))
-    b_line = [Flow(one_hop(b_near.result[1], to_line[1]))]
     moe_blocks = call(
         out_side_kernel,
         "out_side",
@@ -1321,11 +1319,13 @@
         scratch=[pltpu.VMEM((2, slot_rows, D), low)],
         flops=2 * slot_rows * D * (hid_width + 2 * rows),
     )
-    moe_blocks = order.round([b_far] + b_line + core, moe_blocks)
+    moe_blocks = order.round([b_near, b_far] + some(far, 1), moe_blocks)
+    moe = Flow(collect_all(*moe_blocks))
+    b_line = [Flow(one_hop(b_near.result[1], to_line[1]))]
+    order.round([b_far, moe] + b_line + core)
     b_line += [
         Flow(one_hop(piece, to_line[2 + i])) for i, piece in enumerate(by_distance(b_far.result))
     ]
-    moe = Flow(collect_all(*moe_blocks))
     order.round(b_line[1:] + [moe] + some(near, 1))
     grad_sum = total_of([b_near.result[0]] + [flow.result for flow in b_line])
 
@@ -1358,17 +1358,17 @@
     def dense_flow(products):
         return dense_terms(half_at, products, 2, 4 * GROUPS, fine)
 
-    kv_theirs, kv_mine = order.round(
-        [moe] + some(far, 2) + near, (kv_theirs, kv_mine)
+    early_blocks = dense_flow([(branch_grad, attended, 0), (normed_in, query_back, q_width)])
+    kv_theirs, kv_mine, early_blocks = order.round(
+        [moe] + some(far, 2) + near, (kv_theirs, kv_mine, early_blocks)
     )
     kv_core = Flow(one_hop(kv_theirs, to_core))
-    order.round([kv_core])
+    early = Flow(collect_all(*early_blocks))
+    order.round([kv_core, early])
     kv_half = add_low(kv_mine, kv_core.result).reshape(4, rows, 2 * kv_width)
     kv = [Flow(one_hop(kv_half[k], to_line[k])) for k in (1, 2, 3)]
-    early_blocks = dense_flow([(branch_grad, attended, 0), (normed_in, query_back, q_width)])
-    early_blocks = order.round(kv + [moe], early_blocks)
+    order.round(kv + [early])
     m_line = Flow(line_collect(moe.result[:2], moe.result[2:]))
-    early = Flow(collect_all(*early_blocks))
     kv_grad = total_of([kv_half[0]] + [flow.result for flow in kv])
 
     def line_of(blocks):
@@ -1400,16 +1400,15 @@
             ((scaled_two * normal_two).astype(low), marker(EXPERTS), 2 * kv_width),
         ]
     )
-    late_blocks = order.round([early, m_line] + some(far, 1), late_blocks)
+    late_blocks = order.round([early, m_line] + some(far, 2), late_blocks)
     late = Flow(collect_all(*late_blocks))
     input_grad = order.round(
-        [late, early, m_line], input_grad.astype(low)
-    )
-    order.round([late, early, m_line] + some(far, 1))
+        [late, m_line], input_grad.astype(low)
+    )
+    early_line = line_of(early.result)
+    order.round([late, m_line] + early_line)
     order.round([late] + far)
-    dense_line = line_of(
-        [jnp.concatenate(pair, 1) for pair in zip(early.result, late.result)]
-    )
+    late_line = line_of(late.result)
     spots = jnp.arange(GROUPS, dtype=jnp.int32) ^ group_at
     mate = 1 + shard_at % 2
     spots = jnp.where(spots == mate, 1, jnp.where(spots == 3 - mate, 2, spots))
@@ -1429,9 +1428,14 @@
         (ids,) + tuple(t_parts) + (gain_two,),
         steps=own_experts,
     )
-    gate_up_grad, down_grad = order.round(dense_line, (gate_up_grad, down_grad))
-    own_sum = jnp.concatenate([early.result[0], late.result[0]], 1)
-    own_sum = total_of([own_sum] + [flow.result for flow in dense_line]).astype(low)
+    gate_up_grad, down_grad = order.round(late_line, (gate_up_grad, down_grad))
+    own_sum = jnp.concatenate(
+        [
+            total_of([flow.result[0]] + [piece.result for piece in line]).astype(low)
+            for flow, line in ((early, early_line), (late, late_line))
+        ],
+        1,
+    )
     share_all = Flow(share_flow(own_sum, places))
     order.round([share_all])
     order.round([share_all])

time: 811 us -> 798 us (0.984)
  waiting for transfers between devices: 361 us -> 343 us
  starting transfers between devices: 120 us -> 136 us
    ppermute x90 -> x93, waiting for transfers between devices: 361 us -> 343 us  [hop(): return lax.ppermute(values, ('expert', 'shard'), pairs)]
    ppermute x90 -> x93, starting transfers between devices: 120 us -> 136 us  [hop(): return lax.ppermute(values, ('expert', 'shard'), pairs)]
    unnamed x197 -> x191, local copies, waits for them, and re-layouts: 21.7 us -> 20.7 us
  transfers between devices with their start and end apart: 90 -> 93, of which waited for: 44 -> 43; matrix products, arithmetic and copies ran while one was open for 7% -> 6% of each run, Pallas kernels for 22% -> 23%
where the time goes in v6:
time: 798 us; the launch traced here: 790 us
  waiting for transfers between devices  343 us (43%)
  Pallas kernels  178 us (22%)
  starting transfers between devices  136 us (17%)
  other arithmetic  74.1 us (9%)
  local copies, waits for them, and re-layouts  37.1 us (5%)
  matrix products  11.5 us (1%)
  between operations  10.4 us (1%)
    ppermute x93, waiting for transfers between devices, hop(): return lax.ppermute(values, ('expert', 'shard'), pairs)  343 us
    pallas_call x17, Pallas kernels, call(): pl.pallas_call(kernel, name=name, out_shape=out_shape, grid_spec=pltpu.Pr...  178 us
    ppermute x93, starting transfers between devices, hop(): return lax.ppermute(values, ('expert', 'shard'), pairs)  136 us
    convert_element_type x16, other arithmetic, add_low(): (one.astype(jnp.float32) + two.astype(jnp.float32)).astype(jnp.bfloat16)  30.5 us
    unnamed x191, local copies, waits for them, and re-layouts  20.7 us
  transfers between devices with their start and end apart: 93, of which 43 were waited for; matrix products, arithmetic and copies ran while one was open for 6% of the time, Pallas kernels for 23%

profile of v6, /device:TPU:0, one launch (start us, length us, event | category | flops | bytes accessed | tf_op | source)
XLA Modules:
  0.0 790.3 jit_solution(11523092292728501996)
XLA Ops:
  27.0 9.2 %pack.1 = (bf16[1,192,640]{2,1,0:T(8,128)(2,1)}, bf16[1,192,1280]{2,1,0:T(8,128)(2,1)}, bf16[1,192,640]{2,1,0:T(8,128)(2,1)}, bf16[1,192,1280]{2,1,0:T(8,128)(2,...) custom-call(s32[3]{0:T(128)} %pad_add_fusion.ids, ...), custom_call_target="tpu_custom_call" | custom-call | bytes 15729408 | tf_op jit(solution)/shard_map/pack/pallas_call | solution.py:472
  135.6 9.5 %collective-permute-done.23 = bf16[128,1024]{1,0:T(8,128)(2,1)S(1)} collective-permute-done((bf16[128,1024]{1,0:T(8,128)(2,1)S(1)}, bf16[128,1024]{1,0:T(8,128)(2,1)S(1)}, u32[]{:S(2)}, u32[]{:S(2)}) %collective-permute-start.23) | collective-permute-done | bytes 262176 | tf_op jit(solution)/shard_map/ppermute | solution.py:825
  169.4 14.8 %attend.1 = (bf16[128,1536]{1,0:T(8,128)(2,1)}, f32[4,128,128]{2,1,0:T(8,128)}) custom-call(s32[3]{0:T(128)} %pad_add_fusion.ids, bf16[128,1536]{1,0:T(8,128)(2,1)} %get-tuple-element.360.queries, bf16[512,1024]{1,0:T(8,128)(2,1)} %constant_dynamic-update-slice_fusion.11.key_line.value_line, bf16[512,1024]{1,0:T(8,128)(2,1)} %collective-permute-done.27.key_other.value_other, ...), custom_call_target="tpu_custom_call" | custom-call | flops 805306368 | bytes 5111808 | tf_op jit(solution)/shard_map/attend/pallas_call | solution.py:472
  205.4 17.6 %collective-permute-done.33 = bf16[128,1664]{1,0:T(8,128)(2,1)S(1)} collective-permute-done((bf16[128,1664]{1,0:T(8,128)(2,1)S(1)}, bf16[128,1664]{1,0:T(8,128)(2,1)S(1)}, u32[]{:S(2)}, u32[]{:S(2)}) %collective-permute-start.33) | collective-permute-done | bytes 426016 | tf_op jit(solution)/shard_map/ppermute | solution.py:825
  267.9 9.5 %grad_side.2 = (bf16[2,1024,1536]{2,1,0:T(8,128)(2,1)}, f32[512,640]{1,0:T(8,128)}) custom-call(s32[3]{0:T(128)} %pad_add_fusion.ids, bf16[8,128,1664]{2,1,0:T(8,128)(2,1)} %copy-done.3, bf16[8,128,1664]{2,1,0:T(8,128)(2,1)} %collective-permute-done.28.other.slots_other.refs_1_, bf16[1536,640]{1,0:T(8,128)(2,1)} %place_rows.6.down_one.down_two.refs_4_.refs_5_, ...), custom_call_target="tpu_custom_call" | custom-call | flops 1409286144 | bytes 10747904 | tf_op jit(solution)/shard_map/grad_side/pallas_call | solution.py:472
  277.4 13.0 %collective-permute-done.43.refs_5_ = bf16[1,192,1280]{2,1,0:T(8,128)(2,1)} collective-permute-done((bf16[1,192,1280]{2,1,0:T(8,128)(2,1)}, bf16[1,192,1280]{2,1,0:T(8,128)(2,1)}, u32[]{:S(2)}, u32[]{:S(2)}) %collective-permute-start.43) | collective-permute-done | bytes 491552 | tf_op jit(solution)/shard_map/ppermute | solution.py:825
  302.8 9.5 %grad_side.3 = (bf16[2,1024,1536]{2,1,0:T(8,128)(2,1)}, f32[512,640]{1,0:T(8,128)}) custom-call(s32[3]{0:T(128)} %pad_add_fusion.ids, bf16[8,128,1664]{2,1,0:T(8,128)(2,1)} %copy-done.2, bf16[8,128,1664]{2,1,0:T(8,128)(2,1)} %collective-permute-done.42.other.slots_other.refs_3_, ...), custom_call_target="tpu_custom_call", output_to_operand_aliasing={{0}: (5, {})} | custom-call | flops 1409286144 | bytes 17039360 | tf_op jit(solution)/shard_map/grad_side/pallas_call | solution.py:472
  316.8 9.7 %collective-permute-done.47.refs_3_ = bf16[1,192,1280]{2,1,0:T(8,128)(2,1)} collective-permute-done((bf16[1,192,1280]{2,1,0:T(8,128)(2,1)}, bf16[1,192,1280]{2,1,0:T(8,128)(2,1)}, u32[]{:S(2)}, u32[]{:S(2)}) %collective-permute-start.47) | collective-permute-done | bytes 491552 | tf_op jit(solution)/shard_map/ppermute | solution.py:825
  328.8 13.8 %collective-permute-done.49.refs_7_ = bf16[1,192,1280]{2,1,0:T(8,128)(2,1)S(1)} collective-permute-done((bf16[1,192,1280]{2,1,0:T(8,128)(2,1)S(1)}, bf16[1,192,1280]{2,1,0:T(8,128)(2,1)S(1)}, u32[]{:S(2)}, u32[]{:S(2)}) %collective-permute-start.49) | collective-permute-done | bytes 491552 | tf_op jit(solution)/shard_map/ppermute | solution.py:825
  355.5 17.9 %row_side.2 = (bf16[8,128,1664]{2,1,0:T(8,128)(2,1)}, bf16[8,128,1664]{2,1,0:T(8,128)(2,1)}, bf16[2,1024,1536]{2,1,0:T(8,128)(2,1)}, bf16[1024,640]{1,0:T(8,128)(2,1)}, bf16[1024,1280]{1,0:T(8,128)(2,1)}) custom-call(s32[3]{0:T(128)} %pad_add_fusion.ids, bf16[8,128,1664]{2,1,0:T(8,128)(2,1)} %copy-done.6, ...), custom_call_target="tpu_custom_call" | custom-call | flops 4831838208 | bytes 30670848 | tf_op jit(solution)/shard_map/row_side/pallas_call | solution.py:472
  373.5 18.8 %row_side.3 = (bf16[8,128,1664]{2,1,0:T(8,128)(2,1)}, bf16[8,128,1664]{2,1,0:T(8,128)(2,1)}, bf16[2,1024,1536]{2,1,0:T(8,128)(2,1)}, bf16[1024,640]{1,0:T(8,128)(2,1)}, bf16[1024,1280]{1,0:T(8,128)(2,1)}) custom-call(s32[3]{0:T(128)} %pad_add_fusion.ids, ...), custom_call_target="tpu_custom_call", output_to_operand_aliasing={{2}: (10, {}), {3}: (11, {}), {4}: (12, {})} | custom-call | flops 4831838208 | bytes 40894464 | tf_op jit(solution)/shard_map/row_side/pallas_call | solution.py:472
  397.8 13.8 %terms.1 = bf16[8,192,1920]{2,1,0:T(8,128)(2,1)} custom-call(s32[3]{0:T(128)} %pad_add_fusion.ids, bf16[2,1024,1536]{2,1,0:T(8,128)(2,1)} %get-tuple-element.483.xs, bf16[2,1024,1536]{2,1,0:T(8,128)(2,1)} %get-tuple-element.484.gs, bf16[1024,1280]{1,0:T(8,128)(2,1)} %get-tuple-element.485.pg, bf16[1024,640]{1,0:T(8,128)(2,1)} %get-tuple-element.486.hid), custom_call_target="tpu_custom_call" | custom-call | flops 6039797760 | bytes 16515072 | tf_op jit(solution)/shard_map/terms/pallas_call | solution.py:472
  431.8 12.7 %out_side.1 = (bf16[16,128,1536]{2,1,0:T(8,128)(2,1)}, bf16[16,128,1536]{2,1,0:T(8,128)(2,1)}) custom-call(s32[3]{0:T(128)} %pad_add_fusion.ids, bf16[1024,640]{1,0:T(8,128)(2,1)} %get-tuple-element.486.hid, bf16[8,128,1664]{2,1,0:T(8,128)(2,1)} %copy-done.3, bf16[8,128,1664]{2,1,0:T(8,128)(2,1)} %collective-permute-done.28.other.slots_other.refs_1_, ...), custom_call_target="tpu_custom_call" | custom-call | flops 2818572288 | bytes 18874368 | tf_op jit(solution)/shard_map/out_side/pallas_call | solution.py:472
  469.2 10.5 %collective-permute-done.59 = bf16[128,1664]{1,0:T(8,128)(2,1)S(1)} collective-permute-done((bf16[128,1664]{1,0:T(8,128)(2,1)S(1)}, bf16[128,1664]{1,0:T(8,128)(2,1)S(1)}, u32[]{:S(2)}, u32[]{:S(2)}) %collective-permute-start.59) | collective-permute-done | bytes 426016 | tf_op jit(solution)/shard_map/ppermute | solution.py:825
  488.7 23.5 %collective-permute-done.61 = bf16[128,1664]{1,0:T(8,128)(2,1)S(1)} collective-permute-done((bf16[128,1664]{1,0:T(8,128)(2,1)S(1)}, bf16[128,1664]{1,0:T(8,128)(2,1)S(1)}, u32[]{:S(2)}, u32[]{:S(2)}) %collective-permute-start.61) | collective-permute-done | bytes 426016 | tf_op jit(solution)/shard_map/ppermute | solution.py:825
  512.2 9.7 %collective-permute-done.62 = bf16[128,1664]{1,0:T(8,128)(2,1)S(1)} collective-permute-done((bf16[128,1664]{1,0:T(8,128)(2,1)S(1)}, bf16[128,1664]{1,0:T(8,128)(2,1)S(1)}, u32[]{:S(2)}, u32[]{:S(2)}) %collective-permute-start.62) | collective-permute-done | bytes 426016 | tf_op jit(solution)/shard_map/ppermute | solution.py:825
  536.4 18.1 %attend_back.1 = (bf16[128,1536]{1,0:T(8,128)(2,1)}, bf16[512,512]{1,0:T(8,128)(2,1)}, bf16[512,512]{1,0:T(8,128)(2,1)}, bf16[512,512]{1,0:T(8,128)(2,1)}, bf16[512,512]{1,0:T(8,128)(2,1)}) custom-call(s32[3]{0:T(128)} %pad_add_fusion.ids, bf16[128,1536]{1,0:T(8,128)(2,1)} %get-tuple-element.360.queries, bf16[128,1536]{1,0:T(8,128)(2,1)} %convolution_convert_fusion.grads, ...), custom_call_target="tpu_custom_call" | custom-call | flops 2013265920 | bytes 5898240 | tf_op jit(solution)/shard_map/attend_back/pallas_call | solution.py:472
  554.5 8.8 %dense_terms.2 = (bf16[16,48,3072]{2,1,0:T(8,128)(2,1)}, bf16[16,48,3072]{2,1,0:T(8,128)(2,1)}) custom-call(s32[32]{0:T(128)} %multiply_add_fusion.1.at, bf16[128,1536]{1,0:T(8,128)(2,1)} %copy-done.45, bf16[128,1536]{1,0:T(8,128)(2,1)} %get-tuple-element.379.refs_1_, bf16[128,1536]{1,0:T(8,128)(2,1)} %fusion.9.normed.refs_2_.refs_0_, ...), custom_call_target="tpu_custom_call" | custom-call | flops 1207959552 | bytes 1572864 | tf_op jit(solution)/shard_map/dense_terms/pallas_call | solution.py:472
  564.6 15.0 %collective-permute-done.66.refs_4_ = bf16[1,192,1920]{2,1,0:T(8,128)(2,1)S(1)} collective-permute-done((bf16[1,192,1920]{2,1,0:T(8,128)(2,1)}, bf16[1,192,1920]{2,1,0:T(8,128)(2,1)S(1)}, u32[]{:S(2)}, u32[]{:S(2)}) %collective-permute-start.66) | collective-permute-done | bytes 737312 | tf_op jit(solution)/shard_map/ppermute | solution.py:825
  579.7 14.3 %collective-permute-done.67.refs_5_ = bf16[1,192,1920]{2,1,0:T(8,128)(2,1)} collective-permute-done((bf16[1,192,1920]{2,1,0:T(8,128)(2,1)}, bf16[1,192,1920]{2,1,0:T(8,128)(2,1)}, u32[]{:S(2)}, u32[]{:S(2)}) %collective-permute-start.67) | collective-permute-done | bytes 737312 | tf_op jit(solution)/shard_map/ppermute | solution.py:825
  656.5 24.4 %collective-permute-done.77.refs_7_ = bf16[1,192,896]{2,1,0:T(8,128)(2,1)} collective-permute-done((bf16[1,192,896]{2,1,0:T(8,128)(2,1)}, bf16[1,192,896]{2,1,0:T(8,128)(2,1)}, u32[]{:S(2)}, u32[]{:S(2)}) %collective-permute-start.77) | collective-permute-done | bytes 344096 | tf_op jit(solution)/shard_map/ppermute | solution.py:825
  687.5 12.0 %collective-permute-start.82 = (bf16[128,1536]{1,0:T(8,128)(2,1)S(1)}, bf16[128,1536]{1,0:T(8,128)(2,1)S(1)}, u32[]{:S(2)}, u32[]{:S(2)}) collective-permute-start(bf16[128,1536]{1,0:T(8,128)(2,1)S(1)} %fusion.28), channel_id=1, source_target_pairs={{0,2},{1,3},{2,0},{3,1},{4,6},{5,7},{6,4},{7,5},{8,10},{9,11},{10,... | collective-permute-start | bytes 1179656 | tf_op jit(solution)/shard_map/ppermute | solution.py:825
  703.9 18.2 %collective-permute-done.83 = bf16[48,3072]{1,0:T(8,128)(2,1)S(1)} collective-permute-done((bf16[48,3072]{1,0:T(8,128)(2,1)S(1)}, bf16[48,3072]{1,0:T(8,128)(2,1)S(1)}, u32[]{:S(2)}, u32[]{:S(2)}) %collective-permute-start.83) | collective-permute-done | bytes 294944 | tf_op jit(solution)/shard_map/ppermute | solution.py:825
  748.7 10.6 %unpack.1 = (f32[192,10240]{1,0:T(8,128)}, f32[192,5120]{1,0:T(8,128)}) custom-call(s32[3]{0:T(128)} %pad_add_fusion.ids, bf16[1,192,1920]{2,1,0:T(8,128)(2,1)} %get-tuple-element.654.refs_0_, bf16[1,192,1920]{2,1,0:T(8,128)(2,1)} %copy-done.48, bf16[1,192,1920]{2,1,0:T(8,128)(2,1)} %copy-done.49, bf16[1,192,1920]{2,1,0:T(8,128)(2,1)} %collective-permute-done.68.refs_3_, ...), custom_call_target="tpu_custom_call" | custom-call | bytes 5899008 | tf_op jit(solution)/shard_map/unpack/pallas_call | solution.py:472
  (510 shorter events, 445.1 us)
Async XLA Ops:
  156.8 43.5 %collective-permute-start.28 = (bf16[8,128,1664]{2,1,0:T(8,128)(2,1)S(1)}, bf16[8,128,1664]{2,1,0:T(8,128)(2,1)}, u32[]{:S(2)}, u32[]{:S(2)}) collective-permute-start(bf16[8,128,1664]{2,1,0:T(8,128)(2,1)S(1)} %pad_maximum_fusion.half.slots_half.refs_0_), channel_id=1, source_target_pairs={{0,1},{1,0},{2,3},{3,2},{4,5},{5,4},{6,7},{7,6},{8,9},{9,8},{10,11... | collective-permute-start | bytes 10223624 | tf_op jit(solution)/shard_map/ppermute | solution.py:825
  158.9 41.3 %collective-permute-start.29 = (bf16[2,128,1664]{2,1,0:T(8,128)(2,1)}, bf16[2,128,1664]{2,1,0:T(8,128)(2,1)}, u32[]{:S(2)}, u32[]{:S(2)}) collective-permute-start(bf16[2,128,1664]{2,1,0:T(8,128)(2,1)} %collective-permute-done.20), channel_id=1, source_target_pairs={{2,0},{3,1},{4,6},{5,7},{10,8},{11,9},{12,14},{13,15},{18,16},{19,... | collective-permute-start | bytes 2555912 | tf_op jit(solution)/shard_map/ppermute | solution.py:825
  160.5 33.8 %collective-permute-start.30 = (bf16[1,192,640]{2,1,0:T(8,128)(2,1)}, bf16[1,192,640]{2,1,0:T(8,128)(2,1)}, u32[]{:S(2)}, u32[]{:S(2)}) collective-permute-start(bf16[1,192,640]{2,1,0:T(8,128)(2,1)} %get-tuple-element.389), channel_id=1, source_target_pairs={{0,5},{1,4},{2,7},{3,6},{4,1},{5,0},{6,3},{7,2},{8,13},{9,12},{10,... | collective-permute-start | bytes 737288 | tf_op jit(solution)/shard_map/ppermute | solution.py:825
  166.0 28.3 %collective-permute-start.31 = (bf16[1,192,640]{2,1,0:T(8,128)(2,1)}, bf16[1,192,640]{2,1,0:T(8,128)(2,1)}, u32[]{:S(2)}, u32[]{:S(2)}) collective-permute-start(bf16[1,192,640]{2,1,0:T(8,128)(2,1)} %get-tuple-element.390), channel_id=1, source_target_pairs={{0,6},{1,7},{2,4},{3,5},{4,2},{5,3},{6,0},{7,1},{8,14},{9,15},{10,... | collective-permute-start | bytes 737288 | tf_op jit(solution)/shard_map/ppermute | solution.py:825
  227.5 31.1 %collective-permute-start.38 = (bf16[4,128,1664]{2,1,0:T(8,128)(2,1)S(1)}, bf16[4,128,1664]{2,1,0:T(8,128)(2,1)}, u32[]{:S(2)}, u32[]{:S(2)}) collective-permute-start(bf16[4,128,1664]{2,1,0:T(8,128)(2,1)S(1)} %pad_maximum_fusion.7), channel_id=1, source_target_pairs={{0,16},{1,9},{2,18},{3,11},{4,20},{5,13},{6,22},{7,15},{8,24},{9,1... | collective-permute-start | bytes 5111816 | tf_op jit(solution)/shard_map/ppermute | solution.py:825
  261.8 34.6 %collective-permute-start.42 = (bf16[8,128,1664]{2,1,0:T(8,128)(2,1)S(1)}, bf16[8,128,1664]{2,1,0:T(8,128)(2,1)}, u32[]{:S(2)}, u32[]{:S(2)}) collective-permute-start(bf16[8,128,1664]{2,1,0:T(8,128)(2,1)S(1)} %pad_maximum_fusion.1.half.slots_half.refs_2_), channel_id=1, source_target_pairs={{0,1},{1,0},{2,3},{3,2},{4,5},{5,4},{6,7},{7,6},{8,9},{9,8},{10,11... | collective-permute-start | bytes 10223624 | tf_op jit(solution)/shard_map/ppermute | solution.py:825
  261.8 34.6 %collective-permute-start.41 = (bf16[4,128,1664]{2,1,0:T(8,128)(2,1)}, bf16[4,128,1664]{2,1,0:T(8,128)(2,1)}, u32[]{:S(2)}, u32[]{:S(2)}) collective-permute-start(bf16[4,128,1664]{2,1,0:T(8,128)(2,1)} %pad_maximum_fusion.8), channel_id=1, source_target_pairs={{0,16},{1,9},{2,18},{3,11},{4,20},{5,13},{6,22},{7,15},{8,24},{9,1... | collective-permute-start | bytes 5111816 | tf_op jit(solution)/shard_map/ppermute | solution.py:825
  262.2 34.2 %collective-permute-start.40 = (bf16[2,128,1664]{2,1,0:T(8,128)(2,1)S(1)}, bf16[2,128,1664]{2,1,0:T(8,128)(2,1)}, u32[]{:S(2)}, u32[]{:S(2)}) collective-permute-start(bf16[2,128,1664]{2,1,0:T(8,128)(2,1)S(1)} %copy-done.47), channel_id=1, source_target_pairs={{2,0},{3,1},{4,6},{5,7},{10,8},{11,9},{12,14},{13,15},{18,16},{19,... | collective-permute-start | bytes 2555912 | tf_op jit(solution)/shard_map/ppermute | solution.py:825
  299.4 27.1 %collective-permute-start.44 = (bf16[8,128,1664]{2,1,0:T(8,128)(2,1)S(1)}, bf16[8,128,1664]{2,1,0:T(8,128)(2,1)}, u32[]{:S(2)}, u32[]{:S(2)}) collective-permute-start(bf16[8,128,1664]{2,1,0:T(8,128)(2,1)S(1)} %pad_maximum_fusion.2.half), channel_id=1, source_target_pairs={{0,1},{1,0},{2,3},{3,2},{4,5},{5,4},{6,7},{7,6},{8,9},{9,8},{10,11... | collective-permute-start | bytes 10223624 | tf_op jit(solution)/shard_map/ppermute | solution.py:825
  429.7 29.7 %collective-permute-start.55 = (bf16[4,128,1664]{2,1,0:T(8,128)(2,1)}, bf16[4,128,1664]{2,1,0:T(8,128)(2,1)}, u32[]{:S(2)}, u32[]{:S(2)}) collective-permute-start(bf16[4,128,1664]{2,1,0:T(8,128)(2,1)} %get-tuple-element.494), channel_id=1, source_target_pairs={{0,16},{1,9},{2,18},{3,11},{4,20},{5,13},{6,22},{7,15},{8,24},{9,1... | collective-permute-start | bytes 5111816 | tf_op jit(solution)/shard_map/ppermute | solution.py:825
  483.0 38.8 %collective-permute-start.63 = (bf16[8,128,1536]{2,1,0:T(8,128)(2,1)S(1)}, bf16[8,128,1536]{2,1,0:T(8,128)(2,1)S(1)}, u32[]{:S(2)}, u32[]{:S(2)}) collective-permute-start(bf16[8,128,1536]{2,1,0:T(8,128)(2,1)S(1)} %get-tuple-element.514), channel_id=1, source_target_pairs={{0,16},{1,9},{2,18},{3,11},{4,20},{5,13},{6,22},{7,15},{8,24},{9,1... | collective-permute-start | bytes 9437192 | tf_op jit(solution)/shard_map/ppermute | solution.py:825
  484.3 37.5 %collective-permute-start.64 = (bf16[1,192,1920]{2,1,0:T(8,128)(2,1)S(1)}, bf16[1,192,1920]{2,1,0:T(8,128)(2,1)S(1)}, u32[]{:S(2)}, u32[]{:S(2)}) collective-permute-start(bf16[1,192,1920]{2,1,0:T(8,128)(2,1)S(1)} %get-tuple-element.515), channel_id=1, source_target_pairs={{0,2},{1,3},{2,0},{3,1},{4,6},{5,7},{6,4},{7,5},{8,10},{9,11},{10,... | collective-permute-start | bytes 2211848 | tf_op jit(solution)/shard_map/ppermute | solution.py:825
  487.1 34.8 %collective-permute-start.62 = (bf16[128,1664]{1,0:T(8,128)(2,1)S(1)}, bf16[128,1664]{1,0:T(8,128)(2,1)S(1)}, u32[]{:S(2)}, u32[]{:S(2)}) collective-permute-start(bf16[128,1664]{1,0:T(8,128)(2,1)S(1)} %get-tuple-element.513), channel_id=1, source_target_pairs={{0,6},{1,7},{2,4},{3,5},{4,2},{5,3},{6,0},{7,1},{8,14},{9,15},{10,... | collective-permute-start | bytes 1277960 | tf_op jit(solution)/shard_map/ppermute | solution.py:825
  527.1 67.0 %collective-permute-start.65 = (bf16[4,128,1536]{2,1,0:T(8,128)(2,1)}, bf16[4,128,1536]{2,1,0:T(8,128)(2,1)}, u32[]{:S(2)}, u32[]{:S(2)}) collective-permute-start(bf16[4,128,1536]{2,1,0:T(8,128)(2,1)} %get-tuple-element.519), channel_id=1, source_target_pairs={{0,8},{1,17},{2,10},{3,19},{4,12},{5,21},{6,14},{7,23},{8,0},{9,25... | collective-permute-start | bytes 4718600 | tf_op jit(solution)/shard_map/ppermute | solution.py:825
  527.6 52.1 %collective-permute-start.66 = (bf16[1,192,1920]{2,1,0:T(8,128)(2,1)}, bf16[1,192,1920]{2,1,0:T(8,128)(2,1)S(1)}, u32[]{:S(2)}, u32[]{:S(2)}) collective-permute-start(bf16[1,192,1920]{2,1,0:T(8,128)(2,1)} %get-tuple-element.520), channel_id=1, source_target_pairs={{0,4},{1,5},{2,6},{3,7},{4,0},{5,1},{6,2},{7,3},{8,12},{9,13},{10,... | collective-permute-start | bytes 2211848 | tf_op jit(solution)/shard_map/ppermute | solution.py:825
  531.7 62.3 %collective-permute-start.67 = (bf16[1,192,1920]{2,1,0:T(8,128)(2,1)}, bf16[1,192,1920]{2,1,0:T(8,128)(2,1)}, u32[]{:S(2)}, u32[]{:S(2)}) collective-permute-start(bf16[1,192,1920]{2,1,0:T(8,128)(2,1)} %get-tuple-element.521), channel_id=1, source_target_pairs={{0,5},{1,4},{2,7},{3,6},{4,1},{5,0},{6,3},{7,2},{8,13},{9,12},{10,... | collective-permute-start | bytes 2211848 | tf_op jit(solution)/shard_map/ppermute | solution.py:825
  531.7 62.3 %collective-permute-start.68 = (bf16[1,192,1920]{2,1,0:T(8,128)(2,1)}, bf16[1,192,1920]{2,1,0:T(8,128)(2,1)}, u32[]{:S(2)}, u32[]{:S(2)}) collective-permute-start(bf16[1,192,1920]{2,1,0:T(8,128)(2,1)} %get-tuple-element.522), channel_id=1, source_target_pairs={{0,3},{1,2},{2,1},{3,0},{4,7},{5,6},{6,5},{7,4},{8,11},{9,10},{10,... | collective-permute-start | bytes 2211848 | tf_op jit(solution)/shard_map/ppermute | solution.py:825
  606.6 28.9 %collective-permute-start.74 = (bf16[8,48,3072]{2,1,0:T(8,128)(2,1)S(1)}, bf16[8,48,3072]{2,1,0:T(8,128)(2,1)S(1)}, u32[]{:S(2)}, u32[]{:S(2)}) collective-permute-start(bf16[8,48,3072]{2,1,0:T(8,128)(2,1)S(1)} %get-tuple-element.550), channel_id=1, source_target_pairs={{0,16},{1,9},{2,18},{3,11},{4,20},{5,13},{6,22},{7,15},{8,24},{9,1... | collective-permute-start | bytes 7077896 | tf_op jit(solution)/shard_map/ppermute | solution.py:825
  637.9 42.9 %collective-permute-start.75 = (bf16[4,48,3072]{2,1,0:T(8,128)(2,1)}, bf16[4,48,3072]{2,1,0:T(8,128)(2,1)}, u32[]{:S(2)}, u32[]{:S(2)}) collective-permute-start(bf16[4,48,3072]{2,1,0:T(8,128)(2,1)} %get-tuple-element.553), channel_id=1, source_target_pairs={{0,8},{1,17},{2,10},{3,19},{4,12},{5,21},{6,14},{7,23},{8,0},{9,25... | collective-permute-start | bytes 3538952 | tf_op jit(solution)/shard_map/ppermute | solution.py:825
  642.7 38.1 %collective-permute-start.76 = (bf16[2,128,1536]{2,1,0:T(8,128)(2,1)}, bf16[2,128,1536]{2,1,0:T(8,128)(2,1)}, u32[]{:S(2)}, u32[]{:S(2)}) collective-permute-start(bf16[2,128,1536]{2,1,0:T(8,128)(2,1)} %pad_maximum_fusion.18), channel_id=1, source_target_pairs={{0,2},{1,3},{6,4},{7,5},{8,10},{9,11},{14,12},{15,13},{16,18},{17,... | collective-permute-start | bytes 2359304 | tf_op jit(solution)/shard_map/ppermute | solution.py:825
  646.4 34.4 %collective-permute-start.78 = (bf16[1,192,1024]{2,1,0:T(8,128)(2,1)}, bf16[1,192,1024]{2,1,0:T(8,128)(2,1)}, u32[]{:S(2)}, u32[]{:S(2)}) collective-permute-start(bf16[1,192,1024]{2,1,0:T(8,128)(2,1)} %get-tuple-element.556), channel_id=1, source_target_pairs={{0,7},{1,6},{2,5},{3,4},{4,3},{5,2},{6,1},{7,0},{8,15},{9,14},{10,... | collective-permute-start | bytes 1179656 | tf_op jit(solution)/shard_map/ppermute | solution.py:825
  647.4 33.4 %collective-permute-start.77 = (bf16[1,192,896]{2,1,0:T(8,128)(2,1)}, bf16[1,192,896]{2,1,0:T(8,128)(2,1)}, u32[]{:S(2)}, u32[]{:S(2)}) collective-permute-start(bf16[1,192,896]{2,1,0:T(8,128)(2,1)} %get-tuple-element.555), channel_id=1, source_target_pairs={{0,6},{1,7},{2,4},{3,5},{4,2},{5,3},{6,0},{7,1},{8,14},{9,15},{10,... | collective-permute-start | bytes 1032200 | tf_op jit(solution)/shard_map/ppermute | solution.py:825
  686.8 41.6 %collective-permute-start.81 = (bf16[8,48,1152]{2,1,0:T(8,128)(2,1)S(1)}, bf16[8,48,1152]{2,1,0:T(8,128)(2,1)S(1)}, u32[]{:S(2)}, u32[]{:S(2)}) collective-permute-start(bf16[8,48,1152]{2,1,0:T(8,128)(2,1)S(1)} %get-tuple-element.570), channel_id=1, source_target_pairs={{0,16},{1,9},{2,18},{3,11},{4,20},{5,13},{6,22},{7,15},{8,24},{9,1... | collective-permute-start | bytes 2654216 | tf_op jit(solution)/shard_map/ppermute | solution.py:825
  687.5 40.9 %collective-permute-start.82 = (bf16[128,1536]{1,0:T(8,128)(2,1)S(1)}, bf16[128,1536]{1,0:T(8,128)(2,1)S(1)}, u32[]{:S(2)}, u32[]{:S(2)}) collective-permute-start(bf16[128,1536]{1,0:T(8,128)(2,1)S(1)} %fusion.28), channel_id=1, source_target_pairs={{0,2},{1,3},{2,0},{3,1},{4,6},{5,7},{6,4},{7,5},{8,10},{9,11},{10,... | collective-permute-start | bytes 1179656 | tf_op jit(solution)/shard_map/ppermute | solution.py:825
  (159 other events, 2245.4 us)

commit v7 on v6

--- a/solution.py
+++ b/solution.py
@@ -1130,7 +1130,7 @@
         steps=qkv_width // tile,
     )
     queries, key_value = order.round(
-        [o_all, g_near, g_line] + some(near, 1), (queries, key_value)
+        [o_all, g_near, g_line], (queries, key_value)
     )
     kv = line_flows(key_value)
     order.round(kv + [o_all, g_near])
@@ -1267,7 +1267,7 @@
     row_pay = order.round([g_near, g_line] + some(far, 3), row_pay)
     x_line = Flow(line_spread(row_pay, x_marks))
     g_far = Flow(spread_pair(g_line.result))
-    order.round([x_line, g_far] + some(far, 1))
+    order.round([x_line, g_far] + some(far, 1) + some(near, 1))
     x_near = Flow(spread_pair([row_pay, x_marks[0]]))
     owned_down = exchanged(s_pieces, s_flows, 0)
     owned_down = order.round([x_line, x_near, g_far] + some(near, 1), owned_down)
@@ -1307,7 +1307,7 @@
     t_pieces += [[terms[k, :, :t_edge][None], terms[k, :, t_edge:][None]] for k in (6, 7)]
     t_flows = [[Flow(one_hop(piece, to_shard[k])) for piece in t_pieces[k]] for k in range(1, SHARDS)]
     core, near = t_flows[0], t_flows[1] + t_flows[2]
-    far = t_flows[5][:1] + t_flows[3] + t_flows[4] + t_flows[5][1:] + t_flows[6]
+    far = t_flows[5][:1] + t_flows[6][:1] + t_flows[3] + t_flows[4] + t_flows[5][1:] + t_flows[6][1:]
 
     moe_blocks = call(
         out_side_kernel,
@@ -1322,7 +1322,7 @@
     moe_blocks = order.round([b_near, b_far] + some(far, 1), moe_blocks)
     moe = Flow(collect_all(*moe_blocks))
     b_line = [Flow(one_hop(b_near.result[1], to_line[1]))]
-    order.round([b_far, moe] + b_line + core)
+    order.round([b_far, moe] + b_line + core + some(far, 1))
     b_line += [
         Flow(one_hop(piece, to_line[2 + i])) for i, piece in enumerate(by_distance(b_far.result))
     ]
@@ -1400,7 +1400,7 @@
             ((scaled_two * normal_two).astype(low), marker(EXPERTS), 2 * kv_width),
         ]
     )
-    late_blocks = order.round([early, m_line] + some(far, 2), late_blocks)
+    late_blocks = order.round([early, m_line] + some(far, 1), late_blocks)
     late = Flow(collect_all(*late_blocks))
     input_grad = order.round(
         [late, m_line], input_grad.astype(low)

time: 798 us -> 803 us (level)
  waiting for transfers between devices: 343 us -> 353 us
    ppermute x93, waiting for transfers between devices: 343 us -> 353 us  [hop(): return lax.ppermute(values, ('expert', 'shard'), pairs)]
    unnamed x191 -> x201, local copies, waits for them, and re-layouts: 20.7 us -> 19.7 us
  transfers between devices with their start and end apart: 93 -> 93, of which waited for: 43 -> 44; matrix products, arithmetic and copies ran while one was open for 6% -> 6% of each run, Pallas kernels for 23% -> 22%
where the time goes in v7:
time: 803 us; the launch traced here: 795 us
  waiting for transfers between devices  353 us (44%)
  Pallas kernels  178 us (22%)
  starting transfers between devices  130 us (16%)
  other arithmetic  74.4 us (9%)
  local copies, waits for them, and re-layouts  37.3 us (5%)
  matrix products  11.4 us (1%)
  between operations  10.5 us (1%)
    ppermute x93, waiting for transfers between devices, hop(): return lax.ppermute(values, ('expert', 'shard'), pairs)  353 us
    pallas_call x17, Pallas kernels, call(): pl.pallas_call(kernel, name=name, out_shape=out_shape, grid_spec=pltpu.Pr...  178 us
    ppermute x93, starting transfers between devices, hop(): return lax.ppermute(values, ('expert', 'shard'), pairs)  130 us
    convert_element_type x16, other arithmetic, add_low(): (one.astype(jnp.float32) + two.astype(jnp.float32)).astype(jnp.bfloat16)  30.6 us
    unnamed x201, local copies, waits for them, and re-layouts  19.7 us
  transfers between devices with their start and end apart: 93, of which 44 were waited for; matrix products, arithmetic and copies ran while one was open for 6% of the time, Pallas kernels for 22%

profile of v7, /device:TPU:0, one launch (start us, length us, event | category | flops | bytes accessed | tf_op | source)
XLA Modules:
  0.0 794.5 jit_solution(14114167340858597990)
XLA Ops:
  27.0 9.2 %pack.1 = (bf16[1,192,640]{2,1,0:T(8,128)(2,1)}, bf16[1,192,1280]{2,1,0:T(8,128)(2,1)}, bf16[1,192,640]{2,1,0:T(8,128)(2,1)}, bf16[1,192,1280]{2,1,0:T(8,128)(2,...) custom-call(s32[3]{0:T(128)} %pad_add_fusion.ids, ...), custom_call_target="tpu_custom_call" | custom-call | bytes 15729408 | tf_op jit(solution)/shard_map/pack/pallas_call | solution.py:472
  136.0 10.7 %collective-permute-done.22 = bf16[128,1024]{1,0:T(8,128)(2,1)S(1)} collective-permute-done((bf16[128,1024]{1,0:T(8,128)(2,1)S(1)}, bf16[128,1024]{1,0:T(8,128)(2,1)S(1)}, u32[]{:S(2)}, u32[]{:S(2)}) %collective-permute-start.22) | collective-permute-done | bytes 262176 | tf_op jit(solution)/shard_map/ppermute | solution.py:825
  171.6 14.7 %attend.1 = (bf16[128,1536]{1,0:T(8,128)(2,1)}, f32[4,128,128]{2,1,0:T(8,128)}) custom-call(s32[3]{0:T(128)} %pad_add_fusion.ids, bf16[128,1536]{1,0:T(8,128)(2,1)} %get-tuple-element.358.queries, bf16[512,1024]{1,0:T(8,128)(2,1)} %constant_dynamic-update-slice_fusion.11.key_line.value_line, bf16[512,1024]{1,0:T(8,128)(2,1)} %collective-permute-done.26.key_other.value_other, ...), custom_call_target="tpu_custom_call" | custom-call | flops 805306368 | bytes 5111808 | tf_op jit(solution)/shard_map/attend/pallas_call | solution.py:472
  207.7 23.8 %collective-permute-done.35.refs_3_ = bf16[1,192,640]{2,1,0:T(8,128)(2,1)S(1)} collective-permute-done((bf16[1,192,640]{2,1,0:T(8,128)(2,1)S(1)}, bf16[1,192,640]{2,1,0:T(8,128)(2,1)S(1)}, u32[]{:S(2)}, u32[]{:S(2)}) %collective-permute-start.35) | collective-permute-done | bytes 245792 | tf_op jit(solution)/shard_map/ppermute | solution.py:825
  273.0 9.5 %grad_side.2 = (bf16[2,1024,1536]{2,1,0:T(8,128)(2,1)}, f32[512,640]{1,0:T(8,128)}) custom-call(s32[3]{0:T(128)} %pad_add_fusion.ids, bf16[8,128,1664]{2,1,0:T(8,128)(2,1)} %copy-done.3, bf16[8,128,1664]{2,1,0:T(8,128)(2,1)} %collective-permute-done.27.other.slots_other.refs_1_, bf16[1536,640]{1,0:T(8,128)(2,1)} %place_rows.6.down_one.down_two.refs_4_.refs_5_, ...), custom_call_target="tpu_custom_call" | custom-call | flops 1409286144 | bytes 10747904 | tf_op jit(solution)/shard_map/grad_side/pallas_call | solution.py:472
  282.5 13.0 %collective-permute-done.43.refs_5_ = bf16[1,192,1280]{2,1,0:T(8,128)(2,1)} collective-permute-done((bf16[1,192,1280]{2,1,0:T(8,128)(2,1)}, bf16[1,192,1280]{2,1,0:T(8,128)(2,1)}, u32[]{:S(2)}, u32[]{:S(2)}) %collective-permute-start.43) | collective-permute-done | bytes 491552 | tf_op jit(solution)/shard_map/ppermute | solution.py:825
  307.2 9.5 %grad_side.3 = (bf16[2,1024,1536]{2,1,0:T(8,128)(2,1)}, f32[512,640]{1,0:T(8,128)}) custom-call(s32[3]{0:T(128)} %pad_add_fusion.ids, bf16[8,128,1664]{2,1,0:T(8,128)(2,1)} %copy-done.2, bf16[8,128,1664]{2,1,0:T(8,128)(2,1)} %collective-permute-done.42.other.slots_other.refs_3_, ...), custom_call_target="tpu_custom_call", output_to_operand_aliasing={{0}: (5, {})} | custom-call | flops 1409286144 | bytes 17039360 | tf_op jit(solution)/shard_map/grad_side/pallas_call | solution.py:472
  322.0 9.5 %collective-permute-done.47.refs_3_ = bf16[1,192,1280]{2,1,0:T(8,128)(2,1)} collective-permute-done((bf16[1,192,1280]{2,1,0:T(8,128)(2,1)}, bf16[1,192,1280]{2,1,0:T(8,128)(2,1)}, u32[]{:S(2)}, u32[]{:S(2)}) %collective-permute-start.47) | collective-permute-done | bytes 491552 | tf_op jit(solution)/shard_map/ppermute | solution.py:825
  333.2 13.8 %collective-permute-done.49.refs_7_ = bf16[1,192,1280]{2,1,0:T(8,128)(2,1)S(1)} collective-permute-done((bf16[1,192,1280]{2,1,0:T(8,128)(2,1)S(1)}, bf16[1,192,1280]{2,1,0:T(8,128)(2,1)S(1)}, u32[]{:S(2)}, u32[]{:S(2)}) %collective-permute-start.49) | collective-permute-done | bytes 491552 | tf_op jit(solution)/shard_map/ppermute | solution.py:825
  360.6 17.9 %row_side.2 = (bf16[8,128,1664]{2,1,0:T(8,128)(2,1)}, bf16[8,128,1664]{2,1,0:T(8,128)(2,1)}, bf16[2,1024,1536]{2,1,0:T(8,128)(2,1)}, bf16[1024,640]{1,0:T(8,128)(2,1)}, bf16[1024,1280]{1,0:T(8,128)(2,1)}) custom-call(s32[3]{0:T(128)} %pad_add_fusion.ids, bf16[8,128,1664]{2,1,0:T(8,128)(2,1)} %copy-done.6, ...), custom_call_target="tpu_custom_call" | custom-call | flops 4831838208 | bytes 30670848 | tf_op jit(solution)/shard_map/row_side/pallas_call | solution.py:472
  378.5 18.7 %row_side.3 = (bf16[8,128,1664]{2,1,0:T(8,128)(2,1)}, bf16[8,128,1664]{2,1,0:T(8,128)(2,1)}, bf16[2,1024,1536]{2,1,0:T(8,128)(2,1)}, bf16[1024,640]{1,0:T(8,128)(2,1)}, bf16[1024,1280]{1,0:T(8,128)(2,1)}) custom-call(s32[3]{0:T(128)} %pad_add_fusion.ids, ...), custom_call_target="tpu_custom_call", output_to_operand_aliasing={{2}: (10, {}), {3}: (11, {}), {4}: (12, {})} | custom-call | flops 4831838208 | bytes 40894464 | tf_op jit(solution)/shard_map/row_side/pallas_call | solution.py:472
  401.9 13.8 %terms.1 = bf16[8,192,1920]{2,1,0:T(8,128)(2,1)} custom-call(s32[3]{0:T(128)} %pad_add_fusion.ids, bf16[2,1024,1536]{2,1,0:T(8,128)(2,1)} %get-tuple-element.483.xs, bf16[2,1024,1536]{2,1,0:T(8,128)(2,1)} %get-tuple-element.484.gs, bf16[1024,1280]{1,0:T(8,128)(2,1)} %get-tuple-element.485.pg, bf16[1024,640]{1,0:T(8,128)(2,1)} %get-tuple-element.486.hid), custom_call_target="tpu_custom_call" | custom-call | flops 6039797760 | bytes 16515072 | tf_op jit(solution)/shard_map/terms/pallas_call | solution.py:472
  436.5 12.7 %out_side.1 = (bf16[16,128,1536]{2,1,0:T(8,128)(2,1)}, bf16[16,128,1536]{2,1,0:T(8,128)(2,1)}) custom-call(s32[3]{0:T(128)} %pad_add_fusion.ids, bf16[1024,640]{1,0:T(8,128)(2,1)} %get-tuple-element.486.hid, bf16[8,128,1664]{2,1,0:T(8,128)(2,1)} %copy-done.3, bf16[8,128,1664]{2,1,0:T(8,128)(2,1)} %collective-permute-done.27.other.slots_other.refs_1_, ...), custom_call_target="tpu_custom_call" | custom-call | flops 2818572288 | bytes 18874368 | tf_op jit(solution)/shard_map/out_side/pallas_call | solution.py:472
  475.4 18.4 %collective-permute-done.61.refs_8_ = bf16[1,192,1024]{2,1,0:T(8,128)(2,1)S(1)} collective-permute-done((bf16[1,192,1024]{2,1,0:T(8,128)(2,1)S(1)}, bf16[1,192,1024]{2,1,0:T(8,128)(2,1)S(1)}, u32[]{:S(2)}, u32[]{:S(2)}) %collective-permute-start.61) | collective-permute-done | bytes 393248 | tf_op jit(solution)/shard_map/ppermute | solution.py:825
  503.0 21.6 %collective-permute-done.62 = bf16[128,1664]{1,0:T(8,128)(2,1)S(1)} collective-permute-done((bf16[128,1664]{1,0:T(8,128)(2,1)S(1)}, bf16[128,1664]{1,0:T(8,128)(2,1)S(1)}, u32[]{:S(2)}, u32[]{:S(2)}) %collective-permute-start.62) | collective-permute-done | bytes 426016 | tf_op jit(solution)/shard_map/ppermute | solution.py:825
  524.6 11.2 %collective-permute-done.63 = bf16[128,1664]{1,0:T(8,128)(2,1)S(1)} collective-permute-done((bf16[128,1664]{1,0:T(8,128)(2,1)S(1)}, bf16[128,1664]{1,0:T(8,128)(2,1)S(1)}, u32[]{:S(2)}, u32[]{:S(2)}) %collective-permute-start.63) | collective-permute-done | bytes 426016 | tf_op jit(solution)/shard_map/ppermute | solution.py:825
  549.6 18.2 %attend_back.1 = (bf16[128,1536]{1,0:T(8,128)(2,1)}, bf16[512,512]{1,0:T(8,128)(2,1)}, bf16[512,512]{1,0:T(8,128)(2,1)}, bf16[512,512]{1,0:T(8,128)(2,1)}, bf16[512,512]{1,0:T(8,128)(2,1)}) custom-call(s32[3]{0:T(128)} %pad_add_fusion.ids, bf16[128,1536]{1,0:T(8,128)(2,1)} %get-tuple-element.358.queries, bf16[128,1536]{1,0:T(8,128)(2,1)} %convolution_convert_fusion.grads, ...), custom_call_target="tpu_custom_call" | custom-call | flops 2013265920 | bytes 5898240 | tf_op jit(solution)/shard_map/attend_back/pallas_call | solution.py:472
  577.9 16.8 %collective-permute-done.67.refs_4_ = bf16[1,192,1920]{2,1,0:T(8,128)(2,1)S(1)} collective-permute-done((bf16[1,192,1920]{2,1,0:T(8,128)(2,1)}, bf16[1,192,1920]{2,1,0:T(8,128)(2,1)S(1)}, u32[]{:S(2)}, u32[]{:S(2)}) %collective-permute-start.67) | collective-permute-done | bytes 737312 | tf_op jit(solution)/shard_map/ppermute | solution.py:825
  594.7 13.2 %collective-permute-done.68.refs_5_ = bf16[1,192,1920]{2,1,0:T(8,128)(2,1)} collective-permute-done((bf16[1,192,1920]{2,1,0:T(8,128)(2,1)}, bf16[1,192,1920]{2,1,0:T(8,128)(2,1)}, u32[]{:S(2)}, u32[]{:S(2)}) %collective-permute-start.68) | collective-permute-done | bytes 737312 | tf_op jit(solution)/shard_map/ppermute | solution.py:825
  670.1 16.0 %collective-permute-done.78.refs_7_ = bf16[1,192,896]{2,1,0:T(8,128)(2,1)} collective-permute-done((bf16[1,192,896]{2,1,0:T(8,128)(2,1)}, bf16[1,192,896]{2,1,0:T(8,128)(2,1)}, u32[]{:S(2)}, u32[]{:S(2)}) %collective-permute-start.78) | collective-permute-done | bytes 344096 | tf_op jit(solution)/shard_map/ppermute | solution.py:825
  693.5 12.3 %collective-permute-start.82 = (bf16[128,1536]{1,0:T(8,128)(2,1)S(1)}, bf16[128,1536]{1,0:T(8,128)(2,1)S(1)}, u32[]{:S(2)}, u32[]{:S(2)}) collective-permute-start(bf16[128,1536]{1,0:T(8,128)(2,1)S(1)} %fusion.28), channel_id=1, source_target_pairs={{0,2},{1,3},{2,0},{3,1},{4,6},{5,7},{6,4},{7,5},{8,10},{9,11},{10,... | collective-permute-start | bytes 1179656 | tf_op jit(solution)/shard_map/ppermute | solution.py:825
  710.2 18.6 %collective-permute-done.83 = bf16[48,3072]{1,0:T(8,128)(2,1)S(1)} collective-permute-done((bf16[48,3072]{1,0:T(8,128)(2,1)S(1)}, bf16[48,3072]{1,0:T(8,128)(2,1)S(1)}, u32[]{:S(2)}, u32[]{:S(2)}) %collective-permute-start.83) | collective-permute-done | bytes 294944 | tf_op jit(solution)/shard_map/ppermute | solution.py:825
  737.4 10.4 %collective-permute-done.87.refs_9_ = bf16[1,192,896]{2,1,0:T(8,128)(2,1)S(1)} collective-permute-done((bf16[1,192,896]{2,1,0:T(8,128)(2,1)S(1)}, bf16[1,192,896]{2,1,0:T(8,128)(2,1)S(1)}, u32[]{:S(2)}, u32[]{:S(2)}) %collective-permute-start.87) | collective-permute-done | bytes 344096 | tf_op jit(solution)/shard_map/ppermute | solution.py:825
  754.7 10.6 %unpack.1 = (f32[192,10240]{1,0:T(8,128)}, f32[192,5120]{1,0:T(8,128)}) custom-call(s32[3]{0:T(128)} %pad_add_fusion.ids, bf16[1,192,1920]{2,1,0:T(8,128)(2,1)} %get-tuple-element.654.refs_0_, bf16[1,192,1920]{2,1,0:T(8,128)(2,1)} %copy-done.49, bf16[1,192,1920]{2,1,0:T(8,128)(2,1)} %copy-done.50, bf16[1,192,1920]{2,1,0:T(8,128)(2,1)} %collective-permute-done.69.refs_3_, ...), custom_call_target="tpu_custom_call" | custom-call | bytes 5899008 | tf_op jit(solution)/shard_map/unpack/pallas_call | solution.py:472
  (520 shorter events, 439.9 us)
Async XLA Ops:
  158.5 43.6 %collective-permute-start.27 = (bf16[8,128,1664]{2,1,0:T(8,128)(2,1)S(1)}, bf16[8,128,1664]{2,1,0:T(8,128)(2,1)}, u32[]{:S(2)}, u32[]{:S(2)}) collective-permute-start(bf16[8,128,1664]{2,1,0:T(8,128)(2,1)S(1)} %pad_maximum_fusion.half.slots_half.refs_0_), channel_id=1, source_target_pairs={{0,1},{1,0},{2,3},{3,2},{4,5},{5,4},{6,7},{7,6},{8,9},{9,8},{10,11... | collective-permute-start | bytes 10223624 | tf_op jit(solution)/shard_map/ppermute | solution.py:825
  160.6 41.5 %collective-permute-start.28 = (bf16[2,128,1664]{2,1,0:T(8,128)(2,1)}, bf16[2,128,1664]{2,1,0:T(8,128)(2,1)}, u32[]{:S(2)}, u32[]{:S(2)}) collective-permute-start(bf16[2,128,1664]{2,1,0:T(8,128)(2,1)} %copy-done.46), channel_id=1, source_target_pairs={{2,0},{3,1},{4,6},{5,7},{10,8},{11,9},{12,14},{13,15},{18,16},{19,... | collective-permute-start | bytes 2555912 | tf_op jit(solution)/shard_map/ppermute | solution.py:825
  162.2 34.3 %collective-permute-start.29 = (bf16[1,192,640]{2,1,0:T(8,128)(2,1)}, bf16[1,192,640]{2,1,0:T(8,128)(2,1)}, u32[]{:S(2)}, u32[]{:S(2)}) collective-permute-start(bf16[1,192,640]{2,1,0:T(8,128)(2,1)} %get-tuple-element.387), channel_id=1, source_target_pairs={{0,5},{1,4},{2,7},{3,6},{4,1},{5,0},{6,3},{7,2},{8,13},{9,12},{10,... | collective-permute-start | bytes 737288 | tf_op jit(solution)/shard_map/ppermute | solution.py:825
  168.2 28.3 %collective-permute-start.30 = (bf16[1,192,640]{2,1,0:T(8,128)(2,1)}, bf16[1,192,640]{2,1,0:T(8,128)(2,1)}, u32[]{:S(2)}, u32[]{:S(2)}) collective-permute-start(bf16[1,192,640]{2,1,0:T(8,128)(2,1)} %get-tuple-element.388), channel_id=1, source_target_pairs={{0,6},{1,7},{2,4},{3,5},{4,2},{5,3},{6,0},{7,1},{8,14},{9,15},{10,... | collective-permute-start | bytes 737288 | tf_op jit(solution)/shard_map/ppermute | solution.py:825
  203.3 28.2 %collective-permute-start.33 = (bf16[2,128,1664]{2,1,0:T(8,128)(2,1)S(1)}, bf16[2,128,1664]{2,1,0:T(8,128)(2,1)S(1)}, u32[]{:S(2)}, u32[]{:S(2)}) collective-permute-start(bf16[2,128,1664]{2,1,0:T(8,128)(2,1)S(1)} %broadcast_select_fusion.1), channel_id=1, source_target_pairs={{0,8},{1,17},{2,10},{3,19},{4,12},{5,21},{6,14},{7,23},{8,0},{9,25... | collective-permute-start | bytes 2555912 | tf_op jit(solution)/shard_map/ppermute | solution.py:825
  232.7 31.1 %collective-permute-start.38 = (bf16[4,128,1664]{2,1,0:T(8,128)(2,1)S(1)}, bf16[4,128,1664]{2,1,0:T(8,128)(2,1)}, u32[]{:S(2)}, u32[]{:S(2)}) collective-permute-start(bf16[4,128,1664]{2,1,0:T(8,128)(2,1)S(1)} %pad_maximum_fusion.7), channel_id=1, source_target_pairs={{0,16},{1,9},{2,18},{3,11},{4,20},{5,13},{6,22},{7,15},{8,24},{9,1... | collective-permute-start | bytes 5111816 | tf_op jit(solution)/shard_map/ppermute | solution.py:825
  267.0 34.4 %collective-permute-start.42 = (bf16[8,128,1664]{2,1,0:T(8,128)(2,1)S(1)}, bf16[8,128,1664]{2,1,0:T(8,128)(2,1)}, u32[]{:S(2)}, u32[]{:S(2)}) collective-permute-start(bf16[8,128,1664]{2,1,0:T(8,128)(2,1)S(1)} %pad_maximum_fusion.1.half.slots_half.refs_2_), channel_id=1, source_target_pairs={{0,1},{1,0},{2,3},{3,2},{4,5},{5,4},{6,7},{7,6},{8,9},{9,8},{10,11... | collective-permute-start | bytes 10223624 | tf_op jit(solution)/shard_map/ppermute | solution.py:825
  267.1 34.3 %collective-permute-start.41 = (bf16[4,128,1664]{2,1,0:T(8,128)(2,1)}, bf16[4,128,1664]{2,1,0:T(8,128)(2,1)}, u32[]{:S(2)}, u32[]{:S(2)}) collective-permute-start(bf16[4,128,1664]{2,1,0:T(8,128)(2,1)} %pad_maximum_fusion.8), channel_id=1, source_target_pairs={{0,16},{1,9},{2,18},{3,11},{4,20},{5,13},{6,22},{7,15},{8,24},{9,1... | collective-permute-start | bytes 5111816 | tf_op jit(solution)/shard_map/ppermute | solution.py:825
  267.4 34.1 %collective-permute-start.40 = (bf16[2,128,1664]{2,1,0:T(8,128)(2,1)S(1)}, bf16[2,128,1664]{2,1,0:T(8,128)(2,1)}, u32[]{:S(2)}, u32[]{:S(2)}) collective-permute-start(bf16[2,128,1664]{2,1,0:T(8,128)(2,1)S(1)} %copy-done.48), channel_id=1, source_target_pairs={{2,0},{3,1},{4,6},{5,7},{10,8},{11,9},{12,14},{13,15},{18,16},{19,... | collective-permute-start | bytes 2555912 | tf_op jit(solution)/shard_map/ppermute | solution.py:825
  304.4 27.1 %collective-permute-start.44 = (bf16[8,128,1664]{2,1,0:T(8,128)(2,1)S(1)}, bf16[8,128,1664]{2,1,0:T(8,128)(2,1)}, u32[]{:S(2)}, u32[]{:S(2)}) collective-permute-start(bf16[8,128,1664]{2,1,0:T(8,128)(2,1)S(1)} %pad_maximum_fusion.2.half), channel_id=1, source_target_pairs={{0,1},{1,0},{2,3},{3,2},{4,5},{5,4},{6,7},{7,6},{8,9},{9,8},{10,11... | collective-permute-start | bytes 10223624 | tf_op jit(solution)/shard_map/ppermute | solution.py:825
  304.5 27.0 %collective-permute-start.45 = (bf16[2,128,1664]{2,1,0:T(8,128)(2,1)S(1)}, bf16[2,128,1664]{2,1,0:T(8,128)(2,1)S(1)}, u32[]{:S(2)}, u32[]{:S(2)}) collective-permute-start(bf16[2,128,1664]{2,1,0:T(8,128)(2,1)S(1)} %broadcast_select_fusion), channel_id=1, source_target_pairs={{0,8},{1,17},{2,10},{3,19},{4,12},{5,21},{6,14},{7,23},{8,0},{9,25... | collective-permute-start | bytes 2555912 | tf_op jit(solution)/shard_map/ppermute | solution.py:825
  434.7 29.6 %collective-permute-start.55 = (bf16[4,128,1664]{2,1,0:T(8,128)(2,1)}, bf16[4,128,1664]{2,1,0:T(8,128)(2,1)}, u32[]{:S(2)}, u32[]{:S(2)}) collective-permute-start(bf16[4,128,1664]{2,1,0:T(8,128)(2,1)} %get-tuple-element.494), channel_id=1, source_target_pairs={{0,16},{1,9},{2,18},{3,11},{4,20},{5,13},{6,22},{7,15},{8,24},{9,1... | collective-permute-start | bytes 5111816 | tf_op jit(solution)/shard_map/ppermute | solution.py:825
  497.2 38.6 %collective-permute-start.64 = (bf16[8,128,1536]{2,1,0:T(8,128)(2,1)S(1)}, bf16[8,128,1536]{2,1,0:T(8,128)(2,1)S(1)}, u32[]{:S(2)}, u32[]{:S(2)}) collective-permute-start(bf16[8,128,1536]{2,1,0:T(8,128)(2,1)S(1)} %get-tuple-element.515), channel_id=1, source_target_pairs={{0,16},{1,9},{2,18},{3,11},{4,20},{5,13},{6,22},{7,15},{8,24},{9,1... | collective-permute-start | bytes 9437192 | tf_op jit(solution)/shard_map/ppermute | solution.py:825
  498.6 37.2 %collective-permute-start.65 = (bf16[1,192,1920]{2,1,0:T(8,128)(2,1)S(1)}, bf16[1,192,1920]{2,1,0:T(8,128)(2,1)S(1)}, u32[]{:S(2)}, u32[]{:S(2)}) collective-permute-start(bf16[1,192,1920]{2,1,0:T(8,128)(2,1)S(1)} %get-tuple-element.516), channel_id=1, source_target_pairs={{0,2},{1,3},{2,0},{3,1},{4,6},{5,7},{6,4},{7,5},{8,10},{9,11},{10,... | collective-permute-start | bytes 2211848 | tf_op jit(solution)/shard_map/ppermute | solution.py:825
  501.6 34.2 %collective-permute-start.63 = (bf16[128,1664]{1,0:T(8,128)(2,1)S(1)}, bf16[128,1664]{1,0:T(8,128)(2,1)S(1)}, u32[]{:S(2)}, u32[]{:S(2)}) collective-permute-start(bf16[128,1664]{1,0:T(8,128)(2,1)S(1)} %get-tuple-element.514), channel_id=1, source_target_pairs={{0,6},{1,7},{2,4},{3,5},{4,2},{5,3},{6,0},{7,1},{8,14},{9,15},{10,... | collective-permute-start | bytes 1277960 | tf_op jit(solution)/shard_map/ppermute | solution.py:825
  541.0 66.9 %collective-permute-start.66 = (bf16[4,128,1536]{2,1,0:T(8,128)(2,1)}, bf16[4,128,1536]{2,1,0:T(8,128)(2,1)}, u32[]{:S(2)}, u32[]{:S(2)}) collective-permute-start(bf16[4,128,1536]{2,1,0:T(8,128)(2,1)} %get-tuple-element.520), channel_id=1, source_target_pairs={{0,8},{1,17},{2,10},{3,19},{4,12},{5,21},{6,14},{7,23},{8,0},{9,25... | collective-permute-start | bytes 4718600 | tf_op jit(solution)/shard_map/ppermute | solution.py:825
  541.5 53.2 %collective-permute-start.67 = (bf16[1,192,1920]{2,1,0:T(8,128)(2,1)}, bf16[1,192,1920]{2,1,0:T(8,128)(2,1)S(1)}, u32[]{:S(2)}, u32[]{:S(2)}) collective-permute-start(bf16[1,192,1920]{2,1,0:T(8,128)(2,1)} %get-tuple-element.521), channel_id=1, source_target_pairs={{0,4},{1,5},{2,6},{3,7},{4,0},{5,1},{6,2},{7,3},{8,12},{9,13},{10,... | collective-permute-start | bytes 2211848 | tf_op jit(solution)/shard_map/ppermute | solution.py:825
  545.6 62.3 %collective-permute-start.68 = (bf16[1,192,1920]{2,1,0:T(8,128)(2,1)}, bf16[1,192,1920]{2,1,0:T(8,128)(2,1)}, u32[]{:S(2)}, u32[]{:S(2)}) collective-permute-start(bf16[1,192,1920]{2,1,0:T(8,128)(2,1)} %get-tuple-element.522), channel_id=1, source_target_pairs={{0,5},{1,4},{2,7},{3,6},{4,1},{5,0},{6,3},{7,2},{8,13},{9,12},{10,... | collective-permute-start | bytes 2211848 | tf_op jit(solution)/shard_map/ppermute | solution.py:825
  545.6 62.3 %collective-permute-start.69 = (bf16[1,192,1920]{2,1,0:T(8,128)(2,1)}, bf16[1,192,1920]{2,1,0:T(8,128)(2,1)}, u32[]{:S(2)}, u32[]{:S(2)}) collective-permute-start(bf16[1,192,1920]{2,1,0:T(8,128)(2,1)} %get-tuple-element.523), channel_id=1, source_target_pairs={{0,3},{1,2},{2,1},{3,0},{4,7},{5,6},{6,5},{7,4},{8,11},{9,10},{10,... | collective-permute-start | bytes 2211848 | tf_op jit(solution)/shard_map/ppermute | solution.py:825
  621.1 28.9 %collective-permute-start.75 = (bf16[8,48,3072]{2,1,0:T(8,128)(2,1)S(1)}, bf16[8,48,3072]{2,1,0:T(8,128)(2,1)S(1)}, u32[]{:S(2)}, u32[]{:S(2)}) collective-permute-start(bf16[8,48,3072]{2,1,0:T(8,128)(2,1)S(1)} %get-tuple-element.551), channel_id=1, source_target_pairs={{0,16},{1,9},{2,18},{3,11},{4,20},{5,13},{6,22},{7,15},{8,24},{9,1... | collective-permute-start | bytes 7077896 | tf_op jit(solution)/shard_map/ppermute | solution.py:825
  652.4 33.7 %collective-permute-start.76 = (bf16[4,48,3072]{2,1,0:T(8,128)(2,1)}, bf16[4,48,3072]{2,1,0:T(8,128)(2,1)}, u32[]{:S(2)}, u32[]{:S(2)}) collective-permute-start(bf16[4,48,3072]{2,1,0:T(8,128)(2,1)} %get-tuple-element.554), channel_id=1, source_target_pairs={{0,8},{1,17},{2,10},{3,19},{4,12},{5,21},{6,14},{7,23},{8,0},{9,25... | collective-permute-start | bytes 3538952 | tf_op jit(solution)/shard_map/ppermute | solution.py:825
  657.5 28.6 %collective-permute-start.77 = (bf16[2,128,1536]{2,1,0:T(8,128)(2,1)}, bf16[2,128,1536]{2,1,0:T(8,128)(2,1)}, u32[]{:S(2)}, u32[]{:S(2)}) collective-permute-start(bf16[2,128,1536]{2,1,0:T(8,128)(2,1)} %pad_maximum_fusion.18), channel_id=1, source_target_pairs={{0,2},{1,3},{6,4},{7,5},{8,10},{9,11},{14,12},{15,13},{16,18},{17,... | collective-permute-start | bytes 2359304 | tf_op jit(solution)/shard_map/ppermute | solution.py:825
  692.1 43.6 %collective-permute-start.81 = (bf16[8,48,1152]{2,1,0:T(8,128)(2,1)S(1)}, bf16[8,48,1152]{2,1,0:T(8,128)(2,1)S(1)}, u32[]{:S(2)}, u32[]{:S(2)}) collective-permute-start(bf16[8,48,1152]{2,1,0:T(8,128)(2,1)S(1)} %get-tuple-element.570), channel_id=1, source_target_pairs={{0,16},{1,9},{2,18},{3,11},{4,20},{5,13},{6,22},{7,15},{8,24},{9,1... | collective-permute-start | bytes 2654216 | tf_op jit(solution)/shard_map/ppermute | solution.py:825
  693.5 42.2 %collective-permute-start.82 = (bf16[128,1536]{1,0:T(8,128)(2,1)S(1)}, bf16[128,1536]{1,0:T(8,128)(2,1)S(1)}, u32[]{:S(2)}, u32[]{:S(2)}) collective-permute-start(bf16[128,1536]{1,0:T(8,128)(2,1)S(1)} %fusion.28), channel_id=1, source_target_pairs={{0,2},{1,3},{2,0},{3,1},{4,6},{5,7},{6,4},{7,5},{8,10},{9,11},{10,... | collective-permute-start | bytes 1179656 | tf_op jit(solution)/shard_map/ppermute | solution.py:825
  (164 other events, 2338.7 us)

commit v8 on v6

--- a/solution.py
+++ b/solution.py
@@ -1264,10 +1264,10 @@
         kept_rows = tuple(kept_next)
         return half_back, other_back
 
-    row_pay = order.round([g_near, g_line] + some(far, 3), row_pay)
+    row_pay = order.round([g_near, g_line] + some(far, 2), row_pay)
     x_line = Flow(line_spread(row_pay, x_marks))
     g_far = Flow(spread_pair(g_line.result))
-    order.round([x_line, g_far] + some(far, 1))
+    order.round([x_line, g_far] + some(far, 2))
     x_near = Flow(spread_pair([row_pay, x_marks[0]]))
     owned_down = exchanged(s_pieces, s_flows, 0)
     owned_down = order.round([x_line, x_near, g_far] + some(near, 1), owned_down)

time: 798 us -> 799 us (level)
    unnamed x191 -> x195, local copies, waits for them, and re-layouts: 20.7 us -> 20.7 us
  transfers between devices with their start and end apart: 93 -> 93, of which waited for: 43 -> 44; matrix products, arithmetic and copies ran while one was open for 6% -> 6% of each run, Pallas kernels for 23% -> 23%
where the time goes in v8:
time: 799 us; the launch traced here: 791 us
  waiting for transfers between devices  337 us (42%)
  Pallas kernels  178 us (22%)
  starting transfers between devices  142 us (18%)
  other arithmetic  74.2 us (9%)
  local copies, waits for them, and re-layouts  37.1 us (5%)
  matrix products  11.5 us (1%)
  between operations  10.4 us (1%)
    ppermute x93, waiting for transfers between devices, hop(): return lax.ppermute(values, ('expert', 'shard'), pairs)  337 us
    pallas_call x17, Pallas kernels, call(): pl.pallas_call(kernel, name=name, out_shape=out_shape, grid_spec=pltpu.Pr...  178 us
    ppermute x93, starting transfers between devices, hop(): return lax.ppermute(values, ('expert', 'shard'), pairs)  142 us
    convert_element_type x16, other arithmetic, add_low(): (one.astype(jnp.float32) + two.astype(jnp.float32)).astype(jnp.bfloat16)  30.5 us
    unnamed x195, local copies, waits for them, and re-layouts  20.7 us
  transfers between devices with their start and end apart: 93, of which 44 were waited for; matrix products, arithmetic and copies ran while one was open for 6% of the time, Pallas kernels for 23%

profile of v8, /device:TPU:0, one launch (start us, length us, event | category | flops | bytes accessed | tf_op | source)
XLA Modules:
  0.0 790.8 jit_solution(4545897233880855501)
XLA Ops:
  27.1 9.2 %pack.1 = (bf16[1,192,640]{2,1,0:T(8,128)(2,1)}, bf16[1,192,1280]{2,1,0:T(8,128)(2,1)}, bf16[1,192,640]{2,1,0:T(8,128)(2,1)}, bf16[1,192,1280]{2,1,0:T(8,128)(2,...) custom-call(s32[3]{0:T(128)} %pad_add_fusion.ids, ...), custom_call_target="tpu_custom_call" | custom-call | bytes 15729408 | tf_op jit(solution)/shard_map/pack/pallas_call | solution.py:472
  135.6 9.5 %collective-permute-done.23 = bf16[128,1024]{1,0:T(8,128)(2,1)S(1)} collective-permute-done((bf16[128,1024]{1,0:T(8,128)(2,1)S(1)}, bf16[128,1024]{1,0:T(8,128)(2,1)S(1)}, u32[]{:S(2)}, u32[]{:S(2)}) %collective-permute-start.23) | collective-permute-done | bytes 262176 | tf_op jit(solution)/shard_map/ppermute | solution.py:825
  168.2 14.8 %attend.1 = (bf16[128,1536]{1,0:T(8,128)(2,1)}, f32[4,128,128]{2,1,0:T(8,128)}) custom-call(s32[3]{0:T(128)} %pad_add_fusion.ids, bf16[128,1536]{1,0:T(8,128)(2,1)} %get-tuple-element.360.queries, bf16[512,1024]{1,0:T(8,128)(2,1)} %constant_dynamic-update-slice_fusion.11.key_line.value_line, bf16[512,1024]{1,0:T(8,128)(2,1)} %collective-permute-done.27.key_other.value_other, ...), custom_call_target="tpu_custom_call" | custom-call | flops 805306368 | bytes 5111808 | tf_op jit(solution)/shard_map/attend/pallas_call | solution.py:472
  201.0 22.6 %collective-permute-done.34.refs_7_ = bf16[1,192,640]{2,1,0:T(8,128)(2,1)S(1)} collective-permute-done((bf16[1,192,640]{2,1,0:T(8,128)(2,1)S(1)}, bf16[1,192,640]{2,1,0:T(8,128)(2,1)S(1)}, u32[]{:S(2)}, u32[]{:S(2)}) %collective-permute-start.34) | collective-permute-done | bytes 245792 | tf_op jit(solution)/shard_map/ppermute | solution.py:825
  271.3 9.5 %grad_side.2 = (bf16[2,1024,1536]{2,1,0:T(8,128)(2,1)}, f32[512,640]{1,0:T(8,128)}) custom-call(s32[3]{0:T(128)} %pad_add_fusion.ids, bf16[8,128,1664]{2,1,0:T(8,128)(2,1)} %copy-done.3, bf16[8,128,1664]{2,1,0:T(8,128)(2,1)} %collective-permute-done.28.other.slots_other.refs_1_, bf16[1536,640]{1,0:T(8,128)(2,1)} %place_rows.6.down_one.down_two.refs_4_.refs_5_, ...), custom_call_target="tpu_custom_call" | custom-call | flops 1409286144 | bytes 10747904 | tf_op jit(solution)/shard_map/grad_side/pallas_call | solution.py:472
  280.9 13.1 %collective-permute-done.43.refs_5_ = bf16[1,192,1280]{2,1,0:T(8,128)(2,1)} collective-permute-done((bf16[1,192,1280]{2,1,0:T(8,128)(2,1)}, bf16[1,192,1280]{2,1,0:T(8,128)(2,1)}, u32[]{:S(2)}, u32[]{:S(2)}) %collective-permute-start.43) | collective-permute-done | bytes 491552 | tf_op jit(solution)/shard_map/ppermute | solution.py:825
  306.2 9.5 %grad_side.3 = (bf16[2,1024,1536]{2,1,0:T(8,128)(2,1)}, f32[512,640]{1,0:T(8,128)}) custom-call(s32[3]{0:T(128)} %pad_add_fusion.ids, bf16[8,128,1664]{2,1,0:T(8,128)(2,1)} %copy-done.2, bf16[8,128,1664]{2,1,0:T(8,128)(2,1)} %collective-permute-done.42.other.slots_other.refs_3_, ...), custom_call_target="tpu_custom_call", output_to_operand_aliasing={{0}: (5, {})} | custom-call | flops 1409286144 | bytes 17039360 | tf_op jit(solution)/shard_map/grad_side/pallas_call | solution.py:472
  320.3 9.7 %collective-permute-done.47.refs_3_ = bf16[1,192,1280]{2,1,0:T(8,128)(2,1)} collective-permute-done((bf16[1,192,1280]{2,1,0:T(8,128)(2,1)}, bf16[1,192,1280]{2,1,0:T(8,128)(2,1)}, u32[]{:S(2)}, u32[]{:S(2)}) %collective-permute-start.47) | collective-permute-done | bytes 491552 | tf_op jit(solution)/shard_map/ppermute | solution.py:825
  332.3 13.8 %collective-permute-done.49.refs_7_ = bf16[1,192,1280]{2,1,0:T(8,128)(2,1)S(1)} collective-permute-done((bf16[1,192,1280]{2,1,0:T(8,128)(2,1)S(1)}, bf16[1,192,1280]{2,1,0:T(8,128)(2,1)S(1)}, u32[]{:S(2)}, u32[]{:S(2)}) %collective-permute-start.49) | collective-permute-done | bytes 491552 | tf_op jit(solution)/shard_map/ppermute | solution.py:825
  359.0 17.9 %row_side.2 = (bf16[8,128,1664]{2,1,0:T(8,128)(2,1)}, bf16[8,128,1664]{2,1,0:T(8,128)(2,1)}, bf16[2,1024,1536]{2,1,0:T(8,128)(2,1)}, bf16[1024,640]{1,0:T(8,128)(2,1)}, bf16[1024,1280]{1,0:T(8,128)(2,1)}) custom-call(s32[3]{0:T(128)} %pad_add_fusion.ids, bf16[8,128,1664]{2,1,0:T(8,128)(2,1)} %copy-done.6, ...), custom_call_target="tpu_custom_call" | custom-call | flops 4831838208 | bytes 30670848 | tf_op jit(solution)/shard_map/row_side/pallas_call | solution.py:472
  376.9 18.8 %row_side.3 = (bf16[8,128,1664]{2,1,0:T(8,128)(2,1)}, bf16[8,128,1664]{2,1,0:T(8,128)(2,1)}, bf16[2,1024,1536]{2,1,0:T(8,128)(2,1)}, bf16[1024,640]{1,0:T(8,128)(2,1)}, bf16[1024,1280]{1,0:T(8,128)(2,1)}) custom-call(s32[3]{0:T(128)} %pad_add_fusion.ids, ...), custom_call_target="tpu_custom_call", output_to_operand_aliasing={{2}: (10, {}), {3}: (11, {}), {4}: (12, {})} | custom-call | flops 4831838208 | bytes 40894464 | tf_op jit(solution)/shard_map/row_side/pallas_call | solution.py:472
  401.1 13.8 %terms.1 = bf16[8,192,1920]{2,1,0:T(8,128)(2,1)} custom-call(s32[3]{0:T(128)} %pad_add_fusion.ids, bf16[2,1024,1536]{2,1,0:T(8,128)(2,1)} %get-tuple-element.483.xs, bf16[2,1024,1536]{2,1,0:T(8,128)(2,1)} %get-tuple-element.484.gs, bf16[1024,1280]{1,0:T(8,128)(2,1)} %get-tuple-element.485.pg, bf16[1024,640]{1,0:T(8,128)(2,1)} %get-tuple-element.486.hid), custom_call_target="tpu_custom_call" | custom-call | flops 6039797760 | bytes 16515072 | tf_op jit(solution)/shard_map/terms/pallas_call | solution.py:472
  435.2 12.7 %out_side.1 = (bf16[16,128,1536]{2,1,0:T(8,128)(2,1)}, bf16[16,128,1536]{2,1,0:T(8,128)(2,1)}) custom-call(s32[3]{0:T(128)} %pad_add_fusion.ids, bf16[1024,640]{1,0:T(8,128)(2,1)} %get-tuple-element.486.hid, bf16[8,128,1664]{2,1,0:T(8,128)(2,1)} %copy-done.3, bf16[8,128,1664]{2,1,0:T(8,128)(2,1)} %collective-permute-done.28.other.slots_other.refs_1_, ...), custom_call_target="tpu_custom_call" | custom-call | flops 2818572288 | bytes 18874368 | tf_op jit(solution)/shard_map/out_side/pallas_call | solution.py:472
  472.5 10.5 %collective-permute-done.59 = bf16[128,1664]{1,0:T(8,128)(2,1)S(1)} collective-permute-done((bf16[128,1664]{1,0:T(8,128)(2,1)S(1)}, bf16[128,1664]{1,0:T(8,128)(2,1)S(1)}, u32[]{:S(2)}, u32[]{:S(2)}) %collective-permute-start.59) | collective-permute-done | bytes 426016 | tf_op jit(solution)/shard_map/ppermute | solution.py:825
  492.1 23.5 %collective-permute-done.61 = bf16[128,1664]{1,0:T(8,128)(2,1)S(1)} collective-permute-done((bf16[128,1664]{1,0:T(8,128)(2,1)S(1)}, bf16[128,1664]{1,0:T(8,128)(2,1)S(1)}, u32[]{:S(2)}, u32[]{:S(2)}) %collective-permute-start.61) | collective-permute-done | bytes 426016 | tf_op jit(solution)/shard_map/ppermute | solution.py:825
  515.6 9.7 %collective-permute-done.62 = bf16[128,1664]{1,0:T(8,128)(2,1)S(1)} collective-permute-done((bf16[128,1664]{1,0:T(8,128)(2,1)S(1)}, bf16[128,1664]{1,0:T(8,128)(2,1)S(1)}, u32[]{:S(2)}, u32[]{:S(2)}) %collective-permute-start.62) | collective-permute-done | bytes 426016 | tf_op jit(solution)/shard_map/ppermute | solution.py:825
  539.7 18.1 %attend_back.1 = (bf16[128,1536]{1,0:T(8,128)(2,1)}, bf16[512,512]{1,0:T(8,128)(2,1)}, bf16[512,512]{1,0:T(8,128)(2,1)}, bf16[512,512]{1,0:T(8,128)(2,1)}, bf16[512,512]{1,0:T(8,128)(2,1)}) custom-call(s32[3]{0:T(128)} %pad_add_fusion.ids, bf16[128,1536]{1,0:T(8,128)(2,1)} %get-tuple-element.360.queries, bf16[128,1536]{1,0:T(8,128)(2,1)} %convolution_convert_fusion.grads, ...), custom_call_target="tpu_custom_call" | custom-call | flops 2013265920 | bytes 5898240 | tf_op jit(solution)/shard_map/attend_back/pallas_call | solution.py:472
  567.9 15.3 %collective-permute-done.66.refs_4_ = bf16[1,192,1920]{2,1,0:T(8,128)(2,1)S(1)} collective-permute-done((bf16[1,192,1920]{2,1,0:T(8,128)(2,1)}, bf16[1,192,1920]{2,1,0:T(8,128)(2,1)S(1)}, u32[]{:S(2)}, u32[]{:S(2)}) %collective-permute-start.66) | collective-permute-done | bytes 737312 | tf_op jit(solution)/shard_map/ppermute | solution.py:825
  583.2 14.0 %collective-permute-done.67.refs_5_ = bf16[1,192,1920]{2,1,0:T(8,128)(2,1)} collective-permute-done((bf16[1,192,1920]{2,1,0:T(8,128)(2,1)}, bf16[1,192,1920]{2,1,0:T(8,128)(2,1)}, u32[]{:S(2)}, u32[]{:S(2)}) %collective-permute-start.67) | collective-permute-done | bytes 737312 | tf_op jit(solution)/shard_map/ppermute | solution.py:825
  659.9 23.9 %collective-permute-done.77.refs_7_ = bf16[1,192,896]{2,1,0:T(8,128)(2,1)} collective-permute-done((bf16[1,192,896]{2,1,0:T(8,128)(2,1)}, bf16[1,192,896]{2,1,0:T(8,128)(2,1)}, u32[]{:S(2)}, u32[]{:S(2)}) %collective-permute-start.77) | collective-permute-done | bytes 344096 | tf_op jit(solution)/shard_map/ppermute | solution.py:825
  690.9 12.0 %collective-permute-start.82 = (bf16[128,1536]{1,0:T(8,128)(2,1)S(1)}, bf16[128,1536]{1,0:T(8,128)(2,1)S(1)}, u32[]{:S(2)}, u32[]{:S(2)}) collective-permute-start(bf16[128,1536]{1,0:T(8,128)(2,1)S(1)} %fusion.28), channel_id=1, source_target_pairs={{0,2},{1,3},{2,0},{3,1},{4,6},{5,7},{6,4},{7,5},{8,10},{9,11},{10,... | collective-permute-start | bytes 1179656 | tf_op jit(solution)/shard_map/ppermute | solution.py:825
  707.2 17.5 %collective-permute-done.83 = bf16[48,3072]{1,0:T(8,128)(2,1)S(1)} collective-permute-done((bf16[48,3072]{1,0:T(8,128)(2,1)S(1)}, bf16[48,3072]{1,0:T(8,128)(2,1)S(1)}, u32[]{:S(2)}, u32[]{:S(2)}) %collective-permute-start.83) | collective-permute-done | bytes 294944 | tf_op jit(solution)/shard_map/ppermute | solution.py:825
  733.9 11.0 %collective-permute-done.87.refs_9_ = bf16[1,192,896]{2,1,0:T(8,128)(2,1)S(1)} collective-permute-done((bf16[1,192,896]{2,1,0:T(8,128)(2,1)S(1)}, bf16[1,192,896]{2,1,0:T(8,128)(2,1)S(1)}, u32[]{:S(2)}, u32[]{:S(2)}) %collective-permute-start.87) | collective-permute-done | bytes 344096 | tf_op jit(solution)/shard_map/ppermute | solution.py:825
  750.9 10.6 %unpack.1 = (f32[192,10240]{1,0:T(8,128)}, f32[192,5120]{1,0:T(8,128)}) custom-call(s32[3]{0:T(128)} %pad_add_fusion.ids, bf16[1,192,1920]{2,1,0:T(8,128)(2,1)} %get-tuple-element.654.refs_0_, bf16[1,192,1920]{2,1,0:T(8,128)(2,1)} %copy-done.48, bf16[1,192,1920]{2,1,0:T(8,128)(2,1)} %copy-done.49, bf16[1,192,1920]{2,1,0:T(8,128)(2,1)} %collective-permute-done.68.refs_3_, ...), custom_call_target="tpu_custom_call" | custom-call | bytes 5899008 | tf_op jit(solution)/shard_map/unpack/pallas_call | solution.py:472
  (514 shorter events, 439.5 us)
Async XLA Ops:
  156.8 38.2 %collective-permute-start.28 = (bf16[8,128,1664]{2,1,0:T(8,128)(2,1)S(1)}, bf16[8,128,1664]{2,1,0:T(8,128)(2,1)}, u32[]{:S(2)}, u32[]{:S(2)}) collective-permute-start(bf16[8,128,1664]{2,1,0:T(8,128)(2,1)S(1)} %pad_maximum_fusion.half.slots_half.refs_0_), channel_id=1, source_target_pairs={{0,1},{1,0},{2,3},{3,2},{4,5},{5,4},{6,7},{7,6},{8,9},{9,8},{10,11... | collective-permute-start | bytes 10223624 | tf_op jit(solution)/shard_map/ppermute | solution.py:825
  159.0 36.1 %collective-permute-start.29 = (bf16[2,128,1664]{2,1,0:T(8,128)(2,1)}, bf16[2,128,1664]{2,1,0:T(8,128)(2,1)}, u32[]{:S(2)}, u32[]{:S(2)}) collective-permute-start(bf16[2,128,1664]{2,1,0:T(8,128)(2,1)} %collective-permute-done.20), channel_id=1, source_target_pairs={{2,0},{3,1},{4,6},{5,7},{10,8},{11,9},{12,14},{13,15},{18,16},{19,... | collective-permute-start | bytes 2555912 | tf_op jit(solution)/shard_map/ppermute | solution.py:825
  160.5 32.6 %collective-permute-start.30 = (bf16[1,192,640]{2,1,0:T(8,128)(2,1)}, bf16[1,192,640]{2,1,0:T(8,128)(2,1)}, u32[]{:S(2)}, u32[]{:S(2)}) collective-permute-start(bf16[1,192,640]{2,1,0:T(8,128)(2,1)} %get-tuple-element.388), channel_id=1, source_target_pairs={{0,5},{1,4},{2,7},{3,6},{4,1},{5,0},{6,3},{7,2},{8,13},{9,12},{10,... | collective-permute-start | bytes 737288 | tf_op jit(solution)/shard_map/ppermute | solution.py:825
  196.3 30.2 %collective-permute-start.33 = (bf16[2,128,1664]{2,1,0:T(8,128)(2,1)S(1)}, bf16[2,128,1664]{2,1,0:T(8,128)(2,1)S(1)}, u32[]{:S(2)}, u32[]{:S(2)}) collective-permute-start(bf16[2,128,1664]{2,1,0:T(8,128)(2,1)S(1)} %broadcast_select_fusion.1), channel_id=1, source_target_pairs={{0,8},{1,17},{2,10},{3,19},{4,12},{5,21},{6,14},{7,23},{8,0},{9,25... | collective-permute-start | bytes 2555912 | tf_op jit(solution)/shard_map/ppermute | solution.py:825
  227.6 31.1 %collective-permute-start.38 = (bf16[4,128,1664]{2,1,0:T(8,128)(2,1)S(1)}, bf16[4,128,1664]{2,1,0:T(8,128)(2,1)}, u32[]{:S(2)}, u32[]{:S(2)}) collective-permute-start(bf16[4,128,1664]{2,1,0:T(8,128)(2,1)S(1)} %pad_maximum_fusion.7), channel_id=1, source_target_pairs={{0,16},{1,9},{2,18},{3,11},{4,20},{5,13},{6,22},{7,15},{8,24},{9,1... | collective-permute-start | bytes 5111816 | tf_op jit(solution)/shard_map/ppermute | solution.py:825
  261.9 37.6 %collective-permute-start.42 = (bf16[8,128,1664]{2,1,0:T(8,128)(2,1)S(1)}, bf16[8,128,1664]{2,1,0:T(8,128)(2,1)}, u32[]{:S(2)}, u32[]{:S(2)}) collective-permute-start(bf16[8,128,1664]{2,1,0:T(8,128)(2,1)S(1)} %pad_maximum_fusion.1.half.slots_half.refs_2_), channel_id=1, source_target_pairs={{0,1},{1,0},{2,3},{3,2},{4,5},{5,4},{6,7},{7,6},{8,9},{9,8},{10,11... | collective-permute-start | bytes 10223624 | tf_op jit(solution)/shard_map/ppermute | solution.py:825
  261.9 37.6 %collective-permute-start.41 = (bf16[4,128,1664]{2,1,0:T(8,128)(2,1)}, bf16[4,128,1664]{2,1,0:T(8,128)(2,1)}, u32[]{:S(2)}, u32[]{:S(2)}) collective-permute-start(bf16[4,128,1664]{2,1,0:T(8,128)(2,1)} %pad_maximum_fusion.8), channel_id=1, source_target_pairs={{0,16},{1,9},{2,18},{3,11},{4,20},{5,13},{6,22},{7,15},{8,24},{9,1... | collective-permute-start | bytes 5111816 | tf_op jit(solution)/shard_map/ppermute | solution.py:825
  262.3 37.2 %collective-permute-start.40 = (bf16[2,128,1664]{2,1,0:T(8,128)(2,1)S(1)}, bf16[2,128,1664]{2,1,0:T(8,128)(2,1)}, u32[]{:S(2)}, u32[]{:S(2)}) collective-permute-start(bf16[2,128,1664]{2,1,0:T(8,128)(2,1)S(1)} %copy-done.47), channel_id=1, source_target_pairs={{2,0},{3,1},{4,6},{5,7},{10,8},{11,9},{12,14},{13,15},{18,16},{19,... | collective-permute-start | bytes 2555912 | tf_op jit(solution)/shard_map/ppermute | solution.py:825
  263.6 30.4 %collective-permute-start.43 = (bf16[1,192,1280]{2,1,0:T(8,128)(2,1)}, bf16[1,192,1280]{2,1,0:T(8,128)(2,1)}, u32[]{:S(2)}, u32[]{:S(2)}) collective-permute-start(bf16[1,192,1280]{2,1,0:T(8,128)(2,1)} %get-tuple-element.426), channel_id=1, source_target_pairs={{0,5},{1,4},{2,7},{3,6},{4,1},{5,0},{6,3},{7,2},{8,13},{9,12},{10,... | collective-permute-start | bytes 1474568 | tf_op jit(solution)/shard_map/ppermute | solution.py:825
  433.2 29.7 %collective-permute-start.55 = (bf16[4,128,1664]{2,1,0:T(8,128)(2,1)}, bf16[4,128,1664]{2,1,0:T(8,128)(2,1)}, u32[]{:S(2)}, u32[]{:S(2)}) collective-permute-start(bf16[4,128,1664]{2,1,0:T(8,128)(2,1)} %get-tuple-element.494), channel_id=1, source_target_pairs={{0,16},{1,9},{2,18},{3,11},{4,20},{5,13},{6,22},{7,15},{8,24},{9,1... | collective-permute-start | bytes 5111816 | tf_op jit(solution)/shard_map/ppermute | solution.py:825
  486.3 39.0 %collective-permute-start.63 = (bf16[8,128,1536]{2,1,0:T(8,128)(2,1)S(1)}, bf16[8,128,1536]{2,1,0:T(8,128)(2,1)S(1)}, u32[]{:S(2)}, u32[]{:S(2)}) collective-permute-start(bf16[8,128,1536]{2,1,0:T(8,128)(2,1)S(1)} %get-tuple-element.514), channel_id=1, source_target_pairs={{0,16},{1,9},{2,18},{3,11},{4,20},{5,13},{6,22},{7,15},{8,24},{9,1... | collective-permute-start | bytes 9437192 | tf_op jit(solution)/shard_map/ppermute | solution.py:825
  487.7 37.6 %collective-permute-start.64 = (bf16[1,192,1920]{2,1,0:T(8,128)(2,1)S(1)}, bf16[1,192,1920]{2,1,0:T(8,128)(2,1)S(1)}, u32[]{:S(2)}, u32[]{:S(2)}) collective-permute-start(bf16[1,192,1920]{2,1,0:T(8,128)(2,1)S(1)} %get-tuple-element.515), channel_id=1, source_target_pairs={{0,2},{1,3},{2,0},{3,1},{4,6},{5,7},{6,4},{7,5},{8,10},{9,11},{10,... | collective-permute-start | bytes 2211848 | tf_op jit(solution)/shard_map/ppermute | solution.py:825
  490.5 34.8 %collective-permute-start.62 = (bf16[128,1664]{1,0:T(8,128)(2,1)S(1)}, bf16[128,1664]{1,0:T(8,128)(2,1)S(1)}, u32[]{:S(2)}, u32[]{:S(2)}) collective-permute-start(bf16[128,1664]{1,0:T(8,128)(2,1)S(1)} %get-tuple-element.513), channel_id=1, source_target_pairs={{0,6},{1,7},{2,4},{3,5},{4,2},{5,3},{6,0},{7,1},{8,14},{9,15},{10,... | collective-permute-start | bytes 1277960 | tf_op jit(solution)/shard_map/ppermute | solution.py:825
  530.5 66.7 %collective-permute-start.65 = (bf16[4,128,1536]{2,1,0:T(8,128)(2,1)}, bf16[4,128,1536]{2,1,0:T(8,128)(2,1)}, u32[]{:S(2)}, u32[]{:S(2)}) collective-permute-start(bf16[4,128,1536]{2,1,0:T(8,128)(2,1)} %get-tuple-element.519), channel_id=1, source_target_pairs={{0,8},{1,17},{2,10},{3,19},{4,12},{5,21},{6,14},{7,23},{8,0},{9,25... | collective-permute-start | bytes 4718600 | tf_op jit(solution)/shard_map/ppermute | solution.py:825
  531.0 52.2 %collective-permute-start.66 = (bf16[1,192,1920]{2,1,0:T(8,128)(2,1)}, bf16[1,192,1920]{2,1,0:T(8,128)(2,1)S(1)}, u32[]{:S(2)}, u32[]{:S(2)}) collective-permute-start(bf16[1,192,1920]{2,1,0:T(8,128)(2,1)} %get-tuple-element.520), channel_id=1, source_target_pairs={{0,4},{1,5},{2,6},{3,7},{4,0},{5,1},{6,2},{7,3},{8,12},{9,13},{10,... | collective-permute-start | bytes 2211848 | tf_op jit(solution)/shard_map/ppermute | solution.py:825
  535.2 62.1 %collective-permute-start.67 = (bf16[1,192,1920]{2,1,0:T(8,128)(2,1)}, bf16[1,192,1920]{2,1,0:T(8,128)(2,1)}, u32[]{:S(2)}, u32[]{:S(2)}) collective-permute-start(bf16[1,192,1920]{2,1,0:T(8,128)(2,1)} %get-tuple-element.521), channel_id=1, source_target_pairs={{0,5},{1,4},{2,7},{3,6},{4,1},{5,0},{6,3},{7,2},{8,13},{9,12},{10,... | collective-permute-start | bytes 2211848 | tf_op jit(solution)/shard_map/ppermute | solution.py:825
  535.2 62.1 %collective-permute-start.68 = (bf16[1,192,1920]{2,1,0:T(8,128)(2,1)}, bf16[1,192,1920]{2,1,0:T(8,128)(2,1)}, u32[]{:S(2)}, u32[]{:S(2)}) collective-permute-start(bf16[1,192,1920]{2,1,0:T(8,128)(2,1)} %get-tuple-element.522), channel_id=1, source_target_pairs={{0,3},{1,2},{2,1},{3,0},{4,7},{5,6},{6,5},{7,4},{8,11},{9,10},{10,... | collective-permute-start | bytes 2211848 | tf_op jit(solution)/shard_map/ppermute | solution.py:825
  610.0 28.9 %collective-permute-start.74 = (bf16[8,48,3072]{2,1,0:T(8,128)(2,1)S(1)}, bf16[8,48,3072]{2,1,0:T(8,128)(2,1)S(1)}, u32[]{:S(2)}, u32[]{:S(2)}) collective-permute-start(bf16[8,48,3072]{2,1,0:T(8,128)(2,1)S(1)} %get-tuple-element.550), channel_id=1, source_target_pairs={{0,16},{1,9},{2,18},{3,11},{4,20},{5,13},{6,22},{7,15},{8,24},{9,1... | collective-permute-start | bytes 7077896 | tf_op jit(solution)/shard_map/ppermute | solution.py:825
  641.3 42.6 %collective-permute-start.75 = (bf16[4,48,3072]{2,1,0:T(8,128)(2,1)}, bf16[4,48,3072]{2,1,0:T(8,128)(2,1)}, u32[]{:S(2)}, u32[]{:S(2)}) collective-permute-start(bf16[4,48,3072]{2,1,0:T(8,128)(2,1)} %get-tuple-element.553), channel_id=1, source_target_pairs={{0,8},{1,17},{2,10},{3,19},{4,12},{5,21},{6,14},{7,23},{8,0},{9,25... | collective-permute-start | bytes 3538952 | tf_op jit(solution)/shard_map/ppermute | solution.py:825
  646.2 37.7 %collective-permute-start.76 = (bf16[2,128,1536]{2,1,0:T(8,128)(2,1)}, bf16[2,128,1536]{2,1,0:T(8,128)(2,1)}, u32[]{:S(2)}, u32[]{:S(2)}) collective-permute-start(bf16[2,128,1536]{2,1,0:T(8,128)(2,1)} %pad_maximum_fusion.18), channel_id=1, source_target_pairs={{0,2},{1,3},{6,4},{7,5},{8,10},{9,11},{14,12},{15,13},{16,18},{17,... | collective-permute-start | bytes 2359304 | tf_op jit(solution)/shard_map/ppermute | solution.py:825
  649.8 34.1 %collective-permute-start.78 = (bf16[1,192,1024]{2,1,0:T(8,128)(2,1)}, bf16[1,192,1024]{2,1,0:T(8,128)(2,1)}, u32[]{:S(2)}, u32[]{:S(2)}) collective-permute-start(bf16[1,192,1024]{2,1,0:T(8,128)(2,1)} %get-tuple-element.556), channel_id=1, source_target_pairs={{0,7},{1,6},{2,5},{3,4},{4,3},{5,2},{6,1},{7,0},{8,15},{9,14},{10,... | collective-permute-start | bytes 1179656 | tf_op jit(solution)/shard_map/ppermute | solution.py:825
  650.5 33.4 %collective-permute-start.77 = (bf16[1,192,896]{2,1,0:T(8,128)(2,1)}, bf16[1,192,896]{2,1,0:T(8,128)(2,1)}, u32[]{:S(2)}, u32[]{:S(2)}) collective-permute-start(bf16[1,192,896]{2,1,0:T(8,128)(2,1)} %get-tuple-element.555), channel_id=1, source_target_pairs={{0,6},{1,7},{2,4},{3,5},{4,2},{5,3},{6,0},{7,1},{8,14},{9,15},{10,... | collective-permute-start | bytes 1032200 | tf_op jit(solution)/shard_map/ppermute | solution.py:825
  689.9 42.1 %collective-permute-start.81 = (bf16[8,48,1152]{2,1,0:T(8,128)(2,1)S(1)}, bf16[8,48,1152]{2,1,0:T(8,128)(2,1)S(1)}, u32[]{:S(2)}, u32[]{:S(2)}) collective-permute-start(bf16[8,48,1152]{2,1,0:T(8,128)(2,1)S(1)} %get-tuple-element.570), channel_id=1, source_target_pairs={{0,16},{1,9},{2,18},{3,11},{4,20},{5,13},{6,22},{7,15},{8,24},{9,1... | collective-permute-start | bytes 2654216 | tf_op jit(solution)/shard_map/ppermute | solution.py:825
  690.9 41.1 %collective-permute-start.82 = (bf16[128,1536]{1,0:T(8,128)(2,1)S(1)}, bf16[128,1536]{1,0:T(8,128)(2,1)S(1)}, u32[]{:S(2)}, u32[]{:S(2)}) collective-permute-start(bf16[128,1536]{1,0:T(8,128)(2,1)S(1)} %fusion.28), channel_id=1, source_target_pairs={{0,2},{1,3},{2,0},{3,1},{4,6},{5,7},{6,4},{7,5},{8,10},{9,11},{10,... | collective-permute-start | bytes 1179656 | tf_op jit(solution)/shard_map/ppermute | solution.py:825
  (161 other events, 2249.6 us)
